TPU v7x, 32 devices: a whole 2x2x4 slice. The times are simulated.
32 devices in a mesh: shard: 8 (over y, x, core), rep: 4 (over z).
Axes of the slice: x: 2, y: 2, z: 4, core: 2. Of those that a mesh axis runs over, the one named last changes fastest.
Arguments:
- inputs: bfloat16 [4, 3, 512, 2048], P('rep', None, 'shard'), may hold values from -6 to 6
- ln1_gain: bfloat16 [2048], replicated, may hold values from 0.5 to 1.5
- ln1_bias: bfloat16 [2048], replicated, may hold values from -1.1953125 to 1.1953125
- w_query: bfloat16 [2048, 2048], P('shard'), may hold values from -0.125 to 0.125
- b_query: bfloat16 [2048], replicated, may hold values from -1.1953125 to 1.1953125
- w_key: bfloat16 [2048, 2048], P('shard'), may hold values from -0.125 to 0.125
- w_value: bfloat16 [2048, 2048], P('shard'), may hold values from -0.125 to 0.125
- b_value: bfloat16 [2048], replicated, may hold values from -1.1953125 to 1.1953125
- w_out: bfloat16 [2048, 2048], P('shard'), may hold values from -0.375 to 0.375
- b_out: bfloat16 [2048], replicated, may hold values from -1.1953125 to 1.1953125
- ln2_gain: bfloat16 [2048], replicated, may hold values from 0.5 to 1.5
- ln2_bias: bfloat16 [2048], replicated, may hold values from -1.1953125 to 1.1953125
- w_up: bfloat16 [2048, 8192], P('shard'), may hold values from -0.125 to 0.125
- b_up: bfloat16 [8192], replicated, may hold values from -1.1953125 to 1.1953125
- w_down: bfloat16 [8192, 2048], P('shard'), may hold values from -0.0625 to 0.0625
- b_down: bfloat16 [2048], replicated, may hold values from -1.1953125 to 1.1953125
- in_query: bfloat16 [8, 16, 2048], P(None, None, 'shard'), may hold values from -0.125 to 0.125
- out_query: bfloat16 [8, 16, 2048], P(None, None, 'shard'), may hold values from -0.75 to 0.75
- in_key: bfloat16 [8, 16, 2048], P(None, None, 'shard'), may hold values from -0.125 to 0.125
- out_key: bfloat16 [8, 16, 2048], P(None, None, 'shard'), may hold values from -0.75 to 0.75
- in_value: bfloat16 [8, 16, 2048], P(None, None, 'shard'), may hold values from -0.125 to 0.125
- out_value: bfloat16 [8, 16, 2048], P(None, None, 'shard'), may hold values from -0.75 to 0.75
- in_attn: bfloat16 [8, 16, 2048], P(None, None, 'shard'), may hold values from -0.125 to 0.125
- out_attn: bfloat16 [8, 16, 2048], P(None, None, 'shard'), may hold values from -0.75 to 0.75
- in_expand: bfloat16 [8, 16, 2048], P(None, None, 'shard'), may hold values from -0.125 to 0.125
- out_expand: bfloat16 [8, 16, 8192], P(None, None, 'shard'), may hold values from -0.75 to 0.75
- in_reduce: bfloat16 [8, 16, 8192], P(None, None, 'shard'), may hold values from -0.0625 to 0.0625
- out_reduce: bfloat16 [8, 16, 2048], P(None, None, 'shard'), may hold values from -0.75 to 0.75
- adapter_pick: int32 [4, 3], P('rep'), may hold values from 0 to 7
- piece_start: int32 [4, 3, 1], P('rep'), may hold values from 0 to 256, as said below
- cotangent: bfloat16 [4, 3, 512, 2048], P('rep', None, 'shard'), may hold values from -6 to 6
Outputs:
- layer_out: bfloat16 [4, 3, 512, 2048], P('rep', None, 'shard')
- input_grad: bfloat16 [4, 3, 512, 2048], P('rep', None, 'shard')
- grad_in_query: float32 [8, 16, 2048], P(None, None, 'shard')
- grad_out_query: float32 [8, 16, 2048], P(None, None, 'shard')
- grad_in_key: float32 [8, 16, 2048], P(None, None, 'shard')
- grad_out_key: float32 [8, 16, 2048], P(None, None, 'shard')
- grad_in_value: float32 [8, 16, 2048], P(None, None, 'shard')
- grad_out_value: float32 [8, 16, 2048], P(None, None, 'shard')
- grad_in_attn: float32 [8, 16, 2048], P(None, None, 'shard')
- grad_out_attn: float32 [8, 16, 2048], P(None, None, 'shard')
- grad_in_expand: float32 [8, 16, 2048], P(None, None, 'shard')
- grad_out_expand: float32 [8, 16, 8192], P(None, None, 'shard')
- grad_in_reduce: float32 [8, 16, 8192], P(None, None, 'shard')
- grad_out_reduce: float32 [8, 16, 2048], P(None, None, 'shard')
Inputs may be any that keep to these rules, and one draw needn't show every extreme that they name: `piece_start`: piece k (from 0) of a sequence starts within its own region of 512 positions beginning at k * 512, and ends inside that region unless the region is shorter than 256, in which case it runs to the sequence's end; pieces of one sequence never share a position.
All inputs are finite; a program needn't handle non-finite values.
Results may differ from a plain program's by a relative error of at most 0.023.
Values may be sent and summed in bfloat16 or wider, within the bound.
No kernel may reach another device: no remote copies, remote signals or barrier semaphores. Data moves between devices by JAX's collectives and lax.ppermute only.
A program may use at most 448 MiB of HBM per device.

v0:
```python
import jax
import jax.numpy as jnp
from jax import lax
from jax.sharding import PartitionSpec as P

HEADS = 16
HEAD = 128
ADAPTERS = 8
PIECE = 256


EPSILON = 1e-05
MASKED = -1e30


def layer_norm(values, gain_vec, shift_vec):
    centre = jnp.mean(values, axis=-1, keepdims=True)
    offset = values - centre
    spread = jnp.mean(offset * offset, axis=-1, keepdims=True)
    return offset * lax.rsqrt(spread + EPSILON) * gain_vec + shift_vec


def gelu_exact(values):
    return jax.nn.gelu(values, approximate=False)


def piece_labels(starts, positions):
    inside = (positions[:, None] >= starts[None, :]) & (
        positions[:, None] < starts[None, :] + PIECE
    )
    labels = jnp.arange(1, starts.shape[0] + 1, dtype=jnp.int32)
    return jnp.sum(jnp.where(inside, labels[None, :], 0), axis=1)


def visible(query_pos, key_pos, query_label, key_label):
    causal = key_pos[None, :] <= query_pos[:, None]
    shared = (query_label[:, None] == key_label[None, :]) & (query_label[:, None] > 0)
    return causal | shared


def split_heads(weight_matrix):
    return weight_matrix.reshape(weight_matrix.shape[0], HEADS, HEAD)


def masked_scores(queries, keys_all, allowed, factor):
    raw_scores = (
        jnp.einsum("qhd,khd->hqk", queries, keys_all, preferred_element_type=jnp.float32) * factor
    )
    return jnp.where(allowed[None], raw_scores, MASKED)


def project(hidden_states, weight_matrix):
    return jnp.einsum(
        "std,de->ste", hidden_states, weight_matrix, preferred_element_type=jnp.float32
    )


def project_back(grad_rows, weight_matrix):
    return jnp.einsum("ste,de->std", grad_rows, weight_matrix, preferred_element_type=jnp.float32)


def adapter_inner(hidden_states, entry_projection):
    return jnp.einsum(
        "std,srd->str", hidden_states, entry_projection, preferred_element_type=jnp.float32
    ).astype(jnp.bfloat16)


def adapter_term(adapter_rank_size, leave_map):
    return jnp.einsum(
        "str,sre->ste", adapter_rank_size, leave_map, preferred_element_type=jnp.float32
    )


def adapter_back(adapter_rank_size, hidden_states, grad_rows, entry_projection, leave_map):
    grad_leave = jnp.einsum(
        "str,ste->sre", adapter_rank_size, grad_rows, preferred_element_type=jnp.float32
    )
    grad_inner = jnp.einsum(
        "ste,sre->str", grad_rows, leave_map, preferred_element_type=jnp.float32
    ).astype(jnp.bfloat16)
    grad_enter = jnp.einsum(
        "str,std->srd", grad_inner, hidden_states, preferred_element_type=jnp.float32
    )
    returned = jnp.einsum(
        "str,srd->std", grad_inner, entry_projection, preferred_element_type=jnp.float32
    )
    return (grad_enter, grad_leave, returned)


def on_device(
    inputs,
    ln1_gain,
    ln1_bias,
    w_query,
    b_query,
    w_key,
    w_value,
    b_value,
    w_out,
    b_out,
    ln2_gain,
    ln2_bias,
    w_up,
    b_up,
    w_down,
    b_down,
    in_query,
    out_query,
    in_key,
    out_key,
    in_value,
    out_value,
    in_attn,
    out_attn,
    in_expand,
    out_expand,
    in_reduce,
    out_reduce,
    adapter_pick,
    piece_start,
    cotangent,
):
    sequences = inputs.shape[1]
    tok_rows = inputs.shape[2]
    width = inputs.shape[3]
    length_all = tok_rows * lax.axis_size("shard")
    shard_index = lax.axis_index("shard")
    factor = HEAD ** (-0.5)
    features = inputs[0].astype(jnp.float32)
    chosen_ids = adapter_pick[0]
    starts_all = piece_start[0]
    pick_table = (chosen_ids[:, None] == jnp.arange(ADAPTERS, dtype=jnp.int32)[None, :]).astype(
        jnp.float32
    )
    query_pos = shard_index * tok_rows + jnp.arange(tok_rows, dtype=jnp.int32)
    key_pos = jnp.arange(length_all, dtype=jnp.int32)

    def select_rows(table):
        return jnp.stack(
            [
                lax.dynamic_index_in_dim(table, chosen_ids[which], 0, keepdims=False)
                for which in range(sequences)
            ]
        )

    def spread_out(grad_seq):
        return jnp.einsum("se,srw->erw", pick_table, grad_seq, precision=lax.Precision.HIGHEST)

    w_query_all, w_key_all, w_value_all, w_out_all = (
        lax.all_gather(w_query, "shard", axis=0, tiled=True),
        lax.all_gather(w_key, "shard", axis=0, tiled=True),
        lax.all_gather(w_value, "shard", axis=0, tiled=True),
        lax.all_gather(w_out, "shard", axis=0, tiled=True),
    )
    gathered = (
        lax.all_gather(in_query, "shard", axis=2, tiled=True),
        lax.all_gather(out_query, "shard", axis=2, tiled=True),
        lax.all_gather(in_key, "shard", axis=2, tiled=True),
        lax.all_gather(out_key, "shard", axis=2, tiled=True),
        lax.all_gather(in_value, "shard", axis=2, tiled=True),
        lax.all_gather(out_value, "shard", axis=2, tiled=True),
        lax.all_gather(in_attn, "shard", axis=2, tiled=True),
        lax.all_gather(out_attn, "shard", axis=2, tiled=True),
        lax.all_gather(in_expand, "shard", axis=2, tiled=True),
        lax.all_gather(out_expand, "shard", axis=2, tiled=True),
        lax.all_gather(in_reduce, "shard", axis=2, tiled=True),
        lax.all_gather(out_reduce, "shard", axis=2, tiled=True),
    )
    chosen = tuple((select_rows(table) for table in gathered))
    gain_one = ln1_gain.astype(jnp.float32)
    shift_one = ln1_bias.astype(jnp.float32)
    gain_two = ln2_gain.astype(jnp.float32)
    shift_two = ln2_bias.astype(jnp.float32)
    normed_one, norm_one_back = jax.vjp(
        lambda values: layer_norm(values, gain_one, shift_one), features
    )
    hidden_one = normed_one.astype(jnp.bfloat16)
    inner_query = adapter_inner(hidden_one, chosen[0])
    inner_key = adapter_inner(hidden_one, chosen[2])
    inner_value = adapter_inner(hidden_one, chosen[4])
    queries = (
        project(hidden_one, w_query_all)
        + b_query.astype(jnp.float32)
        + adapter_term(inner_query, chosen[1])
    ).astype(jnp.bfloat16)
    keys_mine = (project(hidden_one, w_key_all) + adapter_term(inner_key, chosen[3])).astype(
        jnp.bfloat16
    )
    values_mine = (
        project(hidden_one, w_value_all)
        + b_value.astype(jnp.float32)
        + adapter_term(inner_value, chosen[5])
    ).astype(jnp.bfloat16)
    keys_all, values_all = (
        lax.all_gather(keys_mine, "shard", axis=1, tiled=True),
        lax.all_gather(values_mine, "shard", axis=1, tiled=True),
    )
    masks = []
    mixed_rows = []
    log_totals = []
    for which in range(sequences):
        allowed = visible(
            query_pos,
            key_pos,
            piece_labels(starts_all[which], query_pos),
            piece_labels(starts_all[which], key_pos),
        )
        masks.append(allowed)
        scores = masked_scores(
            split_heads(queries[which]), split_heads(keys_all[which]), allowed, factor
        )
        row_top = jnp.max(scores, axis=-1, keepdims=True)
        exponent = jnp.exp(scores - row_top)
        row_total = jnp.sum(exponent, axis=-1, keepdims=True)
        weights_attn = (exponent / row_total).astype(jnp.bfloat16)
        mixed_heads = jnp.einsum(
            "hqk,khd->qhd",
            weights_attn,
            split_heads(values_all[which]),
            preferred_element_type=jnp.float32,
        )
        mixed_rows.append(mixed_heads.reshape(tok_rows, width))
        log_totals.append(row_top + jnp.log(row_total))
    attended = jnp.stack(mixed_rows).astype(jnp.bfloat16)
    inner_attn = adapter_inner(attended, chosen[6])
    branch = (
        project(attended, w_out_all)
        + b_out.astype(jnp.float32)
        + adapter_term(inner_attn, chosen[7])
    )
    residual = features + branch
    normed_two, norm_two_back = jax.vjp(
        lambda values: layer_norm(values, gain_two, shift_two), residual
    )
    hidden_two = normed_two.astype(jnp.bfloat16)
    w_up_all, w_down_all = (
        lax.all_gather(w_up, "shard", axis=0, tiled=True),
        lax.all_gather(w_down, "shard", axis=0, tiled=True),
    )
    inner_expand = adapter_inner(hidden_two, chosen[8])
    pre_act = (
        project(hidden_two, w_up_all)
        + b_up.astype(jnp.float32)
        + adapter_term(inner_expand, chosen[9])
    )
    activated_full, gelu_back = jax.vjp(gelu_exact, pre_act)
    activated = activated_full.astype(jnp.bfloat16)
    inner_reduce = adapter_inner(activated, chosen[10])
    output_rows = residual + (
        project(activated, w_down_all)
        + b_down.astype(jnp.float32)
        + adapter_term(inner_reduce, chosen[11])
    )
    layer_out = output_rows.astype(jnp.bfloat16)[None]
    w_up_back, w_down_back = (
        lax.all_gather(w_up, "shard", axis=0, tiled=True),
        lax.all_gather(w_down, "shard", axis=0, tiled=True),
    )
    grad_out = cotangent[0]
    reduce_enter, reduce_leave, reduce_back = adapter_back(
        inner_reduce, activated, grad_out, chosen[10], chosen[11]
    )
    grad_act = project_back(grad_out, w_down_back) + reduce_back
    grad_pre = gelu_back(grad_act)[0].astype(jnp.bfloat16)
    expand_enter, expand_leave, expand_back = adapter_back(
        inner_expand, hidden_two, grad_pre, chosen[8], chosen[9]
    )
    grad_hidden_two = project_back(grad_pre, w_up_back) + expand_back
    grad_residual = grad_out.astype(jnp.float32) + norm_two_back(grad_hidden_two)[0]
    grad_branch = grad_residual.astype(jnp.bfloat16)
    w_query_back, w_key_back, w_value_back, w_out_back = (
        lax.all_gather(w_query, "shard", axis=0, tiled=True),
        lax.all_gather(w_key, "shard", axis=0, tiled=True),
        lax.all_gather(w_value, "shard", axis=0, tiled=True),
        lax.all_gather(w_out, "shard", axis=0, tiled=True),
    )
    attn_enter, attn_leave, attn_back = adapter_back(
        inner_attn, attended, grad_branch, chosen[6], chosen[7]
    )
    grad_attended = (project_back(grad_branch, w_out_back) + attn_back).astype(jnp.bfloat16)
    grad_query_rows = []
    key_terms = []
    value_terms = []
    row_deltas = []
    for which in range(sequences):
        query_heads = split_heads(queries[which])
        key_heads = split_heads(keys_all[which])
        value_heads = split_heads(values_all[which])
        scores = masked_scores(query_heads, key_heads, masks[which], factor)
        probs_full = jnp.exp(scores - log_totals[which])
        grad_mix = split_heads(grad_attended[which])
        grad_probs = jnp.einsum(
            "qhd,khd->hqk", grad_mix, value_heads, preferred_element_type=jnp.float32
        )
        inner_sum = jnp.sum(probs_full * grad_probs, axis=-1, keepdims=True)
        grad_scores = (probs_full * (grad_probs - inner_sum)).astype(jnp.bfloat16)
        grad_query_heads = (
            jnp.einsum("hqk,khd->qhd", grad_scores, key_heads, preferred_element_type=jnp.float32)
            * factor
        )
        grad_query_rows.append(grad_query_heads.reshape(tok_rows, width))
        row_deltas.append(inner_sum[:, :, 0])
        probs_low = probs_full.astype(jnp.bfloat16)
        grad_key_part = (
            jnp.einsum("hqk,qhd->khd", grad_scores, query_heads, preferred_element_type=jnp.float32)
            * factor
        )
        grad_value_part = jnp.einsum(
            "hqk,qhd->khd", probs_low, grad_mix, preferred_element_type=jnp.float32
        )
        key_terms.append(grad_key_part.reshape(length_all, width))
        value_terms.append(grad_value_part.reshape(length_all, width))
    grad_queries = jnp.stack(grad_query_rows).astype(jnp.bfloat16)
    grad_key_sum, grad_value_sum = (
        lax.psum_scatter(
            jnp.stack(key_terms).astype(jnp.bfloat16), "shard", scatter_dimension=1, tiled=True
        ).astype(jnp.float32),
        lax.psum_scatter(
            jnp.stack(value_terms).astype(jnp.bfloat16), "shard", scatter_dimension=1, tiled=True
        ).astype(jnp.float32),
    )
    grad_keys = grad_key_sum.astype(jnp.bfloat16)
    grad_values = grad_value_sum.astype(jnp.bfloat16)
    query_enter, query_leave, query_back = adapter_back(
        inner_query, hidden_one, grad_queries, chosen[0], chosen[1]
    )
    key_enter, key_leave, key_back = adapter_back(
        inner_key, hidden_one, grad_keys, chosen[2], chosen[3]
    )
    value_enter, value_leave, value_back = adapter_back(
        inner_value, hidden_one, grad_values, chosen[4], chosen[5]
    )
    grad_hidden_one = (
        project_back(grad_queries, w_query_back)
        + project_back(grad_keys, w_key_back)
        + project_back(grad_values, w_value_back)
        + query_back
        + key_back
        + value_back
    )
    grad_input = grad_residual + norm_one_back(grad_hidden_one)[0]
    input_grad = grad_input.astype(jnp.bfloat16)[None]
    shares = (
        lax.psum_scatter(
            spread_out(query_enter).astype(jnp.bfloat16), "shard", scatter_dimension=2, tiled=True
        ).astype(jnp.float32),
        lax.psum_scatter(
            spread_out(query_leave).astype(jnp.bfloat16), "shard", scatter_dimension=2, tiled=True
        ).astype(jnp.float32),
        lax.psum_scatter(
            spread_out(key_enter).astype(jnp.bfloat16), "shard", scatter_dimension=2, tiled=True
        ).astype(jnp.float32),
        lax.psum_scatter(
            spread_out(key_leave).astype(jnp.bfloat16), "shard", scatter_dimension=2, tiled=True
        ).astype(jnp.float32),
        lax.psum_scatter(
            spread_out(value_enter).astype(jnp.bfloat16), "shard", scatter_dimension=2, tiled=True
        ).astype(jnp.float32),
        lax.psum_scatter(
            spread_out(value_leave).astype(jnp.bfloat16), "shard", scatter_dimension=2, tiled=True
        ).astype(jnp.float32),
        lax.psum_scatter(
            spread_out(attn_enter).astype(jnp.bfloat16), "shard", scatter_dimension=2, tiled=True
        ).astype(jnp.float32),
        lax.psum_scatter(
            spread_out(attn_leave).astype(jnp.bfloat16), "shard", scatter_dimension=2, tiled=True
        ).astype(jnp.float32),
        lax.psum_scatter(
            spread_out(expand_enter).astype(jnp.bfloat16), "shard", scatter_dimension=2, tiled=True
        ).astype(jnp.float32),
        lax.psum_scatter(
            spread_out(expand_leave).astype(jnp.bfloat16), "shard", scatter_dimension=2, tiled=True
        ).astype(jnp.float32),
        lax.psum_scatter(
            spread_out(reduce_enter).astype(jnp.bfloat16), "shard", scatter_dimension=2, tiled=True
        ).astype(jnp.float32),
        lax.psum_scatter(
            spread_out(reduce_leave).astype(jnp.bfloat16), "shard", scatter_dimension=2, tiled=True
        ).astype(jnp.float32),
    )
    summed = (
        lax.psum(shares[0].astype(jnp.bfloat16), "rep").astype(jnp.float32),
        lax.psum(shares[1].astype(jnp.bfloat16), "rep").astype(jnp.float32),
        lax.psum(shares[2].astype(jnp.bfloat16), "rep").astype(jnp.float32),
        lax.psum(shares[3].astype(jnp.bfloat16), "rep").astype(jnp.float32),
        lax.psum(shares[4].astype(jnp.bfloat16), "rep").astype(jnp.float32),
        lax.psum(shares[5].astype(jnp.bfloat16), "rep").astype(jnp.float32),
        lax.psum(shares[6].astype(jnp.bfloat16), "rep").astype(jnp.float32),
        lax.psum(shares[7].astype(jnp.bfloat16), "rep").astype(jnp.float32),
        lax.psum(shares[8].astype(jnp.bfloat16), "rep").astype(jnp.float32),
        lax.psum(shares[9].astype(jnp.bfloat16), "rep").astype(jnp.float32),
        lax.psum(shares[10].astype(jnp.bfloat16), "rep").astype(jnp.float32),
        lax.psum(shares[11].astype(jnp.bfloat16), "rep").astype(jnp.float32),
    )
    return (
        layer_out,
        input_grad,
        summed[0],
        summed[1],
        summed[2],
        summed[3],
        summed[4],
        summed[5],
        summed[6],
        summed[7],
        summed[8],
        summed[9],
        summed[10],
        summed[11],
    )


def solution(mesh):
    in_specs = (
        P("rep", None, "shard", None),
        P(),
        P(),
        P("shard", None),
        P(),
        P("shard", None),
        P("shard", None),
        P(),
        P("shard", None),
        P(),
        P(),
        P(),
        P("shard", None),
        P(),
        P("shard", None),
        P(),
        P(None, None, "shard"),
        P(None, None, "shard"),
        P(None, None, "shard"),
        P(None, None, "shard"),
        P(None, None, "shard"),
        P(None, None, "shard"),
        P(None, None, "shard"),
        P(None, None, "shard"),
        P(None, None, "shard"),
        P(None, None, "shard"),
        P(None, None, "shard"),
        P(None, None, "shard"),
        P("rep", None),
        P("rep", None, None),
        P("rep", None, "shard", None),
    )
    out_specs = (
        P("rep", None, "shard", None),
        P("rep", None, "shard", None),
        P(None, None, "shard"),
        P(None, None, "shard"),
        P(None, None, "shard"),
        P(None, None, "shard"),
        P(None, None, "shard"),
        P(None, None, "shard"),
        P(None, None, "shard"),
        P(None, None, "shard"),
        P(None, None, "shard"),
        P(None, None, "shard"),
        P(None, None, "shard"),
        P(None, None, "shard"),
    )
    return jax.shard_map(
        on_device, mesh=mesh, in_specs=in_specs, out_specs=out_specs, check_vma=False
    )
```

profile of v0, /device:TPU:0, one launch (start us, length us, event | category | flops | bytes accessed | tf_op | source)
XLA Modules:
  0.0 1486.4 jit_solution(7457713230538145797)
XLA Ops:
  17.2 17.0 %all_gather.74 = bf16[8,16,2048]{2,1,0:T(8,128)(2,1)S(1)} all-gather(bf16[8,16,256]{2,1,0:T(8,128)(2,1)S(1)} %copy-done.117), channel_id=1, replica_groups=mesh['shard'=8,'rep'=4] {'shard'}, dimensions={2}, use_global_device_ids=true | all-gather | bytes 589824 | tf_op jit(solution)/shard_map/all_gather | solution.py:158
  48.0 21.3 %all-gather.17.cloned.1.call-done = bf16[2048,2048]{1,0:T(8,128)(2,1)} async-done(((bf16[256,2048]{1,0:T(8,128)(2,1)}), bf16[2048,2048]{1,0:T(8,128)(2,1)}) %all-gather.17.cloned.1.call-update) | async-done | bytes 8388624 | tf_op jit(solution)/shard_map/all_gather | solution.py:151
  102.3 25.6 %all-gather.11.cloned.1.call-done = bf16[2048,2048]{1,0:T(8,128)(2,1)} async-done(((bf16[256,2048]{1,0:T(8,128)(2,1)}), bf16[2048,2048]{1,0:T(8,128)(2,1)}) %all-gather.11.cloned.1.call-update) | async-done | bytes 8388624 | tf_op jit(solution)/shard_map/all_gather | solution.py:152
  232.4 17.5 %all-gather.15.cloned.1.call-done = bf16[2048,2048]{1,0:T(8,128)(2,1)} async-done(((bf16[256,2048]{1,0:T(8,128)(2,1)}), bf16[2048,2048]{1,0:T(8,128)(2,1)}) %all-gather.15.cloned.1.call-update) | async-done | bytes 8388624 | tf_op jit(solution)/shard_map/all_gather | solution.py:150
  256.6 41.0 %all-gather.19.cloned.1.call-done = bf16[3,512,2048]{2,1,0:T(8,128)(2,1)} async-done(((bf16[3,64,2048]{2,1,0:T(8,128)(2,1)}), bf16[3,512,2048]{2,1,0:T(8,128)(2,1)}) %all-gather.19.cloned.1.call-update) | async-done | bytes 6291472 | tf_op jit(solution)/shard_map/all_gather | solution.py:195
  305.7 39.8 %all-gather.13.cloned.1.call-done = bf16[3,512,2048]{2,1,0:T(8,128)(2,1)} async-done(((bf16[3,64,2048]{2,1,0:T(8,128)(2,1)}), bf16[3,512,2048]{2,1,0:T(8,128)(2,1)}) %all-gather.13.cloned.1.call-update) | async-done | bytes 6291472 | tf_op jit(solution)/shard_map/all_gather | solution.py:196
  375.0 26.7 %all-gather.21.cloned.1.call-done = bf16[2048,2048]{1,0:T(8,128)(2,1)} async-done(((bf16[256,2048]{1,0:T(8,128)(2,1)}), bf16[2048,2048]{1,0:T(8,128)(2,1)}) %all-gather.21.cloned.1.call-update) | async-done | bytes 8388624 | tf_op jit(solution)/shard_map/all_gather | solution.py:153
  410.0 154.3 %all-gather.23.cloned.1.call-done = bf16[2048,8192]{1,0:T(8,128)(2,1)} async-done(((bf16[256,8192]{1,0:T(8,128)(2,1)}), bf16[2048,8192]{1,0:T(8,128)(2,1)}) %all-gather.23.cloned.1.call-update) | async-done | bytes 33554448 | tf_op jit(solution)/shard_map/all_gather | solution.py:237
  564.3 16.4 %fusion.11 = f32[3,64,8192]{2,1,0:T(8,128)S(1)} fusion(bf16[3,64,2048]{2,1,0:T(8,128)(2,1)S(1)} %add_convert_fusion.2, bf16[2048,8192]{1,0:T(8,128)(2,1)} %all-gather.23.cloned.1.call-done, f32[8192]{0:T(1024)} %convert_element_type.259), kind=kOutput, calls=%fused_computation.10 | convolution fusion | flops 6444023808 | bytes 40665088 | tf_op jit(solution)/shard_map/std,de->ste/dot_general | solution.py:53
  587.1 139.5 %all-gather.27.cloned.1.call-done = bf16[8192,2048]{1,0:T(8,128)(2,1)} async-done(((bf16[1024,2048]{1,0:T(8,128)(2,1)}), bf16[8192,2048]{1,0:T(8,128)(2,1)}) %all-gather.27.cloned.1.call-update) | async-done | bytes 33554448 | tf_op jit(solution)/shard_map/all_gather | solution.py:238
  726.7 30.2 %add_convert_fusion = bf16[3,64,8192]{2,1,0:T(8,128)(2,1)S(1)} fusion(f32[3,64,8192]{2,1,0:T(8,128)} %fusion.187, bf16[8192,2048]{1,0:T(8,128)(2,1)} %all-gather.27.cloned.1.call-done, f32[3,64,8192]{2,1,0:T(8,128)} %get-tuple-element.129, bf16[1,3,64,2048]{3,2,1,0:T(8,128)(2,1)S(1)} %copy-done.22, u8[64,8192]{1,0:T(8,128)(4,1)} %get-tuple-element.43, ...), kind=kOutput, calls=%fused_computation.38 | convolution fusion | flops 6565134336 | bytes 51118080 | tf_op jit(solution)/shard_map/ste,de->std/dot_general | solution.py:59
  758.6 17.4 %fusion.4 = f32[3,64,2048]{2,1,0:T(8,128)} fusion(bf16[3,64,8192]{2,1,0:T(8,128)(2,1)S(1)} %add_convert_fusion, bf16[2048,8192]{1,0:T(8,128)(2,1)} %all-gather.23.cloned.1.call-done), kind=kOutput, calls=%fused_computation.4 | convolution fusion | flops 6442450944 | bytes 38273024 | tf_op jit(solution)/shard_map/ste,de->std/dot_general | solution.py:59
  985.5 33.3 %reduce-scatter.31.cloned.1.call-done = bf16[8,16,256]{2,0,1:T(8,128)(2,1)} async-done(((bf16[8,16,2048]{2,0,1:T(8,128)(2,1)}), bf16[8,16,256]{2,0,1:T(8,128)(2,1)}) %reduce-scatter.31.cloned.1.call-update) | async-done | bytes 65552 | tf_op jit(solution)/shard_map/reduce_scatter | solution.py:362
  1018.8 37.1 %reduce-scatter.35.cloned.1.call-done = bf16[8,16,256]{2,0,1:T(8,128)(2,1)} async-done(((bf16[8,16,2048]{2,0,1:T(8,128)(2,1)}), bf16[8,16,256]{2,0,1:T(8,128)(2,1)}) %reduce-scatter.35.cloned.1.call-update) | async-done | bytes 65552 | tf_op jit(solution)/shard_map/reduce_scatter | solution.py:368
  1055.9 37.1 %reduce-scatter.19.cloned.1.call-done = bf16[8,16,256]{2,0,1:T(8,128)(2,1)} async-done(((bf16[8,16,2048]{2,0,1:T(8,128)(2,1)}), bf16[8,16,256]{2,0,1:T(8,128)(2,1)}) %reduce-scatter.19.cloned.1.call-update) | async-done | bytes 65552 | tf_op jit(solution)/shard_map/reduce_scatter | solution.py:344
  1093.0 37.7 %reduce-scatter.21.cloned.1.call-done = bf16[8,16,256]{2,0,1:T(8,128)(2,1)} async-done(((bf16[8,16,2048]{2,0,1:T(8,128)(2,1)}), bf16[8,16,256]{2,0,1:T(8,128)(2,1)}) %reduce-scatter.21.cloned.1.call-update) | async-done | bytes 65552 | tf_op jit(solution)/shard_map/reduce_scatter | solution.py:347
  1130.7 37.1 %reduce-scatter.41.cloned.1.call-done = bf16[8,16,256]{2,0,1:T(8,128)(2,1)} async-done(((bf16[8,16,2048]{2,0,1:T(8,128)(2,1)}), bf16[8,16,256]{2,0,1:T(8,128)(2,1)}) %reduce-scatter.41.cloned.1.call-update) | async-done | bytes 65552 | tf_op jit(solution)/shard_map/reduce_scatter | solution.py:377
  1167.8 44.4 %reduce-scatter.37.cloned.1.call-done = bf16[8,16,1024]{2,0,1:T(8,128)(2,1)} async-done(((bf16[8,16,8192]{2,0,1:T(8,128)(2,1)}), bf16[8,16,1024]{2,0,1:T(8,128)(2,1)}) %reduce-scatter.37.cloned.1.call-update) | async-done | bytes 262160 | tf_op jit(solution)/shard_map/reduce_scatter | solution.py:371
  1212.2 44.3 %reduce-scatter.39.cloned.1.call-done = bf16[8,16,1024]{2,0,1:T(8,128)(2,1)} async-done(((bf16[8,16,8192]{2,0,1:T(8,128)(2,1)}), bf16[8,16,1024]{2,0,1:T(8,128)(2,1)}) %reduce-scatter.39.cloned.1.call-update) | async-done | bytes 262160 | tf_op jit(solution)/shard_map/reduce_scatter | solution.py:374
  1256.5 37.3 %reduce-scatter.27.cloned.1.call-done = bf16[8,16,256]{2,0,1:T(8,128)(2,1)} async-done(((bf16[8,16,2048]{2,0,1:T(8,128)(2,1)}), bf16[8,16,256]{2,0,1:T(8,128)(2,1)}) %reduce-scatter.27.cloned.1.call-update) | async-done | bytes 65552 | tf_op jit(solution)/shard_map/reduce_scatter | solution.py:356
  1293.7 37.2 %reduce-scatter.29.cloned.1.call-done = bf16[8,16,256]{2,0,1:T(8,128)(2,1)} async-done(((bf16[8,16,2048]{2,0,1:T(8,128)(2,1)}), bf16[8,16,256]{2,0,1:T(8,128)(2,1)}) %reduce-scatter.29.cloned.1.call-update) | async-done | bytes 65552 | tf_op jit(solution)/shard_map/reduce_scatter | solution.py:359
  1331.0 37.8 %reduce-scatter.23.cloned.1.call-done = bf16[8,16,256]{2,0,1:T(8,128)(2,1)} async-done(((bf16[8,16,2048]{2,0,1:T(8,128)(2,1)}), bf16[8,16,256]{2,0,1:T(8,128)(2,1)}) %reduce-scatter.23.cloned.1.call-update) | async-done | bytes 65552 | tf_op jit(solution)/shard_map/reduce_scatter | solution.py:350
  1368.8 37.1 %reduce-scatter.25.cloned.1.call-done = bf16[8,16,256]{2,0,1:T(8,128)(2,1)} async-done(((bf16[8,16,2048]{2,0,1:T(8,128)(2,1)}), bf16[8,16,256]{2,0,1:T(8,128)(2,1)}) %reduce-scatter.25.cloned.1.call-update) | async-done | bytes 65552 | tf_op jit(solution)/shard_map/reduce_scatter | solution.py:353
  1408.9 57.4 %all-reduce.3.cloned.1.call-done = (bf16[8,16,256]{2,0,1:T(8,128)(2,1)}, bf16[8,16,256]{2,0,1:T(8,128)(2,1)}, bf16[8,16,256]{2,0,1:T(8,128)(2,1)}, bf16[8,16,256...) async-done(((bf16[8,16,256]{2,0,1:T(8,128)(2,1)}, ...) | async-done | bytes 1179664 | tf_op jit(solution)/shard_map/psum | solution.py:382
  (621 shorter events, 437.2 us)
Async XLA Ops:
  8.0 120.0 %all-gather.11.cloned.1.call-start = ((), (), s32[]{:S(2)}) async-start(), calls=%async_computation.14 | async-start | bytes 9437184 | tf_op jit(solution)/shard_map/all_gather | solution.py:152
  8.7 215.9 %all-gather.29.cloned.1.call-start = ((), (), s32[]{:S(2)}) async-start(), calls=%async_computation.23 | async-start | bytes 2359296 | tf_op jit(solution)/shard_map/all_gather | solution.py:166
  9.5 220.9 %all-gather.25.cloned.1.call-start = ((), (), s32[]{:S(2)}) async-start(), calls=%async_computation.21 | async-start | bytes 2359296 | tf_op jit(solution)/shard_map/all_gather | solution.py:165
  10.0 239.8 %all-gather.15.cloned.1.call-start = ((), (), s32[]{:S(2)}) async-start(), calls=%async_computation.16 | async-start | bytes 9437184 | tf_op jit(solution)/shard_map/all_gather | solution.py:150
  10.6 287.0 %all-gather.19.cloned.1.call-start = ((), (), s32[]{:S(2)}) async-start(), calls=%async_computation.18 | async-start | bytes 7077888 | tf_op jit(solution)/shard_map/all_gather | solution.py:195
  75.9 269.5 %all-gather.13.cloned.1.call-start = ((), (), s32[]{:S(2)}) async-start(), calls=%async_computation.15 | async-start | bytes 7077888 | tf_op jit(solution)/shard_map/all_gather | solution.py:196
  134.6 267.2 %all-gather.21.cloned.1.call-start = ((), (), s32[]{:S(2)}) async-start(), calls=%async_computation.19 | async-start | bytes 9437184 | tf_op jit(solution)/shard_map/all_gather | solution.py:153
  135.3 429.0 %all-gather.23.cloned.1.call-start = ((), (), s32[]{:S(2)}) async-start(), calls=%async_computation.20 | async-start | bytes 37748736 | tf_op jit(solution)/shard_map/all_gather | solution.py:237
  136.2 590.5 %all-gather.27.cloned.1.call-start = ((), (), s32[]{:S(2)}) async-start(), calls=%async_computation.22 | async-start | bytes 37748736 | tf_op jit(solution)/shard_map/all_gather | solution.py:238
  136.8 798.7 %reduce-scatter.17.cloned.1.call-start = ((), (), s32[]{:S(2)}) async-start(), calls=%async_computation.25 | async-start | bytes 7077888 | tf_op jit(solution)/shard_map/reduce_scatter | solution.py:318
  817.7 126.8 %reduce-scatter.15.cloned.1.call-start = ((), (), s32[]{:S(2)}) async-start(), calls=%async_computation.24 | async-start | bytes 7077888 | tf_op jit(solution)/shard_map/reduce_scatter | solution.py:315
  860.4 125.1 %reduce-scatter.33.cloned.1.call-start = ((), (), s32[]{:S(2)}) async-start(), calls=%async_computation.33 | async-start | bytes 589824 | tf_op jit(solution)/shard_map/reduce_scatter | solution.py:365
  865.5 153.3 %reduce-scatter.31.cloned.1.call-start = ((), (), s32[]{:S(2)}) async-start(), calls=%async_computation.32 | async-start | bytes 589824 | tf_op jit(solution)/shard_map/reduce_scatter | solution.py:362
  872.8 183.1 %reduce-scatter.35.cloned.1.call-start = ((), (), s32[]{:S(2)}) async-start(), calls=%async_computation.34 | async-start | bytes 589824 | tf_op jit(solution)/shard_map/reduce_scatter | solution.py:368
  889.7 203.3 %reduce-scatter.19.cloned.1.call-start = ((), (), s32[]{:S(2)}) async-start(), calls=%async_computation.26 | async-start | bytes 589824 | tf_op jit(solution)/shard_map/reduce_scatter | solution.py:344
  896.7 233.9 %reduce-scatter.21.cloned.1.call-start = ((), (), s32[]{:S(2)}) async-start(), calls=%async_computation.27 | async-start | bytes 589824 | tf_op jit(solution)/shard_map/reduce_scatter | solution.py:347
  915.0 252.8 %reduce-scatter.41.cloned.1.call-start = ((), (), s32[]{:S(2)}) async-start(), calls=%async_computation.37 | async-start | bytes 589824 | tf_op jit(solution)/shard_map/reduce_scatter | solution.py:377
  919.9 292.3 %reduce-scatter.37.cloned.1.call-start = ((), (), s32[]{:S(2)}) async-start(), calls=%async_computation.35 | async-start | bytes 2359296 | tf_op jit(solution)/shard_map/reduce_scatter | solution.py:371
  927.4 329.1 %reduce-scatter.39.cloned.1.call-start = ((), (), s32[]{:S(2)}) async-start(), calls=%async_computation.36 | async-start | bytes 2359296 | tf_op jit(solution)/shard_map/reduce_scatter | solution.py:374
  935.4 358.3 %reduce-scatter.27.cloned.1.call-start = ((), (), s32[]{:S(2)}) async-start(), calls=%async_computation.30 | async-start | bytes 589824 | tf_op jit(solution)/shard_map/reduce_scatter | solution.py:356
  940.0 391.0 %reduce-scatter.29.cloned.1.call-start = ((), (), s32[]{:S(2)}) async-start(), calls=%async_computation.31 | async-start | bytes 589824 | tf_op jit(solution)/shard_map/reduce_scatter | solution.py:359
  943.2 425.6 %reduce-scatter.23.cloned.1.call-start = ((), (), s32[]{:S(2)}) async-start(), calls=%async_computation.28 | async-start | bytes 589824 | tf_op jit(solution)/shard_map/reduce_scatter | solution.py:350
  948.1 457.8 %reduce-scatter.25.cloned.1.call-start = ((), (), s32[]{:S(2)}) async-start(), calls=%async_computation.29 | async-start | bytes 589824 | tf_op jit(solution)/shard_map/reduce_scatter | solution.py:353
  966.8 499.5 %all-reduce.3.cloned.1.call-start = ((), (), s32[]{:S(2)}) async-start(), calls=%async_computation.38 | async-start | bytes 2359296 | tf_op jit(solution)/shard_map/psum | solution.py:382
  (187 other events, 3885.2 us)
Sparse Core Ops, SparseCore 0:
  9.9 59.2 all-gather.16
  71.1 56.7 all-gather.10
  129.9 30.4 all-gather.28
  194.1 55.6 all-gather.14
  252.2 45.3 all-gather.18
  300.1 45.3 all-gather.12
  347.4 54.3 all-gather.20
  403.6 160.5 all-gather.22
  566.0 160.6 all-gather.26
  817.8 61.6 reduce-scatter.16
  882.7 61.6 reduce-scatter.14
  947.5 34.1 reduce-scatter.32
  984.6 34.1 reduce-scatter.30
  1021.7 34.1 reduce-scatter.34
  1058.8 34.1 reduce-scatter.18
  1096.5 34.1 reduce-scatter.20
  1133.6 34.1 reduce-scatter.40
  1171.0 41.1 reduce-scatter.36
  1215.3 41.1 reduce-scatter.38
  1259.6 34.1 reduce-scatter.26
  1296.8 34.1 reduce-scatter.28
  1334.6 34.1 reduce-scatter.22
  1371.7 34.1 reduce-scatter.24
  1409.3 56.9 all-reduce.2
  (1 shorter events, 30.2 us)
where the time goes:
time: 1500 us; the launch traced here: 1490 us
  waiting for transfers between devices  950 us (63%)
  matrix products  239 us (16%)
  blocking collectives  129 us (9%)
  local copies, waits for them, and re-layouts  97.5 us (6%)
  other arithmetic  44.2 us (3%)
  between operations  24.7 us (2%)
    all_gather x1, waiting for transfers between devices, on_device(): lax.all_gather(w_up, 'shard', axis=0, tiled=True)  154 us
    all_gather x1, waiting for transfers between devices, on_device(): lax.all_gather(w_down, 'shard', axis=0, tiled=True)  140 us
    dot_general x6, matrix products, project_back(): jnp.einsum('ste,de->std', grad_rows, weight_matrix, preferred_element_typ...  69.7 us
    psum x1, waiting for transfers between devices, on_device(): lax.psum(shares[0].astype(jnp.bfloat16), 'rep').astype(jnp.float32)  57.4 us
    unnamed x404, local copies, waits for them, and re-layouts  52.7 us
    dot_general x6, matrix products, project(): jnp.einsum('std,de->ste', hidden_states, weight_matrix, preferred_element...  52.6 us
    reduce_scatter x1, waiting for transfers between devices, on_device(): lax.psum_scatter(spread_out(expand_leave).astype(jnp.bfloat16), 'shard',...  44.4 us
    reduce_scatter x1, waiting for transfers between devices, on_device(): lax.psum_scatter(spread_out(reduce_enter).astype(jnp.bfloat16), 'shard',...  44.3 us
  transfers between devices with their start and end apart: 25, of which 21 were waited for; matrix products, arithmetic and copies ran while one was open for 18% of the time, Pallas kernels for 0%

commit v1 on v0

v1 whole, which is shorter than its diff:
```python
import functools

import jax
import jax.numpy as jnp
import numpy as np
from jax import lax
from jax.experimental import pallas as pl
from jax.experimental.pallas import tpu as pltpu
from jax.sharding import PartitionSpec as P

HEADS = 16
HEAD = 128
ADAPTERS = 8
PIECE = 256

EPSILON = 1e-05
MASKED = -1e30
F32 = jnp.float32
BF16 = jnp.bfloat16


def layer_norm(values, gain_vec, shift_vec):
    centre = jnp.mean(values, axis=-1, keepdims=True)
    offset = values - centre
    spread = jnp.mean(offset * offset, axis=-1, keepdims=True)
    return offset * lax.rsqrt(spread + EPSILON) * gain_vec + shift_vec


def piece_labels(starts, positions):
    inside = (positions[:, None] >= starts[None, :]) & (
        positions[:, None] < starts[None, :] + PIECE
    )
    labels = jnp.arange(1, starts.shape[0] + 1, dtype=jnp.int32)
    return jnp.sum(jnp.where(inside, labels[None, :], 0), axis=1)


def mm(a, b):
    return lax.dot_general(a, b, (((1,), (0,)), ((), ())), preferred_element_type=F32)


def mm_t(a, b):
    return lax.dot_general(a, b, (((1,), (1,)), ((), ())), preferred_element_type=F32)


def t_mm(a, b):
    return lax.dot_general(a, b, (((0,), (0,)), ((), ())), preferred_element_type=F32)


def swap(value, axis, mask):
    size = lax.axis_size(axis)
    return lax.ppermute(value, axis, [(i, i ^ mask) for i in range(size)])


def bits_of(size):
    bits = []
    while (1 << len(bits)) < size:
        bits.append(1 << len(bits))
    return bits


def row_plan(size, rows, parts):
    masks, locs = [], []
    for core in (0, 1):
        for low, high, order in parts:
            group = [0]
            for bit in order:
                group = group + [m | bit for m in group]
            for mask in group:
                masks += [mask | core] * (high - low)
                locs += list(range(low, high))
    return np.array(masks, np.int32), np.array(locs, np.int32)


def spread_rows(value, parts):
    pieces = []
    for low, high, order in parts:
        current = value[low:high]
        for bit in order:
            current = jnp.concatenate([current, swap(current, "shard", bit)], 0)
        pieces.append(current)
    current = jnp.concatenate(pieces, 0) if len(pieces) > 1 else pieces[0]
    return jnp.concatenate([current, swap(current, "shard", 1)], 0)


def sum_rows(value, parts):
    def fold(current, bit):
        half = current.shape[0] // 2
        other = swap(current[half:].astype(BF16), "shard", bit)
        return current[:half].astype(F32) + other.astype(F32)

    current = fold(value, 1)
    done, start = [], 0
    for low, high, order in parts:
        count = (high - low) << len(order)
        piece = current[start : start + count]
        start += count
        for bit in reversed(order):
            piece = fold(piece.astype(BF16), bit)
        done.append(piece)
    return jnp.concatenate(done, 0) if len(done) > 1 else done[0]


def gather_blocks(value, axis):
    current = value[None]
    for bit in bits_of(lax.axis_size(axis)):
        current = jnp.concatenate([current, swap(current, axis, bit)], 0)
    return current


def place_kernel(me_ref, *refs, rows):
    pieces, out_ref, sems = refs[:-2], refs[-2], refs[-1]
    me = me_ref[0]
    copies = []
    for mask, piece in enumerate(pieces):
        copies.append(
            pltpu.make_async_copy(
                piece, out_ref.at[pl.ds(pl.multiple_of((me ^ mask) * rows, rows), rows)], sems.at[mask]
            )
        )
    for copy in copies:
        copy.start()
    for copy in copies:
        copy.wait()


def place_rows(me, pieces):
    rows, width = pieces[0].shape
    count = len(pieces)
    return pl.pallas_call(
        functools.partial(place_kernel, rows=rows),
        out_shape=jax.ShapeDtypeStruct((rows * count, width), pieces[0].dtype),
        in_specs=[pl.BlockSpec(memory_space=pltpu.SMEM)]
        + [pl.BlockSpec(memory_space=pl.ANY)] * count,
        out_specs=pl.BlockSpec(memory_space=pltpu.VMEM),
        scratch_shapes=[pltpu.SemaphoreType.DMA((count,))],
        cost_estimate=pl.CostEstimate(
            flops=0, bytes_accessed=4 * rows * count * width, transcendentals=0
        ),
        name="place_rows",
    )(me, *pieces)


def cols_kernel(me_ref, in_ref, out_ref):
    out_ref[...] = in_ref[0]


def place_columns(me, stacked):
    count, rows, width = stacked.shape
    return pl.pallas_call(
        cols_kernel,
        out_shape=jax.ShapeDtypeStruct((rows, count * width), stacked.dtype),
        grid_spec=pltpu.PrefetchScalarGridSpec(
            num_scalar_prefetch=1,
            grid=(count,),
            in_specs=[pl.BlockSpec((1, rows, width), lambda k, me: (me[0] ^ k, 0, 0))],
            out_specs=pl.BlockSpec((rows, width), lambda k, me: (0, k)),
        ),
        name="place_columns",
    )(me, stacked)


def seen(pos_q, pos_k, lab_q, lab_k):
    return (pos_k <= pos_q) | ((lab_q == lab_k) & (lab_q > 0))


def attend_kernel(pq, pk, lq, lk, qkv_ref, out_ref, lse_ref, *, heads, factor):
    allowed = seen(pq[...], pk[...], lq[...], lk[...])
    span = heads * HEAD
    for h in range(heads):
        q = qkv_ref[:, h * HEAD : (h + 1) * HEAD]
        k = qkv_ref[:, span + h * HEAD : span + (h + 1) * HEAD]
        v = qkv_ref[:, 2 * span + h * HEAD : 2 * span + (h + 1) * HEAD]
        scores = jnp.where(allowed, mm_t(q, k) * factor, MASKED)
        top = jnp.max(scores, axis=-1, keepdims=True)
        expo = jnp.exp(scores - top)
        total = jnp.sum(expo, axis=-1, keepdims=True)
        probs = (expo * (1.0 / total)).astype(BF16)
        out_ref[:, h * HEAD : (h + 1) * HEAD] = mm(probs, v).astype(BF16)
        lse_ref[:, h : h + 1] = top + jnp.log(total)


def attend(where, qkv, heads):
    length = qkv.shape[0]
    vmem = pl.BlockSpec(memory_space=pltpu.VMEM)
    return pl.pallas_call(
        functools.partial(attend_kernel, heads=heads, factor=HEAD ** (-0.5)),
        out_shape=(
            jax.ShapeDtypeStruct((length, heads * HEAD), BF16),
            jax.ShapeDtypeStruct((length, heads), F32),
        ),
        in_specs=[vmem] * 5,
        out_specs=(vmem, vmem),
        cost_estimate=pl.CostEstimate(
            flops=heads * length * length * HEAD * 4,
            bytes_accessed=length * heads * HEAD * 8,
            transcendentals=heads * length * length,
        ),
        name="attend",
    )(*where, qkv)


def attend_back_kernel(pq, pk, lq, lk, qkv_ref, lse_ref, ga_ref, out_ref, *, heads, factor):
    allowed = seen(pq[...], pk[...], lq[...], lk[...])
    span = heads * HEAD
    for h in range(heads):
        q = qkv_ref[:, h * HEAD : (h + 1) * HEAD]
        k = qkv_ref[:, span + h * HEAD : span + (h + 1) * HEAD]
        v = qkv_ref[:, 2 * span + h * HEAD : 2 * span + (h + 1) * HEAD]
        ga = ga_ref[:, h * HEAD : (h + 1) * HEAD]
        scores = jnp.where(allowed, mm_t(q, k) * factor, MASKED)
        probs = jnp.exp(scores - lse_ref[:, h : h + 1])
        grad_probs = mm_t(ga, v)
        inner = jnp.sum(probs * grad_probs, axis=-1, keepdims=True)
        grad_scores = (probs * (grad_probs - inner)).astype(BF16)
        low = probs.astype(BF16)
        out_ref[:, h * HEAD : (h + 1) * HEAD] = (mm(grad_scores, k) * factor).astype(BF16)
        out_ref[:, span + h * HEAD : span + (h + 1) * HEAD] = (
            t_mm(grad_scores, q) * factor
        ).astype(BF16)
        out_ref[:, 2 * span + h * HEAD : 2 * span + (h + 1) * HEAD] = t_mm(low, ga).astype(BF16)


def attend_back(where, qkv, lse, grad_attended, heads):
    length = qkv.shape[0]
    vmem = pl.BlockSpec(memory_space=pltpu.VMEM)
    return pl.pallas_call(
        functools.partial(attend_back_kernel, heads=heads, factor=HEAD ** (-0.5)),
        out_shape=jax.ShapeDtypeStruct((length, 3 * heads * HEAD), BF16),
        in_specs=[vmem] * 7,
        out_specs=vmem,
        cost_estimate=pl.CostEstimate(
            flops=heads * length * length * HEAD * 10,
            bytes_accessed=length * heads * HEAD * 14,
            transcendentals=heads * length * length,
        ),
        name="attend_back",
    )(*where, qkv, lse, grad_attended)


def on_device(
    inputs,
    ln1_gain,
    ln1_bias,
    w_query,
    b_query,
    w_key,
    w_value,
    b_value,
    w_out,
    b_out,
    ln2_gain,
    ln2_bias,
    w_up,
    b_up,
    w_down,
    b_down,
    in_query,
    out_query,
    in_key,
    out_key,
    in_value,
    out_value,
    in_attn,
    out_attn,
    in_expand,
    out_expand,
    in_reduce,
    out_reduce,
    adapter_pick,
    piece_start,
    cotangent,
):
    count = inputs.shape[1]
    rows = inputs.shape[2]
    size = lax.axis_size("shard")
    me = lax.axis_index("shard").astype(jnp.int32)
    me_arr = me[None]
    heads = HEADS // size
    span = heads * HEAD
    ff_part = w_up.shape[1] // size
    rank = in_query.shape[1]
    chosen = adapter_pick[0]
    starts = piece_start[0]

    def pick(table, which):
        return lax.dynamic_index_in_dim(table, chosen[which], 0, keepdims=False)

    upper = tuple(bits_of(size)[1:])
    half = rows // 2
    parts = [(0, half, upper), (half, rows, tuple(reversed(upper)))]
    masks, locs = row_plan(size, rows, parts)
    positions = (me ^ jnp.asarray(masks)) * rows + jnp.asarray(locs)
    wheres = []
    for s in range(count):
        labels = piece_labels(starts[s], positions)
        wheres.append((positions[:, None], positions[None, :], labels[:, None], labels[None, :]))

    def block(table, mask, width):
        return lax.dynamic_slice_in_dim(table, (me ^ mask) * width, width, 1)

    def turn(tables, width):
        pieces = []
        for mask in range(size):
            piece = [block(t, mask, width) for t in tables]
            piece = jnp.concatenate(piece, 1) if len(piece) > 1 else piece[0]
            pieces.append(swap(piece, "shard", mask) if mask else piece)
        return place_rows(me_arr, pieces)

    gain_one, shift_one = ln1_gain.astype(F32), ln1_bias.astype(F32)
    gain_two, shift_two = ln2_gain.astype(F32), ln2_bias.astype(F32)

    features = [inputs[0, s].astype(F32) for s in range(count)]
    hidden_one, norm_one_back = [], []
    for s in range(count):
        normed, back = jax.vjp(lambda v: layer_norm(v, gain_one, shift_one), features[s])
        norm_one_back.append(back)
        hidden_one.append(spread_rows(normed.astype(BF16), parts))

    mine = jnp.concatenate(
        [
            pick(t, s)
            for s in range(count)
            for t in (in_query, in_key, in_value, in_expand, out_attn, out_reduce)
        ],
        0,
    )
    whole = place_columns(me_arr, gather_blocks(mine, "shard"))
    whole = whole.reshape(count, 6 * rank, -1)
    in_qkv = [whole[s, : 3 * rank] for s in range(count)]
    in_exp = [whole[s, 3 * rank : 4 * rank] for s in range(count)]
    out_att = [whole[s, 4 * rank : 5 * rank] for s in range(count)]
    out_red = [whole[s, 5 * rank :] for s in range(count)]
    none = jnp.zeros((rank, span), BF16)
    out_qkv = [
        jnp.concatenate(
            [
                jnp.concatenate([pick(out_query, s), none, none], 1),
                jnp.concatenate([none, pick(out_key, s), none], 1),
                jnp.concatenate([none, none, pick(out_value, s)], 1),
            ],
            0,
        )
        for s in range(count)
    ]
    in_att = [pick(in_attn, s) for s in range(count)]
    out_exp = [pick(out_expand, s) for s in range(count)]
    in_red = [pick(in_reduce, s) for s in range(count)]

    w_qkv = turn([w_query, w_key, w_value], span)
    b_qkv = jnp.concatenate(
        [
            lax.dynamic_slice_in_dim(b_query, me * span, span).astype(F32),
            jnp.zeros((span,), F32),
            lax.dynamic_slice_in_dim(b_value, me * span, span).astype(F32),
        ]
    )
    b_up_mine = lax.dynamic_slice_in_dim(b_up, me * ff_part, ff_part).astype(F32)

    low_qkv, qkv, lses, attended, low_att, residual, norm_two_back, hidden_two = (
        [],
        [],
        [],
        [],
        [],
        [],
        [],
        [],
    )
    for s in range(count):
        low = mm_t(hidden_one[s], in_qkv[s]).astype(BF16)
        made = (mm(hidden_one[s], w_qkv) + mm(low, out_qkv[s]) + b_qkv).astype(BF16)
        att, lse = attend(wheres[s], made, heads)
        low_a = mm_t(att, in_att[s]).astype(BF16)
        part = (mm(att, w_out) + mm(low_a, out_att[s])).astype(BF16)
        branch = sum_rows(part, parts) + b_out.astype(F32)
        res = features[s] + branch
        normed, back = jax.vjp(lambda v: layer_norm(v, gain_two, shift_two), res)
        low_qkv.append(low)
        qkv.append(made)
        lses.append(lse)
        attended.append(att)
        low_att.append(low_a)
        residual.append(res)
        norm_two_back.append(back)
        hidden_two.append(spread_rows(normed.astype(BF16), parts))

    w_up_mine = turn([w_up], ff_part)
    grad_out = [spread_rows(cotangent[0, s], parts) for s in range(count)]
    grad_act, glow_red = [], []
    for s in range(count):
        glow = mm_t(grad_out[s], out_red[s]).astype(BF16)
        glow_red.append(glow)
        grad_act.append((mm_t(grad_out[s], w_down) + mm(glow, in_red[s])).astype(BF16))

    layer_rows, grad_residual, grad_branch = [], [], []
    g_in_red, g_out_red, g_in_exp, g_out_exp = [], [], [], []
    for s in range(count):
        low_e = mm_t(hidden_two[s], in_exp[s]).astype(BF16)
        pre = mm(hidden_two[s], w_up_mine) + mm(low_e, out_exp[s]) + b_up_mine
        act, gelu_back = jax.vjp(lambda v: jax.nn.gelu(v, approximate=False), pre)
        act = act.astype(BF16)
        grad_pre = gelu_back(grad_act[s].astype(F32))[0].astype(BF16)
        glow_e = mm_t(grad_pre, out_exp[s]).astype(BF16)
        part = (mm_t(grad_pre, w_up_mine) + mm(glow_e, in_exp[s])).astype(BF16)
        grad_two = sum_rows(part, parts)
        g_res = cotangent[0, s].astype(F32) + norm_two_back[s](grad_two)[0]
        grad_residual.append(g_res)
        grad_branch.append(spread_rows(g_res.astype(BF16), parts))
        low_r = mm_t(act, in_red[s]).astype(BF16)
        part = (mm(act, w_down) + mm(low_r, out_red[s])).astype(BF16)
        layer_rows.append(residual[s] + sum_rows(part, parts) + b_down.astype(F32))
        g_in_red.append(t_mm(glow_red[s], act))
        g_out_exp.append(t_mm(low_e, grad_pre))
        g_out_red.append(t_mm(low_r, grad_out[s]))
        g_in_exp.append(t_mm(glow_e, hidden_two[s]))

    input_rows = []
    g_out_att, g_in_att, g_in_qkv, g_out_qkv = [], [], [], []
    for s in range(count):
        glow_a = mm_t(grad_branch[s], out_att[s]).astype(BF16)
        grad_att = (mm_t(grad_branch[s], w_out) + mm(glow_a, in_att[s])).astype(BF16)
        grad_qkv = attend_back(wheres[s], qkv[s], lses[s], grad_att, heads)
        glow = mm_t(grad_qkv, out_qkv[s]).astype(BF16)
        part = (mm_t(grad_qkv, w_qkv) + mm(glow, in_qkv[s])).astype(BF16)
        grad_one = sum_rows(part, parts)
        input_rows.append(grad_residual[s] + norm_one_back[s](grad_one)[0])
        g_in_att.append(t_mm(glow_a, attended[s]))
        g_out_att.append(t_mm(low_att[s], grad_branch[s]))
        g_in_qkv.append(t_mm(glow, hidden_one[s]))
        full = t_mm(low_qkv[s], grad_qkv)
        g_out_qkv.append([full[t * rank : (t + 1) * rank, t * span : (t + 1) * span] for t in range(3)])

    def sum_columns(value):
        width = value.shape[1] // size

        def side(which):
            return jnp.stack(
                [
                    lax.dynamic_slice_in_dim(value, (2 * k + which) * width, width, 1)
                    for k in range(size // 2)
                ]
            )

        core = me & 1
        current = side(core).astype(F32) + swap(side(1 - core).astype(BF16), "shard", 1).astype(F32)
        for bit in reversed(upper):
            current = current.reshape((2, current.shape[0] // 2) + current.shape[1:])
            own = (me // bit) & 1
            current = lax.dynamic_index_in_dim(current, own, 0, False) + swap(
                lax.dynamic_index_in_dim(current, 1 - own, 0, False).astype(BF16), "shard", bit
            ).astype(F32)
        return current[0]

    table = (chosen[:, None] == jnp.arange(ADAPTERS, dtype=jnp.int32)[None, :]).astype(BF16)

    def over_groups(wide):
        flat = [w.reshape(-1, span).astype(BF16) for w in wide]
        mark = jnp.zeros((16, span), BF16).at[:count, :ADAPTERS].set(table)
        payload = jnp.concatenate(flat + [mark], 0)
        every = gather_blocks(payload, "rep")
        groups = every.shape[0]
        marks = every[:, -16:][:, :count, :ADAPTERS].reshape(groups * count, ADAPTERS)
        outs, start = [], 0
        for w, f in zip(wide, flat):
            taken = every[:, start : start + f.shape[0]]
            start += f.shape[0]
            taken = taken.reshape(groups * count, -1)
            out = lax.dot_general(
                marks, taken, (((0,), (0,)), ((), ())), preferred_element_type=F32
            )
            outs.append(out.reshape((ADAPTERS,) + w.shape[1:]))
        return outs

    first = sum_columns(jnp.concatenate(g_out_att + g_in_exp + g_out_red, 0))
    first = first.reshape(3, count, rank, span)
    s_in_att, s_in_red, s_out_exp, s_out_att, s_in_exp, s_out_red = over_groups(
        [
            jnp.stack(g_in_att),
            jnp.stack(g_in_red),
            jnp.stack(g_out_exp),
            first[0],
            first[1],
            first[2],
        ]
    )
    second = sum_columns(jnp.concatenate(g_in_qkv, 0)).reshape(count, 3, rank, span)
    late = over_groups(
        [second[:, t] for t in range(3)]
        + [jnp.stack([g_out_qkv[s][t] for s in range(count)]) for t in range(3)]
    )
    return (
        jnp.stack(layer_rows).astype(BF16)[None],
        jnp.stack(input_rows).astype(BF16)[None],
        late[0],
        late[3],
        late[1],
        late[4],
        late[2],
        late[5],
        s_in_att,
        s_out_att,
        s_in_exp,
        s_out_exp,
        s_in_red,
        s_out_red,
    )


def solution(mesh):
    row = P("shard", None)
    wide = P(None, None, "shard")
    acts = P("rep", None, "shard", None)
    in_specs = (
        (acts, P(), P(), row, P(), row, row, P(), row, P(), P(), P(), row, P(), row, P())
        + (wide,) * 12
        + (P("rep", None), P("rep", None, None), acts)
    )
    out_specs = (acts, acts) + (wide,) * 12
    return jax.shard_map(
        on_device, mesh=mesh, in_specs=in_specs, out_specs=out_specs, check_vma=False
    )
```

time: 1500 us -> 898 us (0.60)
  the two profiles are of different devices: /device:TPU:0 before, /device:TPU:24 now
where the time goes in v1:
time: 898 us; the launch traced here: 882 us
  waiting for transfers between devices  311 us (35%)
  matrix products  188 us (21%)
  local copies, waits for them, and re-layouts  134 us (15%)
  starting transfers between devices  129 us (14%)
  other arithmetic  68.2 us (8%)
  Pallas kernels  39.3 us (4%)
  between operations  13.4 us (1%)
    ppermute x147, waiting for transfers between devices, swap(): return lax.ppermute(value, axis, [(i, i ^ mask) for i in range(size)])  311 us
    ppermute x147, starting transfers between devices, swap(): return lax.ppermute(value, axis, [(i, i ^ mask) for i in range(size)])  129 us
    dot_general x36, matrix products, mm(): lax.dot_general(a, b, (((1,), (0,)), ((), ())), preferred_element_type=F32)  79.2 us
    dot_general x36, matrix products, mm_t(): lax.dot_general(a, b, (((1,), (1,)), ((), ())), preferred_element_type=F32)  76.8 us
    unnamed x648, local copies, waits for them, and re-layouts  72.7 us
    dot_general x24, matrix products, t_mm(): lax.dot_general(a, b, (((0,), (0,)), ((), ())), preferred_element_type=F32)  21.3 us
  transfers between devices with their start and end apart: 147, of which 73 were waited for; matrix products, arithmetic and copies ran while one was open for 33% of the time, Pallas kernels for 4%

profile of v1, /device:TPU:24, one launch (start us, length us, event | category | flops | bytes accessed | tf_op | source)
XLA Modules:
  0.0 882.2 jit_solution(3073560451126062898)
XLA Ops:
  72.4 9.9 %collective-permute-done.1 = bf16[64,2048]{1,0:T(8,128)(2,1)S(1)} collective-permute-done((bf16[64,2048]{1,0:T(8,128)(2,1)S(1)}, bf16[64,2048]{1,0:T(8,128)(2,1)S(1)}, u32[]{:S(2)}, u32[]{:S(2)}) %collective-permute-start.1) | collective-permute-done | bytes 262176 | tf_op jit(solution)/shard_map/ppermute | solution.py:51
  119.0 15.7 %collective-permute-done.8.refs_4_ = bf16[256,768]{1,0:T(8,128)(2,1)S(1)} collective-permute-done((bf16[256,768]{1,0:T(8,128)(2,1)S(1)}, bf16[256,768]{1,0:T(8,128)(2,1)S(1)}, u32[]{:S(2)}, u32[]{:S(2)}) %collective-permute-start.8) | collective-permute-done | bytes 393248 | tf_op jit(solution)/shard_map/ppermute | solution.py:51
  135.4 17.1 %collective-permute-done.9.refs_5_ = bf16[256,768]{1,0:T(8,128)(2,1)} collective-permute-done((bf16[256,768]{1,0:T(8,128)(2,1)S(1)}, bf16[256,768]{1,0:T(8,128)(2,1)}, u32[]{:S(2)}, u32[]{:S(2)}) %collective-permute-start.9) | collective-permute-done | bytes 393248 | tf_op jit(solution)/shard_map/ppermute | solution.py:51
  205.5 10.3 %collective-permute-done.19 = bf16[32,2048]{1,0:T(8,128)(2,1)S(1)} collective-permute-done((bf16[32,2048]{1,0:T(8,128)(2,1)S(1)}, bf16[32,2048]{1,0:T(8,128)(2,1)S(1)}, u32[]{:S(2)}, u32[]{:S(2)}) %collective-permute-start.19) | collective-permute-done | bytes 131104 | tf_op jit(solution)/shard_map/ppermute | solution.py:51
  235.1 7.8 collective-permute-done.27.refs_3_
  242.9 10.2 %collective-permute-done.26.refs_2_ = bf16[256,1024]{1,0:T(8,128)(2,1)} collective-permute-done((bf16[256,1024]{1,0:T(8,128)(2,1)S(1)}, bf16[256,1024]{1,0:T(8,128)(2,1)}, u32[]{:S(2)}, u32[]{:S(2)}) %collective-permute-start.26) | collective-permute-done | bytes 524320 | tf_op jit(solution)/shard_map/ppermute | solution.py:51
  254.3 10.2 %collective-permute-done.30.refs_6_ = bf16[256,1024]{1,0:T(8,128)(2,1)} collective-permute-done((bf16[256,1024]{1,0:T(8,128)(2,1)S(1)}, bf16[256,1024]{1,0:T(8,128)(2,1)}, u32[]{:S(2)}, u32[]{:S(2)}) %collective-permute-start.30) | collective-permute-done | bytes 524320 | tf_op jit(solution)/shard_map/ppermute | solution.py:51
  280.3 5.8 collective-permute-done.23
  297.7 7.8 multiply_convert_fusion.2
  305.5 8.4 fusion.5
  354.5 6.1 collective-permute-done.88
  409.9 5.8 collective-permute-done.93
  434.7 7.7 collective-permute-done.58
  459.5 6.1 collective-permute-done.60
  532.1 9.8 %collective-permute-done.68 = bf16[64,2048]{1,0:T(8,128)(2,1)S(1)} collective-permute-done((bf16[64,2048]{1,0:T(8,128)(2,1)S(1)}, bf16[64,2048]{1,0:T(8,128)(2,1)S(1)}, u32[]{:S(2)}, u32[]{:S(2)}) %collective-permute-start.68) | collective-permute-done | bytes 262176 | tf_op jit(solution)/shard_map/ppermute | solution.py:51
  554.8 7.5 collective-permute-done.50
  565.6 7.7 multiply_convert_fusion
  573.3 8.3 fusion.19
  585.9 7.3 multiply_convert_fusion.1
  593.2 8.5 fusion.12
  688.6 9.2 %collective-permute-done.128 = bf16[64,2048]{1,0:T(8,128)(2,1)S(1)} collective-permute-done((bf16[64,2048]{1,0:T(8,128)(2,1)S(1)}, bf16[64,2048]{1,0:T(8,128)(2,1)S(1)}, u32[]{:S(2)}, u32[]{:S(2)}) %collective-permute-start.128) | collective-permute-done | bytes 262176 | tf_op jit(solution)/shard_map/ppermute | solution.py:51
  711.4 6.9 collective-permute-done.110
  786.8 8.2 collective-permute-done.145
  797.9 16.0 %collective-permute-done.141 = bf16[2,304,256]{2,1,0:T(8,128)(2,1)S(1)} collective-permute-done((bf16[2,304,256]{2,1,0:T(8,128)(2,1)S(1)}, bf16[2,304,256]{2,1,0:T(8,128)(2,1)S(1)}, u32[]{:S(2)}, u32[]{:S(2)}) %collective-permute-start.141) | collective-permute-done | bytes 311328 | tf_op jit(solution)/shard_map/ppermute | solution.py:51
  (1328 shorter events, 650.7 us)
Async XLA Ops:
  20.6 50.9 %collective-permute-start.12 = (bf16[1,288,256]{2,1,0:T(8,128)(2,1)S(1)}, bf16[1,288,256]{2,1,0:T(8,128)(2,1)S(1)}, u32[]{:S(2)}, u32[]{:S(2)}) collective-permute-start(bf16[1,288,256]{2,1,0:T(8,128)(2,1)S(1)} %bitcast.801), channel_id=1, source_target_pairs={{0,4},{4,0},{8,12},{12,8},{16,20},{20,16},{24,28},{28,24},{1,5},{5... | collective-permute-start | bytes 442376 | tf_op jit(solution)/shard_map/ppermute | solution.py:51
  22.7 34.1 %collective-permute-start.99 = (bf16[32,2048]{1,0:T(8,128)(2,1)}, bf16[32,2048]{1,0:T(8,128)(2,1)S(1)}, u32[]{:S(2)}, u32[]{:S(2)}) collective-permute-start(bf16[32,2048]{1,0:T(8,128)(2,1)} %get-tuple-element.222), channel_id=1, source_target_pairs={{0,16},{4,20},{8,24},{12,28},{16,0},{20,4},{24,8},{28,12},{1,17},{... | collective-permute-start | bytes 393224 | tf_op jit(solution)/shard_map/ppermute | solution.py:51
  24.2 35.8 %collective-permute-start.97 = (bf16[32,2048]{1,0:T(8,128)(2,1)}, bf16[32,2048]{1,0:T(8,128)(2,1)}, u32[]{:S(2)}, u32[]{:S(2)}) collective-permute-start(bf16[32,2048]{1,0:T(8,128)(2,1)} %get-tuple-element.223), channel_id=1, source_target_pairs={{0,8},{4,12},{8,0},{12,4},{16,24},{20,28},{24,16},{28,20},{1,9},{5... | collective-permute-start | bytes 393224 | tf_op jit(solution)/shard_map/ppermute | solution.py:51
  25.7 37.5 %collective-permute-start.79 = (bf16[32,2048]{1,0:T(8,128)(2,1)}, bf16[32,2048]{1,0:T(8,128)(2,1)S(1)}, u32[]{:S(2)}, u32[]{:S(2)}) collective-permute-start(bf16[32,2048]{1,0:T(8,128)(2,1)} %get-tuple-element.224), channel_id=1, source_target_pairs={{0,16},{4,20},{8,24},{12,28},{16,0},{20,4},{24,8},{28,12},{1,17},{... | collective-permute-start | bytes 393224 | tf_op jit(solution)/shard_map/ppermute | solution.py:51
  26.2 39.2 %collective-permute-start.77 = (bf16[32,2048]{1,0:T(8,128)(2,1)}, bf16[32,2048]{1,0:T(8,128)(2,1)}, u32[]{:S(2)}, u32[]{:S(2)}) collective-permute-start(bf16[32,2048]{1,0:T(8,128)(2,1)} %get-tuple-element.225), channel_id=1, source_target_pairs={{0,8},{4,12},{8,0},{12,4},{16,24},{20,28},{24,16},{28,20},{1,9},{5... | collective-permute-start | bytes 393224 | tf_op jit(solution)/shard_map/ppermute | solution.py:51
  60.0 38.8 %collective-permute-start.117 = (bf16[32,2048]{1,0:T(8,128)(2,1)}, bf16[32,2048]{1,0:T(8,128)(2,1)S(1)}, u32[]{:S(2)}, u32[]{:S(2)}) collective-permute-start(bf16[32,2048]{1,0:T(8,128)(2,1)} %get-tuple-element.227), channel_id=1, source_target_pairs={{0,8},{4,12},{8,0},{12,4},{16,24},{20,28},{24,16},{28,20},{1,9},{5... | collective-permute-start | bytes 393224 | tf_op jit(solution)/shard_map/ppermute | solution.py:51
  65.4 36.0 %collective-permute-start.10 = (bf16[256,768]{1,0:T(8,128)(2,1)S(1)}, bf16[256,768]{1,0:T(8,128)(2,1)S(1)}, u32[]{:S(2)}, u32[]{:S(2)}) collective-permute-start(bf16[256,768]{1,0:T(8,128)(2,1)S(1)} %pad_maximum_fusion.14), channel_id=1, source_target_pairs={{0,24},{4,28},{8,16},{12,20},{16,8},{20,12},{24,0},{28,4},{1,25},{... | collective-permute-start | bytes 1179656 | tf_op jit(solution)/shard_map/ppermute | solution.py:51
  69.8 34.4 %collective-permute-start.5 = (bf16[256,768]{1,0:T(8,128)(2,1)S(1)}, bf16[256,768]{1,0:T(8,128)(2,1)S(1)}, u32[]{:S(2)}, u32[]{:S(2)}) collective-permute-start(bf16[256,768]{1,0:T(8,128)(2,1)S(1)} %copy-done.120), channel_id=1, source_target_pairs={{0,4},{4,0},{8,12},{12,8},{16,20},{20,16},{24,28},{28,24},{1,5},{5... | collective-permute-start | bytes 1179656 | tf_op jit(solution)/shard_map/ppermute | solution.py:51
  98.8 68.7 %collective-permute-start.4 = (bf16[256,2048]{1,0:T(8,128)(2,1)}, bf16[256,2048]{1,0:T(8,128)(2,1)}, u32[]{:S(2)}, u32[]{:S(2)}) collective-permute-start(bf16[256,2048]{1,0:T(8,128)(2,1)} %get-tuple-element.338), channel_id=1, source_target_pairs={{0,4},{4,0},{8,12},{12,8},{16,20},{20,16},{24,28},{28,24},{1,5},{5... | collective-permute-start | bytes 3145736 | tf_op jit(solution)/shard_map/ppermute | solution.py:51
  101.4 57.1 %collective-permute-start.14 = (bf16[4,288,256]{2,1,0:T(8,128)(2,1)}, bf16[4,288,256]{2,1,0:T(8,128)(2,1)}, u32[]{:S(2)}, u32[]{:S(2)}) collective-permute-start(bf16[4,288,256]{2,1,0:T(8,128)(2,1)} %pad_maximum_fusion.5), channel_id=1, source_target_pairs={{0,16},{4,20},{8,24},{12,28},{16,0},{20,4},{24,8},{28,12},{1,17},{... | collective-permute-start | bytes 1769480 | tf_op jit(solution)/shard_map/ppermute | solution.py:51
  108.8 43.7 %collective-permute-start.9 = (bf16[256,768]{1,0:T(8,128)(2,1)S(1)}, bf16[256,768]{1,0:T(8,128)(2,1)}, u32[]{:S(2)}, u32[]{:S(2)}) collective-permute-start(bf16[256,768]{1,0:T(8,128)(2,1)S(1)} %copy-done.116), channel_id=1, source_target_pairs={{0,20},{4,16},{8,28},{12,24},{16,4},{20,0},{24,12},{28,8},{1,21},{... | collective-permute-start | bytes 1179656 | tf_op jit(solution)/shard_map/ppermute | solution.py:51
  113.2 40.8 %collective-permute-start.11 = (bf16[256,768]{1,0:T(8,128)(2,1)S(1)}, bf16[256,768]{1,0:T(8,128)(2,1)}, u32[]{:S(2)}, u32[]{:S(2)}) collective-permute-start(bf16[256,768]{1,0:T(8,128)(2,1)S(1)} %copy-done.115), channel_id=1, source_target_pairs={{0,28},{4,24},{8,20},{12,16},{16,12},{20,8},{24,4},{28,0},{1,29},{... | collective-permute-start | bytes 1179656 | tf_op jit(solution)/shard_map/ppermute | solution.py:51
  135.4 93.2 %collective-permute-start.31 = (bf16[256,1024]{1,0:T(8,128)(2,1)}, bf16[256,1024]{1,0:T(8,128)(2,1)}, u32[]{:S(2)}, u32[]{:S(2)}) collective-permute-start(bf16[256,1024]{1,0:T(8,128)(2,1)} %get-tuple-element.99), channel_id=1, source_target_pairs={{0,28},{4,24},{8,20},{12,16},{16,12},{20,8},{24,4},{28,0},{1,29},{... | collective-permute-start | bytes 1572872 | tf_op jit(solution)/shard_map/ppermute | solution.py:51
  152.5 77.1 %collective-permute-start.29 = (bf16[256,1024]{1,0:T(8,128)(2,1)}, bf16[256,1024]{1,0:T(8,128)(2,1)}, u32[]{:S(2)}, u32[]{:S(2)}) collective-permute-start(bf16[256,1024]{1,0:T(8,128)(2,1)} %get-tuple-element.100), channel_id=1, source_target_pairs={{0,20},{4,16},{8,28},{12,24},{16,4},{20,0},{24,12},{28,8},{1,21},{... | collective-permute-start | bytes 1572872 | tf_op jit(solution)/shard_map/ppermute | solution.py:51
  196.1 37.3 %collective-permute-start.28 = (bf16[256,1024]{1,0:T(8,128)(2,1)S(1)}, bf16[256,1024]{1,0:T(8,128)(2,1)}, u32[]{:S(2)}, u32[]{:S(2)}) collective-permute-start(bf16[256,1024]{1,0:T(8,128)(2,1)S(1)} %copy-done.103), channel_id=1, source_target_pairs={{0,16},{4,20},{8,24},{12,28},{16,0},{20,4},{24,8},{28,12},{1,17},{... | collective-permute-start | bytes 1572872 | tf_op jit(solution)/shard_map/ppermute | solution.py:51
  230.5 34.0 %collective-permute-start.30 = (bf16[256,1024]{1,0:T(8,128)(2,1)S(1)}, bf16[256,1024]{1,0:T(8,128)(2,1)}, u32[]{:S(2)}, u32[]{:S(2)}) collective-permute-start(bf16[256,1024]{1,0:T(8,128)(2,1)S(1)} %copy-done.99), channel_id=1, source_target_pairs={{0,24},{4,28},{8,16},{12,20},{16,8},{20,12},{24,0},{28,4},{1,25},{... | collective-permute-start | bytes 1572872 | tf_op jit(solution)/shard_map/ppermute | solution.py:51
  233.4 36.0 %collective-permute-start.21 = (bf16[64,2048]{1,0:T(8,128)(2,1)}, bf16[64,2048]{1,0:T(8,128)(2,1)}, u32[]{:S(2)}, u32[]{:S(2)}) collective-permute-start(bf16[64,2048]{1,0:T(8,128)(2,1)} %pad_maximum_fusion.22), channel_id=1, source_target_pairs={{0,16},{4,20},{8,24},{12,28},{16,0},{20,4},{24,8},{28,12},{1,17},{... | collective-permute-start | bytes 786440 | tf_op jit(solution)/shard_map/ppermute | solution.py:51
  242.9 44.0 %collective-permute-start.101 = (bf16[256,2048]{1,0:T(8,128)(2,1)}, bf16[256,2048]{1,0:T(8,128)(2,1)}, u32[]{:S(2)}, u32[]{:S(2)}) collective-permute-start(bf16[256,2048]{1,0:T(8,128)(2,1)} %get-tuple-element.284), channel_id=1, source_target_pairs={{0,4},{4,0},{8,12},{12,8},{16,20},{20,16},{24,28},{28,24},{1,5},{5... | collective-permute-start | bytes 3145736 | tf_op jit(solution)/shard_map/ppermute | solution.py:51
  253.1 66.7 %collective-permute-start.121 = (bf16[256,2048]{1,0:T(8,128)(2,1)}, bf16[256,2048]{1,0:T(8,128)(2,1)}, u32[]{:S(2)}, u32[]{:S(2)}) collective-permute-start(bf16[256,2048]{1,0:T(8,128)(2,1)} %get-tuple-element.288), channel_id=1, source_target_pairs={{0,4},{4,0},{8,12},{12,8},{16,20},{20,16},{24,28},{28,24},{1,5},{5... | collective-permute-start | bytes 3145736 | tf_op jit(solution)/shard_map/ppermute | solution.py:51
  254.3 35.0 %collective-permute-start.81 = (bf16[256,2048]{1,0:T(8,128)(2,1)}, bf16[256,2048]{1,0:T(8,128)(2,1)}, u32[]{:S(2)}, u32[]{:S(2)}) collective-permute-start(bf16[256,2048]{1,0:T(8,128)(2,1)} %get-tuple-element.327), channel_id=1, source_target_pairs={{0,4},{4,0},{8,12},{12,8},{16,20},{20,16},{24,28},{28,24},{1,5},{5... | collective-permute-start | bytes 3145736 | tf_op jit(solution)/shard_map/ppermute | solution.py:51
  644.9 37.0 %collective-permute-start.56 = (bf16[32,2048]{1,0:T(8,128)(2,1)S(1)}, bf16[32,2048]{1,0:T(8,128)(2,1)S(1)}, u32[]{:S(2)}, u32[]{:S(2)}) collective-permute-start(bf16[32,2048]{1,0:T(8,128)(2,1)S(1)} %slice.1064), channel_id=1, source_target_pairs={{0,16},{4,20},{8,24},{12,28},{16,0},{20,4},{24,8},{28,12},{1,17},{... | collective-permute-start | bytes 393224 | tf_op jit(solution)/shard_map/ppermute | solution.py:51
  781.4 58.1 %collective-permute-start.112 = (bf16[256,2048]{1,0:T(8,128)(2,1)}, bf16[256,2048]{1,0:T(8,128)(2,1)}, u32[]{:S(2)}, u32[]{:S(2)}) collective-permute-start(bf16[256,2048]{1,0:T(8,128)(2,1)} %slice.1128), channel_id=1, source_target_pairs={{0,4},{4,0},{8,12},{12,8},{16,20},{20,16},{24,28},{28,24},{1,5},{5... | collective-permute-start | bytes 3145736 | tf_op jit(solution)/shard_map/ppermute | solution.py:51
  786.8 56.5 %collective-permute-start.132 = (bf16[256,2048]{1,0:T(8,128)(2,1)}, bf16[256,2048]{1,0:T(8,128)(2,1)}, u32[]{:S(2)}, u32[]{:S(2)}) collective-permute-start(bf16[256,2048]{1,0:T(8,128)(2,1)} %slice.1150), channel_id=1, source_target_pairs={{0,4},{4,0},{8,12},{12,8},{16,20},{20,16},{24,28},{28,24},{1,5},{5... | collective-permute-start | bytes 3145736 | tf_op jit(solution)/shard_map/ppermute | solution.py:51
  795.9 59.9 %collective-permute-start.146 = (bf16[2,592,256]{2,1,0:T(8,128)(2,1)}, bf16[2,592,256]{2,1,0:T(8,128)(2,1)S(1)}, u32[]{:S(2)}, u32[]{:S(2)}) collective-permute-start(bf16[2,592,256]{2,1,0:T(8,128)(2,1)} %pad_maximum_fusion.4), channel_id=1, source_target_pairs={{0,2},{1,3},{2,0},{3,1},{4,6},{5,7},{6,4},{7,5},{8,10},{9,11},{10,... | collective-permute-start | bytes 1818632 | tf_op jit(solution)/shard_map/ppermute | solution.py:51
  (379 other events, 4801.8 us)

commit v2 on v1

v2 whole, which is shorter than its diff:
```python
import functools

import jax
import jax.numpy as jnp
import numpy as np
from jax import lax
from jax.experimental import pallas as pl
from jax.experimental.pallas import tpu as pltpu
from jax.sharding import PartitionSpec as P

HEADS = 16
HEAD = 128
ADAPTERS = 8
PIECE = 256

EPSILON = 1e-05
MASKED = -1e30
F32 = jnp.float32
BF16 = jnp.bfloat16


def layer_norm(values, gain_vec, shift_vec):
    centre = jnp.mean(values, axis=-1, keepdims=True)
    offset = values - centre
    spread = jnp.mean(offset * offset, axis=-1, keepdims=True)
    return offset * lax.rsqrt(spread + EPSILON) * gain_vec + shift_vec


def piece_labels(starts, positions):
    inside = (positions[:, None] >= starts[None, :]) & (
        positions[:, None] < starts[None, :] + PIECE
    )
    labels = jnp.arange(1, starts.shape[0] + 1, dtype=jnp.int32)
    return jnp.sum(jnp.where(inside, labels[None, :], 0), axis=1)


def mm(a, b):
    return lax.dot_general(a, b, (((1,), (0,)), ((), ())), preferred_element_type=F32)


def mm_t(a, b):
    return lax.dot_general(a, b, (((1,), (1,)), ((), ())), preferred_element_type=F32)


def t_mm(a, b):
    return lax.dot_general(a, b, (((0,), (0,)), ((), ())), preferred_element_type=F32)


def swap(value, axis, mask):
    size = lax.axis_size(axis)
    return lax.ppermute(value, axis, [(i, i ^ mask) for i in range(size)])


def bits_of(size):
    bits = []
    while (1 << len(bits)) < size:
        bits.append(1 << len(bits))
    return bits


def subsets(bits):
    masks = [0]
    for bit in bits:
        masks = masks + [m | bit for m in masks]
    return masks


def gather_rows(block, bits):
    half = block.shape[0] // 2
    got = {0: [block]}
    upper, lower = {}, {}
    for bit in bits:
        there = swap(block, "shard", bit)
        got[bit] = [there]
        upper[bit], lower[bit] = there[:half], there[half:]
    for which, order in ((upper, bits), (lower, bits[::-1])):
        for k, bit in enumerate(order):
            for sub in subsets(order[:k])[1:]:
                which[sub | bit] = swap(which[sub], "shard", bit)
    pieces = []
    for mask in subsets(bits):
        pieces += got[mask] if mask in got else [upper[mask], lower[mask]]
    return jnp.concatenate(pieces, 0)


def scatter_rows(parts, bits):
    half = parts[0].shape[0] // 2
    upper = {m: p[:half] for m, p in parts.items()}
    lower = {m: p[half:] for m, p in parts.items()}
    for which, order in ((upper, bits), (lower, bits[::-1])):
        for k in reversed(range(len(order))):
            for sub in subsets(order[:k])[1:]:
                other = swap(which[sub | order[k]], "shard", order[k])
                which[sub] = (which[sub].astype(F32) + other.astype(F32)).astype(BF16)
    total = parts[0].astype(F32)
    for bit in bits:
        total = total + swap(jnp.concatenate([upper[bit], lower[bit]], 0), "shard", bit).astype(F32)
    return total


def gather_blocks(value, axis):
    current = value[None]
    for bit in bits_of(lax.axis_size(axis)):
        current = jnp.concatenate([current, swap(current, axis, bit)], 0)
    return current


def run_copies(copies):
    for copy in copies:
        copy.start()
    for copy in copies:
        copy.wait()


def place_kernel(me_ref, *refs, count, terms, width, rows, joined):
    pieces, outs, sems = refs[: 2 * count], refs[2 * count : -1], refs[-1]
    me = me_ref[0]

    def copies(core):
        made = []
        for side in range(2):
            for i in range(count):
                row = pl.multiple_of((me ^ (2 * i) ^ side) * rows, rows)
                piece = pieces[side * count + i]
                for term in range(terms):
                    for k in range(2):
                        own = k ^ core
                        source = piece.at[:, pl.ds((2 * term + k) * width, width)]
                        if joined:
                            target = outs[0].at[pl.ds(row, rows), pl.ds(own * width, width)]
                        else:
                            target = outs[own].at[pl.ds(row, rows), pl.ds(term * width, width)]
                        made.append(pltpu.make_async_copy(source, target, sems.at[len(made)]))
        return made

    @pl.when((me & 1) == 0)
    def _():
        run_copies(copies(0))

    @pl.when((me & 1) == 1)
    def _():
        run_copies(copies(1))


def place_weights(me, pieces, terms, width, joined):
    count = len(pieces) // 2
    rows = pieces[0].shape[0]
    if joined:
        shapes = [jax.ShapeDtypeStruct((rows * count * 2, 2 * width), BF16)]
    else:
        shapes = [jax.ShapeDtypeStruct((rows * count * 2, terms * width), BF16)] * 2
    return pl.pallas_call(
        functools.partial(
            place_kernel, count=count, terms=terms, width=width, rows=rows, joined=joined
        ),
        out_shape=shapes,
        in_specs=[pl.BlockSpec(memory_space=pltpu.SMEM)]
        + [pl.BlockSpec(memory_space=pl.ANY)] * (2 * count),
        out_specs=[pl.BlockSpec(memory_space=pltpu.VMEM)] * len(shapes),
        scratch_shapes=[pltpu.SemaphoreType.DMA((4 * count * terms,))],
        cost_estimate=pl.CostEstimate(
            flops=0, bytes_accessed=16 * rows * count * width * terms, transcendentals=0
        ),
        name="place_weights",
    )(me, *pieces)


def cols_kernel(me_ref, in_ref, out_ref, sems):
    count, _, width = in_ref.shape
    run_copies(
        [
            pltpu.make_async_copy(
                in_ref.at[mask],
                out_ref.at[:, pl.ds(pl.multiple_of((me_ref[0] ^ mask) * width, width), width)],
                sems.at[mask],
            )
            for mask in range(count)
        ]
    )


def place_columns(me, stacked):
    count, rows, width = stacked.shape
    return pl.pallas_call(
        cols_kernel,
        out_shape=jax.ShapeDtypeStruct((rows, count * width), stacked.dtype),
        in_specs=[pl.BlockSpec(memory_space=pltpu.SMEM), pl.BlockSpec(memory_space=pltpu.VMEM)],
        out_specs=pl.BlockSpec(memory_space=pltpu.VMEM),
        scratch_shapes=[pltpu.SemaphoreType.DMA((count,))],
        cost_estimate=pl.CostEstimate(
            flops=0, bytes_accessed=4 * count * rows * width, transcendentals=0
        ),
        name="place_columns",
    )(me, stacked)


def seen(pos_q, pos_k, lab_q, lab_k):
    return (pos_k <= pos_q) | ((lab_q == lab_k) & (lab_q > 0))


def both(own_ref, other_ref, low, high):
    own, other = own_ref[:, 0, :, low:high], other_ref[:, 0, :, low:high]
    chips, rows, width = own.shape
    return jnp.concatenate([own.reshape(chips * rows, width), other.reshape(chips * rows, width)], 0)


def put(own_ref, other_ref, low, high, value):
    chips, _, rows, _ = own_ref.shape
    half = chips * rows
    own_ref[:, 0, :, low:high] = value[:half].reshape(chips, rows, high - low)
    other_ref[:, 0, :, low:high] = value[half:].reshape(chips, rows, high - low)


def attend_kernel(pq, pk, lq, lk, own, other, out_own, out_other, lse_ref, *, heads, factor):
    allowed = seen(pq[...], pk[...], lq[0], lk[0])
    span = heads * HEAD
    for h in range(heads):
        low, high = h * HEAD, (h + 1) * HEAD
        q = both(own, other, low, high)
        k = both(own, other, span + low, span + high)
        v = both(own, other, 2 * span + low, 2 * span + high)
        scores = jnp.where(allowed, mm_t(q, k) * factor, MASKED)
        top = jnp.max(scores, axis=-1, keepdims=True)
        expo = jnp.exp(scores - top)
        total = jnp.sum(expo, axis=-1, keepdims=True)
        probs = (expo * (1.0 / total)).astype(BF16)
        put(out_own, out_other, low, high, mm(probs, v).astype(BF16))
        lse_ref[0, :, h : h + 1] = top + jnp.log(total)


def attend_specs(chips, count, rows, length):
    whole = pl.BlockSpec(memory_space=pltpu.VMEM)
    where = [
        pl.BlockSpec((length, 1), lambda s: (0, 0)),
        pl.BlockSpec((1, length), lambda s: (0, 0)),
        pl.BlockSpec((1, length, 1), lambda s: (s, 0, 0)),
        pl.BlockSpec((1, 1, length), lambda s: (s, 0, 0)),
    ]

    def of(width):
        return pl.BlockSpec((chips, 1, rows, width), lambda s: (0, s, 0, 0))

    return where, of


def attend(where, own, other, heads):
    chips, count, rows, _ = own.shape
    length = 2 * chips * rows
    span = heads * HEAD
    places, of = attend_specs(chips, count, rows, length)
    return pl.pallas_call(
        functools.partial(attend_kernel, heads=heads, factor=HEAD ** (-0.5)),
        out_shape=(
            jax.ShapeDtypeStruct((chips, count, rows, span), BF16),
            jax.ShapeDtypeStruct((chips, count, rows, span), BF16),
            jax.ShapeDtypeStruct((count, length, heads), F32),
        ),
        grid=(count,),
        in_specs=places + [of(3 * span), of(3 * span)],
        out_specs=(of(span), of(span), pl.BlockSpec((1, length, heads), lambda s: (s, 0, 0))),
        cost_estimate=pl.CostEstimate(
            flops=count * heads * length * length * HEAD * 4,
            bytes_accessed=count * length * heads * HEAD * 8,
            transcendentals=count * heads * length * length,
        ),
        name="attend",
    )(*where, own, other)


def attend_back_kernel(
    pq, pk, lq, lk, own, other, lse_ref, ga_own, ga_other, out_own, out_other, *, heads, factor
):
    allowed = seen(pq[...], pk[...], lq[0], lk[0])
    span = heads * HEAD
    for h in range(heads):
        low, high = h * HEAD, (h + 1) * HEAD
        q = both(own, other, low, high)
        k = both(own, other, span + low, span + high)
        v = both(own, other, 2 * span + low, 2 * span + high)
        ga = both(ga_own, ga_other, low, high)
        scores = jnp.where(allowed, mm_t(q, k) * factor, MASKED)
        probs = jnp.exp(scores - lse_ref[0, :, h : h + 1])
        grad_probs = mm_t(ga, v)
        inner = jnp.sum(probs * grad_probs, axis=-1, keepdims=True)
        grad_scores = (probs * (grad_probs - inner)).astype(BF16)
        put(out_own, out_other, low, high, (mm(grad_scores, k) * factor).astype(BF16))
        put(
            out_own,
            out_other,
            span + low,
            span + high,
            (t_mm(grad_scores, q) * factor).astype(BF16),
        )
        put(
            out_own,
            out_other,
            2 * span + low,
            2 * span + high,
            t_mm(probs.astype(BF16), ga).astype(BF16),
        )


def attend_back(where, own, other, lse, ga_own, ga_other, heads):
    chips, count, rows, _ = own.shape
    length = 2 * chips * rows
    span = heads * HEAD
    places, of = attend_specs(chips, count, rows, length)
    return pl.pallas_call(
        functools.partial(attend_back_kernel, heads=heads, factor=HEAD ** (-0.5)),
        out_shape=(jax.ShapeDtypeStruct((chips, count, rows, 3 * span), BF16),) * 2,
        grid=(count,),
        in_specs=places
        + [of(3 * span), of(3 * span)]
        + [pl.BlockSpec((1, length, heads), lambda s: (s, 0, 0)), of(span), of(span)],
        out_specs=(of(3 * span), of(3 * span)),
        cost_estimate=pl.CostEstimate(
            flops=count * heads * length * length * HEAD * 10,
            bytes_accessed=count * length * heads * HEAD * 14,
            transcendentals=count * heads * length * length,
        ),
        name="attend_back",
    )(*where, own, other, lse, ga_own, ga_other)


def on_device(
    inputs,
    ln1_gain,
    ln1_bias,
    w_query,
    b_query,
    w_key,
    w_value,
    b_value,
    w_out,
    b_out,
    ln2_gain,
    ln2_bias,
    w_up,
    b_up,
    w_down,
    b_down,
    in_query,
    out_query,
    in_key,
    out_key,
    in_value,
    out_value,
    in_attn,
    out_attn,
    in_expand,
    out_expand,
    in_reduce,
    out_reduce,
    adapter_pick,
    piece_start,
    cotangent,
):
    count, rows, wide = inputs.shape[1:]
    size = lax.axis_size("shard")
    chips = size // 2
    bits = bits_of(size)[1:]
    me = lax.axis_index("shard").astype(jnp.int32)
    me_arr = me[None]
    heads = HEADS // size
    span = heads * HEAD
    slice_wide = wide // size
    ff_part = w_up.shape[1] // size
    rank = in_query.shape[1]
    block = count * rows
    chosen = adapter_pick[0]
    starts = piece_start[0]

    def pick(table):
        return jnp.concatenate(
            [lax.dynamic_index_in_dim(table, chosen[s], 0, keepdims=False) for s in range(count)], 0
        )

    owners = np.concatenate([np.arange(chips) * 2, np.arange(chips) * 2 + 1]).astype(np.int32)
    locs = np.tile(np.arange(rows, dtype=np.int32), 2 * chips)
    positions = (me ^ jnp.asarray(np.repeat(owners, rows))) * rows + jnp.asarray(locs)
    labels = jnp.stack([piece_labels(starts[s], positions) for s in range(count)])
    where = (positions[:, None], positions[None, :], labels[:, :, None], labels[:, None, :])

    row_seq = np.tile(np.repeat(np.arange(count), rows), chips)

    def keep_own(value, terms=1):
        of_row = lax.broadcasted_iota(jnp.int32, value.shape, 0) // rows % count
        of_col = lax.broadcasted_iota(jnp.int32, value.shape, 1) // (terms * rank)
        return jnp.where(of_row == of_col, value, 0.0).astype(BF16)

    def with_other(value, axis=-1):
        return jnp.concatenate([value, swap(value, "shard", 1)], axis)

    gain_one, shift_one = ln1_gain.astype(F32), ln1_bias.astype(F32)
    gain_two, shift_two = ln2_gain.astype(F32), ln2_bias.astype(F32)

    features = inputs[0].reshape(block, wide).astype(F32)
    cot_mine = cotangent[0].reshape(block, wide)
    normed, norm_one_back = jax.vjp(lambda v: layer_norm(v, gain_one, shift_one), features)
    hidden_one = gather_rows(normed.astype(BF16), bits)

    chip = me // 2

    def turn(tables, width):
        own, other = [], []
        for i in range(chips):
            piece = [
                lax.dynamic_slice_in_dim(t, (chip ^ i) * 2 * width, 2 * width, 1) for t in tables
            ]
            piece = jnp.concatenate(piece, 1) if len(piece) > 1 else piece[0]
            own.append(swap(piece, "shard", 2 * i) if i else piece)
        for piece in own:
            other.append(swap(piece, "shard", 1))
        return own + other

    w_qkv_mine, w_qkv_other = place_weights(
        me_arr, turn([w_query, w_key, w_value], span), 3, span, False
    )

    mine = jnp.concatenate(
        [pick(t) for t in (in_query, in_key, in_value, in_expand, out_attn, out_reduce)], 0
    )
    whole = place_columns(me_arr, gather_blocks(mine, "shard")).reshape(6, count, rank, wide)
    in_qkv = jnp.swapaxes(whole[:3], 0, 1).reshape(count * 3 * rank, wide)
    in_exp, out_att, out_red = (whole[3 + i].reshape(count * rank, wide) for i in range(3))
    narrow = [pick(t) for t in (out_query, out_key, out_value, in_attn, out_expand, in_reduce)]
    packed = jnp.concatenate(narrow, 1)
    packed_other = swap(packed, "shard", 1)
    edges = np.cumsum([0] + [n.shape[1] for n in narrow])

    def unpack(table, i):
        return table[:, edges[i] : edges[i + 1]]

    def out_qkv_of(table):
        stacked = jnp.stack([unpack(table, t).reshape(count, rank, span) for t in range(3)], 1)
        spread = stacked[:, :, :, None, :] * jnp.eye(3, dtype=BF16)[None, :, None, :, None]
        return spread.reshape(count * 3 * rank, 3 * span)

    out_qkv_mine, out_qkv_other = out_qkv_of(packed), out_qkv_of(packed_other)
    in_att, out_exp, in_red = (
        jnp.concatenate([unpack(packed, i), unpack(packed_other, i)], 1) for i in (3, 4, 5)
    )

    def slice_of(bias, index, width):
        return lax.dynamic_slice_in_dim(bias, index * width, width).astype(F32)

    def b_qkv_of(index):
        return jnp.concatenate(
            [slice_of(b_query, index, span), jnp.zeros((span,), F32), slice_of(b_value, index, span)]
        )

    b_up_chip = jnp.concatenate([slice_of(b_up, me, ff_part), slice_of(b_up, me ^ 1, ff_part)])
    w_out_chip = with_other(w_out, 0)
    w_down_chip = with_other(w_down, 0)

    def by_chip(value):
        return value.reshape((chips, count, rows) + value.shape[1:])

    def flat(value):
        return value.reshape(chips * block, value.shape[-1])

    def project_back(value, low, weight, table, transposed):
        main = mm_t if transposed else mm
        parts = {}
        for i in reversed(range(chips)):
            at = slice(i * block, (i + 1) * block)
            parts[2 * i] = (main(value[at], weight) + mm(low[at], table)).astype(BF16)
        return scatter_rows(parts, bits)

    low_qkv = keep_own(mm_t(hidden_one, in_qkv), 3)
    qkv_away = (
        mm(hidden_one, w_qkv_other) + mm(low_qkv, out_qkv_other) + b_qkv_of(me ^ 1)
    ).astype(BF16)
    qkv_other = by_chip(swap(qkv_away, "shard", 1))
    qkv_own = by_chip(
        (mm(hidden_one, w_qkv_mine) + mm(low_qkv, out_qkv_mine) + b_qkv_of(me)).astype(BF16)
    )
    att_own, att_away, lse = attend(where, qkv_own, qkv_other, heads)
    attended = jnp.concatenate([flat(att_own), swap(flat(att_away), "shard", 1)], 1)
    low_att = keep_own(mm_t(attended, in_att))
    branch = project_back(attended, low_att, w_out_chip, out_att, False) + b_out.astype(F32)
    residual = features + branch
    normed, norm_two_back = jax.vjp(lambda v: layer_norm(v, gain_two, shift_two), residual)
    hidden_two = gather_rows(normed.astype(BF16), bits)

    (w_up_chip,) = place_weights(me_arr, turn([w_up], ff_part), 1, ff_part, True)
    cot = gather_rows(cot_mine, bits)
    glow_red = keep_own(mm_t(cot, out_red))
    grad_act = mm_t(cot, w_down_chip) + mm(glow_red, in_red)
    low_exp = keep_own(mm_t(hidden_two, in_exp))
    pre = mm(hidden_two, w_up_chip) + mm(low_exp, out_exp) + b_up_chip
    share = 0.5 * (1.0 + lax.erf(pre * np.float32(0.5**0.5)))
    act = (pre * share).astype(BF16)
    slope = share + pre * (jnp.exp(-0.5 * pre * pre) * np.float32((2 * np.pi) ** -0.5))
    grad_pre = (slope * grad_act).astype(BF16)
    glow_exp = keep_own(mm_t(grad_pre, out_exp))
    grad_two = project_back(grad_pre, glow_exp, w_up_chip, in_exp, True)
    grad_residual = cot_mine.astype(F32) + norm_two_back(grad_two)[0]
    grad_branch = gather_rows(grad_residual.astype(BF16), bits)

    low_red = keep_own(mm_t(act, in_red))
    down = project_back(act, low_red, w_down_chip, out_red, False)
    layer_rows = residual + down + b_down.astype(F32)

    glow_att = keep_own(mm_t(grad_branch, out_att))
    grad_att = (mm_t(grad_branch, w_out_chip) + mm(glow_att, in_att)).astype(BF16)
    ga_own = by_chip(grad_att[:, :span])
    ga_other = by_chip(swap(grad_att[:, span:], "shard", 1))
    grad_own, grad_away = attend_back(where, qkv_own, qkv_other, lse, ga_own, ga_other, heads)
    grad_own = flat(grad_own)
    grad_other = swap(flat(grad_away), "shard", 1)
    glow_qkv = keep_own(mm_t(grad_own, out_qkv_mine) + mm_t(grad_other, out_qkv_other), 3)
    parts = {}
    for i in reversed(range(chips)):
        at = slice(i * block, (i + 1) * block)
        parts[2 * i] = (
            mm_t(grad_own[at], w_qkv_mine)
            + mm_t(grad_other[at], w_qkv_other)
            + mm(glow_qkv[at], in_qkv)
        ).astype(BF16)
    grad_one = scatter_rows(parts, bits)
    input_rows = grad_residual + norm_one_back(grad_one)[0]

    def sum_columns(value):
        width = value.shape[1] // size

        def side(which):
            return jnp.stack(
                [
                    lax.dynamic_slice_in_dim(value, (2 * k + which) * width, width, 1)
                    for k in range(chips)
                ]
            )

        core = me & 1
        current = side(core).astype(F32) + swap(side(1 - core).astype(BF16), "shard", 1).astype(F32)
        for bit in bits[::-1]:
            current = current.reshape((2, current.shape[0] // 2) + current.shape[1:])
            own = (me // bit) & 1
            current = lax.dynamic_index_in_dim(current, own, 0, False) + swap(
                lax.dynamic_index_in_dim(current, 1 - own, 0, False).astype(BF16), "shard", bit
            ).astype(F32)
        return current[0]

    def sum_cores(own, away):
        return own + swap(away.astype(BF16), "shard", 1).astype(F32)

    def over_groups(terms):
        widths = [t.shape[1] for t in terms]
        data = jnp.concatenate([t.astype(BF16) for t in terms], 1)
        mark = (chosen[:, None] == jnp.arange(ADAPTERS, dtype=jnp.int32)[None, :]).astype(BF16)
        mark = jnp.pad(mark, ((0, 16 - count), (0, data.shape[1] - ADAPTERS)))
        every = gather_blocks(jnp.concatenate([data, mark], 0), "rep")
        groups = every.shape[0]
        marks = every[:, count * rank : count * rank + count, :ADAPTERS]
        marks = marks.reshape(groups * count, 1, ADAPTERS, 1)
        place = marks * jnp.eye(rank, dtype=BF16)[None, :, None, :]
        place = place.reshape(groups * count * rank, ADAPTERS * rank)
        taken = every[:, : count * rank].reshape(groups * count * rank, -1)
        outs, start = [], 0
        for width in widths:
            out = t_mm(place, taken[:, start : start + width])
            outs.append(out.reshape(ADAPTERS, rank, width))
            start += width
        return outs

    first = sum_columns(
        jnp.concatenate(
            [t_mm(low_att, grad_branch), t_mm(glow_exp, hidden_two), t_mm(low_red, cot)], 0
        )
    ).reshape(3, count * rank, slice_wide)
    chip_wide = jnp.concatenate(
        [t_mm(glow_att, attended), t_mm(glow_red, act), t_mm(low_exp, grad_pre)], 1
    )
    cut = [0, span, 2 * span, 2 * span + ff_part, 2 * span + 2 * ff_part, 2 * span + 3 * ff_part]
    cut.append(chip_wide.shape[1])
    side = [chip_wide[:, cut[i] : cut[i + 1]] for i in range(6)]
    local = sum_cores(jnp.concatenate(side[::2], 1), jnp.concatenate(side[1::2], 1))
    s_in_att, s_in_red, s_out_exp, s_out_att, s_in_exp, s_out_red = over_groups(
        [
            local[:, :span],
            local[:, span : span + ff_part],
            local[:, span + ff_part :],
            first[0],
            first[1],
            first[2],
        ]
    )

    second = sum_columns(t_mm(glow_qkv, hidden_one)).reshape(count, 3, rank, slice_wide)

    def own_terms(full):
        full = full.reshape(count, 3, rank, 3, span)
        return jnp.concatenate(
            [full[:, t, :, t].reshape(count * rank, span) for t in range(3)], 1
        )

    outer = sum_cores(own_terms(t_mm(low_qkv, grad_own)), own_terms(t_mm(low_qkv, grad_other)))
    late = over_groups(
        [second[:, t].reshape(count * rank, slice_wide) for t in range(3)]
        + [outer[:, t * span : (t + 1) * span] for t in range(3)]
    )
    shape = (1, count, rows, wide)
    return (
        layer_rows.astype(BF16).reshape(shape),
        input_rows.astype(BF16).reshape(shape),
        late[0],
        late[3],
        late[1],
        late[4],
        late[2],
        late[5],
        s_in_att,
        s_out_att,
        s_in_exp,
        s_out_exp,
        s_in_red,
        s_out_red,
    )


def solution(mesh):
    row = P("shard", None)
    wide = P(None, None, "shard")
    acts = P("rep", None, "shard", None)
    in_specs = (
        (acts, P(), P(), row, P(), row, row, P(), row, P(), P(), P(), row, P(), row, P())
        + (wide,) * 12
        + (P("rep", None), P("rep", None, None), acts)
    )
    out_specs = (acts, acts) + (wide,) * 12
    return jax.shard_map(
        on_device, mesh=mesh, in_specs=in_specs, out_specs=out_specs, check_vma=False
    )
```

time: 898 us -> 634 us (0.71)
  the two profiles are of different devices: /device:TPU:24 before, /device:TPU:0 now
where the time goes in v2:
time: 634 us; the launch traced here: 624 us
  waiting for transfers between devices  192 us (30%)
  matrix products  159 us (25%)
  local copies, waits for them, and re-layouts  109 us (17%)
  starting transfers between devices  55.7 us (9%)
  other arithmetic  53.5 us (8%)
  Pallas kernels  43.3 us (7%)
  between operations  11.5 us (2%)
    ppermute x68, waiting for transfers between devices, swap(): return lax.ppermute(value, axis, [(i, i ^ mask) for i in range(size)])  192 us
    dot_general x23, matrix products, mm_t(): lax.dot_general(a, b, (((1,), (1,)), ((), ())), preferred_element_type=F32)  65.4 us
    dot_general x32, matrix products, mm(): lax.dot_general(a, b, (((1,), (0,)), ((), ())), preferred_element_type=F32)  63.5 us
    ppermute x68, starting transfers between devices, swap(): return lax.ppermute(value, axis, [(i, i ^ mask) for i in range(size)])  55.7 us
    unnamed x429, local copies, waits for them, and re-layouts  53 us
    dot_general x21, matrix products, t_mm(): lax.dot_general(a, b, (((0,), (0,)), ((), ())), preferred_element_type=F32)  30.2 us
    pallas_call x2, Pallas kernels, place_weights(): pl.pallas_call(functools.partial(place_kernel, count=count, terms=terms,...  24.2 us
  transfers between devices with their start and end apart: 68, of which 28 were waited for; matrix products, arithmetic and copies ran while one was open for 37% of the time, Pallas kernels for 7%

profile of v2, /device:TPU:0, one launch (start us, length us, event | category | flops | bytes accessed | tf_op | source)
XLA Modules:
  0.0 624.1 jit_solution(8103269367645990287)
XLA Ops:
  80.0 22.4 %collective-permute-done.12 = bf16[2,288,256]{2,1,0:T(8,128)(2,1)S(1)} collective-permute-done((bf16[2,288,256]{2,1,0:T(8,128)(2,1)S(1)}, bf16[2,288,256]{2,1,0:T(8,128)(2,1)S(1)}, u32[]{:S(2)}, u32[]{:S(2)}) %collective-permute-start.12) | collective-permute-done | bytes 294944 | tf_op jit(solution)/shard_map/ppermute | solution.py:51
  115.7 20.0 %collective-permute-done.13 = bf16[4,288,256]{2,1,0:T(8,128)(2,1)S(1)} collective-permute-done((bf16[4,288,256]{2,1,0:T(8,128)(2,1)S(1)}, bf16[4,288,256]{2,1,0:T(8,128)(2,1)S(1)}, u32[]{:S(2)}, u32[]{:S(2)}) %collective-permute-start.13) | collective-permute-done | bytes 589856 | tf_op jit(solution)/shard_map/ppermute | solution.py:51
  145.8 13.2 %collective-permute-done.2 = bf16[96,2048]{1,0:T(8,128)(2,1)} collective-permute-done((bf16[96,2048]{1,0:T(8,128)(2,1)}, bf16[96,2048]{1,0:T(8,128)(2,1)}, u32[]{:S(2)}, u32[]{:S(2)}) %collective-permute-start.2) | collective-permute-done | bytes 393248 | tf_op jit(solution)/shard_map/ppermute | solution.py:51
  174.3 17.4 %place_weights.2 = (bf16[2048,768]{1,0:T(8,128)(2,1)}, bf16[2048,768]{1,0:T(8,128)(2,1)}) custom-call(s32[1]{0:T(128)} %bitcast.13.me_ref, bf16[256,1536]{1,0:T(8,128)(2,1)} %copy-done.33, bf16[256,1536]{1,0:T(8,128)(2,1)} %collective-permute-done.4.refs_1_, bf16[256,1536]{1,0:T(8,128)(2,1)} %collective-permute-done.5.refs_2_, ...), custom_call_target="tpu_custom_call" | custom-call | bytes 12582912 | tf_op jit(solution)/shard_map/place_weights/pallas_call | solution.py:152
  191.7 6.1 add_convert_fusion
  202.4 5.5 add_convert_fusion.1
  208.8 7.1 %attend.1 = (bf16[4,3,64,256]{3,2,1,0:T(8,128)(2,1)}, bf16[4,3,64,256]{3,2,1,0:T(8,128)(2,1)}, f32[3,512,2]{2,1,0:T(8,128)}) custom-call(s32[512,1]{1,0:T(8,128)} %copy.91.pq, s32[1,512]{1,0:T(1,128)} %bitcast.483, s32[3,512,1]{2,1,0:T(8,128)} %copy.92.lq, s32[3,1,512]{2,1,0:T(1,128)} %broadcast_in_dim.104.lk, bf16[4,3,64,768]{3,2,1,0:T(8,128)(2,1)} %bitcast.455, ...), custom_call_target="tpu_custom_call" | custom-call | flops 805306368 | bytes 3145728 | tf_op jit(solution)/shard_map/attend/pallas_call | solution.py:251
  227.5 25.6 %collective-permute-done.20 = bf16[96,2048]{1,0:T(8,128)(2,1)S(1)} collective-permute-done((bf16[96,2048]{1,0:T(8,128)(2,1)S(1)}, bf16[96,2048]{1,0:T(8,128)(2,1)S(1)}, u32[]{:S(2)}, u32[]{:S(2)}) %collective-permute-start.20) | collective-permute-done | bytes 393248 | tf_op jit(solution)/shard_map/ppermute | solution.py:51
  254.1 9.7 %collective-permute-done.18 = bf16[96,2048]{1,0:T(8,128)(2,1)S(1)} collective-permute-done((bf16[96,2048]{1,0:T(8,128)(2,1)S(1)}, bf16[96,2048]{1,0:T(8,128)(2,1)S(1)}, u32[]{:S(2)}, u32[]{:S(2)}) %collective-permute-start.18) | collective-permute-done | bytes 393248 | tf_op jit(solution)/shard_map/ppermute | solution.py:51
  265.6 8.1 %collective-permute-done.41 = bf16[96,2048]{1,0:T(8,128)(2,1)S(1)} collective-permute-done((bf16[96,2048]{1,0:T(8,128)(2,1)S(1)}, bf16[96,2048]{1,0:T(8,128)(2,1)S(1)}, u32[]{:S(2)}, u32[]{:S(2)}) %collective-permute-start.41) | collective-permute-done | bytes 393248 | tf_op jit(solution)/shard_map/ppermute | solution.py:51
  282.7 8.4 %collective-permute-done.19 = bf16[192,2048]{1,0:T(8,128)(2,1)S(1)} collective-permute-done((bf16[192,2048]{1,0:T(8,128)(2,1)S(1)}, bf16[192,2048]{1,0:T(8,128)(2,1)S(1)}, u32[]{:S(2)}, u32[]{:S(2)}) %collective-permute-start.19) | collective-permute-done | bytes 786464 | tf_op jit(solution)/shard_map/ppermute | solution.py:51
  301.7 6.7 %place_weights.3 = bf16[2048,2048]{1,0:T(8,128)(2,1)} custom-call(s32[1]{0:T(128)} %bitcast.13.me_ref, bf16[256,2048]{1,0:T(8,128)(2,1)} %get-tuple-element.34.refs_0_, bf16[256,2048]{1,0:T(8,128)(2,1)} %collective-permute-done.26.refs_1_, bf16[256,2048]{1,0:T(8,128)(2,1)} %collective-permute-done.27.refs_2_, bf16[256,2048]{1,0:T(8,128)(2,1)} %copy-done.59, ...), custom_call_target="tpu_custom_call" | custom-call | bytes 16777216 | tf_op jit(solution)/shard_map/place_weights/pallas_call | solution.py:152
  308.4 5.0 constant_dynamic-update-slice_fusion.36
  321.0 5.7 collective-permute-done.24
  333.4 12.1 %multiply_convert_fusion = (bf16[768,2048]{1,0:T(8,128)(2,1)}, f32[768,2048]{1,0:T(8,128)}) fusion(f32[2048]{0:T(1024)S(1)} %copy-done.152, f32[768,2048]{1,0:T(8,128)S(1)} %fusion.158, bf16[768,2048]{1,0:T(8,128)(2,1)} %copy-done.25, bf16[2048,2048]{1,0:T(8,128)(2,1)S(1)} %bitcast.392), kind=kOutput, calls=%fused_computation.7 | convolution fusion | flops 6453460992 | bytes 27271168 | tf_op jit(solution)/shard_map/dot_general | solution.py:38
  354.9 14.1 %fusion.5 = bf16[768,2048]{1,0:T(8,128)(2,1)} fusion(f32[768,2048]{1,0:T(8,128)} %get-tuple-element.151, f32[768,2048]{1,0:T(8,128)S(1)} %bitcast.396, bf16[768,2048]{1,0:T(8,128)(2,1)} %constant_dynamic-update-slice_fusion.38, bf16[2048,2048]{1,0:T(8,128)(2,1)} %constant_dynamic-update-slice_fusion.36), kind=kOutput, calls=%fused_computation.6 | convolution fusion | flops 6459752448 | bytes 27262976 | tf_op jit(solution)/shard_map/dot_general | solution.py:42
  380.3 5.4 fusion.35
  411.1 6.7 %collective-permute-done.42 = bf16[96,2048]{1,0:T(8,128)(2,1)S(1)} collective-permute-done((bf16[96,2048]{1,0:T(8,128)(2,1)S(1)}, bf16[96,2048]{1,0:T(8,128)(2,1)S(1)}, u32[]{:S(2)}, u32[]{:S(2)}) %collective-permute-start.42) | collective-permute-done | bytes 393248 | tf_op jit(solution)/shard_map/ppermute | solution.py:51
  425.1 9.6 %collective-permute-done.45 = bf16[192,2048]{1,0:T(8,128)(2,1)S(1)} collective-permute-done((bf16[192,2048]{1,0:T(8,128)(2,1)S(1)}, bf16[192,2048]{1,0:T(8,128)(2,1)S(1)}, u32[]{:S(2)}, u32[]{:S(2)}) %collective-permute-start.45) | collective-permute-done | bytes 786464 | tf_op jit(solution)/shard_map/ppermute | solution.py:51
  446.7 5.0 collective-permute-done.37
  455.4 6.8 %fusion.33 = bf16[192,2048]{1,0:T(8,128)(2,1)} fusion(f32[192,2048]{1,0:T(8,128)S(1)} %copy-done.5, f32[192,2048]{1,0:T(8,128)S(1)} %copy-done.48, bf16[2048,2048]{1,0:T(8,128)(2,1)} %constant_dynamic-update-slice_fusion.36, bf16[192,2048]{1,0:T(8,128)(2,1)} %collective-permute-done.37, bf16[192,2048]{1,0:T(8,128)(2,1)} %collective-permute-done.35, ...), kind=kOutput, calls=%fused_computation.53 | convolution fusion | flops 1614544896 | bytes 14688256 | tf_op jit(solution)/shard_map/dot_general | solution.py:38
  488.5 9.5 %attend_back.1 = (bf16[4,3,64,768]{3,2,1,0:T(8,128)(2,1)}, bf16[4,3,64,768]{3,2,1,0:T(8,128)(2,1)}) custom-call(s32[512,1]{1,0:T(8,128)} %copy.91.pq, s32[1,512]{1,0:T(1,128)} %bitcast.484, s32[3,512,1]{2,1,0:T(8,128)} %copy.92.lq, s32[3,1,512]{2,1,0:T(1,128)} %broadcast_in_dim.104.lk, bf16[4,3,64,768]{3,2,1,0:T(8,128)(2,1)} %bitcast.456, ...), custom_call_target="tpu_custom_call" | custom-call | flops 2013265920 | bytes 5505024 | tf_op jit(solution)/shard_map/attend_back/pallas_call | solution.py:308
  509.7 7.6 %collective-permute-done.66 = bf16[1,64,3072]{2,1,0:T(8,128)(2,1)S(1)} collective-permute-done((bf16[1,64,3072]{2,1,0:T(8,128)(2,1)S(1)}, bf16[1,64,3072]{2,1,0:T(8,128)(2,1)S(1)}, u32[]{:S(2)}, u32[]{:S(2)}) %collective-permute-start.66) | collective-permute-done | bytes 393248 | tf_op jit(solution)/shard_map/ppermute | solution.py:51
  580.6 13.8 %collective-permute-done.61 = bf16[2,64,1536]{2,1,0:T(8,128)(2,1)S(1)} collective-permute-done((bf16[2,64,1536]{2,1,0:T(8,128)(2,1)S(1)}, bf16[2,64,1536]{2,1,0:T(8,128)(2,1)S(1)}, u32[]{:S(2)}, u32[]{:S(2)}) %collective-permute-start.61) | collective-permute-done | bytes 393248 | tf_op jit(solution)/shard_map/ppermute | solution.py:51
  (804 shorter events, 361.2 us)
Async XLA Ops:
  5.4 99.9 %collective-permute-start = (bf16[192,2048]{1,0:T(8,128)(2,1)}, bf16[192,2048]{1,0:T(8,128)(2,1)}, u32[]{:S(2)}, u32[]{:S(2)}) collective-permute-start(bf16[192,2048]{1,0:T(8,128)(2,1)} %get-tuple-element.145), channel_id=1, source_target_pairs={{0,8},{4,12},{8,0},{12,4},{16,24},{20,28},{24,16},{28,20},{1,9},{5... | collective-permute-start | bytes 2359304 | tf_op jit(solution)/shard_map/ppermute | solution.py:51
  8.3 102.6 %collective-permute-start.1 = (bf16[192,2048]{1,0:T(8,128)(2,1)}, bf16[192,2048]{1,0:T(8,128)(2,1)S(1)}, u32[]{:S(2)}, u32[]{:S(2)}) collective-permute-start(bf16[192,2048]{1,0:T(8,128)(2,1)} %get-tuple-element.145), channel_id=1, source_target_pairs={{0,16},{4,20},{8,24},{12,28},{16,0},{20,4},{24,8},{28,12},{1,17},{... | collective-permute-start | bytes 2359304 | tf_op jit(solution)/shard_map/ppermute | solution.py:51
  28.9 47.8 %collective-permute-start.11 = (bf16[1,288,256]{2,1,0:T(8,128)(2,1)S(1)}, bf16[1,288,256]{2,1,0:T(8,128)(2,1)S(1)}, u32[]{:S(2)}, u32[]{:S(2)}) collective-permute-start(bf16[1,288,256]{2,1,0:T(8,128)(2,1)S(1)} %bitcast.447), channel_id=1, source_target_pairs={{0,4},{4,0},{8,12},{12,8},{16,20},{20,16},{24,28},{28,24},{1,5},{5... | collective-permute-start | bytes 442376 | tf_op jit(solution)/shard_map/ppermute | solution.py:51
  36.7 41.6 %collective-permute-start.14 = (bf16[48,3072]{1,0:T(8,128)(2,1)}, bf16[48,3072]{1,0:T(8,128)(2,1)}, u32[]{:S(2)}, u32[]{:S(2)}) collective-permute-start(bf16[48,3072]{1,0:T(8,128)(2,1)} %constant_dynamic-update-slice_fusion.23), channel_id=1, source_target_pairs={{0,4},{4,0},{8,12},{12,8},{16,20},{20,16},{24,28},{28,24},{1,5},{5... | collective-permute-start | bytes 884744 | tf_op jit(solution)/shard_map/ppermute | solution.py:51
  37.2 75.2 %collective-permute-start.38 = (bf16[192,2048]{1,0:T(8,128)(2,1)S(1)}, bf16[192,2048]{1,0:T(8,128)(2,1)}, u32[]{:S(2)}, u32[]{:S(2)}) collective-permute-start(bf16[192,2048]{1,0:T(8,128)(2,1)S(1)} %bitcast.403), channel_id=1, source_target_pairs={{0,8},{4,12},{8,0},{12,4},{16,24},{20,28},{24,16},{28,20},{1,9},{5... | collective-permute-start | bytes 2359304 | tf_op jit(solution)/shard_map/ppermute | solution.py:51
  76.7 84.1 %collective-permute-start.4 = (bf16[256,1536]{1,0:T(8,128)(2,1)}, bf16[256,1536]{1,0:T(8,128)(2,1)}, u32[]{:S(2)}, u32[]{:S(2)}) collective-permute-start(bf16[256,1536]{1,0:T(8,128)(2,1)} %pad_maximum_fusion.6), channel_id=1, source_target_pairs={{0,8},{4,12},{8,0},{12,4},{16,24},{20,28},{24,16},{28,20},{1,9},{5... | collective-permute-start | bytes 2359304 | tf_op jit(solution)/shard_map/ppermute | solution.py:51
  102.5 33.1 %collective-permute-start.13 = (bf16[4,288,256]{2,1,0:T(8,128)(2,1)S(1)}, bf16[4,288,256]{2,1,0:T(8,128)(2,1)S(1)}, u32[]{:S(2)}, u32[]{:S(2)}) collective-permute-start(bf16[4,288,256]{2,1,0:T(8,128)(2,1)S(1)} %pad_maximum_fusion.20), channel_id=1, source_target_pairs={{0,16},{4,20},{8,24},{12,28},{16,0},{20,4},{24,8},{28,12},{1,17},{... | collective-permute-start | bytes 1769480 | tf_op jit(solution)/shard_map/ppermute | solution.py:51
  105.2 56.0 %collective-permute-start.5 = (bf16[256,1536]{1,0:T(8,128)(2,1)}, bf16[256,1536]{1,0:T(8,128)(2,1)}, u32[]{:S(2)}, u32[]{:S(2)}) collective-permute-start(bf16[256,1536]{1,0:T(8,128)(2,1)} %pad_maximum_fusion.7), channel_id=1, source_target_pairs={{0,16},{4,20},{8,24},{12,28},{16,0},{20,4},{24,8},{28,12},{1,17},{... | collective-permute-start | bytes 2359304 | tf_op jit(solution)/shard_map/ppermute | solution.py:51
  110.9 50.4 %collective-permute-start.6 = (bf16[256,1536]{1,0:T(8,128)(2,1)}, bf16[256,1536]{1,0:T(8,128)(2,1)}, u32[]{:S(2)}, u32[]{:S(2)}) collective-permute-start(bf16[256,1536]{1,0:T(8,128)(2,1)} %pad_maximum_fusion.8), channel_id=1, source_target_pairs={{0,24},{4,28},{8,16},{12,20},{16,8},{20,12},{24,0},{28,4},{1,25},{... | collective-permute-start | bytes 2359304 | tf_op jit(solution)/shard_map/ppermute | solution.py:51
  112.4 46.6 %collective-permute-start.2 = (bf16[96,2048]{1,0:T(8,128)(2,1)}, bf16[96,2048]{1,0:T(8,128)(2,1)}, u32[]{:S(2)}, u32[]{:S(2)}) collective-permute-start(bf16[96,2048]{1,0:T(8,128)(2,1)} %slice.589), channel_id=1, source_target_pairs={{0,16},{4,20},{8,24},{12,28},{16,0},{20,4},{24,8},{28,12},{1,17},{... | collective-permute-start | bytes 1179656 | tf_op jit(solution)/shard_map/ppermute | solution.py:51
  159.0 57.0 %collective-permute-start.17 = (bf16[256,2048]{1,0:T(8,128)(2,1)}, bf16[256,2048]{1,0:T(8,128)(2,1)}, u32[]{:S(2)}, u32[]{:S(2)}) collective-permute-start(bf16[256,2048]{1,0:T(8,128)(2,1)} %param.41), channel_id=1, source_target_pairs={{0,4},{4,0},{8,12},{12,8},{16,20},{20,16},{24,28},{28,24},{1,5},{5... | collective-permute-start | bytes 3145736 | tf_op jit(solution)/shard_map/ppermute | solution.py:51
  169.4 139.0 %collective-permute-start.33 = (bf16[1024,2048]{1,0:T(8,128)(2,1)}, bf16[1024,2048]{1,0:T(8,128)(2,1)}, u32[]{:S(2)}, u32[]{:S(2)}) collective-permute-start(bf16[1024,2048]{1,0:T(8,128)(2,1)} %param.47), channel_id=1, source_target_pairs={{0,4},{4,0},{8,12},{12,8},{16,20},{20,16},{24,28},{28,24},{1,5},{5... | collective-permute-start | bytes 12582920 | tf_op jit(solution)/shard_map/ppermute | solution.py:51
  171.6 93.0 %collective-permute-start.26 = (bf16[256,2048]{1,0:T(8,128)(2,1)}, bf16[256,2048]{1,0:T(8,128)(2,1)}, u32[]{:S(2)}, u32[]{:S(2)}) collective-permute-start(bf16[256,2048]{1,0:T(8,128)(2,1)} %get-tuple-element.33), channel_id=1, source_target_pairs={{0,8},{4,12},{8,0},{12,4},{16,24},{20,28},{24,16},{28,20},{1,9},{5... | collective-permute-start | bytes 3145736 | tf_op jit(solution)/shard_map/ppermute | solution.py:51
  173.1 45.4 %collective-permute-start.40 = (bf16[96,2048]{1,0:T(8,128)(2,1)}, bf16[96,2048]{1,0:T(8,128)(2,1)}, u32[]{:S(2)}, u32[]{:S(2)}) collective-permute-start(bf16[96,2048]{1,0:T(8,128)(2,1)} %slice.635), channel_id=1, source_target_pairs={{0,16},{4,20},{8,24},{12,28},{16,0},{20,4},{24,8},{28,12},{1,17},{... | collective-permute-start | bytes 1179656 | tf_op jit(solution)/shard_map/ppermute | solution.py:51
  207.9 70.5 %collective-permute-start.27 = (bf16[256,2048]{1,0:T(8,128)(2,1)}, bf16[256,2048]{1,0:T(8,128)(2,1)}, u32[]{:S(2)}, u32[]{:S(2)}) collective-permute-start(bf16[256,2048]{1,0:T(8,128)(2,1)} %get-tuple-element.35), channel_id=1, source_target_pairs={{0,16},{4,20},{8,24},{12,28},{16,0},{20,4},{24,8},{28,12},{1,17},{... | collective-permute-start | bytes 3145736 | tf_op jit(solution)/shard_map/ppermute | solution.py:51
  218.5 60.0 %collective-permute-start.28 = (bf16[256,2048]{1,0:T(8,128)(2,1)S(1)}, bf16[256,2048]{1,0:T(8,128)(2,1)S(1)}, u32[]{:S(2)}, u32[]{:S(2)}) collective-permute-start(bf16[256,2048]{1,0:T(8,128)(2,1)S(1)} %copy-done.58), channel_id=1, source_target_pairs={{0,24},{4,28},{8,16},{12,20},{16,8},{20,12},{24,0},{28,4},{1,25},{... | collective-permute-start | bytes 3145736 | tf_op jit(solution)/shard_map/ppermute | solution.py:51
  386.6 32.3 %collective-permute-start.36 = (bf16[96,2048]{1,0:T(8,128)(2,1)}, bf16[96,2048]{1,0:T(8,128)(2,1)}, u32[]{:S(2)}, u32[]{:S(2)}) collective-permute-start(bf16[96,2048]{1,0:T(8,128)(2,1)} %get-tuple-element.75), channel_id=1, source_target_pairs={{0,8},{4,12},{8,0},{12,4},{16,24},{20,28},{24,16},{28,20},{1,9},{5... | collective-permute-start | bytes 1179656 | tf_op jit(solution)/shard_map/ppermute | solution.py:51
  420.9 30.7 %collective-permute-start.37 = (bf16[192,2048]{1,0:T(8,128)(2,1)}, bf16[192,2048]{1,0:T(8,128)(2,1)}, u32[]{:S(2)}, u32[]{:S(2)}) collective-permute-start(bf16[192,2048]{1,0:T(8,128)(2,1)} %pad_maximum_fusion.12), channel_id=1, source_target_pairs={{0,16},{4,20},{8,24},{12,28},{16,0},{20,4},{24,8},{28,12},{1,17},{... | collective-permute-start | bytes 2359304 | tf_op jit(solution)/shard_map/ppermute | solution.py:51
  423.8 31.6 %collective-permute-start.35 = (bf16[192,2048]{1,0:T(8,128)(2,1)}, bf16[192,2048]{1,0:T(8,128)(2,1)}, u32[]{:S(2)}, u32[]{:S(2)}) collective-permute-start(bf16[192,2048]{1,0:T(8,128)(2,1)} %pad_maximum_fusion.11), channel_id=1, source_target_pairs={{0,8},{4,12},{8,0},{12,4},{16,24},{20,28},{24,16},{28,20},{1,9},{5... | collective-permute-start | bytes 2359304 | tf_op jit(solution)/shard_map/ppermute | solution.py:51
  518.3 41.5 %collective-permute-start.67 = (bf16[2,64,3072]{2,1,0:T(8,128)(2,1)}, bf16[2,64,3072]{2,1,0:T(8,128)(2,1)}, u32[]{:S(2)}, u32[]{:S(2)}) collective-permute-start(bf16[2,64,3072]{2,1,0:T(8,128)(2,1)} %pad_maximum_fusion.17), channel_id=1, source_target_pairs={{0,2},{1,3},{2,0},{3,1},{4,6},{5,7},{6,4},{7,5},{8,10},{9,11},{10,... | collective-permute-start | bytes 2359304 | tf_op jit(solution)/shard_map/ppermute | solution.py:51
  534.9 32.9 %collective-permute-start.54 = (bf16[96,2048]{1,0:T(8,128)(2,1)}, bf16[96,2048]{1,0:T(8,128)(2,1)}, u32[]{:S(2)}, u32[]{:S(2)}) collective-permute-start(bf16[96,2048]{1,0:T(8,128)(2,1)} %get-tuple-element.69), channel_id=1, source_target_pairs={{0,8},{4,12},{8,0},{12,4},{16,24},{20,28},{24,16},{28,20},{1,9},{5... | collective-permute-start | bytes 1179656 | tf_op jit(solution)/shard_map/ppermute | solution.py:51
  543.5 33.8 %collective-permute-start.52 = (bf16[96,2048]{1,0:T(8,128)(2,1)}, bf16[96,2048]{1,0:T(8,128)(2,1)}, u32[]{:S(2)}, u32[]{:S(2)}) collective-permute-start(bf16[96,2048]{1,0:T(8,128)(2,1)} %get-tuple-element.68), channel_id=1, source_target_pairs={{0,16},{4,20},{8,24},{12,28},{16,0},{20,4},{24,8},{28,12},{1,17},{... | collective-permute-start | bytes 1179656 | tf_op jit(solution)/shard_map/ppermute | solution.py:51
  573.5 42.7 %collective-permute-start.55 = (bf16[192,2048]{1,0:T(8,128)(2,1)}, bf16[192,2048]{1,0:T(8,128)(2,1)}, u32[]{:S(2)}, u32[]{:S(2)}) collective-permute-start(bf16[192,2048]{1,0:T(8,128)(2,1)} %pad_maximum_fusion.16), channel_id=1, source_target_pairs={{0,16},{4,20},{8,24},{12,28},{16,0},{20,4},{24,8},{28,12},{1,17},{... | collective-permute-start | bytes 2359304 | tf_op jit(solution)/shard_map/ppermute | solution.py:51
  579.4 36.9 %collective-permute-start.53 = (bf16[192,2048]{1,0:T(8,128)(2,1)}, bf16[192,2048]{1,0:T(8,128)(2,1)}, u32[]{:S(2)}, u32[]{:S(2)}) collective-permute-start(bf16[192,2048]{1,0:T(8,128)(2,1)} %pad_maximum_fusion.15), channel_id=1, source_target_pairs={{0,8},{4,12},{8,0},{12,4},{16,24},{20,28},{24,16},{28,20},{1,9},{5... | collective-permute-start | bytes 2359304 | tf_op jit(solution)/shard_map/ppermute | solution.py:51
  (247 other events, 3328.3 us)

commit v3 on v2

--- a/solution.py
+++ b/solution.py
@@ -49,6 +49,10 @@
 def swap(value, axis, mask):
     size = lax.axis_size(axis)
     return lax.ppermute(value, axis, [(i, i ^ mask) for i in range(size)])
+
+
+def after(value, *others):
+    return lax.optimization_barrier((value,) + others)[0]
 
 
 def bits_of(size):
@@ -80,10 +84,10 @@
     pieces = []
     for mask in subsets(bits):
         pieces += got[mask] if mask in got else [upper[mask], lower[mask]]
-    return jnp.concatenate(pieces, 0)
-
-
-def scatter_rows(parts, bits):
+    return jnp.concatenate(pieces, 0), pieces[1], pieces[-1]
+
+
+def scatter_rows(parts, bits, gate=()):
     half = parts[0].shape[0] // 2
     upper = {m: p[:half] for m, p in parts.items()}
     lower = {m: p[half:] for m, p in parts.items()}
@@ -91,6 +95,7 @@
         for k in reversed(range(len(order))):
             for sub in subsets(order[:k])[1:]:
                 other = swap(which[sub | order[k]], "shard", order[k])
+                other = after(other, *gate) if gate else other
                 which[sub] = (which[sub].astype(F32) + other.astype(F32)).astype(BF16)
     total = parts[0].astype(F32)
     for bit in bits:
@@ -98,10 +103,13 @@
     return total
 
 
-def gather_blocks(value, axis):
+def gather_blocks(value, axis, bits, gates=None):
     current = value[None]
-    for bit in bits_of(lax.axis_size(axis)):
-        current = jnp.concatenate([current, swap(current, axis, bit)], 0)
+    for bit in bits:
+        there = swap(current, axis, bit)
+        if gates:
+            there = after(there, *gates[bit])
+        current = jnp.concatenate([current, there], 0)
     return current
 
 
@@ -112,7 +120,7 @@
         copy.wait()
 
 
-def place_kernel(me_ref, *refs, count, terms, width, rows, joined):
+def place_kernel(me_ref, *refs, count, width, rows, joined):
     pieces, outs, sems = refs[: 2 * count], refs[2 * count : -1], refs[-1]
     me = me_ref[0]
 
@@ -122,15 +130,14 @@
             for i in range(count):
                 row = pl.multiple_of((me ^ (2 * i) ^ side) * rows, rows)
                 piece = pieces[side * count + i]
-                for term in range(terms):
-                    for k in range(2):
-                        own = k ^ core
-                        source = piece.at[:, pl.ds((2 * term + k) * width, width)]
-                        if joined:
-                            target = outs[0].at[pl.ds(row, rows), pl.ds(own * width, width)]
-                        else:
-                            target = outs[own].at[pl.ds(row, rows), pl.ds(term * width, width)]
-                        made.append(pltpu.make_async_copy(source, target, sems.at[len(made)]))
+                for k in range(2):
+                    own = k ^ core
+                    source = piece.at[:, pl.ds(k * width, width)]
+                    if joined:
+                        target = outs[0].at[pl.ds(row, rows), pl.ds(own * width, width)]
+                    else:
+                        target = outs[own].at[pl.ds(row, rows)]
+                    made.append(pltpu.make_async_copy(source, target, sems.at[len(made)]))
         return made
 
     @pl.when((me & 1) == 0)
@@ -142,47 +149,88 @@
         run_copies(copies(1))
 
 
-def place_weights(me, pieces, terms, width, joined):
+def place_weights(me, pieces, width, joined):
     count = len(pieces) // 2
     rows = pieces[0].shape[0]
     if joined:
         shapes = [jax.ShapeDtypeStruct((rows * count * 2, 2 * width), BF16)]
     else:
-        shapes = [jax.ShapeDtypeStruct((rows * count * 2, terms * width), BF16)] * 2
+        shapes = [jax.ShapeDtypeStruct((rows * count * 2, width), BF16)] * 2
     return pl.pallas_call(
         functools.partial(
-            place_kernel, count=count, terms=terms, width=width, rows=rows, joined=joined
+            place_kernel, count=count, width=width, rows=rows, joined=joined
         ),
         out_shape=shapes,
         in_specs=[pl.BlockSpec(memory_space=pltpu.SMEM)]
         + [pl.BlockSpec(memory_space=pl.ANY)] * (2 * count),
         out_specs=[pl.BlockSpec(memory_space=pltpu.VMEM)] * len(shapes),
-        scratch_shapes=[pltpu.SemaphoreType.DMA((4 * count * terms,))],
+        scratch_shapes=[pltpu.SemaphoreType.DMA((4 * count,))],
         cost_estimate=pl.CostEstimate(
-            flops=0, bytes_accessed=16 * rows * count * width * terms, transcendentals=0
+            flops=0, bytes_accessed=16 * rows * count * width, transcendentals=0
         ),
         name="place_weights",
     )(me, *pieces)
 
 
-def cols_kernel(me_ref, in_ref, out_ref, sems):
-    count, _, width = in_ref.shape
+def pick_kernel(chosen_ref, *refs, tall, rank):
+    tables, (tall_ref, flat_ref, sems) = refs[:-3], refs[-3:]
+    count = chosen_ref.shape[0]
+    copies = []
+    for s in range(count):
+        column = 0
+        for i, table in enumerate(tables):
+            if i < tall:
+                target = tall_ref.at[pl.ds((i * count + s) * rank, rank)]
+            else:
+                width = table.shape[2]
+                target = flat_ref.at[pl.ds(s * rank, rank), pl.ds(column, width)]
+                column += width
+            copies.append(
+                pltpu.make_async_copy(table.at[chosen_ref[s]], target, sems.at[len(copies)])
+            )
+    run_copies(copies)
+
+
+def pick_maps(chosen, upright, flat):
+    count, rank = chosen.shape[0], upright[0].shape[1]
+    total = sum(t.shape[2] for t in flat)
+    shapes = (
+        jax.ShapeDtypeStruct((len(upright) * count * rank, upright[0].shape[2]), BF16),
+        jax.ShapeDtypeStruct((count * rank, total), BF16),
+    )
+    tables = upright + flat
+    return pl.pallas_call(
+        functools.partial(pick_kernel, tall=len(upright), rank=rank),
+        out_shape=shapes,
+        in_specs=[pl.BlockSpec(memory_space=pltpu.SMEM)]
+        + [pl.BlockSpec(memory_space=pl.ANY)] * len(tables),
+        out_specs=[pl.BlockSpec(memory_space=pltpu.VMEM)] * 2,
+        scratch_shapes=[pltpu.SemaphoreType.DMA((count * len(tables),))],
+        cost_estimate=pl.CostEstimate(
+            flops=0, bytes_accessed=8 * count * rank * total, transcendentals=0
+        ),
+        name="pick_maps",
+    )(chosen, *tables)
+
+
+def cols_kernel(me_ref, in_ref, out_ref, sems, *, masks):
+    width = in_ref.shape[2]
     run_copies(
         [
             pltpu.make_async_copy(
-                in_ref.at[mask],
+                in_ref.at[i],
                 out_ref.at[:, pl.ds(pl.multiple_of((me_ref[0] ^ mask) * width, width), width)],
-                sems.at[mask],
+                sems.at[i],
             )
-            for mask in range(count)
+            for i, mask in enumerate(masks)
         ]
     )
 
 
-def place_columns(me, stacked):
+def place_columns(me, stacked, masks):
     count, rows, width = stacked.shape
     return pl.pallas_call(
-        cols_kernel,
+        functools.partial(cols_kernel, masks=masks),
         out_shape=jax.ShapeDtypeStruct((rows, count * width), stacked.dtype),
         in_specs=[pl.BlockSpec(memory_space=pltpu.SMEM), pl.BlockSpec(memory_space=pltpu.VMEM)],
         out_specs=pl.BlockSpec(memory_space=pltpu.VMEM),
@@ -370,11 +418,6 @@
     chosen = adapter_pick[0]
     starts = piece_start[0]
 
-    def pick(table):
-        return jnp.concatenate(
-            [lax.dynamic_index_in_dim(table, chosen[s], 0, keepdims=False) for s in range(count)], 0
-        )
-
     owners = np.concatenate([np.arange(chips) * 2, np.arange(chips) * 2 + 1]).astype(np.int32)
     locs = np.tile(np.arange(rows, dtype=np.int32), 2 * chips)
     positions = (me ^ jnp.asarray(np.repeat(owners, rows))) * rows + jnp.asarray(locs)
@@ -388,45 +431,70 @@
         of_col = lax.broadcasted_iota(jnp.int32, value.shape, 1) // (terms * rank)
         return jnp.where(of_row == of_col, value, 0.0).astype(BF16)
 
-    def with_other(value, axis=-1):
-        return jnp.concatenate([value, swap(value, "shard", 1)], axis)
-
     gain_one, shift_one = ln1_gain.astype(F32), ln1_bias.astype(F32)
     gain_two, shift_two = ln2_gain.astype(F32), ln2_bias.astype(F32)
 
-    features = inputs[0].reshape(block, wide).astype(F32)
-    cot_mine = cotangent[0].reshape(block, wide)
-    normed, norm_one_back = jax.vjp(lambda v: layer_norm(v, gain_one, shift_one), features)
-    hidden_one = gather_rows(normed.astype(BF16), bits)
+    narrow = [out_query, out_key, out_value, in_attn, out_expand, in_reduce]
+    edges = np.cumsum([0] + [n.shape[2] for n in narrow])
+    mine, packed = pick_maps(
+        chosen, [in_query, in_key, in_value, in_expand, out_attn, out_reduce], narrow
+    )
+    packed_other = swap(packed, "shard", 1)
+    order = bits + [1]
+    near = gather_blocks(mine, "shard", bits)
+    stacked = jnp.concatenate([near, swap(near, "shard", 1)], 0)
+    w_out_other = swap(w_out, "shard", 1)
+    w_down_other = swap(w_down, "shard", 1)
 
     chip = me // 2
 
-    def turn(tables, width):
-        own, other = [], []
+    def slices(tables, width):
+        pieces = []
         for i in range(chips):
-            piece = [
+            both = [
                 lax.dynamic_slice_in_dim(t, (chip ^ i) * 2 * width, 2 * width, 1) for t in tables
             ]
-            piece = jnp.concatenate(piece, 1) if len(piece) > 1 else piece[0]
-            own.append(swap(piece, "shard", 2 * i) if i else piece)
-        for piece in own:
-            other.append(swap(piece, "shard", 1))
-        return own + other
-
-    w_qkv_mine, w_qkv_other = place_weights(
-        me_arr, turn([w_query, w_key, w_value], span), 3, span, False
-    )
-
-    mine = jnp.concatenate(
-        [pick(t) for t in (in_query, in_key, in_value, in_expand, out_attn, out_reduce)], 0
-    )
-    whole = place_columns(me_arr, gather_blocks(mine, "shard")).reshape(6, count, rank, wide)
+            if len(both) > 1:
+                both = jnp.concatenate(
+                    [t[:, k * width : (k + 1) * width] for k in range(2) for t in both], 1
+                )
+            else:
+                both = both[0]
+            pieces.append(both)
+        return pieces
+
+    def turn(pieces):
+        own = [swap(piece, "shard", 2 * i) if i else piece for i, piece in enumerate(pieces)]
+        return own + [swap(piece, "shard", 1) for piece in own]
+
+    first_tables = after((w_query, w_key, w_value), mine)
+    pieces_qkv = after(
+        tuple(slices(first_tables, span)), near, packed_other, w_out_other, w_down_other
+    )
+    turned = turn(pieces_qkv)
+    w_qkv_mine, w_qkv_other = place_weights(me_arr, turned, 3 * span, False)
+
+    features = after(inputs[0].reshape(block, wide), *pieces_qkv).astype(F32)
+    normed, norm_one_back = jax.vjp(lambda v: layer_norm(v, gain_one, shift_one), features)
+    hidden_block = after(normed.astype(BF16), *[turned[bit // 2] for bit in bits])
+    hidden_one, one_first, one_last = gather_rows(hidden_block, bits)
+
+    cot_mine = cotangent[0].reshape(block, wide)
+    cot, cot_first, cot_last = gather_rows(after(cot_mine, one_first), bits)
+    pieces_up = slices([after(w_up, one_last, cot_first)], ff_part)
+
+    whole = place_columns(me_arr, stacked, subsets(order)).reshape(6, count, rank, wide)
     in_qkv = jnp.swapaxes(whole[:3], 0, 1).reshape(count * 3 * rank, wide)
     in_exp, out_att, out_red = (whole[3 + i].reshape(count * rank, wide) for i in range(3))
-    narrow = [pick(t) for t in (out_query, out_key, out_value, in_attn, out_expand, in_reduce)]
-    packed = jnp.concatenate(narrow, 1)
-    packed_other = swap(packed, "shard", 1)
-    edges = np.cumsum([0] + [n.shape[1] for n in narrow])
+
+    rep_bits = bits_of(lax.axis_size("rep"))
+    mark = (chosen[:, None] == jnp.arange(ADAPTERS, dtype=jnp.int32)[None, :]).astype(BF16)
+    marks = gather_blocks(jnp.pad(mark, ((0, 16 - count), (0, 128 - ADAPTERS))), "rep", rep_bits)
+    groups = marks.shape[0]
+    marks = marks[:, :count, :ADAPTERS].reshape(groups * count, 1, ADAPTERS, 1)
+    place = (marks * jnp.eye(rank, dtype=BF16)[None, :, None, :]).reshape(
+        groups * count * rank, ADAPTERS * rank
+    )
 
     def unpack(table, i):
         return table[:, edges[i] : edges[i + 1]]
@@ -450,8 +518,8 @@
         )
 
     b_up_chip = jnp.concatenate([slice_of(b_up, me, ff_part), slice_of(b_up, me ^ 1, ff_part)])
-    w_out_chip = with_other(w_out, 0)
-    w_down_chip = with_other(w_down, 0)
+    w_out_chip = jnp.concatenate([w_out, w_out_other], 0)
+    w_down_chip = jnp.concatenate([w_down, w_down_other], 0)
 
     def by_chip(value):
         return value.reshape((chips, count, rows) + value.shape[1:])
@@ -459,13 +527,15 @@
     def flat(value):
         return value.reshape(chips * block, value.shape[-1])
 
-    def project_back(value, low, weight, table, transposed):
-        main = mm_t if transposed else mm
+    def block_products(products, low, table):
         parts = {}
         for i in reversed(range(chips)):
             at = slice(i * block, (i + 1) * block)
-            parts[2 * i] = (main(value[at], weight) + mm(low[at], table)).astype(BF16)
-        return scatter_rows(parts, bits)
+            total = mm(low[at], table)
+            for value, weight, main in products:
+                total = total + main(value[at], weight)
+            parts[2 * i] = total.astype(BF16)
+        return parts
 
     low_qkv = keep_own(mm_t(hidden_one, in_qkv), 3)
     qkv_away = (
@@ -478,30 +548,32 @@
     att_own, att_away, lse = attend(where, qkv_own, qkv_other, heads)
     attended = jnp.concatenate([flat(att_own), swap(flat(att_away), "shard", 1)], 1)
     low_att = keep_own(mm_t(attended, in_att))
-    branch = project_back(attended, low_att, w_out_chip, out_att, False) + b_out.astype(F32)
+    glow_red = keep_own(mm_t(cot, out_red))
+    grad_act = (mm_t(cot, w_down_chip) + mm(glow_red, in_red)).astype(BF16)
+    parts = block_products([(attended, w_out_chip, mm)], low_att, out_att)
+    parts[0] = after(parts[0], grad_act)
+    branch = scatter_rows(parts, bits) + b_out.astype(F32)
     residual = features + branch
     normed, norm_two_back = jax.vjp(lambda v: layer_norm(v, gain_two, shift_two), residual)
-    hidden_two = gather_rows(normed.astype(BF16), bits)
-
-    (w_up_chip,) = place_weights(me_arr, turn([w_up], ff_part), 1, ff_part, True)
-    cot = gather_rows(cot_mine, bits)
-    glow_red = keep_own(mm_t(cot, out_red))
-    grad_act = mm_t(cot, w_down_chip) + mm(glow_red, in_red)
+    hidden_two, _, _ = gather_rows(normed.astype(BF16), bits)
+
+    (w_up_chip,) = place_weights(me_arr, turn(pieces_up), ff_part, True)
     low_exp = keep_own(mm_t(hidden_two, in_exp))
     pre = mm(hidden_two, w_up_chip) + mm(low_exp, out_exp) + b_up_chip
     share = 0.5 * (1.0 + lax.erf(pre * np.float32(0.5**0.5)))
     act = (pre * share).astype(BF16)
     slope = share + pre * (jnp.exp(-0.5 * pre * pre) * np.float32((2 * np.pi) ** -0.5))
-    grad_pre = (slope * grad_act).astype(BF16)
+    grad_pre = (slope * grad_act.astype(F32)).astype(BF16)
     glow_exp = keep_own(mm_t(grad_pre, out_exp))
-    grad_two = project_back(grad_pre, glow_exp, w_up_chip, in_exp, True)
+    grad_two = scatter_rows(block_products([(grad_pre, w_up_chip, mm_t)], glow_exp, in_exp), bits)
     grad_residual = cot_mine.astype(F32) + norm_two_back(grad_two)[0]
-    grad_branch = gather_rows(grad_residual.astype(BF16), bits)
-
-    low_red = keep_own(mm_t(act, in_red))
-    down = project_back(act, low_red, w_down_chip, out_red, False)
-    layer_rows = residual + down + b_down.astype(F32)
-
+    grad_block = grad_residual.astype(BF16)
+    grad_branch, _, branch_last = gather_rows(grad_block, bits)
+
+    act_late = after(act, grad_block)
+    low_red = keep_own(mm_t(act_late, in_red))
+    down_parts = block_products([(act_late, w_down_chip, mm)], low_red, out_red)
+    down_parts = {m: after(p, branch_last) for m, p in down_parts.items()}
     glow_att = keep_own(mm_t(grad_branch, out_att))
     grad_att = (mm_t(grad_branch, w_out_chip) + mm(glow_att, in_att)).astype(BF16)
     ga_own = by_chip(grad_att[:, :span])
@@ -510,18 +582,7 @@
     grad_own = flat(grad_own)
     grad_other = swap(flat(grad_away), "shard", 1)
     glow_qkv = keep_own(mm_t(grad_own, out_qkv_mine) + mm_t(grad_other, out_qkv_other), 3)
-    parts = {}
-    for i in reversed(range(chips)):
-        at = slice(i * block, (i + 1) * block)
-        parts[2 * i] = (
-            mm_t(grad_own[at], w_qkv_mine)
-            + mm_t(grad_other[at], w_qkv_other)
-            + mm(glow_qkv[at], in_qkv)
-        ).astype(BF16)
-    grad_one = scatter_rows(parts, bits)
-    input_rows = grad_residual + norm_one_back(grad_one)[0]
-
-    def sum_columns(value):
+    def sum_columns(value, gates=None):
         width = value.shape[1] // size
 
         def side(which):
@@ -537,26 +598,21 @@
         for bit in bits[::-1]:
             current = current.reshape((2, current.shape[0] // 2) + current.shape[1:])
             own = (me // bit) & 1
-            current = lax.dynamic_index_in_dim(current, own, 0, False) + swap(
+            there = swap(
                 lax.dynamic_index_in_dim(current, 1 - own, 0, False).astype(BF16), "shard", bit
-            ).astype(F32)
+            )
+            if gates:
+                there = after(there, *gates[bit])
+            current = lax.dynamic_index_in_dim(current, own, 0, False) + there.astype(F32)
         return current[0]
 
     def sum_cores(own, away):
         return own + swap(away.astype(BF16), "shard", 1).astype(F32)
 
-    def over_groups(terms):
+    def over_groups(terms, gates=None):
         widths = [t.shape[1] for t in terms]
         data = jnp.concatenate([t.astype(BF16) for t in terms], 1)
-        mark = (chosen[:, None] == jnp.arange(ADAPTERS, dtype=jnp.int32)[None, :]).astype(BF16)
-        mark = jnp.pad(mark, ((0, 16 - count), (0, data.shape[1] - ADAPTERS)))
-        every = gather_blocks(jnp.concatenate([data, mark], 0), "rep")
-        groups = every.shape[0]
-        marks = every[:, count * rank : count * rank + count, :ADAPTERS]
-        marks = marks.reshape(groups * count, 1, ADAPTERS, 1)
-        place = marks * jnp.eye(rank, dtype=BF16)[None, :, None, :]
-        place = place.reshape(groups * count * rank, ADAPTERS * rank)
-        taken = every[:, : count * rank].reshape(groups * count * rank, -1)
+        taken = gather_blocks(data, "rep", rep_bits, gates).reshape(groups * count * rank, -1)
         outs, start = [], 0
         for width in widths:
             out = t_mm(place, taken[:, start : start + width])
@@ -564,19 +620,25 @@
             start += width
         return outs
 
+    glow_late, low_late = after((glow_exp, low_exp), grad_block)
+    arrived = {bit: (grad_away,) for bit in bits}
     first = sum_columns(
         jnp.concatenate(
-            [t_mm(low_att, grad_branch), t_mm(glow_exp, hidden_two), t_mm(low_red, cot)], 0
-        )
+            [t_mm(low_att, grad_branch), t_mm(glow_late, hidden_two), t_mm(low_red, cot)], 0
+        ),
+        arrived,
     ).reshape(3, count * rank, slice_wide)
     chip_wide = jnp.concatenate(
-        [t_mm(glow_att, attended), t_mm(glow_red, act), t_mm(low_exp, grad_pre)], 1
+        [t_mm(glow_att, attended), t_mm(glow_red, act_late), t_mm(low_late, grad_pre)], 1
     )
     cut = [0, span, 2 * span, 2 * span + ff_part, 2 * span + 2 * ff_part, 2 * span + 3 * ff_part]
     cut.append(chip_wide.shape[1])
     side = [chip_wide[:, cut[i] : cut[i + 1]] for i in range(6)]
     local = sum_cores(jnp.concatenate(side[::2], 1), jnp.concatenate(side[1::2], 1))
-    s_in_att, s_in_red, s_out_exp, s_out_att, s_in_exp, s_out_red = over_groups(
+    products = [(grad_own, w_qkv_mine, mm_t), (grad_other, w_qkv_other, mm_t)]
+    parts = block_products(products, glow_qkv, in_qkv)
+    far_part = parts[2 * (chips - 1)]
+    early = over_groups(
         [
             local[:, :span],
             local[:, span : span + ff_part],
@@ -584,10 +646,20 @@
             first[0],
             first[1],
             first[2],
-        ]
-    )
-
-    second = sum_columns(t_mm(glow_qkv, hidden_one)).reshape(count, 3, rank, slice_wide)
+        ],
+        {bit: (far_part,) for bit in rep_bits},
+    )
+    parts[0] = after(parts[0], *early)
+    grad_one = scatter_rows(parts, bits)
+    input_rows = grad_residual + norm_one_back(grad_one)[0]
+
+    down_parts[0] = after(down_parts[0], far_part)
+    down = scatter_rows(down_parts, bits, (grad_away,))
+    layer_rows = residual + down + b_down.astype(F32)
+
+    s_in_att, s_in_red, s_out_exp, s_out_att, s_in_exp, s_out_red = early
+    glow_last, own_last, other_last = after((glow_qkv, grad_own, grad_other), far_part)
+    second = sum_columns(t_mm(glow_last, hidden_one)).reshape(count, 3, rank, slice_wide)
 
     def own_terms(full):
         full = full.reshape(count, 3, rank, 3, span)
@@ -595,7 +667,7 @@
             [full[:, t, :, t].reshape(count * rank, span) for t in range(3)], 1
         )
 
-    outer = sum_cores(own_terms(t_mm(low_qkv, grad_own)), own_terms(t_mm(low_qkv, grad_other)))
+    outer = sum_cores(own_terms(t_mm(low_qkv, own_last)), own_terms(t_mm(low_qkv, other_last)))
     late = over_groups(
         [second[:, t].reshape(count * rank, slice_wide) for t in range(3)]
         + [outer[:, t * span : (t + 1) * span] for t in range(3)]

time: 634 us -> 545 us (0.86)
  matrix products: 159 us -> 124 us
  local copies, waits for them, and re-layouts: 109 us -> 88.6 us
  waiting for transfers between devices: 192 us -> 173 us
  starting transfers between devices: 55.7 us -> 64.4 us
  Pallas kernels: 43.3 us -> 35.1 us
    ppermute x68 -> x70, waiting for transfers between devices: 192 us -> 173 us  [swap(): return lax.ppermute(value, axis, [(i, i ^ mask) for i in range(size)])]
    dot_general x32, matrix products: 63.5 us -> 48.4 us  [mm(): lax.dot_general(a, b, (((1,), (0,)), ((), ())), preferred_element_type=F32)]
    dot_general x21, matrix products: 30.2 us -> 20 us  [t_mm(): lax.dot_general(a, b, (((0,), (0,)), ((), ())), preferred_element_type=F32)]
    dot_general x23, matrix products: 65.4 us -> 55.9 us  [mm_t(): lax.dot_general(a, b, (((1,), (1,)), ((), ())), preferred_element_type=F32)]
    unnamed x429 -> x319, local copies, waits for them, and re-layouts: 53 us -> 43.7 us
    ppermute x68 -> x70, starting transfers between devices: 55.7 us -> 64.4 us  [swap(): return lax.ppermute(value, axis, [(i, i ^ mask) for i in range(size)])]
    pallas_call x3 -> x4, Pallas kernels: 26.7 us -> 18.1 us  [the longest x2 12.4 us: place_weights(): pl.pallas_call(functools.partial(place_kernel, count=count, width=width,...]
    concatenate x13 -> x10, other arithmetic: 11.7 us -> 3.49 us  [the longest x8 2.28 us: gather_blocks(): current = jnp.concatenate([current, there], 0)]
  transfers between devices with their start and end apart: 68 -> 70, of which waited for: 28 -> 25; matrix products, arithmetic and copies ran while one was open for 37% -> 42% of each run, Pallas kernels for 7% -> 7%
where the time goes in v3:
time: 545 us; the launch traced here: 538 us
  waiting for transfers between devices  173 us (32%)
  matrix products  124 us (23%)
  local copies, waits for them, and re-layouts  88.6 us (16%)
  starting transfers between devices  64.4 us (12%)
  other arithmetic  47.9 us (9%)
  Pallas kernels  35.1 us (6%)
    ppermute x70, waiting for transfers between devices, swap(): return lax.ppermute(value, axis, [(i, i ^ mask) for i in range(size)])  173 us
    ppermute x70, starting transfers between devices, swap(): return lax.ppermute(value, axis, [(i, i ^ mask) for i in range(size)])  64.4 us
    dot_general x23, matrix products, mm_t(): lax.dot_general(a, b, (((1,), (1,)), ((), ())), preferred_element_type=F32)  55.9 us
    dot_general x32, matrix products, mm(): lax.dot_general(a, b, (((1,), (0,)), ((), ())), preferred_element_type=F32)  48.4 us
    unnamed x319, local copies, waits for them, and re-layouts  43.7 us
    dot_general x21, matrix products, t_mm(): lax.dot_general(a, b, (((0,), (0,)), ((), ())), preferred_element_type=F32)  20 us
    pallas_call x2, Pallas kernels, place_weights(): pl.pallas_call(functools.partial(place_kernel, count=count, width=width,...  12.4 us
  transfers between devices with their start and end apart: 70, of which 25 were waited for; matrix products, arithmetic and copies ran while one was open for 42% of the time, Pallas kernels for 7%

profile of v3, /device:TPU:0, one launch (start us, length us, event | category | flops | bytes accessed | tf_op | source)
XLA Modules:
  0.0 538.5 jit_solution(2172054897349941973)
XLA Ops:
  49.2 6.2 %collective-permute-done.1 = bf16[2,288,256]{2,1,0:T(8,128)(2,1)S(1)} collective-permute-done((bf16[2,288,256]{2,1,0:T(8,128)(2,1)S(1)}, bf16[2,288,256]{2,1,0:T(8,128)(2,1)S(1)}, u32[]{:S(2)}, u32[]{:S(2)}) %collective-permute-start.1) | collective-permute-done | bytes 294944 | tf_op jit(solution)/shard_map/ppermute | solution.py:51
  61.0 15.0 %collective-permute-done.5.refs_1_ = bf16[256,1536]{1,0:T(8,128)(2,1)S(1)} collective-permute-done((bf16[256,1536]{1,0:T(8,128)(2,1)S(1)}, bf16[256,1536]{1,0:T(8,128)(2,1)S(1)}, u32[]{:S(2)}, u32[]{:S(2)}) %collective-permute-start.5) | collective-permute-done | bytes 786464 | tf_op jit(solution)/shard_map/ppermute | solution.py:51
  76.0 15.7 %collective-permute-done.6.refs_2_ = bf16[256,1536]{1,0:T(8,128)(2,1)S(1)} collective-permute-done((bf16[256,1536]{1,0:T(8,128)(2,1)S(1)}, bf16[256,1536]{1,0:T(8,128)(2,1)S(1)}, u32[]{:S(2)}, u32[]{:S(2)}) %collective-permute-start.6) | collective-permute-done | bytes 786464 | tf_op jit(solution)/shard_map/ppermute | solution.py:51
  106.1 4.3 collective-permute-done.7
  110.4 4.8 constant_dynamic-update-slice_fusion.12
  128.7 5.7 %place_weights.2 = (bf16[2048,768]{1,0:T(8,128)(2,1)}, bf16[2048,768]{1,0:T(8,128)(2,1)}) custom-call(s32[1]{0:T(128)} %bitcast.15.me_ref, bf16[256,1536]{1,0:T(8,128)(2,1)} %get-tuple-element.58.refs_0_, bf16[256,1536]{1,0:T(8,128)(2,1)} %copy-done.62, bf16[256,1536]{1,0:T(8,128)(2,1)} %copy-done.64, bf16[256,1536]{1,0:T(8,128)(2,1)} %collective-permute-done.11.refs_3_, ...), custom_call_target="tpu_custom_call" | custom-call | bytes 12582912 | tf_op jit(solution)/shard_map/place_weights/pallas_call | solution.py:159
  137.6 15.3 %collective-permute-done.9 = bf16[96,2048]{1,0:T(8,128)(2,1)} collective-permute-done((bf16[96,2048]{1,0:T(8,128)(2,1)}, bf16[96,2048]{1,0:T(8,128)(2,1)}, u32[]{:S(2)}, u32[]{:S(2)}) %collective-permute-start.9) | collective-permute-done | bytes 393248 | tf_op jit(solution)/shard_map/ppermute | solution.py:51
  164.0 3.7 add_convert_fusion.2
  180.2 24.6 %collective-permute-done.21 = bf16[96,2048]{1,0:T(8,128)(2,1)S(1)} collective-permute-done((bf16[96,2048]{1,0:T(8,128)(2,1)S(1)}, bf16[96,2048]{1,0:T(8,128)(2,1)S(1)}, u32[]{:S(2)}, u32[]{:S(2)}) %collective-permute-start.21) | collective-permute-done | bytes 393248 | tf_op jit(solution)/shard_map/ppermute | solution.py:51
  208.5 7.5 %attend.1 = (bf16[4,3,64,256]{3,2,1,0:T(8,128)(2,1)}, bf16[4,3,64,256]{3,2,1,0:T(8,128)(2,1)}, f32[3,512,2]{2,1,0:T(8,128)}) custom-call(s32[512,1]{1,0:T(8,128)} %copy.77.pq, s32[1,512]{1,0:T(1,128)} %bitcast.336, s32[3,512,1]{2,1,0:T(8,128)} %copy.78.lq, s32[3,1,512]{2,1,0:T(1,128)} %broadcast_in_dim.107.lk, bf16[4,3,64,768]{3,2,1,0:T(8,128)(2,1)} %bitcast.309, ...), custom_call_target="tpu_custom_call" | custom-call | flops 805306368 | bytes 3145728 | tf_op jit(solution)/shard_map/attend/pallas_call | solution.py:299
  226.4 12.3 %collective-permute-done.23 = bf16[96,2048]{1,0:T(8,128)(2,1)S(1)} collective-permute-done((bf16[96,2048]{1,0:T(8,128)(2,1)S(1)}, bf16[96,2048]{1,0:T(8,128)(2,1)S(1)}, u32[]{:S(2)}, u32[]{:S(2)}) %collective-permute-start.23) | collective-permute-done | bytes 393248 | tf_op jit(solution)/shard_map/ppermute | solution.py:51
  243.4 11.9 %add_convert_fusion = bf16[768,2048]{1,0:T(8,128)(2,1)} fusion(f32[768,2048]{1,0:T(8,128)S(1)} %fusion.89, bf16[768,2048]{1,0:T(8,128)(2,1)} %constant_dynamic-update-slice_fusion.7, bf16[2048,2048]{1,0:T(8,128)(2,1)} %constant_dynamic-update-slice_fusion.12), kind=kOutput, calls=%fused_computation.10 | convolution fusion | flops 6445596672 | bytes 20971520 | tf_op jit(solution)/shard_map/dot_general | solution.py:42
  271.8 6.7 %place_weights.3 = bf16[2048,2048]{1,0:T(8,128)(2,1)} custom-call(s32[1]{0:T(128)} %bitcast.15.me_ref, bf16[256,2048]{1,0:T(8,128)(2,1)} %get-tuple-element.105.refs_0_, bf16[256,2048]{1,0:T(8,128)(2,1)} %collective-permute-done.31.refs_1_, bf16[256,2048]{1,0:T(8,128)(2,1)} %collective-permute-done.32.refs_2_, ...), custom_call_target="tpu_custom_call" | custom-call | bytes 16777216 | tf_op jit(solution)/shard_map/place_weights/pallas_call | solution.py:159
  278.5 5.6 %collective-permute-done.27 = bf16[192,2048]{1,0:T(8,128)(2,1)} collective-permute-done((bf16[192,2048]{1,0:T(8,128)(2,1)}, bf16[192,2048]{1,0:T(8,128)(2,1)}, u32[]{:S(2)}, u32[]{:S(2)}) %collective-permute-start.27) | collective-permute-done | bytes 786464 | tf_op jit(solution)/shard_map/ppermute | solution.py:51
  303.1 13.3 %fusion.5 = (bf16[768,2048]{1,0:T(8,128)(2,1)S(1)}, bf16[768,2048]{1,0:T(8,128)(2,1)}) fusion(bf16[768,2048]{1,0:T(8,128)(2,1)} %add_convert_fusion, f32[2048]{0:T(1024)S(1)} %maximum_convert_fusion, f32[768,2048]{1,0:T(8,128)S(1)} %fusion.88, bf16[768,2048]{1,0:T(8,128)(2,1)} %constant_dynamic-update-slice_fusion.14, bf16[2048,2048]{1,0:T(8,128)(2,1)S(1)} %bitcast.248), kind=kOutput, calls=%fused_computation.6 | convolution fusion | flops 6466043904 | bytes 27271168 | tf_op jit(solution)/shard_map/dot_general | solution.py:38
  343.3 7.0 %collective-permute-done.39 = bf16[192,2048]{1,0:T(8,128)(2,1)} collective-permute-done((bf16[192,2048]{1,0:T(8,128)(2,1)}, bf16[192,2048]{1,0:T(8,128)(2,1)}, u32[]{:S(2)}, u32[]{:S(2)}) %collective-permute-start.39) | collective-permute-done | bytes 786464 | tf_op jit(solution)/shard_map/ppermute | solution.py:51
  351.6 7.3 %multiply_reduce_fusion = (f32[192]{0:T(256)S(1)}, f32[192,2048]{1,0:T(8,128)S(1)}) fusion(f32[192,2048]{1,0:T(8,128)S(1)} %get-tuple-element.99, f32[192]{0:T(256)S(1)} %broadcast_multiply_fusion.3, f32[2048]{0:T(1024)S(1)} %copy-done.87, bf16[192,2048]{1,0:T(8,128)(2,1)} %collective-permute-done.41, bf16[192,2048]{1,0:T(8,128)(2,1)} %collective-permute-done.39, ...), kind=kOutput, calls=%fused_computation.72 | convolution fusion | flops 1614937856 | bytes 15476224 | tf_op jit(solution)/shard_map/dot_general | solution.py:42
  367.7 5.4 fusion.55
  388.0 5.1 collective-permute-done.45
  408.2 9.6 %attend_back.1 = (bf16[4,3,64,768]{3,2,1,0:T(8,128)(2,1)}, bf16[4,3,64,768]{3,2,1,0:T(8,128)(2,1)}) custom-call(s32[512,1]{1,0:T(8,128)} %copy.77.pq, s32[1,512]{1,0:T(1,128)} %bitcast.337, s32[3,512,1]{2,1,0:T(8,128)} %copy.78.lq, s32[3,1,512]{2,1,0:T(1,128)} %broadcast_in_dim.107.lk, bf16[4,3,64,768]{3,2,1,0:T(8,128)(2,1)} %bitcast.310, ...), custom_call_target="tpu_custom_call" | custom-call | flops 2013265920 | bytes 5505024 | tf_op jit(solution)/shard_map/attend_back/pallas_call | solution.py:356
  425.9 15.9 %collective-permute-done.57 = bf16[1,144,256]{2,1,0:T(8,128)(2,1)S(1)} collective-permute-done((bf16[1,144,256]{2,1,0:T(8,128)(2,1)S(1)}, bf16[1,144,256]{2,1,0:T(8,128)(2,1)S(1)}, u32[]{:S(2)}, u32[]{:S(2)}) %collective-permute-start.57) | collective-permute-done | bytes 73760 | tf_op jit(solution)/shard_map/ppermute | solution.py:51
  487.7 4.3 collective-permute-done.60
  496.0 14.9 %collective-permute-done.66 = bf16[1,144,256]{2,1,0:T(8,128)(2,1)S(1)} collective-permute-done((bf16[1,144,256]{2,1,0:T(8,128)(2,1)S(1)}, bf16[1,144,256]{2,1,0:T(8,128)(2,1)S(1)}, u32[]{:S(2)}, u32[]{:S(2)}) %collective-permute-start.66) | collective-permute-done | bytes 73760 | tf_op jit(solution)/shard_map/ppermute | solution.py:51
  518.4 10.3 %collective-permute-done.69 = bf16[2,48,1536]{2,1,0:T(8,128)(2,1)S(1)} collective-permute-done((bf16[2,48,1536]{2,1,0:T(8,128)(2,1)S(1)}, bf16[2,48,1536]{2,1,0:T(8,128)(2,1)S(1)}, u32[]{:S(2)}, u32[]{:S(2)}) %collective-permute-start.69) | collective-permute-done | bytes 294944 | tf_op jit(solution)/shard_map/ppermute | solution.py:51
  (675 shorter events, 300.6 us)
Async XLA Ops:
  0.7 54.8 %collective-permute-start.4 = (bf16[1024,2048]{1,0:T(8,128)(2,1)}, bf16[1024,2048]{1,0:T(8,128)(2,1)}, u32[]{:S(2)}, u32[]{:S(2)}) collective-permute-start(bf16[1024,2048]{1,0:T(8,128)(2,1)} %param.47), channel_id=1, source_target_pairs={{0,4},{4,0},{8,12},{12,8},{16,20},{20,16},{24,28},{28,24},{1,5},{5... | collective-permute-start | bytes 12582920 | tf_op jit(solution)/shard_map/ppermute | solution.py:51
  4.2 42.0 %collective-permute-start = (bf16[1,288,256]{2,1,0:T(8,128)(2,1)}, bf16[1,288,256]{2,1,0:T(8,128)(2,1)S(1)}, u32[]{:S(2)}, u32[]{:S(2)}) collective-permute-start(bf16[1,288,256]{2,1,0:T(8,128)(2,1)} %bitcast.301), channel_id=1, source_target_pairs={{0,8},{4,12},{8,0},{12,4},{16,24},{20,28},{24,16},{28,20},{1,9},{5... | collective-permute-start | bytes 442376 | tf_op jit(solution)/shard_map/ppermute | solution.py:51
  6.7 41.0 %collective-permute-start.2 = (bf16[48,3072]{1,0:T(8,128)(2,1)}, bf16[48,3072]{1,0:T(8,128)(2,1)}, u32[]{:S(2)}, u32[]{:S(2)}) collective-permute-start(bf16[48,3072]{1,0:T(8,128)(2,1)} %get-tuple-element.57), channel_id=1, source_target_pairs={{0,4},{4,0},{8,12},{12,8},{16,20},{20,16},{24,28},{28,24},{1,5},{5... | collective-permute-start | bytes 884744 | tf_op jit(solution)/shard_map/ppermute | solution.py:51
  6.9 48.6 %collective-permute-start.3 = (bf16[256,2048]{1,0:T(8,128)(2,1)}, bf16[256,2048]{1,0:T(8,128)(2,1)}, u32[]{:S(2)}, u32[]{:S(2)}) collective-permute-start(bf16[256,2048]{1,0:T(8,128)(2,1)} %param.41), channel_id=1, source_target_pairs={{0,4},{4,0},{8,12},{12,8},{16,20},{20,16},{24,28},{28,24},{1,5},{5... | collective-permute-start | bytes 3145736 | tf_op jit(solution)/shard_map/ppermute | solution.py:51
  55.4 42.1 %collective-permute-start.16 = (bf16[4,288,256]{2,1,0:T(8,128)(2,1)S(1)}, bf16[4,288,256]{2,1,0:T(8,128)(2,1)S(1)}, u32[]{:S(2)}, u32[]{:S(2)}) collective-permute-start(bf16[4,288,256]{2,1,0:T(8,128)(2,1)S(1)} %pad_maximum_fusion.12), channel_id=1, source_target_pairs={{0,4},{4,0},{8,12},{12,8},{16,20},{20,16},{24,28},{28,24},{1,5},{5... | collective-permute-start | bytes 1769480 | tf_op jit(solution)/shard_map/ppermute | solution.py:51
  56.0 35.7 %collective-permute-start.6 = (bf16[256,1536]{1,0:T(8,128)(2,1)S(1)}, bf16[256,1536]{1,0:T(8,128)(2,1)S(1)}, u32[]{:S(2)}, u32[]{:S(2)}) collective-permute-start(bf16[256,1536]{1,0:T(8,128)(2,1)S(1)} %copy-done.95), channel_id=1, source_target_pairs={{0,16},{4,20},{8,24},{12,28},{16,0},{20,4},{24,8},{28,12},{1,17},{... | collective-permute-start | bytes 2359304 | tf_op jit(solution)/shard_map/ppermute | solution.py:51
  57.7 48.4 %collective-permute-start.11 = (bf16[256,1536]{1,0:T(8,128)(2,1)}, bf16[256,1536]{1,0:T(8,128)(2,1)}, u32[]{:S(2)}, u32[]{:S(2)}) collective-permute-start(bf16[256,1536]{1,0:T(8,128)(2,1)} %get-tuple-element.61), channel_id=1, source_target_pairs={{0,24},{4,28},{8,16},{12,20},{16,8},{20,12},{24,0},{28,4},{1,25},{... | collective-permute-start | bytes 2359304 | tf_op jit(solution)/shard_map/ppermute | solution.py:51
  121.1 46.6 %collective-permute-start.19 = (bf16[192,2048]{1,0:T(8,128)(2,1)}, bf16[192,2048]{1,0:T(8,128)(2,1)}, u32[]{:S(2)}, u32[]{:S(2)}) collective-permute-start(bf16[192,2048]{1,0:T(8,128)(2,1)} %bitcast.29), channel_id=1, source_target_pairs={{0,8},{4,12},{8,0},{12,4},{16,24},{20,28},{24,16},{28,20},{1,9},{5... | collective-permute-start | bytes 2359304 | tf_op jit(solution)/shard_map/ppermute | solution.py:51
  124.9 49.2 %collective-permute-start.20 = (bf16[192,2048]{1,0:T(8,128)(2,1)}, bf16[192,2048]{1,0:T(8,128)(2,1)}, u32[]{:S(2)}, u32[]{:S(2)}) collective-permute-start(bf16[192,2048]{1,0:T(8,128)(2,1)} %bitcast.29), channel_id=1, source_target_pairs={{0,16},{4,20},{8,24},{12,28},{16,0},{20,4},{24,8},{28,12},{1,17},{... | collective-permute-start | bytes 2359304 | tf_op jit(solution)/shard_map/ppermute | solution.py:51
  126.6 28.1 %collective-permute-start.10 = (bf16[96,2048]{1,0:T(8,128)(2,1)}, bf16[96,2048]{1,0:T(8,128)(2,1)}, u32[]{:S(2)}, u32[]{:S(2)}) collective-permute-start(bf16[96,2048]{1,0:T(8,128)(2,1)} %slice.650), channel_id=1, source_target_pairs={{0,8},{4,12},{8,0},{12,4},{16,24},{20,28},{24,16},{28,20},{1,9},{5... | collective-permute-start | bytes 1179656 | tf_op jit(solution)/shard_map/ppermute | solution.py:51
  163.3 45.2 %collective-permute-start.17 = (bf16[768,768]{1,0:T(8,128)(2,1)S(1)}, bf16[768,768]{1,0:T(8,128)(2,1)}, u32[]{:S(2)}, u32[]{:S(2)}) collective-permute-start(bf16[768,768]{1,0:T(8,128)(2,1)S(1)} %add_convert_fusion.1), channel_id=1, source_target_pairs={{0,4},{4,0},{8,12},{12,8},{16,20},{20,16},{24,28},{28,24},{1,5},{5... | collective-permute-start | bytes 3538952 | tf_op jit(solution)/shard_map/ppermute | solution.py:51
  169.7 86.6 %collective-permute-start.31 = (bf16[256,2048]{1,0:T(8,128)(2,1)}, bf16[256,2048]{1,0:T(8,128)(2,1)}, u32[]{:S(2)}, u32[]{:S(2)}) collective-permute-start(bf16[256,2048]{1,0:T(8,128)(2,1)} %get-tuple-element.104), channel_id=1, source_target_pairs={{0,8},{4,12},{8,0},{12,4},{16,24},{20,28},{24,16},{28,20},{1,9},{5... | collective-permute-start | bytes 3145736 | tf_op jit(solution)/shard_map/ppermute | solution.py:51
  170.9 86.3 %collective-permute-start.32 = (bf16[256,2048]{1,0:T(8,128)(2,1)}, bf16[256,2048]{1,0:T(8,128)(2,1)}, u32[]{:S(2)}, u32[]{:S(2)}) collective-permute-start(bf16[256,2048]{1,0:T(8,128)(2,1)} %get-tuple-element.103), channel_id=1, source_target_pairs={{0,16},{4,20},{8,24},{12,28},{16,0},{20,4},{24,8},{28,12},{1,17},{... | collective-permute-start | bytes 3145736 | tf_op jit(solution)/shard_map/ppermute | solution.py:51
  173.7 31.1 %collective-permute-start.21 = (bf16[96,2048]{1,0:T(8,128)(2,1)S(1)}, bf16[96,2048]{1,0:T(8,128)(2,1)S(1)}, u32[]{:S(2)}, u32[]{:S(2)}) collective-permute-start(bf16[96,2048]{1,0:T(8,128)(2,1)S(1)} %slice.660), channel_id=1, source_target_pairs={{0,16},{4,20},{8,24},{12,28},{16,0},{20,4},{24,8},{28,12},{1,17},{... | collective-permute-start | bytes 1179656 | tf_op jit(solution)/shard_map/ppermute | solution.py:51
  175.0 32.6 %collective-permute-start.22 = (bf16[96,2048]{1,0:T(8,128)(2,1)S(1)}, bf16[96,2048]{1,0:T(8,128)(2,1)S(1)}, u32[]{:S(2)}, u32[]{:S(2)}) collective-permute-start(bf16[96,2048]{1,0:T(8,128)(2,1)S(1)} %slice.661), channel_id=1, source_target_pairs={{0,8},{4,12},{8,0},{12,4},{16,24},{20,28},{24,16},{28,20},{1,9},{5... | collective-permute-start | bytes 1179656 | tf_op jit(solution)/shard_map/ppermute | solution.py:51
  204.8 52.9 %collective-permute-start.33 = (bf16[256,2048]{1,0:T(8,128)(2,1)}, bf16[256,2048]{1,0:T(8,128)(2,1)}, u32[]{:S(2)}, u32[]{:S(2)}) collective-permute-start(bf16[256,2048]{1,0:T(8,128)(2,1)} %get-tuple-element.102), channel_id=1, source_target_pairs={{0,24},{4,28},{8,16},{12,20},{16,8},{20,12},{24,0},{28,4},{1,25},{... | collective-permute-start | bytes 3145736 | tf_op jit(solution)/shard_map/ppermute | solution.py:51
  270.1 66.8 %collective-permute-start.52 = (bf16[1,16,128]{2,1,0:T(8,128)(2,1)S(1)}, bf16[1,16,128]{2,1,0:T(8,128)(2,1)S(1)}, u32[]{:S(2)}, u32[]{:S(2)}) collective-permute-start(bf16[1,16,128]{2,1,0:T(8,128)(2,1)S(1)} %fusion.151), channel_id=1, source_target_pairs={{0,1},{1,0},{2,3},{3,2},{4,5},{5,4},{6,7},{7,6},{8,9},{9,8},{10,11... | collective-permute-start | bytes 12296 | tf_op jit(solution)/shard_map/ppermute | solution.py:51
  417.8 25.7 %collective-permute-start.47 = (bf16[768,768]{1,0:T(8,128)(2,1)}, bf16[768,768]{1,0:T(8,128)(2,1)S(1)}, u32[]{:S(2)}, u32[]{:S(2)}) collective-permute-start(bf16[768,768]{1,0:T(8,128)(2,1)} %bitcast.343), channel_id=1, source_target_pairs={{0,4},{4,0},{8,12},{12,8},{16,20},{20,16},{24,28},{28,24},{1,5},{5... | collective-permute-start | bytes 3538952 | tf_op jit(solution)/shard_map/ppermute | solution.py:51
  420.1 59.8 %collective-permute-start.49 = (bf16[192,2048]{1,0:T(8,128)(2,1)}, bf16[192,2048]{1,0:T(8,128)(2,1)}, u32[]{:S(2)}, u32[]{:S(2)}) collective-permute-start(bf16[192,2048]{1,0:T(8,128)(2,1)} %pad_maximum_fusion.8), channel_id=1, source_target_pairs={{0,8},{4,12},{8,0},{12,4},{16,24},{20,28},{24,16},{28,20},{1,9},{5... | collective-permute-start | bytes 2359304 | tf_op jit(solution)/shard_map/ppermute | solution.py:51
  425.3 55.2 %collective-permute-start.51 = (bf16[192,2048]{1,0:T(8,128)(2,1)}, bf16[192,2048]{1,0:T(8,128)(2,1)}, u32[]{:S(2)}, u32[]{:S(2)}) collective-permute-start(bf16[192,2048]{1,0:T(8,128)(2,1)} %pad_maximum_fusion.9), channel_id=1, source_target_pairs={{0,16},{4,20},{8,24},{12,28},{16,0},{20,4},{24,8},{28,12},{1,17},{... | collective-permute-start | bytes 2359304 | tf_op jit(solution)/shard_map/ppermute | solution.py:51
  454.8 30.5 %collective-permute-start.64 = (bf16[4,144,256]{2,1,0:T(8,128)(2,1)}, bf16[4,144,256]{2,1,0:T(8,128)(2,1)}, u32[]{:S(2)}, u32[]{:S(2)}) collective-permute-start(bf16[4,144,256]{2,1,0:T(8,128)(2,1)} %pad_maximum_fusion.19), channel_id=1, source_target_pairs={{0,4},{4,0},{8,12},{12,8},{16,20},{20,16},{24,28},{28,24},{1,5},{5... | collective-permute-start | bytes 884744 | tf_op jit(solution)/shard_map/ppermute | solution.py:51
  468.2 43.3 %collective-permute-start.59 = (bf16[2,48,3072]{2,1,0:T(8,128)(2,1)S(1)}, bf16[2,48,3072]{2,1,0:T(8,128)(2,1)S(1)}, u32[]{:S(2)}, u32[]{:S(2)}) collective-permute-start(bf16[2,48,3072]{2,1,0:T(8,128)(2,1)S(1)} %pad_maximum_fusion.13), channel_id=1, source_target_pairs={{0,2},{1,3},{2,0},{3,1},{4,6},{5,7},{6,4},{7,5},{8,10},{9,11},{10,... | collective-permute-start | bytes 1769480 | tf_op jit(solution)/shard_map/ppermute | solution.py:51
  492.2 41.5 %collective-permute-start.61 = (bf16[192,2048]{1,0:T(8,128)(2,1)S(1)}, bf16[192,2048]{1,0:T(8,128)(2,1)S(1)}, u32[]{:S(2)}, u32[]{:S(2)}) collective-permute-start(bf16[192,2048]{1,0:T(8,128)(2,1)S(1)} %pad_maximum_fusion.10), channel_id=1, source_target_pairs={{0,8},{4,12},{8,0},{12,4},{16,24},{20,28},{24,16},{28,20},{1,9},{5... | collective-permute-start | bytes 2359304 | tf_op jit(solution)/shard_map/ppermute | solution.py:51
  495.0 38.7 %collective-permute-start.63 = (bf16[192,2048]{1,0:T(8,128)(2,1)S(1)}, bf16[192,2048]{1,0:T(8,128)(2,1)S(1)}, u32[]{:S(2)}, u32[]{:S(2)}) collective-permute-start(bf16[192,2048]{1,0:T(8,128)(2,1)S(1)} %pad_maximum_fusion.11), channel_id=1, source_target_pairs={{0,16},{4,20},{8,24},{12,28},{16,0},{20,4},{24,8},{28,12},{1,17},{... | collective-permute-start | bytes 2359304 | tf_op jit(solution)/shard_map/ppermute | solution.py:51
  (196 other events, 1889.0 us)

commit v4 on v3

--- a/solution.py
+++ b/solution.py
@@ -69,12 +69,13 @@
     return masks
 
 
-def gather_rows(block, bits):
+def gather_rows(block, bits, gate=()):
     half = block.shape[0] // 2
     got = {0: [block]}
     upper, lower = {}, {}
     for bit in bits:
         there = swap(block, "shard", bit)
+        there = after(there, *gate) if gate else there
         got[bit] = [there]
         upper[bit], lower[bit] = there[:half], there[half:]
     for which, order in ((upper, bits), (lower, bits[::-1])):
@@ -84,7 +85,7 @@
     pieces = []
     for mask in subsets(bits):
         pieces += got[mask] if mask in got else [upper[mask], lower[mask]]
-    return jnp.concatenate(pieces, 0), pieces[1], pieces[-1]
+    return jnp.concatenate(pieces, 0), [got[bit][0] for bit in bits], pieces[-1]
 
 
 def scatter_rows(parts, bits, gate=()):
@@ -97,17 +98,15 @@
                 other = swap(which[sub | order[k]], "shard", order[k])
                 other = after(other, *gate) if gate else other
                 which[sub] = (which[sub].astype(F32) + other.astype(F32)).astype(BF16)
-    total = parts[0].astype(F32)
-    for bit in bits:
-        total = total + swap(jnp.concatenate([upper[bit], lower[bit]], 0), "shard", bit).astype(F32)
-    return total
+    blocks = [jnp.concatenate([upper[bit], lower[bit]], 0) for bit in bits]
+    return [parts[0]] + [swap(b, "shard", bit) for b, bit in zip(blocks, bits)], blocks[-1]
 
 
 def gather_blocks(value, axis, bits, gates=None):
     current = value[None]
     for bit in bits:
         there = swap(current, axis, bit)
-        if gates:
+        if gates and bit in gates:
             there = after(there, *gates[bit])
         current = jnp.concatenate([current, there], 0)
     return current
@@ -240,6 +239,62 @@
         ),
         name="place_columns",
     )(me, stacked)
+
+
+def total_of(refs):
+    total = refs[0][...].astype(F32)
+    for ref in refs[1:]:
+        total = total + ref[...].astype(F32)
+    return total
+
+
+def normalised(values):
+    centre = jnp.mean(values, axis=-1, keepdims=True)
+    offset = values - centre
+    scale = lax.rsqrt(jnp.mean(offset * offset, axis=-1, keepdims=True) + EPSILON)
+    return offset * scale, scale
+
+
+def norm_kernel(base, shift, gain, bias, *refs):
+    terms, (res_ref, out_ref) = refs[:-2], refs[-2:]
+    values = base[...].astype(F32) + (total_of(terms) + shift[...].astype(F32))
+    res_ref[...] = values
+    unit, _ = normalised(values)
+    out_ref[...] = (unit * gain[...].astype(F32) + bias[...].astype(F32)).astype(BF16)
+
+
+def norm_back_kernel(values, gain, base, *refs, outs):
+    terms, outputs = refs[: len(refs) - outs], refs[len(refs) - outs :]
+    unit, scale = normalised(values[...].astype(F32))
+    grad = total_of(terms) * gain[...].astype(F32)
+    mean_one = jnp.mean(grad, axis=-1, keepdims=True)
+    mean_two = jnp.mean(grad * unit, axis=-1, keepdims=True)
+    total = base[...].astype(F32) + scale * (grad - mean_one - unit * mean_two)
+    for out in outputs:
+        out[...] = total.astype(out.dtype)
+
+
+def row_call(kernel, order, rows, wide, dtypes, name):
+    tile = 32 if rows % 32 == 0 else rows
+    args, specs = [], []
+    for value in order:
+        if value.ndim == 1:
+            args.append(value[None])
+            specs.append(pl.BlockSpec((1, wide), lambda i: (0, 0)))
+        else:
+            args.append(value)
+            specs.append(pl.BlockSpec((tile, wide), lambda i: (i, 0)))
+    return pl.pallas_call(
+        kernel,
+        out_shape=[jax.ShapeDtypeStruct((rows, wide), d) for d in dtypes],
+        grid=(rows // tile,),
+        in_specs=specs,
+        out_specs=[pl.BlockSpec((tile, wide), lambda i: (i, 0))] * len(dtypes),
+        cost_estimate=pl.CostEstimate(
+            flops=20 * rows * wide, bytes_accessed=16 * rows * wide, transcendentals=0
+        ),
+        name=name,
+    )(*args)
 
 
 def seen(pos_q, pos_k, lab_q, lab_k):
@@ -418,22 +473,11 @@
     chosen = adapter_pick[0]
     starts = piece_start[0]
 
-    owners = np.concatenate([np.arange(chips) * 2, np.arange(chips) * 2 + 1]).astype(np.int32)
-    locs = np.tile(np.arange(rows, dtype=np.int32), 2 * chips)
-    positions = (me ^ jnp.asarray(np.repeat(owners, rows))) * rows + jnp.asarray(locs)
-    labels = jnp.stack([piece_labels(starts[s], positions) for s in range(count)])
-    where = (positions[:, None], positions[None, :], labels[:, :, None], labels[:, None, :])
-
-    row_seq = np.tile(np.repeat(np.arange(count), rows), chips)
-
     def keep_own(value, terms=1):
         of_row = lax.broadcasted_iota(jnp.int32, value.shape, 0) // rows % count
         of_col = lax.broadcasted_iota(jnp.int32, value.shape, 1) // (terms * rank)
         return jnp.where(of_row == of_col, value, 0.0).astype(BF16)
 
-    gain_one, shift_one = ln1_gain.astype(F32), ln1_bias.astype(F32)
-    gain_two, shift_two = ln2_gain.astype(F32), ln2_bias.astype(F32)
-
     narrow = [out_query, out_key, out_value, in_attn, out_expand, in_reduce]
     edges = np.cumsum([0] + [n.shape[2] for n in narrow])
     mine, packed = pick_maps(
@@ -441,11 +485,6 @@
     )
     packed_other = swap(packed, "shard", 1)
     order = bits + [1]
-    near = gather_blocks(mine, "shard", bits)
-    stacked = jnp.concatenate([near, swap(near, "shard", 1)], 0)
-    w_out_other = swap(w_out, "shard", 1)
-    w_down_other = swap(w_down, "shard", 1)
-
     chip = me // 2
 
     def slices(tables, width):
@@ -463,32 +502,45 @@
             pieces.append(both)
         return pieces
 
-    def turn(pieces):
-        own = [swap(piece, "shard", 2 * i) if i else piece for i, piece in enumerate(pieces)]
+    def exchange(pieces):
+        return [swap(piece, "shard", 2 * i) if i else piece for i, piece in enumerate(pieces)]
+
+    def both_cores(own):
         return own + [swap(piece, "shard", 1) for piece in own]
 
     first_tables = after((w_query, w_key, w_value), mine)
-    pieces_qkv = after(
-        tuple(slices(first_tables, span)), near, packed_other, w_out_other, w_down_other
-    )
-    turned = turn(pieces_qkv)
-    w_qkv_mine, w_qkv_other = place_weights(me_arr, turned, 3 * span, False)
-
-    features = after(inputs[0].reshape(block, wide), *pieces_qkv).astype(F32)
-    normed, norm_one_back = jax.vjp(lambda v: layer_norm(v, gain_one, shift_one), features)
-    hidden_block = after(normed.astype(BF16), *[turned[bit // 2] for bit in bits])
+    pieces_qkv = after(tuple(slices(first_tables, span)), packed_other)
+    turned = exchange(pieces_qkv)
+
+    rows_in = after(inputs[0].reshape(block, wide), *pieces_qkv)
+    features = rows_in.astype(F32)
+    normed = layer_norm(features, ln1_gain.astype(F32), ln1_bias.astype(F32)).astype(BF16)
+    starts, b_query, b_value, b_up, me_late, chosen, packed = after(
+        (starts, b_query, b_value, b_up, me, chosen, packed), normed
+    )
+    hidden_block = after(normed, *[turned[bit // 2] for bit in bits])
     hidden_one, one_first, one_last = gather_rows(hidden_block, bits)
 
-    cot_mine = cotangent[0].reshape(block, wide)
-    cot, cot_first, cot_last = gather_rows(after(cot_mine, one_first), bits)
-    pieces_up = slices([after(w_up, one_last, cot_first)], ff_part)
+    w_out, w_down, turned[0] = after((w_out, w_down, turned[0]), *one_first)
+    w_qkv_mine, w_qkv_other = place_weights(me_arr, both_cores(turned), 3 * span, False)
+    w_out_other = swap(w_out, "shard", 1)
+    w_down_other = swap(w_down, "shard", 1)
+    hidden_one = after(hidden_one, w_out_other, w_down_other)
+    near = gather_blocks(mine, "shard", bits, {bit: one_first for bit in bits[1:]})
+    stacked = jnp.concatenate([near, swap(near, "shard", 1)], 0)
+
+    owners = np.concatenate([np.arange(chips) * 2, np.arange(chips) * 2 + 1]).astype(np.int32)
+    locs = np.tile(np.arange(rows, dtype=np.int32), 2 * chips)
+    positions = (me_late ^ jnp.asarray(np.repeat(owners, rows))) * rows + jnp.asarray(locs)
+    labels = jnp.stack([piece_labels(starts[s], positions) for s in range(count)])
+    where = (positions[:, None], positions[None, :], labels[:, :, None], labels[:, None, :])
 
     whole = place_columns(me_arr, stacked, subsets(order)).reshape(6, count, rank, wide)
     in_qkv = jnp.swapaxes(whole[:3], 0, 1).reshape(count * 3 * rank, wide)
     in_exp, out_att, out_red = (whole[3 + i].reshape(count * rank, wide) for i in range(3))
 
     rep_bits = bits_of(lax.axis_size("rep"))
-    mark = (chosen[:, None] == jnp.arange(ADAPTERS, dtype=jnp.int32)[None, :]).astype(BF16)
+    mark = (after(chosen, *one_first)[:, None] == jnp.arange(ADAPTERS, dtype=jnp.int32)[None, :]).astype(BF16)
     marks = gather_blocks(jnp.pad(mark, ((0, 16 - count), (0, 128 - ADAPTERS))), "rep", rep_bits)
     groups = marks.shape[0]
     marks = marks[:, :count, :ADAPTERS].reshape(groups * count, 1, ADAPTERS, 1)
@@ -546,18 +598,23 @@
         (mm(hidden_one, w_qkv_mine) + mm(low_qkv, out_qkv_mine) + b_qkv_of(me)).astype(BF16)
     )
     att_own, att_away, lse = attend(where, qkv_own, qkv_other, heads)
+    cot_mine = cotangent[0].reshape(block, wide)
     attended = jnp.concatenate([flat(att_own), swap(flat(att_away), "shard", 1)], 1)
     low_att = keep_own(mm_t(attended, in_att))
+    parts = block_products([(attended, w_out_chip, mm)], low_att, out_att)
+    terms, relayed = scatter_rows(parts, bits)
+    cot, _, _ = gather_rows(after(cot_mine, one_last), bits, (relayed,))
     glow_red = keep_own(mm_t(cot, out_red))
     grad_act = (mm_t(cot, w_down_chip) + mm(glow_red, in_red)).astype(BF16)
-    parts = block_products([(attended, w_out_chip, mm)], low_att, out_att)
-    parts[0] = after(parts[0], grad_act)
-    branch = scatter_rows(parts, bits) + b_out.astype(F32)
-    residual = features + branch
-    normed, norm_two_back = jax.vjp(lambda v: layer_norm(v, gain_two, shift_two), residual)
-    hidden_two, _, _ = gather_rows(normed.astype(BF16), bits)
-
-    (w_up_chip,) = place_weights(me_arr, turn(pieces_up), ff_part, True)
+    pieces_up = slices([after(w_up, one_last)], ff_part)
+    pieces_up = pieces_up[:1] + [after(p, relayed) for p in pieces_up[1:-1]] + pieces_up[-1:]
+    residual, hidden_block = row_call(
+        norm_kernel, [rows_in, b_out, ln2_gain, ln2_bias] + terms, block, wide, [F32, BF16], "norm"
+    )
+    hidden_two, _, _ = gather_rows(hidden_block, bits)
+
+    (w_up_chip,) = place_weights(me_arr, both_cores(exchange(pieces_up)), ff_part, True)
+    hidden_two = after(hidden_two, grad_act)
     low_exp = keep_own(mm_t(hidden_two, in_exp))
     pre = mm(hidden_two, w_up_chip) + mm(low_exp, out_exp) + b_up_chip
     share = 0.5 * (1.0 + lax.erf(pre * np.float32(0.5**0.5)))
@@ -565,15 +622,20 @@
     slope = share + pre * (jnp.exp(-0.5 * pre * pre) * np.float32((2 * np.pi) ** -0.5))
     grad_pre = (slope * grad_act.astype(F32)).astype(BF16)
     glow_exp = keep_own(mm_t(grad_pre, out_exp))
-    grad_two = scatter_rows(block_products([(grad_pre, w_up_chip, mm_t)], glow_exp, in_exp), bits)
-    grad_residual = cot_mine.astype(F32) + norm_two_back(grad_two)[0]
-    grad_block = grad_residual.astype(BF16)
+    terms, grad_sent = scatter_rows(block_products([(grad_pre, w_up_chip, mm_t)], glow_exp, in_exp), bits)
+    grad_residual, grad_block = row_call(
+        functools.partial(norm_back_kernel, outs=2),
+        [residual, ln2_gain, cot_mine] + terms,
+        block,
+        wide,
+        [F32, BF16],
+        "norm_back",
+    )
     grad_branch, _, branch_last = gather_rows(grad_block, bits)
 
     act_late = after(act, grad_block)
     low_red = keep_own(mm_t(act_late, in_red))
     down_parts = block_products([(act_late, w_down_chip, mm)], low_red, out_red)
-    down_parts = {m: after(p, branch_last) for m, p in down_parts.items()}
     glow_att = keep_own(mm_t(grad_branch, out_att))
     grad_att = (mm_t(grad_branch, w_out_chip) + mm(glow_att, in_att)).astype(BF16)
     ga_own = by_chip(grad_att[:, :span])
@@ -582,7 +644,10 @@
     grad_own = flat(grad_own)
     grad_other = swap(flat(grad_away), "shard", 1)
     glow_qkv = keep_own(mm_t(grad_own, out_qkv_mine) + mm_t(grad_other, out_qkv_other), 3)
-    def sum_columns(value, gates=None):
+    def sum_cores(own, away):
+        return own + swap(away.astype(BF16), "shard", 1).astype(F32)
+
+    def core_columns(value):
         width = value.shape[1] // size
 
         def side(which):
@@ -594,20 +659,19 @@
             )
 
         core = me & 1
-        current = side(core).astype(F32) + swap(side(1 - core).astype(BF16), "shard", 1).astype(F32)
+        return sum_cores(side(core), side(1 - core))
+
+    def sum_chips(current):
+        sent = None
         for bit in bits[::-1]:
             current = current.reshape((2, current.shape[0] // 2) + current.shape[1:])
             own = (me // bit) & 1
-            there = swap(
-                lax.dynamic_index_in_dim(current, 1 - own, 0, False).astype(BF16), "shard", bit
-            )
-            if gates:
-                there = after(there, *gates[bit])
-            current = lax.dynamic_index_in_dim(current, own, 0, False) + there.astype(F32)
-        return current[0]
-
-    def sum_cores(own, away):
-        return own + swap(away.astype(BF16), "shard", 1).astype(F32)
+            away = lax.dynamic_index_in_dim(current, 1 - own, 0, False).astype(BF16)
+            sent = away if sent is None else sent
+            current = lax.dynamic_index_in_dim(current, own, 0, False) + swap(
+                away, "shard", bit
+            ).astype(F32)
+        return current[0], sent
 
     def over_groups(terms, gates=None):
         widths = [t.shape[1] for t in terms]
@@ -620,46 +684,36 @@
             start += width
         return outs
 
+    def halves(value):
+        middle = value.shape[1] // 2
+        return value[:, :middle], value[:, middle:]
+
     glow_late, low_late = after((glow_exp, low_exp), grad_block)
-    arrived = {bit: (grad_away,) for bit in bits}
-    first = sum_columns(
+    act_mid, grad_mid, low_mid, glow_mid = after((act, grad_pre, low_exp, glow_red), grad_sent)
+    red_own, red_away = halves(t_mm(glow_mid, act_mid))
+    exp_own, exp_away = halves(t_mm(low_mid, grad_mid))
+    local = sum_cores(
+        jnp.concatenate([red_own, exp_own], 1), jnp.concatenate([red_away, exp_away], 1)
+    )
+    s_in_red, s_out_exp = over_groups(
+        [local[:, :ff_part], local[:, ff_part:]], {rep_bits[-1]: (grad_away,)}
+    )
+
+    near_first = core_columns(
         jnp.concatenate(
             [t_mm(low_att, grad_branch), t_mm(glow_late, hidden_two), t_mm(low_red, cot)], 0
-        ),
-        arrived,
-    ).reshape(3, count * rank, slice_wide)
-    chip_wide = jnp.concatenate(
-        [t_mm(glow_att, attended), t_mm(glow_red, act_late), t_mm(low_late, grad_pre)], 1
-    )
-    cut = [0, span, 2 * span, 2 * span + ff_part, 2 * span + 2 * ff_part, 2 * span + 3 * ff_part]
-    cut.append(chip_wide.shape[1])
-    side = [chip_wide[:, cut[i] : cut[i + 1]] for i in range(6)]
-    local = sum_cores(jnp.concatenate(side[::2], 1), jnp.concatenate(side[1::2], 1))
-    products = [(grad_own, w_qkv_mine, mm_t), (grad_other, w_qkv_other, mm_t)]
-    parts = block_products(products, glow_qkv, in_qkv)
-    far_part = parts[2 * (chips - 1)]
-    early = over_groups(
-        [
-            local[:, :span],
-            local[:, span : span + ff_part],
-            local[:, span + ff_part :],
-            first[0],
-            first[1],
-            first[2],
-        ],
-        {bit: (far_part,) for bit in rep_bits},
-    )
-    parts[0] = after(parts[0], *early)
-    grad_one = scatter_rows(parts, bits)
-    input_rows = grad_residual + norm_one_back(grad_one)[0]
-
-    down_parts[0] = after(down_parts[0], far_part)
-    down = scatter_rows(down_parts, bits, (grad_away,))
-    layer_rows = residual + down + b_down.astype(F32)
-
-    s_in_att, s_in_red, s_out_exp, s_out_att, s_in_exp, s_out_red = early
-    glow_last, own_last, other_last = after((glow_qkv, grad_own, grad_other), far_part)
-    second = sum_columns(t_mm(glow_last, hidden_one)).reshape(count, 3, rank, slice_wide)
+        )
+    ).astype(BF16)
+    tall = near_first.shape[1]
+    riders = {}
+    for i in range(chips):
+        rider = lax.dynamic_index_in_dim(near_first, chip ^ i, 0, False)
+        rider = jnp.pad(rider, ((0, block - tall), (0, 0)))
+        riders[2 * i] = jnp.concatenate([down_parts[2 * i], rider], 1)
+    att_side = sum_cores(*halves(t_mm(glow_att, attended)))
+
+    glow_last = glow_qkv
+    in_terms = t_mm(glow_last, hidden_one)
 
     def own_terms(full):
         full = full.reshape(count, 3, rank, 3, span)
@@ -667,15 +721,42 @@
             [full[:, t, :, t].reshape(count * rank, span) for t in range(3)], 1
         )
 
+    near_second = core_columns(in_terms)
+    products = [(grad_own, w_qkv_mine, mm_t), (grad_other, w_qkv_other, mm_t)]
+    parts = block_products(products, after(glow_qkv, in_terms), in_qkv)
+    second, sent = sum_chips(near_second)
+    far = 2 * (chips - 1)
+    parts[far] = after(parts[far], sent)
+    far_part = parts[far]
+
+    terms, relayed = scatter_rows(parts, bits)
+    down, _ = scatter_rows(riders, bits, (grad_away,))
+    down[0] = after(down[0], relayed)
+    first = sum(t[:tall, wide:].astype(F32) for t in down).reshape(3, count * rank, slice_wide)
+    layer_rows = residual + b_down.astype(F32) + sum(t[:, :wide].astype(F32) for t in down)
+
+    own_last, other_last = after((grad_own, grad_other), relayed)
     outer = sum_cores(own_terms(t_mm(low_qkv, own_last)), own_terms(t_mm(low_qkv, other_last)))
+    second = second.reshape(count, 3, rank, slice_wide)
+    s_in_att, s_out_att, s_in_exp, s_out_red = over_groups(
+        [att_side, first[0], first[1], first[2]]
+    )
     late = over_groups(
         [second[:, t].reshape(count * rank, slice_wide) for t in range(3)]
         + [outer[:, t * span : (t + 1) * span] for t in range(3)]
     )
+    (input_rows,) = row_call(
+        functools.partial(norm_back_kernel, outs=1),
+        [rows_in, ln1_gain, grad_residual] + terms,
+        block,
+        wide,
+        [BF16],
+        "norm_back",
+    )
     shape = (1, count, rows, wide)
     return (
         layer_rows.astype(BF16).reshape(shape),
-        input_rows.astype(BF16).reshape(shape),
+        input_rows.reshape(shape),
         late[0],
         late[3],
         late[1],

time: 545 us -> 513 us (0.941)
  waiting for transfers between devices: 173 us -> 151 us
  Pallas kernels: 35.1 us -> 52.8 us
  other arithmetic: 47.9 us -> 31 us
  matrix products: 124 us -> 118 us
    ppermute x70 -> x71, waiting for transfers between devices: 173 us -> 151 us  [swap(): return lax.ppermute(value, axis, [(i, i ^ mask) for i in range(size)])]
    pallas_call x0 -> x3, Pallas kernels: none -> 18.1 us  [row_call(): pl.pallas_call(kernel, out_shape=[jax.ShapeDtypeStruct((rows, wide), d) f...]
    convert_element_type x8 -> x6, other arithmetic: 10.1 us -> 1.73 us  [the longest x1 0.62 us: over_groups(): data = jnp.concatenate([t.astype(BF16) for t in terms], 1)]
    ppermute x70 -> x71, starting transfers between devices: 64.4 us -> 61.6 us  [swap(): return lax.ppermute(value, axis, [(i, i ^ mask) for i in range(size)])]
    unnamed x319 -> x299, local copies, waits for them, and re-layouts: 43.7 us -> 42.4 us
  transfers between devices with their start and end apart: 70 -> 71, of which waited for: 25 -> 18; matrix products, arithmetic and copies ran while one was open for 42% -> 38% of each run, Pallas kernels for 7% -> 7%
where the time goes in v4:
time: 513 us; the launch traced here: 506 us
  waiting for transfers between devices  151 us (29%)
  matrix products  118 us (23%)
  local copies, waits for them, and re-layouts  85.9 us (17%)
  starting transfers between devices  61.6 us (12%)
  Pallas kernels  52.8 us (10%)
  other arithmetic  31 us (6%)
  between operations  5.33 us (1%)
    ppermute x71, waiting for transfers between devices, swap(): return lax.ppermute(value, axis, [(i, i ^ mask) for i in range(size)])  151 us
    ppermute x71, starting transfers between devices, swap(): return lax.ppermute(value, axis, [(i, i ^ mask) for i in range(size)])  61.6 us
    dot_general x23, matrix products, mm_t(): lax.dot_general(a, b, (((1,), (1,)), ((), ())), preferred_element_type=F32)  51.4 us
    dot_general x32, matrix products, mm(): lax.dot_general(a, b, (((1,), (0,)), ((), ())), preferred_element_type=F32)  50.6 us
    unnamed x299, local copies, waits for them, and re-layouts  42.4 us
    pallas_call x3, Pallas kernels, row_call(): pl.pallas_call(kernel, out_shape=[jax.ShapeDtypeStruct((rows, wide), d) f...  18.1 us
    dot_general x21, matrix products, t_mm(): lax.dot_general(a, b, (((0,), (0,)), ((), ())), preferred_element_type=F32)  15.8 us
    pallas_call x2, Pallas kernels, place_weights(): pl.pallas_call(functools.partial(place_kernel, count=count, width=width,...  12.2 us
  transfers between devices with their start and end apart: 71, of which 18 were waited for; matrix products, arithmetic and copies ran while one was open for 38% of the time, Pallas kernels for 7%

profile of v4, /device:TPU:0, one launch (start us, length us, event | category | flops | bytes accessed | tf_op | source)
XLA Modules:
  0.0 505.8 jit_solution(4792566681031239752)
XLA Ops:
  31.1 17.1 %collective-permute-done.1.refs_1_ = bf16[256,1536]{1,0:T(8,128)(2,1)S(1)} collective-permute-done((bf16[256,1536]{1,0:T(8,128)(2,1)}, bf16[256,1536]{1,0:T(8,128)(2,1)S(1)}, u32[]{:S(2)}, u32[]{:S(2)}) %collective-permute-start.1) | collective-permute-done | bytes 786464 | tf_op jit(solution)/shard_map/ppermute | solution.py:51
  62.4 24.0 %collective-permute-done.4 = bf16[192,2048]{1,0:T(8,128)(2,1)S(1)} collective-permute-done((bf16[192,2048]{1,0:T(8,128)(2,1)S(1)}, bf16[192,2048]{1,0:T(8,128)(2,1)S(1)}, u32[]{:S(2)}, u32[]{:S(2)}) %collective-permute-start.4) | collective-permute-done | bytes 786464 | tf_op jit(solution)/shard_map/ppermute | solution.py:51
  123.6 5.6 %constant_dynamic-slice_fusion = (bf16[256,2048]{1,0:T(8,128)(2,1)}, bf16[256,2048]{1,0:T(8,128)(2,1)}, bf16[256,2048]{1,0:T(8,128)(2,1)}, bf16[256,2048]{1,0:T(8,128)(2,1)}) fusion(bf16[256,8192]{1,0:T(8,128)(2,1)} %param.45, s32[]{:T(128)S(6)} %select_n.263, s32[]{:T(128)S(6)} %select_n.262, s32[]{:T(128)S(6)} %select_n.261, s32[]{:T(128)S(6)} %select_n.260), kind=kLoop, calls=%fused_computation.333 | loop fusion | bytes 8388624 | tf_op jit(solution)/shard_map/dynamic_slice | solution.py:494
  138.1 5.5 %place_weights.2 = (bf16[2048,768]{1,0:T(8,128)(2,1)}, bf16[2048,768]{1,0:T(8,128)(2,1)}) custom-call(s32[1]{0:T(128)} %bitcast.15.me_ref, bf16[256,1536]{1,0:T(8,128)(2,1)} %copy-done.51, bf16[256,1536]{1,0:T(8,128)(2,1)} %copy-done.64, bf16[256,1536]{1,0:T(8,128)(2,1)} %copy-done.65, bf16[256,1536]{1,0:T(8,128)(2,1)} %collective-permute-done.9.refs_3_, ...), custom_call_target="tpu_custom_call" | custom-call | bytes 12582912 | tf_op jit(solution)/shard_map/place_weights/pallas_call | solution.py:158
  157.8 7.3 %attend.1 = (bf16[4,3,64,256]{3,2,1,0:T(8,128)(2,1)}, bf16[4,3,64,256]{3,2,1,0:T(8,128)(2,1)}, f32[3,512,2]{2,1,0:T(8,128)}) custom-call(s32[512,1]{1,0:T(8,128)} %copy.77.pq, s32[1,512]{1,0:T(1,128)} %bitcast.330, s32[3,512,1]{2,1,0:T(8,128)} %copy.78.lq, s32[3,1,512]{2,1,0:T(1,128)} %broadcast_in_dim.109.lk, bf16[4,3,64,768]{3,2,1,0:T(8,128)(2,1)} %bitcast.303, ...), custom_call_target="tpu_custom_call" | custom-call | flops 805306368 | bytes 3145728 | tf_op jit(solution)/shard_map/attend/pallas_call | solution.py:354
  167.5 4.9 constant_dynamic-update-slice_fusion.17
  181.6 6.8 %collective-permute-done.19 = bf16[96,2048]{1,0:T(8,128)(2,1)S(1)} collective-permute-done((bf16[96,2048]{1,0:T(8,128)(2,1)S(1)}, bf16[96,2048]{1,0:T(8,128)(2,1)S(1)}, u32[]{:S(2)}, u32[]{:S(2)}) %collective-permute-start.19) | collective-permute-done | bytes 393248 | tf_op jit(solution)/shard_map/ppermute | solution.py:51
  197.4 19.2 %collective-permute-done.29 = bf16[96,2048]{1,0:T(8,128)(2,1)S(1)} collective-permute-done((bf16[96,2048]{1,0:T(8,128)(2,1)S(1)}, bf16[96,2048]{1,0:T(8,128)(2,1)S(1)}, u32[]{:S(2)}, u32[]{:S(2)}) %collective-permute-start.29) | collective-permute-done | bytes 393248 | tf_op jit(solution)/shard_map/ppermute | solution.py:51
  225.6 5.6 %norm.1 = (f32[192,2048]{1,0:T(8,128)}, bf16[192,2048]{1,0:T(8,128)(2,1)}) custom-call(bf16[192,2048]{1,0:T(8,128)(2,1)} %bitcast.246, bf16[1,2048]{1,0:T(2,128)(2,1)} %broadcast_in_dim.101.shift, bf16[1,2048]{1,0:T(2,128)(2,1)} %broadcast_in_dim.102.gain, bf16[1,2048]{1,0:T(2,128)(2,1)} %broadcast_in_dim.103.bias, bf16[192,2048]{1,0:T(8,128)(2,1)} %fusion.14.refs_0_, ...), custom_call_target="tpu_custom_call" | custom-call | flops 7864320 | bytes 6291456 | tf_op jit(solution)/shard_map/norm/pallas_call | solution.py:287
  232.7 13.3 %add_convert_fusion = bf16[768,2048]{1,0:T(8,128)(2,1)} fusion(f32[768,2048]{1,0:T(8,128)} %fusion.90, bf16[768,2048]{1,0:T(8,128)(2,1)} %copy-done.18, bf16[2048,2048]{1,0:T(8,128)(2,1)} %constant_dynamic-update-slice_fusion.17), kind=kOutput, calls=%fused_computation.10 | convolution fusion | flops 6445596672 | bytes 20971520 | tf_op jit(solution)/shard_map/dot_general | solution.py:42
  246.2 11.8 %collective-permute-done.24 = bf16[192,2048]{1,0:T(8,128)(2,1)S(1)} collective-permute-done((bf16[192,2048]{1,0:T(8,128)(2,1)}, bf16[192,2048]{1,0:T(8,128)(2,1)S(1)}, u32[]{:S(2)}, u32[]{:S(2)}) %collective-permute-start.24) | collective-permute-done | bytes 786464 | tf_op jit(solution)/shard_map/ppermute | solution.py:51
  261.4 5.5 %collective-permute-done.25 = bf16[96,2048]{1,0:T(8,128)(2,1)S(1)} collective-permute-done((bf16[96,2048]{1,0:T(8,128)(2,1)S(1)}, bf16[96,2048]{1,0:T(8,128)(2,1)S(1)}, u32[]{:S(2)}, u32[]{:S(2)}) %collective-permute-start.25) | collective-permute-done | bytes 393248 | tf_op jit(solution)/shard_map/ppermute | solution.py:51
  276.1 6.7 %place_weights.3 = bf16[2048,2048]{1,0:T(8,128)(2,1)} custom-call(s32[1]{0:T(128)} %bitcast.15.me_ref, bf16[256,2048]{1,0:T(8,128)(2,1)} %get-tuple-element.131.refs_0_, bf16[256,2048]{1,0:T(8,128)(2,1)} %collective-permute-done.31.refs_1_, bf16[256,2048]{1,0:T(8,128)(2,1)} %collective-permute-done.32.refs_2_, ...), custom_call_target="tpu_custom_call" | custom-call | bytes 16777216 | tf_op jit(solution)/shard_map/place_weights/pallas_call | solution.py:158
  282.9 14.7 %fusion.5 = (bf16[768,2048]{1,0:T(8,128)(2,1)S(1)}, bf16[768,2048]{1,0:T(8,128)(2,1)S(1)}) fusion(bf16[768,2048]{1,0:T(8,128)(2,1)} %add_convert_fusion, f32[2048]{0:T(1024)S(1)} %maximum_convert_fusion, f32[768,2048]{1,0:T(8,128)} %fusion.89, bf16[768,2048]{1,0:T(8,128)(2,1)} %copy-done.20, bf16[2048,2048]{1,0:T(8,128)(2,1)} %place_weights.3), kind=kOutput, calls=%fused_computation.6 | convolution fusion | flops 6466043904 | bytes 27271168 | tf_op jit(solution)/shard_map/dot_general | solution.py:38
  314.5 5.6 %collective-permute-done.40 = bf16[96,2048]{1,0:T(8,128)(2,1)S(1)} collective-permute-done((bf16[96,2048]{1,0:T(8,128)(2,1)S(1)}, bf16[96,2048]{1,0:T(8,128)(2,1)S(1)}, u32[]{:S(2)}, u32[]{:S(2)}) %collective-permute-start.40) | collective-permute-done | bytes 393248 | tf_op jit(solution)/shard_map/ppermute | solution.py:51
  334.2 7.0 %collective-permute-done.41.refs_2_ = bf16[192,2048]{1,0:T(8,128)(2,1)} collective-permute-done((bf16[192,2048]{1,0:T(8,128)(2,1)S(1)}, bf16[192,2048]{1,0:T(8,128)(2,1)}, u32[]{:S(2)}, u32[]{:S(2)}) %collective-permute-start.41) | collective-permute-done | bytes 786464 | tf_op jit(solution)/shard_map/ppermute | solution.py:51
  344.7 6.6 %norm_back.2 = (f32[192,2048]{1,0:T(8,128)}, bf16[192,2048]{1,0:T(8,128)(2,1)}) custom-call(f32[192,2048]{1,0:T(8,128)} %get-tuple-element.95.values, bf16[1,2048]{1,0:T(2,128)(2,1)} %broadcast_in_dim.102.gain, bf16[192,2048]{1,0:T(8,128)(2,1)} %bitcast.30.base, bf16[192,2048]{1,0:T(8,128)(2,1)} %fusion.10.refs_0_, ...), custom_call_target="tpu_custom_call" | custom-call | flops 7864320 | bytes 6291456 | tf_op jit(solution)/shard_map/norm_back/pallas_call | solution.py:287
  356.4 5.3 %fusion.49 = f32[192,2048]{1,0:T(8,128)S(1)} fusion(bf16[2048,2048]{1,0:T(8,128)(2,1)} %constant_dynamic-update-slice_fusion.17, bf16[768,2048]{1,0:T(8,128)(2,1)S(1)} %copy-done.36), kind=kOutput, calls=%fused_computation.113 | convolution fusion | flops 1610612736 | bytes 10747904 | tf_op jit(solution)/shard_map/dot_general | solution.py:38
  375.8 8.2 %collective-permute-done.44 = bf16[96,2048]{1,0:T(8,128)(2,1)S(1)} collective-permute-done((bf16[96,2048]{1,0:T(8,128)(2,1)S(1)}, bf16[96,2048]{1,0:T(8,128)(2,1)S(1)}, u32[]{:S(2)}, u32[]{:S(2)}) %collective-permute-start.44) | collective-permute-done | bytes 393248 | tf_op jit(solution)/shard_map/ppermute | solution.py:51
  397.5 9.5 %attend_back.1 = (bf16[4,3,64,768]{3,2,1,0:T(8,128)(2,1)}, bf16[4,3,64,768]{3,2,1,0:T(8,128)(2,1)}) custom-call(s32[512,1]{1,0:T(8,128)} %copy.77.pq, s32[1,512]{1,0:T(1,128)} %bitcast.331, s32[3,512,1]{2,1,0:T(8,128)} %copy.78.lq, s32[3,1,512]{2,1,0:T(1,128)} %broadcast_in_dim.109.lk, bf16[4,3,64,768]{3,2,1,0:T(8,128)(2,1)} %bitcast.304, ...), custom_call_target="tpu_custom_call" | custom-call | flops 2013265920 | bytes 5505024 | tf_op jit(solution)/shard_map/attend_back/pallas_call | solution.py:411
  432.2 6.7 %collective-permute-done.60 = bf16[2,144,256]{2,1,0:T(8,128)(2,1)S(1)} collective-permute-done((bf16[2,144,256]{2,1,0:T(8,128)(2,1)S(1)}, bf16[2,144,256]{2,1,0:T(8,128)(2,1)S(1)}, u32[]{:S(2)}, u32[]{:S(2)}) %collective-permute-start.60) | collective-permute-done | bytes 147488 | tf_op jit(solution)/shard_map/ppermute | solution.py:51
  444.0 7.9 %collective-permute-done.50 = bf16[96,2048]{1,0:T(8,128)(2,1)S(1)} collective-permute-done((bf16[96,2048]{1,0:T(8,128)(2,1)S(1)}, bf16[96,2048]{1,0:T(8,128)(2,1)S(1)}, u32[]{:S(2)}, u32[]{:S(2)}) %collective-permute-start.50) | collective-permute-done | bytes 393248 | tf_op jit(solution)/shard_map/ppermute | solution.py:51
  473.4 14.4 %collective-permute-done.67 = bf16[2,48,1024]{2,1,0:T(8,128)(2,1)S(1)} collective-permute-done((bf16[2,48,1024]{2,1,0:T(8,128)(2,1)S(1)}, bf16[2,48,1024]{2,1,0:T(8,128)(2,1)S(1)}, u32[]{:S(2)}, u32[]{:S(2)}) %collective-permute-start.67) | collective-permute-done | bytes 196640 | tf_op jit(solution)/shard_map/ppermute | solution.py:51
  499.7 5.9 %norm_back.3 = bf16[192,2048]{1,0:T(8,128)(2,1)} custom-call(bf16[192,2048]{1,0:T(8,128)(2,1)} %bitcast.247, bf16[1,2048]{1,0:T(2,128)(2,1)} %broadcast_in_dim.114.gain, f32[192,2048]{1,0:T(8,128)} %get-tuple-element.116.base, bf16[192,2048]{1,0:T(8,128)(2,1)} %fusion.8.refs_0_, bf16[192,2048]{1,0:T(8,128)(2,1)} %copy-done.70, ...), custom_call_target="tpu_custom_call" | custom-call | flops 7864320 | bytes 6291456 | tf_op jit(solution)/shard_map/norm_back/pallas_call | solution.py:287
  (645 shorter events, 275.2 us)
Async XLA Ops:
  3.6 47.9 %collective-permute-start.14 = (bf16[1,288,256]{2,1,0:T(8,128)(2,1)}, bf16[1,288,256]{2,1,0:T(8,128)(2,1)S(1)}, u32[]{:S(2)}, u32[]{:S(2)}) collective-permute-start(bf16[1,288,256]{2,1,0:T(8,128)(2,1)} %bitcast.295), channel_id=1, source_target_pairs={{0,8},{4,12},{8,0},{12,4},{16,24},{20,28},{24,16},{28,20},{1,9},{5... | collective-permute-start | bytes 442376 | tf_op jit(solution)/shard_map/ppermute | solution.py:51
  49.1 37.3 %collective-permute-start.4 = (bf16[192,2048]{1,0:T(8,128)(2,1)S(1)}, bf16[192,2048]{1,0:T(8,128)(2,1)S(1)}, u32[]{:S(2)}, u32[]{:S(2)}) collective-permute-start(bf16[192,2048]{1,0:T(8,128)(2,1)S(1)} %fusion.31), channel_id=1, source_target_pairs={{0,16},{4,20},{8,24},{12,28},{16,0},{20,4},{24,8},{28,12},{1,17},{... | collective-permute-start | bytes 2359304 | tf_op jit(solution)/shard_map/ppermute | solution.py:51
  50.6 35.8 %collective-permute-start.3 = (bf16[192,2048]{1,0:T(8,128)(2,1)S(1)}, bf16[192,2048]{1,0:T(8,128)(2,1)S(1)}, u32[]{:S(2)}, u32[]{:S(2)}) collective-permute-start(bf16[192,2048]{1,0:T(8,128)(2,1)S(1)} %fusion.31), channel_id=1, source_target_pairs={{0,8},{4,12},{8,0},{12,4},{16,24},{20,28},{24,16},{28,20},{1,9},{5... | collective-permute-start | bytes 2359304 | tf_op jit(solution)/shard_map/ppermute | solution.py:51
  52.2 52.1 %collective-permute-start.15 = (bf16[2,288,256]{2,1,0:T(8,128)(2,1)}, bf16[2,288,256]{2,1,0:T(8,128)(2,1)}, u32[]{:S(2)}, u32[]{:S(2)}) collective-permute-start(bf16[2,288,256]{2,1,0:T(8,128)(2,1)} %pad_maximum_fusion.18), channel_id=1, source_target_pairs={{0,16},{4,20},{8,24},{12,28},{16,0},{20,4},{24,8},{28,12},{1,17},{... | collective-permute-start | bytes 884744 | tf_op jit(solution)/shard_map/ppermute | solution.py:51
  52.8 57.7 %collective-permute-start.9 = (bf16[256,1536]{1,0:T(8,128)(2,1)}, bf16[256,1536]{1,0:T(8,128)(2,1)}, u32[]{:S(2)}, u32[]{:S(2)}) collective-permute-start(bf16[256,1536]{1,0:T(8,128)(2,1)} %get-tuple-element.78), channel_id=1, source_target_pairs={{0,24},{4,28},{8,16},{12,20},{16,8},{20,12},{24,0},{28,4},{1,25},{... | collective-permute-start | bytes 2359304 | tf_op jit(solution)/shard_map/ppermute | solution.py:51
  86.4 57.2 %collective-permute-start.8 = (bf16[1024,2048]{1,0:T(8,128)(2,1)}, bf16[1024,2048]{1,0:T(8,128)(2,1)}, u32[]{:S(2)}, u32[]{:S(2)}) collective-permute-start(bf16[1024,2048]{1,0:T(8,128)(2,1)} %param.47), channel_id=1, source_target_pairs={{0,4},{4,0},{8,12},{12,8},{16,20},{20,16},{24,28},{28,24},{1,5},{5... | collective-permute-start | bytes 12582920 | tf_op jit(solution)/shard_map/ppermute | solution.py:51
  112.1 31.5 %collective-permute-start.7 = (bf16[256,2048]{1,0:T(8,128)(2,1)}, bf16[256,2048]{1,0:T(8,128)(2,1)}, u32[]{:S(2)}, u32[]{:S(2)}) collective-permute-start(bf16[256,2048]{1,0:T(8,128)(2,1)} %param.41), channel_id=1, source_target_pairs={{0,4},{4,0},{8,12},{12,8},{16,20},{20,16},{24,28},{28,24},{1,5},{5... | collective-permute-start | bytes 3145736 | tf_op jit(solution)/shard_map/ppermute | solution.py:51
  135.3 55.9 %collective-permute-start.28 = (bf16[192,2048]{1,0:T(8,128)(2,1)}, bf16[192,2048]{1,0:T(8,128)(2,1)}, u32[]{:S(2)}, u32[]{:S(2)}) collective-permute-start(bf16[192,2048]{1,0:T(8,128)(2,1)} %bitcast.30.base), channel_id=1, source_target_pairs={{0,16},{4,20},{8,24},{12,28},{16,0},{20,4},{24,8},{28,12},{1,17},{... | collective-permute-start | bytes 2359304 | tf_op jit(solution)/shard_map/ppermute | solution.py:51
  136.9 54.3 %collective-permute-start.27 = (bf16[192,2048]{1,0:T(8,128)(2,1)}, bf16[192,2048]{1,0:T(8,128)(2,1)}, u32[]{:S(2)}, u32[]{:S(2)}) collective-permute-start(bf16[192,2048]{1,0:T(8,128)(2,1)} %bitcast.30.base), channel_id=1, source_target_pairs={{0,8},{4,12},{8,0},{12,4},{16,24},{20,28},{24,16},{28,20},{1,9},{5... | collective-permute-start | bytes 2359304 | tf_op jit(solution)/shard_map/ppermute | solution.py:51
  152.7 108.0 %collective-permute-start.33 = (bf16[256,2048]{1,0:T(8,128)(2,1)}, bf16[256,2048]{1,0:T(8,128)(2,1)}, u32[]{:S(2)}, u32[]{:S(2)}) collective-permute-start(bf16[256,2048]{1,0:T(8,128)(2,1)} %get-tuple-element.128), channel_id=1, source_target_pairs={{0,24},{4,28},{8,16},{12,20},{16,8},{20,12},{24,0},{28,4},{1,25},{... | collective-permute-start | bytes 3145736 | tf_op jit(solution)/shard_map/ppermute | solution.py:51
  188.6 36.2 %collective-permute-start.20 = (bf16[192,2048]{1,0:T(8,128)(2,1)S(1)}, bf16[192,2048]{1,0:T(8,128)(2,1)S(1)}, u32[]{:S(2)}, u32[]{:S(2)}) collective-permute-start(bf16[192,2048]{1,0:T(8,128)(2,1)S(1)} %pad_maximum_fusion.5), channel_id=1, source_target_pairs={{0,8},{4,12},{8,0},{12,4},{16,24},{20,28},{24,16},{28,20},{1,9},{5... | collective-permute-start | bytes 2359304 | tf_op jit(solution)/shard_map/ppermute | solution.py:51
  189.7 36.0 %collective-permute-start.22 = (bf16[192,2048]{1,0:T(8,128)(2,1)S(1)}, bf16[192,2048]{1,0:T(8,128)(2,1)}, u32[]{:S(2)}, u32[]{:S(2)}) collective-permute-start(bf16[192,2048]{1,0:T(8,128)(2,1)S(1)} %pad_maximum_fusion.6), channel_id=1, source_target_pairs={{0,16},{4,20},{8,24},{12,28},{16,0},{20,4},{24,8},{28,12},{1,17},{... | collective-permute-start | bytes 2359304 | tf_op jit(solution)/shard_map/ppermute | solution.py:51
  193.3 24.6 %collective-permute-start.30 = (bf16[96,2048]{1,0:T(8,128)(2,1)S(1)}, bf16[96,2048]{1,0:T(8,128)(2,1)S(1)}, u32[]{:S(2)}, u32[]{:S(2)}) collective-permute-start(bf16[96,2048]{1,0:T(8,128)(2,1)S(1)} %slice.560), channel_id=1, source_target_pairs={{0,8},{4,12},{8,0},{12,4},{16,24},{20,28},{24,16},{28,20},{1,9},{5... | collective-permute-start | bytes 1179656 | tf_op jit(solution)/shard_map/ppermute | solution.py:51
  194.5 22.1 %collective-permute-start.29 = (bf16[96,2048]{1,0:T(8,128)(2,1)S(1)}, bf16[96,2048]{1,0:T(8,128)(2,1)S(1)}, u32[]{:S(2)}, u32[]{:S(2)}) collective-permute-start(bf16[96,2048]{1,0:T(8,128)(2,1)S(1)} %slice.559), channel_id=1, source_target_pairs={{0,16},{4,20},{8,24},{12,28},{16,0},{20,4},{24,8},{28,12},{1,17},{... | collective-permute-start | bytes 1179656 | tf_op jit(solution)/shard_map/ppermute | solution.py:51
  216.7 44.1 %collective-permute-start.31 = (bf16[256,2048]{1,0:T(8,128)(2,1)}, bf16[256,2048]{1,0:T(8,128)(2,1)}, u32[]{:S(2)}, u32[]{:S(2)}) collective-permute-start(bf16[256,2048]{1,0:T(8,128)(2,1)} %get-tuple-element.102), channel_id=1, source_target_pairs={{0,8},{4,12},{8,0},{12,4},{16,24},{20,28},{24,16},{28,20},{1,9},{5... | collective-permute-start | bytes 3145736 | tf_op jit(solution)/shard_map/ppermute | solution.py:51
  217.9 43.4 %collective-permute-start.32 = (bf16[256,2048]{1,0:T(8,128)(2,1)}, bf16[256,2048]{1,0:T(8,128)(2,1)}, u32[]{:S(2)}, u32[]{:S(2)}) collective-permute-start(bf16[256,2048]{1,0:T(8,128)(2,1)} %get-tuple-element.103), channel_id=1, source_target_pairs={{0,16},{4,20},{8,24},{12,28},{16,0},{20,4},{24,8},{28,12},{1,17},{... | collective-permute-start | bytes 3145736 | tf_op jit(solution)/shard_map/ppermute | solution.py:51
  231.3 26.7 %collective-permute-start.24 = (bf16[192,2048]{1,0:T(8,128)(2,1)}, bf16[192,2048]{1,0:T(8,128)(2,1)S(1)}, u32[]{:S(2)}, u32[]{:S(2)}) collective-permute-start(bf16[192,2048]{1,0:T(8,128)(2,1)} %get-tuple-element.96), channel_id=1, source_target_pairs={{0,16},{4,20},{8,24},{12,28},{16,0},{20,4},{24,8},{28,12},{1,17},{... | collective-permute-start | bytes 2359304 | tf_op jit(solution)/shard_map/ppermute | solution.py:51
  231.9 27.1 %collective-permute-start.23 = (bf16[192,2048]{1,0:T(8,128)(2,1)}, bf16[192,2048]{1,0:T(8,128)(2,1)S(1)}, u32[]{:S(2)}, u32[]{:S(2)}) collective-permute-start(bf16[192,2048]{1,0:T(8,128)(2,1)} %get-tuple-element.96), channel_id=1, source_target_pairs={{0,8},{4,12},{8,0},{12,4},{16,24},{20,28},{24,16},{28,20},{1,9},{5... | collective-permute-start | bytes 2359304 | tf_op jit(solution)/shard_map/ppermute | solution.py:51
  333.9 73.2 %collective-permute-start.70 = (bf16[2,48,2048]{2,1,0:T(8,128)(2,1)}, bf16[2,48,2048]{2,1,0:T(8,128)(2,1)}, u32[]{:S(2)}, u32[]{:S(2)}) collective-permute-start(bf16[2,48,2048]{2,1,0:T(8,128)(2,1)} %pad_maximum_fusion.17), channel_id=1, source_target_pairs={{0,2},{1,3},{2,0},{3,1},{4,6},{5,7},{6,4},{7,5},{8,10},{9,11},{10,... | collective-permute-start | bytes 1179656 | tf_op jit(solution)/shard_map/ppermute | solution.py:51
  411.9 42.4 %collective-permute-start.52 = (bf16[192,2304]{1,0:T(8,128)(2,1)S(1)}, bf16[192,2304]{1,0:T(8,128)(2,1)S(1)}, u32[]{:S(2)}, u32[]{:S(2)}) collective-permute-start(bf16[192,2304]{1,0:T(8,128)(2,1)S(1)} %pad_maximum_fusion.3), channel_id=1, source_target_pairs={{0,8},{4,12},{8,0},{12,4},{16,24},{20,28},{24,16},{28,20},{1,9},{5... | collective-permute-start | bytes 2654216 | tf_op jit(solution)/shard_map/ppermute | solution.py:51
  414.0 40.2 %collective-permute-start.54 = (bf16[192,2304]{1,0:T(8,128)(2,1)S(1)}, bf16[192,2304]{1,0:T(8,128)(2,1)S(1)}, u32[]{:S(2)}, u32[]{:S(2)}) collective-permute-start(bf16[192,2304]{1,0:T(8,128)(2,1)S(1)} %pad_maximum_fusion.4), channel_id=1, source_target_pairs={{0,16},{4,20},{8,24},{12,28},{16,0},{20,4},{24,8},{28,12},{1,17},{... | collective-permute-start | bytes 2654216 | tf_op jit(solution)/shard_map/ppermute | solution.py:51
  441.1 22.4 %collective-permute-start.55 = (bf16[96,2048]{1,0:T(8,128)(2,1)}, bf16[96,2048]{1,0:T(8,128)(2,1)}, u32[]{:S(2)}, u32[]{:S(2)}) collective-permute-start(bf16[96,2048]{1,0:T(8,128)(2,1)} %get-tuple-element.175), channel_id=1, source_target_pairs={{0,16},{4,20},{8,24},{12,28},{16,0},{20,4},{24,8},{28,12},{1,17},{... | collective-permute-start | bytes 1179656 | tf_op jit(solution)/shard_map/ppermute | solution.py:51
  452.9 45.8 %collective-permute-start.57 = (bf16[192,2048]{1,0:T(8,128)(2,1)}, bf16[192,2048]{1,0:T(8,128)(2,1)}, u32[]{:S(2)}, u32[]{:S(2)}) collective-permute-start(bf16[192,2048]{1,0:T(8,128)(2,1)} %pad_maximum_fusion.9), channel_id=1, source_target_pairs={{0,16},{4,20},{8,24},{12,28},{16,0},{20,4},{24,8},{28,12},{1,17},{... | collective-permute-start | bytes 2359304 | tf_op jit(solution)/shard_map/ppermute | solution.py:51
  465.9 32.8 %collective-permute-start.56 = (bf16[192,2048]{1,0:T(8,128)(2,1)S(1)}, bf16[192,2048]{1,0:T(8,128)(2,1)S(1)}, u32[]{:S(2)}, u32[]{:S(2)}) collective-permute-start(bf16[192,2048]{1,0:T(8,128)(2,1)S(1)} %pad_maximum_fusion.10), channel_id=1, source_target_pairs={{0,8},{4,12},{8,0},{12,4},{16,24},{20,28},{24,16},{28,20},{1,9},{5... | collective-permute-start | bytes 2359304 | tf_op jit(solution)/shard_map/ppermute | solution.py:51
  (183 other events, 1583.5 us)

commit v5 on v4

--- a/solution.py
+++ b/solution.py
@@ -88,7 +88,7 @@
     return jnp.concatenate(pieces, 0), [got[bit][0] for bit in bits], pieces[-1]
 
 
-def scatter_rows(parts, bits, gate=()):
+def scatter_rows(parts, bits, gate=(), between=None):
     half = parts[0].shape[0] // 2
     upper = {m: p[:half] for m, p in parts.items()}
     lower = {m: p[half:] for m, p in parts.items()}
@@ -99,6 +99,8 @@
                 other = after(other, *gate) if gate else other
                 which[sub] = (which[sub].astype(F32) + other.astype(F32)).astype(BF16)
     blocks = [jnp.concatenate([upper[bit], lower[bit]], 0) for bit in bits]
+    if between:
+        blocks = list(after(tuple(blocks), between(blocks[-1])))
     return [parts[0]] + [swap(b, "shard", bit) for b, bit in zip(blocks, bits)], blocks[-1]
 
 
@@ -119,23 +121,69 @@
         copy.wait()
 
 
-def place_kernel(me_ref, *refs, count, width, rows, joined):
-    pieces, outs, sems = refs[: 2 * count], refs[2 * count : -1], refs[-1]
-    me = me_ref[0]
+def cut_kernel(at_ref, *refs, count, terms, width):
+    tables, outs, sems = refs[:terms], refs[terms:-1], refs[-1]
+    me, part = at_ref[0], at_ref[1]
+    copies = []
+    for i in range(count):
+        rows = outs[i].shape[0]
+        first = 0 if i == 0 else pl.multiple_of(part * rows, rows)
+        for k in range(2):
+            column = pl.multiple_of((((me // 2) ^ i) * 2 + k) * width, width)
+            for t in range(terms):
+                copies.append(
+                    pltpu.make_async_copy(
+                        tables[t].at[pl.ds(first, rows), pl.ds(column, width)],
+                        outs[i].at[:, pl.ds((k * terms + t) * width, width)],
+                        sems.at[len(copies)],
+                    )
+                )
+    run_copies(copies)
+
+
+def cut_pieces(at, tables, width, count):
+    rows, terms = tables[0].shape[0], len(tables)
+    shapes = [
+        jax.ShapeDtypeStruct((rows if i == 0 else rows // 2, 2 * terms * width), BF16)
+        for i in range(count)
+    ]
+    return pl.pallas_call(
+        functools.partial(cut_kernel, count=count, terms=terms, width=width),
+        out_shape=shapes,
+        in_specs=[pl.BlockSpec(memory_space=pltpu.SMEM)]
+        + [pl.BlockSpec(memory_space=pl.ANY)] * terms,
+        out_specs=[pl.BlockSpec(memory_space=pltpu.VMEM)] * count,
+        scratch_shapes=[pltpu.SemaphoreType.DMA((2 * terms * count,))],
+        cost_estimate=pl.CostEstimate(
+            flops=0, bytes_accessed=4 * rows * count * terms * width, transcendentals=0
+        ),
+        name="cut_pieces",
+    )(at, *tables)
+
+
+def place_kernel(at_ref, *refs, count, width, rows, joined):
+    each = 2 * count - 1
+    pieces, outs, sems = refs[: 2 * each], refs[2 * each : -1], refs[-1]
+    me, part = at_ref[0], at_ref[1]
 
     def copies(core):
         made = []
         for side in range(2):
-            for i in range(count):
-                row = pl.multiple_of((me ^ (2 * i) ^ side) * rows, rows)
-                piece = pieces[side * count + i]
+            for j in range(each):
+                i, second = (j, 0) if j < count else (j - count + 1, 1)
+                piece = pieces[side * each + j]
+                height = piece.shape[0]
+                row = (me ^ (2 * i) ^ side) * rows
+                if i:
+                    row = row + (part ^ second) * height
+                row = pl.multiple_of(row, height)
                 for k in range(2):
                     own = k ^ core
                     source = piece.at[:, pl.ds(k * width, width)]
                     if joined:
-                        target = outs[0].at[pl.ds(row, rows), pl.ds(own * width, width)]
+                        target = outs[0].at[pl.ds(row, height), pl.ds(own * width, width)]
                     else:
-                        target = outs[own].at[pl.ds(row, rows)]
+                        target = outs[own].at[pl.ds(row, height)]
                     made.append(pltpu.make_async_copy(source, target, sems.at[len(made)]))
         return made
 
@@ -148,27 +196,25 @@
         run_copies(copies(1))
 
 
-def place_weights(me, pieces, width, joined):
-    count = len(pieces) // 2
+def place_weights(at, pieces, width, joined):
+    count = (len(pieces) // 2 + 1) // 2
     rows = pieces[0].shape[0]
     if joined:
         shapes = [jax.ShapeDtypeStruct((rows * count * 2, 2 * width), BF16)]
     else:
         shapes = [jax.ShapeDtypeStruct((rows * count * 2, width), BF16)] * 2
     return pl.pallas_call(
-        functools.partial(
-            place_kernel, count=count, width=width, rows=rows, joined=joined
-        ),
+        functools.partial(place_kernel, count=count, width=width, rows=rows, joined=joined),
         out_shape=shapes,
         in_specs=[pl.BlockSpec(memory_space=pltpu.SMEM)]
-        + [pl.BlockSpec(memory_space=pl.ANY)] * (2 * count),
+        + [pl.BlockSpec(memory_space=pl.ANY)] * len(pieces),
         out_specs=[pl.BlockSpec(memory_space=pltpu.VMEM)] * len(shapes),
-        scratch_shapes=[pltpu.SemaphoreType.DMA((4 * count,))],
+        scratch_shapes=[pltpu.SemaphoreType.DMA((2 * len(pieces),))],
         cost_estimate=pl.CostEstimate(
             flops=0, bytes_accessed=16 * rows * count * width, transcendentals=0
         ),
         name="place_weights",
-    )(me, *pieces)
+    )(at, *pieces)
 
 
 def pick_kernel(chosen_ref, *refs, tall, rank):
@@ -241,13 +287,6 @@
     )(me, stacked)
 
 
-def total_of(refs):
-    total = refs[0][...].astype(F32)
-    for ref in refs[1:]:
-        total = total + ref[...].astype(F32)
-    return total
-
-
 def normalised(values):
     centre = jnp.mean(values, axis=-1, keepdims=True)
     offset = values - centre
@@ -255,41 +294,46 @@
     return offset * scale, scale
 
 
+def total_of(refs, at):
+    total = refs[0][at].astype(F32)
+    for ref in refs[1:]:
+        total = total + ref[at].astype(F32)
+    return total
+
+
+def tiles_of(rows):
+    tile = 32 if rows % 32 == 0 else rows
+    return [slice(i, i + tile) for i in range(0, rows, tile)]
+
+
 def norm_kernel(base, shift, gain, bias, *refs):
     terms, (res_ref, out_ref) = refs[:-2], refs[-2:]
-    values = base[...].astype(F32) + (total_of(terms) + shift[...].astype(F32))
-    res_ref[...] = values
-    unit, _ = normalised(values)
-    out_ref[...] = (unit * gain[...].astype(F32) + bias[...].astype(F32)).astype(BF16)
+    for at in tiles_of(base.shape[0]):
+        values = base[at].astype(F32) + (total_of(terms, at) + shift[...].astype(F32))
+        res_ref[at] = values
+        unit, _ = normalised(values)
+        out_ref[at] = (unit * gain[...].astype(F32) + bias[...].astype(F32)).astype(BF16)
 
 
 def norm_back_kernel(values, gain, base, *refs, outs):
     terms, outputs = refs[: len(refs) - outs], refs[len(refs) - outs :]
-    unit, scale = normalised(values[...].astype(F32))
-    grad = total_of(terms) * gain[...].astype(F32)
-    mean_one = jnp.mean(grad, axis=-1, keepdims=True)
-    mean_two = jnp.mean(grad * unit, axis=-1, keepdims=True)
-    total = base[...].astype(F32) + scale * (grad - mean_one - unit * mean_two)
-    for out in outputs:
-        out[...] = total.astype(out.dtype)
+    for at in tiles_of(values.shape[0]):
+        unit, scale = normalised(values[at].astype(F32))
+        grad = total_of(terms, at) * gain[...].astype(F32)
+        mean_one = jnp.mean(grad, axis=-1, keepdims=True)
+        mean_two = jnp.mean(grad * unit, axis=-1, keepdims=True)
+        total = base[at].astype(F32) + scale * (grad - mean_one - unit * mean_two)
+        for out in outputs:
+            out[at] = total.astype(out.dtype)
 
 
 def row_call(kernel, order, rows, wide, dtypes, name):
-    tile = 32 if rows % 32 == 0 else rows
-    args, specs = [], []
-    for value in order:
-        if value.ndim == 1:
-            args.append(value[None])
-            specs.append(pl.BlockSpec((1, wide), lambda i: (0, 0)))
-        else:
-            args.append(value)
-            specs.append(pl.BlockSpec((tile, wide), lambda i: (i, 0)))
+    args = [value[None] if value.ndim == 1 else value for value in order]
     return pl.pallas_call(
         kernel,
         out_shape=[jax.ShapeDtypeStruct((rows, wide), d) for d in dtypes],
-        grid=(rows // tile,),
-        in_specs=specs,
-        out_specs=[pl.BlockSpec((tile, wide), lambda i: (i, 0))] * len(dtypes),
+        in_specs=[pl.BlockSpec(memory_space=pltpu.VMEM)] * len(args),
+        out_specs=[pl.BlockSpec(memory_space=pltpu.VMEM)] * len(dtypes),
         cost_estimate=pl.CostEstimate(
             flops=20 * rows * wide, bytes_accessed=16 * rows * wide, transcendentals=0
         ),
@@ -464,6 +508,8 @@
     bits = bits_of(size)[1:]
     me = lax.axis_index("shard").astype(jnp.int32)
     me_arr = me[None]
+    part = lax.axis_index("rep").astype(jnp.int32) & 1
+    at = jnp.stack([me, part])
     heads = HEADS // size
     span = heads * HEAD
     slice_wide = wide // size
@@ -478,54 +524,49 @@
         of_col = lax.broadcasted_iota(jnp.int32, value.shape, 1) // (terms * rank)
         return jnp.where(of_row == of_col, value, 0.0).astype(BF16)
 
+    chip = me // 2
+
+    def exchange(pieces):
+        return [pieces[0]] + [swap(p, "shard", 2 * i) for i, p in enumerate(pieces) if i]
+
+    def halves_over_rep(pieces):
+        return [swap(piece, "rep", 1) for piece in pieces]
+
+    def both_cores(own):
+        return list(own) + [swap(piece, "shard", 1) for piece in own]
+
+    pieces_qkv = cut_pieces(at, [w_query, w_key, w_value], span, chips)
+    turned = exchange(pieces_qkv)
+
     narrow = [out_query, out_key, out_value, in_attn, out_expand, in_reduce]
     edges = np.cumsum([0] + [n.shape[2] for n in narrow])
     mine, packed = pick_maps(
-        chosen, [in_query, in_key, in_value, in_expand, out_attn, out_reduce], narrow
+        after(chosen, *pieces_qkv),
+        [in_query, in_key, in_value, in_expand, out_attn, out_reduce],
+        narrow,
     )
     packed_other = swap(packed, "shard", 1)
     order = bits + [1]
-    chip = me // 2
-
-    def slices(tables, width):
-        pieces = []
-        for i in range(chips):
-            both = [
-                lax.dynamic_slice_in_dim(t, (chip ^ i) * 2 * width, 2 * width, 1) for t in tables
-            ]
-            if len(both) > 1:
-                both = jnp.concatenate(
-                    [t[:, k * width : (k + 1) * width] for k in range(2) for t in both], 1
-                )
-            else:
-                both = both[0]
-            pieces.append(both)
-        return pieces
-
-    def exchange(pieces):
-        return [swap(piece, "shard", 2 * i) if i else piece for i, piece in enumerate(pieces)]
-
-    def both_cores(own):
-        return own + [swap(piece, "shard", 1) for piece in own]
-
-    first_tables = after((w_query, w_key, w_value), mine)
-    pieces_qkv = after(tuple(slices(first_tables, span)), packed_other)
-    turned = exchange(pieces_qkv)
-
-    rows_in = after(inputs[0].reshape(block, wide), *pieces_qkv)
+
+    rows_in = after(inputs[0].reshape(block, wide), mine)
     features = rows_in.astype(F32)
     normed = layer_norm(features, ln1_gain.astype(F32), ln1_bias.astype(F32)).astype(BF16)
     starts, b_query, b_value, b_up, me_late, chosen, packed = after(
         (starts, b_query, b_value, b_up, me, chosen, packed), normed
     )
-    hidden_block = after(normed, *[turned[bit // 2] for bit in bits])
+    hidden_block = after(normed, *turned[1:])
     hidden_one, one_first, one_last = gather_rows(hidden_block, bits)
 
     w_out, w_down, turned[0] = after((w_out, w_down, turned[0]), *one_first)
-    w_qkv_mine, w_qkv_other = place_weights(me_arr, both_cores(turned), 3 * span, False)
+    w_qkv_mine, w_qkv_other = place_weights(
+        at, both_cores(turned + halves_over_rep(turned[1:])), 3 * span, False
+    )
     w_out_other = swap(w_out, "shard", 1)
     w_down_other = swap(w_down, "shard", 1)
-    hidden_one = after(hidden_one, w_out_other, w_down_other)
+    w_out_chip = jnp.concatenate([w_out, w_out_other], 0)
+    w_down_chip = jnp.concatenate([w_down, w_down_other], 0)
+    near_up = exchange(after(tuple(cut_pieces(at, [after(w_up, *one_first)], ff_part, chips)), one_last))
+    hidden_one = after(hidden_one, w_out_chip, w_down_chip, near_up[0])
     near = gather_blocks(mine, "shard", bits, {bit: one_first for bit in bits[1:]})
     stacked = jnp.concatenate([near, swap(near, "shard", 1)], 0)
 
@@ -539,15 +580,6 @@
     in_qkv = jnp.swapaxes(whole[:3], 0, 1).reshape(count * 3 * rank, wide)
     in_exp, out_att, out_red = (whole[3 + i].reshape(count * rank, wide) for i in range(3))
 
-    rep_bits = bits_of(lax.axis_size("rep"))
-    mark = (after(chosen, *one_first)[:, None] == jnp.arange(ADAPTERS, dtype=jnp.int32)[None, :]).astype(BF16)
-    marks = gather_blocks(jnp.pad(mark, ((0, 16 - count), (0, 128 - ADAPTERS))), "rep", rep_bits)
-    groups = marks.shape[0]
-    marks = marks[:, :count, :ADAPTERS].reshape(groups * count, 1, ADAPTERS, 1)
-    place = (marks * jnp.eye(rank, dtype=BF16)[None, :, None, :]).reshape(
-        groups * count * rank, ADAPTERS * rank
-    )
-
     def unpack(table, i):
         return table[:, edges[i] : edges[i + 1]]
 
@@ -570,8 +602,6 @@
         )
 
     b_up_chip = jnp.concatenate([slice_of(b_up, me, ff_part), slice_of(b_up, me ^ 1, ff_part)])
-    w_out_chip = jnp.concatenate([w_out, w_out_other], 0)
-    w_down_chip = jnp.concatenate([w_down, w_down_other], 0)
 
     def by_chip(value):
         return value.reshape((chips, count, rows) + value.shape[1:])
@@ -603,17 +633,27 @@
     low_att = keep_own(mm_t(attended, in_att))
     parts = block_products([(attended, w_out_chip, mm)], low_att, out_att)
     terms, relayed = scatter_rows(parts, bits)
-    cot, _, _ = gather_rows(after(cot_mine, one_last), bits, (relayed,))
+    cot, _, _ = gather_rows(after(cot_mine, relayed), bits)
+
+    rep_bits = bits_of(lax.axis_size("rep"))
+    mark = (after(chosen, relayed)[:, None] == jnp.arange(ADAPTERS, dtype=jnp.int32)[None, :]).astype(BF16)
+    marks = gather_blocks(jnp.pad(mark, ((0, 16 - count), (0, 128 - ADAPTERS))), "rep", rep_bits)
+    groups = marks.shape[0]
+    marks = marks[:, :count, :ADAPTERS].reshape(groups * count, 1, ADAPTERS, 1)
+    place = (marks * jnp.eye(rank, dtype=BF16)[None, :, None, :]).reshape(
+        groups * count * rank, ADAPTERS * rank
+    )
+
     glow_red = keep_own(mm_t(cot, out_red))
     grad_act = (mm_t(cot, w_down_chip) + mm(glow_red, in_red)).astype(BF16)
-    pieces_up = slices([after(w_up, one_last)], ff_part)
-    pieces_up = pieces_up[:1] + [after(p, relayed) for p in pieces_up[1:-1]] + pieces_up[-1:]
+    far_up = halves_over_rep(after(tuple(near_up[1:]), att_own))
+    pieces_up = after(tuple(near_up + far_up), relayed)
     residual, hidden_block = row_call(
         norm_kernel, [rows_in, b_out, ln2_gain, ln2_bias] + terms, block, wide, [F32, BF16], "norm"
     )
     hidden_two, _, _ = gather_rows(hidden_block, bits)
 
-    (w_up_chip,) = place_weights(me_arr, both_cores(exchange(pieces_up)), ff_part, True)
+    (w_up_chip,) = place_weights(at, both_cores(pieces_up), ff_part, True)
     hidden_two = after(hidden_two, grad_act)
     low_exp = keep_own(mm_t(hidden_two, in_exp))
     pre = mm(hidden_two, w_up_chip) + mm(low_exp, out_exp) + b_up_chip
@@ -661,17 +701,18 @@
         core = me & 1
         return sum_cores(side(core), side(1 - core))
 
-    def sum_chips(current):
-        sent = None
-        for bit in bits[::-1]:
-            current = current.reshape((2, current.shape[0] // 2) + current.shape[1:])
-            own = (me // bit) & 1
-            away = lax.dynamic_index_in_dim(current, 1 - own, 0, False).astype(BF16)
-            sent = away if sent is None else sent
-            current = lax.dynamic_index_in_dim(current, own, 0, False) + swap(
-                away, "shard", bit
-            ).astype(F32)
-        return current[0], sent
+    def split_chips(current, bit):
+        current = current.reshape((2, current.shape[0] // 2) + current.shape[1:])
+        own = (me // bit) & 1
+        away = lax.dynamic_index_in_dim(current, 1 - own, 0, False).astype(BF16)
+        return lax.dynamic_index_in_dim(current, own, 0, False), away
+
+    def sum_chips(current, gate):
+        for i, bit in enumerate(bits[::-1]):
+            current, away = split_chips(current, bit)
+            there = swap(away, "shard", bit)
+            current = current + (there if i else after(there, gate)).astype(F32)
+        return current[0], away
 
     def over_groups(terms, gates=None):
         widths = [t.shape[1] for t in terms]
@@ -700,20 +741,18 @@
     )
 
     near_first = core_columns(
-        jnp.concatenate(
-            [t_mm(low_att, grad_branch), t_mm(glow_late, hidden_two), t_mm(low_red, cot)], 0
-        )
+        jnp.concatenate([t_mm(glow_late, hidden_two), t_mm(low_red, cot)], 0)
     ).astype(BF16)
     tall = near_first.shape[1]
     riders = {}
     for i in range(chips):
         rider = lax.dynamic_index_in_dim(near_first, chip ^ i, 0, False)
         rider = jnp.pad(rider, ((0, block - tall), (0, 0)))
-        riders[2 * i] = jnp.concatenate([down_parts[2 * i], rider], 1)
+        riders[2 * i] = after(jnp.concatenate([down_parts[2 * i], rider], 1), branch_last)
     att_side = sum_cores(*halves(t_mm(glow_att, attended)))
 
     glow_last = glow_qkv
-    in_terms = t_mm(glow_last, hidden_one)
+    in_terms = jnp.concatenate([t_mm(glow_last, hidden_one), t_mm(low_att, grad_branch)], 0)
 
     def own_terms(full):
         full = full.reshape(count, 3, rank, 3, span)
@@ -724,27 +763,22 @@
     near_second = core_columns(in_terms)
     products = [(grad_own, w_qkv_mine, mm_t), (grad_other, w_qkv_other, mm_t)]
     parts = block_products(products, after(glow_qkv, in_terms), in_qkv)
-    second, sent = sum_chips(near_second)
-    far = 2 * (chips - 1)
-    parts[far] = after(parts[far], sent)
-    far_part = parts[far]
-
-    terms, relayed = scatter_rows(parts, bits)
+    far_part = parts[2 * (chips - 1)]
+    aside = {}
+
+    def hop(relayed):
+        aside["second"], sent = sum_chips(after(near_second, far_part), relayed)
+        return sent
+
+    terms, relayed = scatter_rows(parts, bits, between=hop)
+    second = aside["second"]
     down, _ = scatter_rows(riders, bits, (grad_away,))
     down[0] = after(down[0], relayed)
-    first = sum(t[:tall, wide:].astype(F32) for t in down).reshape(3, count * rank, slice_wide)
+    first = sum(t[:tall, wide:].astype(F32) for t in down).reshape(2, count * rank, slice_wide)
     layer_rows = residual + b_down.astype(F32) + sum(t[:, :wide].astype(F32) for t in down)
 
     own_last, other_last = after((grad_own, grad_other), relayed)
     outer = sum_cores(own_terms(t_mm(low_qkv, own_last)), own_terms(t_mm(low_qkv, other_last)))
-    second = second.reshape(count, 3, rank, slice_wide)
-    s_in_att, s_out_att, s_in_exp, s_out_red = over_groups(
-        [att_side, first[0], first[1], first[2]]
-    )
-    late = over_groups(
-        [second[:, t].reshape(count * rank, slice_wide) for t in range(3)]
-        + [outer[:, t * span : (t + 1) * span] for t in range(3)]
-    )
     (input_rows,) = row_call(
         functools.partial(norm_back_kernel, outs=1),
         [rows_in, ln1_gain, grad_residual] + terms,
@@ -753,6 +787,17 @@
         [BF16],
         "norm_back",
     )
+    out_att_sum = second[count * 3 * rank :]
+    second = second[: count * 3 * rank].reshape(count, 3, rank, slice_wide)
+    ends = {rep_bits[-1]: (input_rows,)}
+    s_in_att, s_in_exp, s_out_red = over_groups([att_side, first[0], first[1]], ends)
+    late = over_groups(
+        [second[:, t].reshape(count * rank, slice_wide) for t in range(3)]
+        + [outer[:, t * span : (t + 1) * span] for t in range(3)]
+        + [out_att_sum],
+        ends,
+    )
+    s_out_att = late.pop()
     shape = (1, count, rows, wide)
     return (
         layer_rows.astype(BF16).reshape(shape),

time: 513 us -> 505 us (0.984)
  local copies, waits for them, and re-layouts: 85.9 us -> 76 us
  starting transfers between devices: 61.6 us -> 68.1 us
  Pallas kernels: 52.8 us -> 58.3 us
    pallas_call x0 -> x2, Pallas kernels: none -> 7.72 us  [cut_pieces(): pl.pallas_call(functools.partial(cut_kernel, count=count, terms=terms, wi...]
    unnamed x299 -> x243, local copies, waits for them, and re-layouts: 42.4 us -> 34.9 us
    ppermute x71 -> x83, starting transfers between devices: 61.6 us -> 68.1 us  [swap(): return lax.ppermute(value, axis, [(i, i ^ mask) for i in range(size)])]
    ppermute x71 -> x83, waiting for transfers between devices: 151 us -> 146 us  [swap(): return lax.ppermute(value, axis, [(i, i ^ mask) for i in range(size)])]
    dynamic_slice x1 -> x0, local copies, waits for them, and re-layouts: 5.56 us -> none  [slices(): lax.dynamic_slice_in_dim(t, (chip ^ i) * 2 * width, 2 * width, 1)]
  transfers between devices with their start and end apart: 71 -> 83, of which waited for: 18 -> 31; matrix products, arithmetic and copies ran while one was open for 38% -> 34% of each run, Pallas kernels for 7% -> 11%
where the time goes in v5:
time: 505 us; the launch traced here: 498 us
  waiting for transfers between devices  146 us (29%)
  matrix products  114 us (23%)
  local copies, waits for them, and re-layouts  76 us (15%)
  starting transfers between devices  68.1 us (13%)
  Pallas kernels  58.3 us (12%)
  other arithmetic  30.4 us (6%)
  between operations  5.16 us (1%)
    ppermute x83, waiting for transfers between devices, swap(): return lax.ppermute(value, axis, [(i, i ^ mask) for i in range(size)])  146 us
    ppermute x83, starting transfers between devices, swap(): return lax.ppermute(value, axis, [(i, i ^ mask) for i in range(size)])  68.1 us
    dot_general x23, matrix products, mm_t(): lax.dot_general(a, b, (((1,), (1,)), ((), ())), preferred_element_type=F32)  50.4 us
    dot_general x32, matrix products, mm(): lax.dot_general(a, b, (((1,), (0,)), ((), ())), preferred_element_type=F32)  45.9 us
    unnamed x243, local copies, waits for them, and re-layouts  34.9 us
    dot_general x21, matrix products, t_mm(): lax.dot_general(a, b, (((0,), (0,)), ((), ())), preferred_element_type=F32)  17.8 us
    pallas_call x2, Pallas kernels, place_weights(): pl.pallas_call(functools.partial(place_kernel, count=count, width=width,...  14.3 us
    pallas_call x3, Pallas kernels, row_call(): pl.pallas_call(kernel, out_shape=[jax.ShapeDtypeStruct((rows, wide), d) f...  13.8 us
  transfers between devices with their start and end apart: 83, of which 31 were waited for; matrix products, arithmetic and copies ran while one was open for 34% of the time, Pallas kernels for 11%

profile of v5, /device:TPU:0, one launch (start us, length us, event | category | flops | bytes accessed | tf_op | source)
XLA Modules:
  0.0 497.6 jit_solution(7174744440129852349)
XLA Ops:
  18.3 9.0 %collective-permute-done.1.refs_2_ = bf16[128,1536]{1,0:T(8,128)(2,1)S(1)} collective-permute-done((bf16[128,1536]{1,0:T(8,128)(2,1)}, bf16[128,1536]{1,0:T(8,128)(2,1)S(1)}, u32[]{:S(2)}, u32[]{:S(2)}) %collective-permute-start.1) | collective-permute-done | bytes 393248 | tf_op jit(solution)/shard_map/ppermute | solution.py:51
  37.5 8.2 %collective-permute-done.4 = bf16[192,2048]{1,0:T(8,128)(2,1)S(1)} collective-permute-done((bf16[192,2048]{1,0:T(8,128)(2,1)S(1)}, bf16[192,2048]{1,0:T(8,128)(2,1)S(1)}, u32[]{:S(2)}, u32[]{:S(2)}) %collective-permute-start.4) | collective-permute-done | bytes 786464 | tf_op jit(solution)/shard_map/ppermute | solution.py:51
  72.5 4.8 constant_dynamic-update-slice_fusion.8
  91.9 6.8 %collective-permute-done.5 = bf16[96,2048]{1,0:T(8,128)(2,1)S(1)} collective-permute-done((bf16[96,2048]{1,0:T(8,128)(2,1)S(1)}, bf16[96,2048]{1,0:T(8,128)(2,1)S(1)}, u32[]{:S(2)}, u32[]{:S(2)}) %collective-permute-start.5) | collective-permute-done | bytes 393248 | tf_op jit(solution)/shard_map/ppermute | solution.py:51
  108.5 6.6 %place_weights.2 = (bf16[2048,768]{1,0:T(8,128)(2,1)}, bf16[2048,768]{1,0:T(8,128)(2,1)}) custom-call(s32[2]{0:T(128)} %pad_add_fusion.1.at_ref, bf16[256,1536]{1,0:T(8,128)(2,1)} %get-tuple-element.111.refs_0_, bf16[128,1536]{1,0:T(8,128)(2,1)} %copy-done.63, bf16[128,1536]{1,0:T(8,128)(2,1)} %copy-done.64, ...), custom_call_target="tpu_custom_call" | custom-call | bytes 12582912 | tf_op jit(solution)/shard_map/place_weights/pallas_call | solution.py:206
  116.6 5.5 %constant_dynamic-update-slice_fusion.7 = bf16[2048,2048]{1,0:T(8,128)(2,1)} fusion(bf16[2048,2048]{1,0:T(8,128)(2,1)} %constant_dynamic-update-slice_fusion.8, bf16[1024,2048]{1,0:T(8,128)(2,1)} %collective-permute-done.8), kind=kLoop, calls=%fused_computation.316 | loop fusion | bytes 8388608 | tf_op jit(solution)/shard_map/concatenate | solution.py:567
  135.1 7.3 %attend.1 = (bf16[4,3,64,256]{3,2,1,0:T(8,128)(2,1)}, bf16[4,3,64,256]{3,2,1,0:T(8,128)(2,1)}, f32[3,512,2]{2,1,0:T(8,128)}) custom-call(s32[512,1]{1,0:T(8,128)} %copy.74.pq, s32[1,512]{1,0:T(1,128)} %bitcast.333, s32[3,512,1]{2,1,0:T(8,128)} %copy.75.lq, s32[3,1,512]{2,1,0:T(1,128)} %broadcast_in_dim.107.lk, bf16[4,3,64,768]{3,2,1,0:T(8,128)(2,1)} %bitcast.300, ...), custom_call_target="tpu_custom_call" | custom-call | flops 805306368 | bytes 3145728 | tf_op jit(solution)/shard_map/attend/pallas_call | solution.py:398
  167.4 6.8 %collective-permute-done.27 = bf16[96,2048]{1,0:T(8,128)(2,1)S(1)} collective-permute-done((bf16[96,2048]{1,0:T(8,128)(2,1)S(1)}, bf16[96,2048]{1,0:T(8,128)(2,1)S(1)}, u32[]{:S(2)}, u32[]{:S(2)}) %collective-permute-start.27) | collective-permute-done | bytes 393248 | tf_op jit(solution)/shard_map/ppermute | solution.py:51
  175.9 4.8 collective-permute-done.41.refs_5_
  180.7 9.6 %collective-permute-done.42.refs_6_ = bf16[128,2048]{1,0:T(8,128)(2,1)S(1)} collective-permute-done((bf16[128,2048]{1,0:T(8,128)(2,1)}, bf16[128,2048]{1,0:T(8,128)(2,1)S(1)}, u32[]{:S(2)}, u32[]{:S(2)}) %collective-permute-start.42) | collective-permute-done | bytes 524320 | tf_op jit(solution)/shard_map/ppermute | solution.py:51
  203.3 9.4 %collective-permute-done.26.refs_1_ = bf16[192,2048]{1,0:T(8,128)(2,1)S(1)} collective-permute-done((bf16[192,2048]{1,0:T(8,128)(2,1)S(1)}, bf16[192,2048]{1,0:T(8,128)(2,1)S(1)}, u32[]{:S(2)}, u32[]{:S(2)}) %collective-permute-start.26) | collective-permute-done | bytes 786464 | tf_op jit(solution)/shard_map/ppermute | solution.py:51
  220.0 9.2 %collective-permute-done.33 = bf16[192,2048]{1,0:T(8,128)(2,1)} collective-permute-done((bf16[192,2048]{1,0:T(8,128)(2,1)}, bf16[192,2048]{1,0:T(8,128)(2,1)}, u32[]{:S(2)}, u32[]{:S(2)}) %collective-permute-start.33) | collective-permute-done | bytes 786464 | tf_op jit(solution)/shard_map/ppermute | solution.py:51
  243.3 7.7 %place_weights.3 = bf16[2048,2048]{1,0:T(8,128)(2,1)} custom-call(s32[2]{0:T(128)} %pad_add_fusion.1.at_ref, bf16[256,2048]{1,0:T(8,128)(2,1)} %get-tuple-element.130.refs_0_, bf16[128,2048]{1,0:T(8,128)(2,1)} %collective-permute-done.37.refs_1_, bf16[128,2048]{1,0:T(8,128)(2,1)} %collective-permute-done.38.refs_2_, ...), custom_call_target="tpu_custom_call" | custom-call | bytes 16777216 | tf_op jit(solution)/shard_map/place_weights/pallas_call | solution.py:206
  258.7 12.8 %add_convert_fusion = bf16[768,2048]{1,0:T(8,128)(2,1)} fusion(f32[768,2048]{1,0:T(8,128)S(1)} %fusion.110, bf16[768,2048]{1,0:T(8,128)(2,1)} %constant_dynamic-update-slice_fusion.14, bf16[2048,2048]{1,0:T(8,128)(2,1)} %constant_dynamic-update-slice_fusion.7), kind=kOutput, calls=%fused_computation.10 | convolution fusion | flops 6445596672 | bytes 20971520 | tf_op jit(solution)/shard_map/dot_general | solution.py:42
  278.1 6.3 %collective-permute-done.31 = bf16[96,2048]{1,0:T(8,128)(2,1)S(1)} collective-permute-done((bf16[96,2048]{1,0:T(8,128)(2,1)S(1)}, bf16[96,2048]{1,0:T(8,128)(2,1)S(1)}, u32[]{:S(2)}, u32[]{:S(2)}) %collective-permute-start.31) | collective-permute-done | bytes 393248 | tf_op jit(solution)/shard_map/ppermute | solution.py:51
  289.1 12.5 %multiply_convert_fusion = (bf16[768,2048]{1,0:T(8,128)(2,1)}, bf16[768,2048]{1,0:T(8,128)(2,1)}) fusion(bf16[768,2048]{1,0:T(8,128)(2,1)} %add_convert_fusion, f32[2048]{0:T(1024)S(1)} %maximum_convert_fusion, f32[768,2048]{1,0:T(8,128)S(1)} %fusion.109, bf16[768,2048]{1,0:T(8,128)(2,1)S(1)} %constant_dynamic-update-slice_fusion.9, ...), kind=kOutput, calls=%fused_computation.7 | convolution fusion | flops 6466043904 | bytes 27271168 | tf_op jit(solution)/shard_map/dot_general | solution.py:38
  330.3 5.2 %collective-permute-done.81 = bf16[1,48,2048]{2,1,0:T(8,128)(2,1)S(1)} collective-permute-done((bf16[1,48,2048]{2,1,0:T(8,128)(2,1)S(1)}, bf16[1,48,2048]{2,1,0:T(8,128)(2,1)S(1)}, u32[]{:S(2)}, u32[]{:S(2)}) %collective-permute-start.81) | collective-permute-done | bytes 196640 | tf_op jit(solution)/shard_map/ppermute | solution.py:51
  342.4 4.9 collective-permute-done.51.refs_1_
  347.3 5.4 %norm_back.2 = (f32[192,2048]{1,0:T(8,128)}, bf16[192,2048]{1,0:T(8,128)(2,1)}) custom-call(f32[192,2048]{1,0:T(8,128)} %get-tuple-element.120.values, bf16[1,2048]{1,0:T(2,128)(2,1)} %broadcast_in_dim.100.gain, bf16[192,2048]{1,0:T(8,128)(2,1)} %bitcast.31.base, bf16[192,2048]{1,0:T(8,128)(2,1)} %fusion.14.refs_0_, ...), custom_call_target="tpu_custom_call" | custom-call | flops 7864320 | bytes 6291456 | tf_op jit(solution)/shard_map/norm_back/pallas_call | solution.py:332
  357.9 5.3 %fusion.53 = f32[192,2048]{1,0:T(8,128)S(1)} fusion(bf16[2048,2048]{1,0:T(8,128)(2,1)} %constant_dynamic-update-slice_fusion.7, bf16[768,2048]{1,0:T(8,128)(2,1)S(1)} %copy-done.33), kind=kOutput, calls=%fused_computation.149 | convolution fusion | flops 1610612736 | bytes 10747904 | tf_op jit(solution)/shard_map/dot_general | solution.py:38
  378.8 9.7 %collective-permute-done.56 = bf16[96,2048]{1,0:T(8,128)(2,1)S(1)} collective-permute-done((bf16[96,2048]{1,0:T(8,128)(2,1)S(1)}, bf16[96,2048]{1,0:T(8,128)(2,1)S(1)}, u32[]{:S(2)}, u32[]{:S(2)}) %collective-permute-start.56) | collective-permute-done | bytes 393248 | tf_op jit(solution)/shard_map/ppermute | solution.py:51
  399.1 9.6 %attend_back.1 = (bf16[4,3,64,768]{3,2,1,0:T(8,128)(2,1)}, bf16[4,3,64,768]{3,2,1,0:T(8,128)(2,1)}) custom-call(s32[512,1]{1,0:T(8,128)} %copy.74.pq, s32[1,512]{1,0:T(1,128)} %bitcast.334, s32[3,512,1]{2,1,0:T(8,128)} %copy.75.lq, s32[3,1,512]{2,1,0:T(1,128)} %broadcast_in_dim.107.lk, bf16[4,3,64,768]{3,2,1,0:T(8,128)(2,1)} %bitcast.301, ...), custom_call_target="tpu_custom_call" | custom-call | flops 2013265920 | bytes 5505024 | tf_op jit(solution)/shard_map/attend_back/pallas_call | solution.py:455
  438.3 6.7 %collective-permute-done.62 = bf16[96,2048]{1,0:T(8,128)(2,1)S(1)} collective-permute-done((bf16[96,2048]{1,0:T(8,128)(2,1)S(1)}, bf16[96,2048]{1,0:T(8,128)(2,1)S(1)}, u32[]{:S(2)}, u32[]{:S(2)}) %collective-permute-start.62) | collective-permute-done | bytes 393248 | tf_op jit(solution)/shard_map/ppermute | solution.py:51
  474.0 7.8 %collective-permute-done.69.refs_1_ = bf16[192,2048]{1,0:T(8,128)(2,1)S(1)} collective-permute-done((bf16[192,2048]{1,0:T(8,128)(2,1)S(1)}, bf16[192,2048]{1,0:T(8,128)(2,1)S(1)}, u32[]{:S(2)}, u32[]{:S(2)}) %collective-permute-start.69) | collective-permute-done | bytes 786464 | tf_op jit(solution)/shard_map/ppermute | solution.py:51
  (616 shorter events, 310.4 us)
Async XLA Ops:
  30.2 25.1 %collective-permute-start.19 = (bf16[1,288,256]{2,1,0:T(8,128)(2,1)S(1)}, bf16[1,288,256]{2,1,0:T(8,128)(2,1)S(1)}, u32[]{:S(2)}, u32[]{:S(2)}) collective-permute-start(bf16[1,288,256]{2,1,0:T(8,128)(2,1)S(1)} %bitcast.292), channel_id=1, source_target_pairs={{0,8},{4,12},{8,0},{12,4},{16,24},{20,28},{24,16},{28,20},{1,9},{5... | collective-permute-start | bytes 442376 | tf_op jit(solution)/shard_map/ppermute | solution.py:51
  31.6 25.3 %collective-permute-start.22 = (bf16[48,3072]{1,0:T(8,128)(2,1)}, bf16[48,3072]{1,0:T(8,128)(2,1)}, u32[]{:S(2)}, u32[]{:S(2)}) collective-permute-start(bf16[48,3072]{1,0:T(8,128)(2,1)} %get-tuple-element.114), channel_id=1, source_target_pairs={{0,4},{4,0},{8,12},{12,8},{16,20},{20,16},{24,28},{28,24},{1,5},{5... | collective-permute-start | bytes 884744 | tf_op jit(solution)/shard_map/ppermute | solution.py:51
  47.5 69.1 %collective-permute-start.8 = (bf16[1024,2048]{1,0:T(8,128)(2,1)}, bf16[1024,2048]{1,0:T(8,128)(2,1)}, u32[]{:S(2)}, u32[]{:S(2)}) collective-permute-start(bf16[1024,2048]{1,0:T(8,128)(2,1)} %param.47), channel_id=1, source_target_pairs={{0,4},{4,0},{8,12},{12,8},{16,20},{20,16},{24,28},{28,24},{1,5},{5... | collective-permute-start | bytes 12582920 | tf_op jit(solution)/shard_map/ppermute | solution.py:51
  87.1 28.1 %collective-permute-start.7 = (bf16[256,2048]{1,0:T(8,128)(2,1)}, bf16[256,2048]{1,0:T(8,128)(2,1)}, u32[]{:S(2)}, u32[]{:S(2)}) collective-permute-start(bf16[256,2048]{1,0:T(8,128)(2,1)} %param.41), channel_id=1, source_target_pairs={{0,4},{4,0},{8,12},{12,8},{16,20},{20,16},{24,28},{28,24},{1,5},{5... | collective-permute-start | bytes 3145736 | tf_op jit(solution)/shard_map/ppermute | solution.py:51
  127.4 23.0 %collective-permute-start.37 = (bf16[128,2048]{1,0:T(8,128)(2,1)}, bf16[128,2048]{1,0:T(8,128)(2,1)}, u32[]{:S(2)}, u32[]{:S(2)}) collective-permute-start(bf16[128,2048]{1,0:T(8,128)(2,1)} %get-tuple-element.124), channel_id=1, source_target_pairs={{0,8},{4,12},{8,0},{12,4},{16,24},{20,28},{24,16},{28,20},{1,9},{5... | collective-permute-start | bytes 1572872 | tf_op jit(solution)/shard_map/ppermute | solution.py:51
  128.9 25.6 %collective-permute-start.38 = (bf16[128,2048]{1,0:T(8,128)(2,1)}, bf16[128,2048]{1,0:T(8,128)(2,1)}, u32[]{:S(2)}, u32[]{:S(2)}) collective-permute-start(bf16[128,2048]{1,0:T(8,128)(2,1)} %get-tuple-element.125), channel_id=1, source_target_pairs={{0,16},{4,20},{8,24},{12,28},{16,0},{20,4},{24,8},{28,12},{1,17},{... | collective-permute-start | bytes 1572872 | tf_op jit(solution)/shard_map/ppermute | solution.py:51
  129.5 25.0 %collective-permute-start.39 = (bf16[128,2048]{1,0:T(8,128)(2,1)}, bf16[128,2048]{1,0:T(8,128)(2,1)}, u32[]{:S(2)}, u32[]{:S(2)}) collective-permute-start(bf16[128,2048]{1,0:T(8,128)(2,1)} %get-tuple-element.126), channel_id=1, source_target_pairs={{0,24},{4,28},{8,16},{12,20},{16,8},{20,12},{24,0},{28,4},{1,25},{... | collective-permute-start | bytes 1572872 | tf_op jit(solution)/shard_map/ppermute | solution.py:51
  156.1 24.7 %collective-permute-start.41 = (bf16[128,2048]{1,0:T(8,128)(2,1)}, bf16[128,2048]{1,0:T(8,128)(2,1)S(1)}, u32[]{:S(2)}, u32[]{:S(2)}) collective-permute-start(bf16[128,2048]{1,0:T(8,128)(2,1)} %collective-permute-done.38.refs_2_), channel_id=1, source_target_pairs={{0,1},{1,0},{2,3},{3,2},{4,5},{5,4},{6,7},{7,6},{8,9},{9,8},{10,11... | collective-permute-start | bytes 1572872 | tf_op jit(solution)/shard_map/ppermute | solution.py:51
  156.5 33.8 %collective-permute-start.42 = (bf16[128,2048]{1,0:T(8,128)(2,1)}, bf16[128,2048]{1,0:T(8,128)(2,1)S(1)}, u32[]{:S(2)}, u32[]{:S(2)}) collective-permute-start(bf16[128,2048]{1,0:T(8,128)(2,1)} %collective-permute-done.39.refs_3_), channel_id=1, source_target_pairs={{0,1},{1,0},{2,3},{3,2},{4,5},{5,4},{6,7},{7,6},{8,9},{9,8},{10,11... | collective-permute-start | bytes 1572872 | tf_op jit(solution)/shard_map/ppermute | solution.py:51
  165.3 26.8 %collective-permute-start.25 = (bf16[96,2048]{1,0:T(8,128)(2,1)S(1)}, bf16[96,2048]{1,0:T(8,128)(2,1)S(1)}, u32[]{:S(2)}, u32[]{:S(2)}) collective-permute-start(bf16[96,2048]{1,0:T(8,128)(2,1)S(1)} %get-tuple-element.199), channel_id=1, source_target_pairs={{0,16},{4,20},{8,24},{12,28},{16,0},{20,4},{24,8},{28,12},{1,17},{... | collective-permute-start | bytes 1179656 | tf_op jit(solution)/shard_map/ppermute | solution.py:51
  175.3 38.4 %collective-permute-start.28 = (bf16[192,2048]{1,0:T(8,128)(2,1)}, bf16[192,2048]{1,0:T(8,128)(2,1)}, u32[]{:S(2)}, u32[]{:S(2)}) collective-permute-start(bf16[192,2048]{1,0:T(8,128)(2,1)} %pad_maximum_fusion.6), channel_id=1, source_target_pairs={{0,16},{4,20},{8,24},{12,28},{16,0},{20,4},{24,8},{28,12},{1,17},{... | collective-permute-start | bytes 2359304 | tf_op jit(solution)/shard_map/ppermute | solution.py:51
  197.3 22.7 %collective-permute-start.34 = (bf16[192,2048]{1,0:T(8,128)(2,1)}, bf16[192,2048]{1,0:T(8,128)(2,1)}, u32[]{:S(2)}, u32[]{:S(2)}) collective-permute-start(bf16[192,2048]{1,0:T(8,128)(2,1)} %bitcast.31.base), channel_id=1, source_target_pairs={{0,16},{4,20},{8,24},{12,28},{16,0},{20,4},{24,8},{28,12},{1,17},{... | collective-permute-start | bytes 2359304 | tf_op jit(solution)/shard_map/ppermute | solution.py:51
  198.7 30.6 %collective-permute-start.33 = (bf16[192,2048]{1,0:T(8,128)(2,1)}, bf16[192,2048]{1,0:T(8,128)(2,1)}, u32[]{:S(2)}, u32[]{:S(2)}) collective-permute-start(bf16[192,2048]{1,0:T(8,128)(2,1)} %bitcast.31.base), channel_id=1, source_target_pairs={{0,8},{4,12},{8,0},{12,4},{16,24},{20,28},{24,16},{28,20},{1,9},{5... | collective-permute-start | bytes 2359304 | tf_op jit(solution)/shard_map/ppermute | solution.py:51
  202.8 32.1 %collective-permute-start.46 = (bf16[128,2048]{1,0:T(8,128)(2,1)}, bf16[128,2048]{1,0:T(8,128)(2,1)}, u32[]{:S(2)}, u32[]{:S(2)}) collective-permute-start(bf16[128,2048]{1,0:T(8,128)(2,1)} %collective-permute-done.39.refs_3_), channel_id=1, source_target_pairs={{0,4},{4,0},{8,12},{12,8},{16,20},{20,16},{24,28},{28,24},{1,5},{5... | collective-permute-start | bytes 1572872 | tf_op jit(solution)/shard_map/ppermute | solution.py:51
  213.6 29.7 %collective-permute-start.43 = (bf16[256,2048]{1,0:T(8,128)(2,1)}, bf16[256,2048]{1,0:T(8,128)(2,1)}, u32[]{:S(2)}, u32[]{:S(2)}) collective-permute-start(bf16[256,2048]{1,0:T(8,128)(2,1)} %get-tuple-element.130.refs_0_), channel_id=1, source_target_pairs={{0,4},{4,0},{8,12},{12,8},{16,20},{20,16},{24,28},{28,24},{1,5},{5... | collective-permute-start | bytes 3145736 | tf_op jit(solution)/shard_map/ppermute | solution.py:51
  213.7 24.0 %collective-permute-start.47 = (bf16[128,2048]{1,0:T(8,128)(2,1)}, bf16[128,2048]{1,0:T(8,128)(2,1)}, u32[]{:S(2)}, u32[]{:S(2)}) collective-permute-start(bf16[128,2048]{1,0:T(8,128)(2,1)} %copy-done.52), channel_id=1, source_target_pairs={{0,4},{4,0},{8,12},{12,8},{16,20},{20,16},{24,28},{28,24},{1,5},{5... | collective-permute-start | bytes 1572872 | tf_op jit(solution)/shard_map/ppermute | solution.py:51
  241.2 30.2 %collective-permute-start.30 = (bf16[192,2048]{1,0:T(8,128)(2,1)}, bf16[192,2048]{1,0:T(8,128)(2,1)}, u32[]{:S(2)}, u32[]{:S(2)}) collective-permute-start(bf16[192,2048]{1,0:T(8,128)(2,1)} %get-tuple-element.121), channel_id=1, source_target_pairs={{0,16},{4,20},{8,24},{12,28},{16,0},{20,4},{24,8},{28,12},{1,17},{... | collective-permute-start | bytes 2359304 | tf_op jit(solution)/shard_map/ppermute | solution.py:51
  241.9 31.2 %collective-permute-start.29 = (bf16[192,2048]{1,0:T(8,128)(2,1)}, bf16[192,2048]{1,0:T(8,128)(2,1)}, u32[]{:S(2)}, u32[]{:S(2)}) collective-permute-start(bf16[192,2048]{1,0:T(8,128)(2,1)} %get-tuple-element.121), channel_id=1, source_target_pairs={{0,8},{4,12},{8,0},{12,4},{16,24},{20,28},{24,16},{28,20},{1,9},{5... | collective-permute-start | bytes 2359304 | tf_op jit(solution)/shard_map/ppermute | solution.py:51
  336.3 72.4 %collective-permute-start.82 = (bf16[2,48,2048]{2,1,0:T(8,128)(2,1)}, bf16[2,48,2048]{2,1,0:T(8,128)(2,1)}, u32[]{:S(2)}, u32[]{:S(2)}) collective-permute-start(bf16[2,48,2048]{2,1,0:T(8,128)(2,1)} %pad_maximum_fusion.17), channel_id=1, source_target_pairs={{0,2},{1,3},{2,0},{3,1},{4,6},{5,7},{6,4},{7,5},{8,10},{9,11},{10,... | collective-permute-start | bytes 1179656 | tf_op jit(solution)/shard_map/ppermute | solution.py:51
  352.7 23.7 %collective-permute-start.57 = (bf16[192,2048]{1,0:T(8,128)(2,1)}, bf16[192,2048]{1,0:T(8,128)(2,1)S(1)}, u32[]{:S(2)}, u32[]{:S(2)}) collective-permute-start(bf16[192,2048]{1,0:T(8,128)(2,1)} %get-tuple-element.138), channel_id=1, source_target_pairs={{0,8},{4,12},{8,0},{12,4},{16,24},{20,28},{24,16},{28,20},{1,9},{5... | collective-permute-start | bytes 2359304 | tf_op jit(solution)/shard_map/ppermute | solution.py:51
  353.4 23.8 %collective-permute-start.55 = (bf16[192,2048]{1,0:T(8,128)(2,1)}, bf16[192,2048]{1,0:T(8,128)(2,1)S(1)}, u32[]{:S(2)}, u32[]{:S(2)}) collective-permute-start(bf16[192,2048]{1,0:T(8,128)(2,1)} %get-tuple-element.138), channel_id=1, source_target_pairs={{0,16},{4,20},{8,24},{12,28},{16,0},{20,4},{24,8},{28,12},{1,17},{... | collective-permute-start | bytes 2359304 | tf_op jit(solution)/shard_map/ppermute | solution.py:51
  414.4 43.8 %collective-permute-start.66 = (bf16[192,2304]{1,0:T(8,128)(2,1)}, bf16[192,2304]{1,0:T(8,128)(2,1)}, u32[]{:S(2)}, u32[]{:S(2)}) collective-permute-start(bf16[192,2304]{1,0:T(8,128)(2,1)} %pad_maximum_fusion.3), channel_id=1, source_target_pairs={{0,8},{4,12},{8,0},{12,4},{16,24},{20,28},{24,16},{28,20},{1,9},{5... | collective-permute-start | bytes 2654216 | tf_op jit(solution)/shard_map/ppermute | solution.py:51
  418.0 40.3 %collective-permute-start.68 = (bf16[192,2304]{1,0:T(8,128)(2,1)}, bf16[192,2304]{1,0:T(8,128)(2,1)}, u32[]{:S(2)}, u32[]{:S(2)}) collective-permute-start(bf16[192,2304]{1,0:T(8,128)(2,1)} %pad_maximum_fusion.4), channel_id=1, source_target_pairs={{0,16},{4,20},{8,24},{12,28},{16,0},{20,4},{24,8},{28,12},{1,17},{... | collective-permute-start | bytes 2654216 | tf_op jit(solution)/shard_map/ppermute | solution.py:51
  453.3 29.4 %collective-permute-start.70 = (bf16[192,2048]{1,0:T(8,128)(2,1)}, bf16[192,2048]{1,0:T(8,128)(2,1)}, u32[]{:S(2)}, u32[]{:S(2)}) collective-permute-start(bf16[192,2048]{1,0:T(8,128)(2,1)} %pad_maximum_fusion.10), channel_id=1, source_target_pairs={{0,16},{4,20},{8,24},{12,28},{16,0},{20,4},{24,8},{28,12},{1,17},{... | collective-permute-start | bytes 2359304 | tf_op jit(solution)/shard_map/ppermute | solution.py:51
  (169 other events, 1969.6 us)

commit v6 on v5

--- a/solution.py
+++ b/solution.py
@@ -69,7 +69,7 @@
     return masks
 
 
-def gather_rows(block, bits, gate=()):
+def gather_rows(block, bits, gate=(), apart=False):
     half = block.shape[0] // 2
     got = {0: [block]}
     upper, lower = {}, {}
@@ -85,7 +85,10 @@
     pieces = []
     for mask in subsets(bits):
         pieces += got[mask] if mask in got else [upper[mask], lower[mask]]
-    return jnp.concatenate(pieces, 0), [got[bit][0] for bit in bits], pieces[-1]
+    firsts = [got[bit][0] for bit in bits]
+    if apart:
+        return pieces, firsts, pieces[-1]
+    return jnp.concatenate(pieces, 0), firsts, pieces[-1]
 
 
 def scatter_rows(parts, bits, gate=(), between=None):
@@ -100,8 +103,8 @@
                 which[sub] = (which[sub].astype(F32) + other.astype(F32)).astype(BF16)
     blocks = [jnp.concatenate([upper[bit], lower[bit]], 0) for bit in bits]
     if between:
-        blocks = list(after(tuple(blocks), between(blocks[-1])))
-    return [parts[0]] + [swap(b, "shard", bit) for b, bit in zip(blocks, bits)], blocks[-1]
+        blocks = list(after(tuple(blocks), between(blocks)))
+    return [parts[0]] + [swap(b, "shard", bit) for b, bit in zip(blocks, bits)], blocks
 
 
 def gather_blocks(value, axis, bits, gates=None):
@@ -127,7 +130,7 @@
     copies = []
     for i in range(count):
         rows = outs[i].shape[0]
-        first = 0 if i == 0 else pl.multiple_of(part * rows, rows)
+        first = pl.multiple_of(part * rows, rows) if rows < tables[0].shape[0] else 0
         for k in range(2):
             column = pl.multiple_of((((me // 2) ^ i) * 2 + k) * width, width)
             for t in range(terms):
@@ -141,10 +144,10 @@
     run_copies(copies)
 
 
-def cut_pieces(at, tables, width, count):
+def cut_pieces(at, tables, width, count, split):
     rows, terms = tables[0].shape[0], len(tables)
     shapes = [
-        jax.ShapeDtypeStruct((rows if i == 0 else rows // 2, 2 * terms * width), BF16)
+        jax.ShapeDtypeStruct((rows // 2 if i and split else rows, 2 * terms * width), BF16)
         for i in range(count)
     ]
     return pl.pallas_call(
@@ -162,7 +165,7 @@
 
 
 def place_kernel(at_ref, *refs, count, width, rows, joined):
-    each = 2 * count - 1
+    each = (len(refs) - 1 - (1 if joined else 2)) // 2
     pieces, outs, sems = refs[: 2 * each], refs[2 * each : -1], refs[-1]
     me, part = at_ref[0], at_ref[1]
 
@@ -174,7 +177,7 @@
                 piece = pieces[side * each + j]
                 height = piece.shape[0]
                 row = (me ^ (2 * i) ^ side) * rows
-                if i:
+                if height < rows:
                     row = row + (part ^ second) * height
                 row = pl.multiple_of(row, height)
                 for k in range(2):
@@ -196,8 +199,7 @@
         run_copies(copies(1))
 
 
-def place_weights(at, pieces, width, joined):
-    count = (len(pieces) // 2 + 1) // 2
+def place_weights(at, pieces, count, width, joined):
     rows = pieces[0].shape[0]
     if joined:
         shapes = [jax.ShapeDtypeStruct((rows * count * 2, 2 * width), BF16)]
@@ -306,20 +308,22 @@
     return [slice(i, i + tile) for i in range(0, rows, tile)]
 
 
-def norm_kernel(base, shift, gain, bias, *refs):
+def norm_kernel(base, vectors, *refs):
     terms, (res_ref, out_ref) = refs[:-2], refs[-2:]
+    shift, gain, bias = vectors[0:1], vectors[1:2], vectors[2:3]
     for at in tiles_of(base.shape[0]):
-        values = base[at].astype(F32) + (total_of(terms, at) + shift[...].astype(F32))
+        values = base[at].astype(F32) + (total_of(terms, at) + shift)
         res_ref[at] = values
         unit, _ = normalised(values)
-        out_ref[at] = (unit * gain[...].astype(F32) + bias[...].astype(F32)).astype(BF16)
-
-
-def norm_back_kernel(values, gain, base, *refs, outs):
+        out_ref[at] = (unit * gain + bias).astype(BF16)
+
+
+def norm_back_kernel(values, vectors, base, *refs, outs, row):
+    gain = vectors[row : row + 1]
     terms, outputs = refs[: len(refs) - outs], refs[len(refs) - outs :]
     for at in tiles_of(values.shape[0]):
         unit, scale = normalised(values[at].astype(F32))
-        grad = total_of(terms, at) * gain[...].astype(F32)
+        grad = total_of(terms, at) * gain
         mean_one = jnp.mean(grad, axis=-1, keepdims=True)
         mean_two = jnp.mean(grad * unit, axis=-1, keepdims=True)
         total = base[at].astype(F32) + scale * (grad - mean_one - unit * mean_two)
@@ -328,17 +332,16 @@
 
 
 def row_call(kernel, order, rows, wide, dtypes, name):
-    args = [value[None] if value.ndim == 1 else value for value in order]
     return pl.pallas_call(
         kernel,
         out_shape=[jax.ShapeDtypeStruct((rows, wide), d) for d in dtypes],
-        in_specs=[pl.BlockSpec(memory_space=pltpu.VMEM)] * len(args),
+        in_specs=[pl.BlockSpec(memory_space=pltpu.VMEM)] * len(order),
         out_specs=[pl.BlockSpec(memory_space=pltpu.VMEM)] * len(dtypes),
         cost_estimate=pl.CostEstimate(
             flops=20 * rows * wide, bytes_accessed=16 * rows * wide, transcendentals=0
         ),
         name=name,
-    )(*args)
+    )(*order)
 
 
 def seen(pos_q, pos_k, lab_q, lab_k):
@@ -535,18 +538,21 @@
     def both_cores(own):
         return list(own) + [swap(piece, "shard", 1) for piece in own]
 
-    pieces_qkv = cut_pieces(at, [w_query, w_key, w_value], span, chips)
+    w_out_other = swap(w_out, "shard", 1)
+    w_down_other = swap(w_down, "shard", 1)
+    pieces_qkv = cut_pieces(at, [w_query, w_key, w_value], span, chips, True)
     turned = exchange(pieces_qkv)
 
     narrow = [out_query, out_key, out_value, in_attn, out_expand, in_reduce]
     edges = np.cumsum([0] + [n.shape[2] for n in narrow])
     mine, packed = pick_maps(
-        after(chosen, *pieces_qkv),
+        after(chosen, w_out_other, w_down_other, *pieces_qkv),
         [in_query, in_key, in_value, in_expand, out_attn, out_reduce],
         narrow,
     )
     packed_other = swap(packed, "shard", 1)
     order = bits + [1]
+    near_one = swap(mine[None], "shard", bits[0])
 
     rows_in = after(inputs[0].reshape(block, wide), mine)
     features = rows_in.astype(F32)
@@ -554,20 +560,24 @@
     starts, b_query, b_value, b_up, me_late, chosen, packed = after(
         (starts, b_query, b_value, b_up, me, chosen, packed), normed
     )
-    hidden_block = after(normed, *turned[1:])
+    vectors = after(jnp.stack([b_out, ln2_gain, ln2_bias, ln1_gain]), normed).astype(F32)
+    hidden_block = after(normed, packed_other, near_one, *turned[1:])
     hidden_one, one_first, one_last = gather_rows(hidden_block, bits)
 
-    w_out, w_down, turned[0] = after((w_out, w_down, turned[0]), *one_first)
+    turned[0] = after(turned[0], *one_first)
     w_qkv_mine, w_qkv_other = place_weights(
-        at, both_cores(turned + halves_over_rep(turned[1:])), 3 * span, False
-    )
-    w_out_other = swap(w_out, "shard", 1)
-    w_down_other = swap(w_down, "shard", 1)
-    w_out_chip = jnp.concatenate([w_out, w_out_other], 0)
-    w_down_chip = jnp.concatenate([w_down, w_down_other], 0)
-    near_up = exchange(after(tuple(cut_pieces(at, [after(w_up, *one_first)], ff_part, chips)), one_last))
-    hidden_one = after(hidden_one, w_out_chip, w_down_chip, near_up[0])
-    near = gather_blocks(mine, "shard", bits, {bit: one_first for bit in bits[1:]})
+        at, both_cores(turned + halves_over_rep(turned[1:])), chips, 3 * span, False
+    )
+    w_out_late, w_down_late = after((w_out, w_down), normed)
+    w_out_chip = jnp.concatenate([w_out_late, w_out_other], 0)
+    w_down_chip = jnp.concatenate([w_down_late, w_down_other], 0)
+    hidden_one = after(hidden_one, w_out_chip, w_down_chip)
+    cot_mine = cotangent[0].reshape(block, wide)
+    cut_up = cut_pieces(at, [after(w_up, *one_first)], ff_part, chips, True)
+    near_up = exchange(after(tuple(cut_up), one_last))
+    near = after(jnp.concatenate([mine[None], near_one], 0), *one_first)
+    for bit in bits[1:]:
+        near = jnp.concatenate([near, swap(near, "shard", bit)], 0)
     stacked = jnp.concatenate([near, swap(near, "shard", 1)], 0)
 
     owners = np.concatenate([np.arange(chips) * 2, np.arange(chips) * 2 + 1]).astype(np.int32)
@@ -617,6 +627,9 @@
             for value, weight, main in products:
                 total = total + main(value[at], weight)
             parts[2 * i] = total.astype(BF16)
+            if i == chips - 1:
+                low = after(low, parts[2 * i])
+                products = [(after(v, parts[2 * i]), w, main) for v, w, main in products]
         return parts
 
     low_qkv = keep_own(mm_t(hidden_one, in_qkv), 3)
@@ -627,16 +640,26 @@
     qkv_own = by_chip(
         (mm(hidden_one, w_qkv_mine) + mm(low_qkv, out_qkv_mine) + b_qkv_of(me)).astype(BF16)
     )
+    qkv_own = after(qkv_own, *near_up[1:])
     att_own, att_away, lse = attend(where, qkv_own, qkv_other, heads)
-    cot_mine = cotangent[0].reshape(block, wide)
+    cot_pieces, _, _ = gather_rows(after(cot_mine, att_own), bits, apart=True)
     attended = jnp.concatenate([flat(att_own), swap(flat(att_away), "shard", 1)], 1)
     low_att = keep_own(mm_t(attended, in_att))
     parts = block_products([(attended, w_out_chip, mm)], low_att, out_att)
     terms, relayed = scatter_rows(parts, bits)
-    cot, _, _ = gather_rows(after(cot_mine, relayed), bits)
+    cot = jnp.concatenate(after(cot_pieces, *relayed), 0)
+    glow_red = keep_own(mm_t(cot, out_red))
+    grad_act = (mm_t(cot, w_down_chip) + mm(glow_red, in_red)).astype(BF16)
+    terms[0] = after(terms[0], grad_act)
+    residual, hidden_block = row_call(
+        norm_kernel, [rows_in, vectors] + terms, block, wide, [F32, BF16], "norm"
+    )
+    far_up = halves_over_rep(after(tuple(near_up[1:]), parts[2 * (chips - 1)]))
+    pieces_up = after((*near_up, *far_up), hidden_block)
+    hidden_two, _, _ = gather_rows(hidden_block, bits)
 
     rep_bits = bits_of(lax.axis_size("rep"))
-    mark = (after(chosen, relayed)[:, None] == jnp.arange(ADAPTERS, dtype=jnp.int32)[None, :]).astype(BF16)
+    mark = (after(chosen, hidden_block)[:, None] == jnp.arange(ADAPTERS, dtype=jnp.int32)[None, :]).astype(BF16)
     marks = gather_blocks(jnp.pad(mark, ((0, 16 - count), (0, 128 - ADAPTERS))), "rep", rep_bits)
     groups = marks.shape[0]
     marks = marks[:, :count, :ADAPTERS].reshape(groups * count, 1, ADAPTERS, 1)
@@ -644,16 +667,8 @@
         groups * count * rank, ADAPTERS * rank
     )
 
-    glow_red = keep_own(mm_t(cot, out_red))
-    grad_act = (mm_t(cot, w_down_chip) + mm(glow_red, in_red)).astype(BF16)
-    far_up = halves_over_rep(after(tuple(near_up[1:]), att_own))
-    pieces_up = after(tuple(near_up + far_up), relayed)
-    residual, hidden_block = row_call(
-        norm_kernel, [rows_in, b_out, ln2_gain, ln2_bias] + terms, block, wide, [F32, BF16], "norm"
-    )
-    hidden_two, _, _ = gather_rows(hidden_block, bits)
-
-    (w_up_chip,) = place_weights(at, both_cores(pieces_up), ff_part, True)
+
+    (w_up_chip,) = place_weights(at, both_cores(pieces_up), chips, ff_part, True)
     hidden_two = after(hidden_two, grad_act)
     low_exp = keep_own(mm_t(hidden_two, in_exp))
     pre = mm(hidden_two, w_up_chip) + mm(low_exp, out_exp) + b_up_chip
@@ -664,8 +679,8 @@
     glow_exp = keep_own(mm_t(grad_pre, out_exp))
     terms, grad_sent = scatter_rows(block_products([(grad_pre, w_up_chip, mm_t)], glow_exp, in_exp), bits)
     grad_residual, grad_block = row_call(
-        functools.partial(norm_back_kernel, outs=2),
-        [residual, ln2_gain, cot_mine] + terms,
+        functools.partial(norm_back_kernel, outs=2, row=1),
+        [residual, vectors, cot_mine] + terms,
         block,
         wide,
         [F32, BF16],
@@ -707,11 +722,11 @@
         away = lax.dynamic_index_in_dim(current, 1 - own, 0, False).astype(BF16)
         return lax.dynamic_index_in_dim(current, own, 0, False), away
 
-    def sum_chips(current, gate):
+    def sum_chips(current, *gate):
         for i, bit in enumerate(bits[::-1]):
             current, away = split_chips(current, bit)
             there = swap(away, "shard", bit)
-            current = current + (there if i else after(there, gate)).astype(F32)
+            current = current + (there if i else after(there, *gate)).astype(F32)
         return current[0], away
 
     def over_groups(terms, gates=None):
@@ -730,7 +745,7 @@
         return value[:, :middle], value[:, middle:]
 
     glow_late, low_late = after((glow_exp, low_exp), grad_block)
-    act_mid, grad_mid, low_mid, glow_mid = after((act, grad_pre, low_exp, glow_red), grad_sent)
+    act_mid, grad_mid, low_mid, glow_mid = after((act, grad_pre, low_exp, glow_red), *grad_sent)
     red_own, red_away = halves(t_mm(glow_mid, act_mid))
     exp_own, exp_away = halves(t_mm(low_mid, grad_mid))
     local = sum_cores(
@@ -767,21 +782,21 @@
     aside = {}
 
     def hop(relayed):
-        aside["second"], sent = sum_chips(after(near_second, far_part), relayed)
+        aside["second"], sent = sum_chips(after(near_second, far_part), *relayed)
         return sent
 
     terms, relayed = scatter_rows(parts, bits, between=hop)
     second = aside["second"]
     down, _ = scatter_rows(riders, bits, (grad_away,))
-    down[0] = after(down[0], relayed)
+    down[0] = after(down[0], *relayed)
     first = sum(t[:tall, wide:].astype(F32) for t in down).reshape(2, count * rank, slice_wide)
     layer_rows = residual + b_down.astype(F32) + sum(t[:, :wide].astype(F32) for t in down)
 
-    own_last, other_last = after((grad_own, grad_other), relayed)
+    own_last, other_last = after((grad_own, grad_other), *relayed)
     outer = sum_cores(own_terms(t_mm(low_qkv, own_last)), own_terms(t_mm(low_qkv, other_last)))
     (input_rows,) = row_call(
-        functools.partial(norm_back_kernel, outs=1),
-        [rows_in, ln1_gain, grad_residual] + terms,
+        functools.partial(norm_back_kernel, outs=1, row=3),
+        [rows_in, vectors, grad_residual] + terms,
         block,
         wide,
         [BF16],

time: 505 us -> 478 us (0.947)
  local copies, waits for them, and re-layouts: 76 us -> 50.6 us
    unnamed x243 -> x235, local copies, waits for them, and re-layouts: 34.9 us -> 25.7 us
    concatenate x6, local copies, waits for them, and re-layouts: 10.5 us -> 5.19 us  [the longest x3 2.59 us: gather_rows(): return (jnp.concatenate(pieces, 0), firsts, pieces[-1])]
  transfers between devices with their start and end apart: 83 -> 83, of which waited for: 31 -> 32; matrix products, arithmetic and copies ran while one was open for 34% -> 29% of each run, Pallas kernels for 11% -> 10%
where the time goes in v6:
time: 478 us; the launch traced here: 471 us
  waiting for transfers between devices  145 us (30%)
  matrix products  119 us (25%)
  starting transfers between devices  68.3 us (14%)
  Pallas kernels  58 us (12%)
  local copies, waits for them, and re-layouts  50.6 us (11%)
  other arithmetic  25.6 us (5%)
  between operations  5.49 us (1%)
    ppermute x83, waiting for transfers between devices, swap(): return lax.ppermute(value, axis, [(i, i ^ mask) for i in range(size)])  145 us
    ppermute x83, starting transfers between devices, swap(): return lax.ppermute(value, axis, [(i, i ^ mask) for i in range(size)])  68.3 us
    dot_general x32, matrix products, mm(): lax.dot_general(a, b, (((1,), (0,)), ((), ())), preferred_element_type=F32)  50.7 us
    dot_general x23, matrix products, mm_t(): lax.dot_general(a, b, (((1,), (1,)), ((), ())), preferred_element_type=F32)  50.1 us
    unnamed x235, local copies, waits for them, and re-layouts  25.7 us
    dot_general x21, matrix products, t_mm(): lax.dot_general(a, b, (((0,), (0,)), ((), ())), preferred_element_type=F32)  17.8 us
    pallas_call x2, Pallas kernels, place_weights(): pl.pallas_call(functools.partial(place_kernel, count=count, width=width,...  14 us
    pallas_call x3, Pallas kernels, row_call(): pl.pallas_call(kernel, out_shape=[jax.ShapeDtypeStruct((rows, wide), d) f...  13.7 us
  transfers between devices with their start and end apart: 83, of which 32 were waited for; matrix products, arithmetic and copies ran while one was open for 29% of the time, Pallas kernels for 10%

profile of v6, /device:TPU:0, one launch (start us, length us, event | category | flops | bytes accessed | tf_op | source)
XLA Modules:
  0.0 471.3 jit_solution(10916155369881402894)
XLA Ops:
  11.3 7.6 %collective-permute-done.4.refs_1_ = bf16[128,1536]{1,0:T(8,128)(2,1)S(1)} collective-permute-done((bf16[128,1536]{1,0:T(8,128)(2,1)}, bf16[128,1536]{1,0:T(8,128)(2,1)S(1)}, u32[]{:S(2)}, u32[]{:S(2)}) %collective-permute-start.4) | collective-permute-done | bytes 393248 | tf_op jit(solution)/shard_map/ppermute | solution.py:51
  40.8 13.8 %collective-permute-done.8 = bf16[192,2048]{1,0:T(8,128)(2,1)S(1)} collective-permute-done((bf16[192,2048]{1,0:T(8,128)(2,1)S(1)}, bf16[192,2048]{1,0:T(8,128)(2,1)S(1)}, u32[]{:S(2)}, u32[]{:S(2)}) %collective-permute-start.8) | collective-permute-done | bytes 786464 | tf_op jit(solution)/shard_map/ppermute | solution.py:51
  61.7 5.1 %collective-permute-done.12.refs_5_ = bf16[128,1536]{1,0:T(8,128)(2,1)S(1)} collective-permute-done((bf16[128,1536]{1,0:T(8,128)(2,1)}, bf16[128,1536]{1,0:T(8,128)(2,1)S(1)}, u32[]{:S(2)}, u32[]{:S(2)}) %collective-permute-start.12) | collective-permute-done | bytes 393248 | tf_op jit(solution)/shard_map/ppermute | solution.py:51
  80.4 6.5 %place_weights.2 = (bf16[2048,768]{1,0:T(8,128)(2,1)}, bf16[2048,768]{1,0:T(8,128)(2,1)}) custom-call(s32[2]{0:T(128)} %pad_add_fusion.1.at_ref, bf16[256,1536]{1,0:T(8,128)(2,1)} %get-tuple-element.123.refs_0_, bf16[128,1536]{1,0:T(8,128)(2,1)} %copy-done.52, bf16[128,1536]{1,0:T(8,128)(2,1)} %collective-permute-done.5.refs_2_, ...), custom_call_target="tpu_custom_call" | custom-call | bytes 12582912 | tf_op jit(solution)/shard_map/place_weights/pallas_call | solution.py:208
  95.7 5.5 %add_convert_fusion.1 = bf16[768,768]{1,0:T(8,128)(2,1)} fusion(f32[768,768]{1,0:T(8,128)S(1)} %fusion.215, bf16[768,2048]{1,0:T(8,128)(2,1)} %constant_dynamic-update-slice_fusion, bf16[2048,768]{1,0:T(8,128)(2,1)S(1)} %copy-done, f32[768]{0:T(1024)S(1)} %get-tuple-element.269), kind=kOutput, calls=%fused_computation.64 | convolution fusion | flops 2417688576 | bytes 9833472 | tf_op jit(solution)/shard_map/dot_general | solution.py:38
  115.6 6.5 %add_convert_fusion.2 = bf16[768,768]{1,0:T(8,128)(2,1)} fusion(f32[768,768]{1,0:T(8,128)S(1)} %fusion.214, bf16[768,2048]{1,0:T(8,128)(2,1)} %constant_dynamic-update-slice_fusion, bf16[2048,768]{1,0:T(8,128)(2,1)} %get-tuple-element.124, f32[768]{0:T(1024)S(1)} %get-tuple-element.270), kind=kOutput, calls=%fused_computation.65 | convolution fusion | flops 2417688576 | bytes 9833472 | tf_op jit(solution)/shard_map/dot_general | solution.py:38
  125.8 10.5 %collective-permute-done.24.refs_2_ = bf16[128,2048]{1,0:T(8,128)(2,1)} collective-permute-done((bf16[128,2048]{1,0:T(8,128)(2,1)}, bf16[128,2048]{1,0:T(8,128)(2,1)}, u32[]{:S(2)}, u32[]{:S(2)}) %collective-permute-start.24) | collective-permute-done | bytes 524320 | tf_op jit(solution)/shard_map/ppermute | solution.py:51
  136.3 7.5 %attend.1 = (bf16[4,3,64,256]{3,2,1,0:T(8,128)(2,1)}, bf16[4,3,64,256]{3,2,1,0:T(8,128)(2,1)}, f32[3,512,2]{2,1,0:T(8,128)}) custom-call(s32[512,1]{1,0:T(8,128)} %copy.74.pq, s32[1,512]{1,0:T(1,128)} %bitcast.327, s32[3,512,1]{2,1,0:T(8,128)} %copy.75.lq, s32[3,1,512]{2,1,0:T(1,128)} %broadcast_in_dim.92.lk, bf16[4,3,64,768]{3,2,1,0:T(8,128)(2,1)} %bitcast.292, ...), custom_call_target="tpu_custom_call" | custom-call | flops 805306368 | bytes 3145728 | tf_op jit(solution)/shard_map/attend/pallas_call | solution.py:401
  158.9 7.5 %collective-permute-done.29 = bf16[192,2048]{1,0:T(8,128)(2,1)S(1)} collective-permute-done((bf16[192,2048]{1,0:T(8,128)(2,1)}, bf16[192,2048]{1,0:T(8,128)(2,1)S(1)}, u32[]{:S(2)}, u32[]{:S(2)}) %collective-permute-start.29) | collective-permute-done | bytes 786464 | tf_op jit(solution)/shard_map/ppermute | solution.py:51
  169.0 6.8 %collective-permute-done.33 = bf16[96,2048]{1,0:T(8,128)(2,1)S(1)} collective-permute-done((bf16[96,2048]{1,0:T(8,128)(2,1)S(1)}, bf16[96,2048]{1,0:T(8,128)(2,1)S(1)}, u32[]{:S(2)}, u32[]{:S(2)}) %collective-permute-start.33) | collective-permute-done | bytes 393248 | tf_op jit(solution)/shard_map/ppermute | solution.py:51
  178.9 7.3 %collective-permute-done.31 = bf16[96,2048]{1,0:T(8,128)(2,1)S(1)} collective-permute-done((bf16[96,2048]{1,0:T(8,128)(2,1)S(1)}, bf16[96,2048]{1,0:T(8,128)(2,1)S(1)}, u32[]{:S(2)}, u32[]{:S(2)}) %collective-permute-start.31) | collective-permute-done | bytes 393248 | tf_op jit(solution)/shard_map/ppermute | solution.py:51
  191.0 10.3 %add_convert_fusion = bf16[768,2048]{1,0:T(8,128)(2,1)} fusion(f32[768,2048]{1,0:T(8,128)S(1)} %fusion.109, bf16[768,2048]{1,0:T(8,128)(2,1)S(1)} %constant_dynamic-update-slice_fusion.9, bf16[2048,2048]{1,0:T(8,128)(2,1)} %copy-done.33), kind=kOutput, calls=%fused_computation.10 | convolution fusion | flops 6445596672 | bytes 20971520 | tf_op jit(solution)/shard_map/dot_general | solution.py:42
  239.0 7.5 %place_weights.3 = bf16[2048,2048]{1,0:T(8,128)(2,1)} custom-call(s32[2]{0:T(128)} %pad_add_fusion.1.at_ref, bf16[256,2048]{1,0:T(8,128)(2,1)} %get-tuple-element.157.refs_0_, bf16[128,2048]{1,0:T(8,128)(2,1)} %collective-permute-done.23.refs_1_, bf16[128,2048]{1,0:T(8,128)(2,1)} %collective-permute-done.24.refs_2_, ...), custom_call_target="tpu_custom_call" | custom-call | bytes 16777216 | tf_op jit(solution)/shard_map/place_weights/pallas_call | solution.py:208
  256.4 12.5 %multiply_convert_fusion = (bf16[768,2048]{1,0:T(8,128)(2,1)}, bf16[768,2048]{1,0:T(8,128)(2,1)}) fusion(bf16[768,2048]{1,0:T(8,128)(2,1)} %add_convert_fusion, f32[2048]{0:T(1024)S(1)} %maximum_convert_fusion, f32[768,2048]{1,0:T(8,128)S(1)} %fusion.108, bf16[768,2048]{1,0:T(8,128)(2,1)S(1)} %copy-done.14, bf16[2048,2048]{1,0:T(8,128)(2,1)S(1)} %bitcast.263), kind=kOutput, calls=%fused_computation.7 | convolution fusion | flops 6466043904 | bytes 27271168 | tf_op jit(solution)/shard_map/dot_general | solution.py:38
  283.7 8.6 %collective-permute-done.52 = bf16[96,2048]{1,0:T(8,128)(2,1)S(1)} collective-permute-done((bf16[96,2048]{1,0:T(8,128)(2,1)S(1)}, bf16[96,2048]{1,0:T(8,128)(2,1)S(1)}, u32[]{:S(2)}, u32[]{:S(2)}) %collective-permute-start.52) | collective-permute-done | bytes 393248 | tf_op jit(solution)/shard_map/ppermute | solution.py:51
  311.2 7.6 %collective-permute-done.53.refs_2_ = bf16[192,2048]{1,0:T(8,128)(2,1)} collective-permute-done((bf16[192,2048]{1,0:T(8,128)(2,1)S(1)}, bf16[192,2048]{1,0:T(8,128)(2,1)}, u32[]{:S(2)}, u32[]{:S(2)}) %collective-permute-start.53) | collective-permute-done | bytes 786464 | tf_op jit(solution)/shard_map/ppermute | solution.py:51
  319.2 5.4 %norm_back.2 = (f32[192,2048]{1,0:T(8,128)}, bf16[192,2048]{1,0:T(8,128)(2,1)}) custom-call(f32[192,2048]{1,0:T(8,128)} %get-tuple-element.150.values, f32[4,2048]{1,0:T(4,128)} %convert_element_type.313.vectors, bf16[192,2048]{1,0:T(8,128)(2,1)} %bitcast.271, bf16[192,2048]{1,0:T(8,128)(2,1)} %fusion.15.refs_0_, ...), custom_call_target="tpu_custom_call" | custom-call | flops 7864320 | bytes 6291456 | tf_op jit(solution)/shard_map/norm_back/pallas_call | solution.py:335
  329.7 5.3 %fusion.53 = f32[192,2048]{1,0:T(8,128)S(1)} fusion(bf16[2048,2048]{1,0:T(8,128)(2,1)} %copy-done.33, bf16[768,2048]{1,0:T(8,128)(2,1)S(1)} %copy-done.31), kind=kOutput, calls=%fused_computation.145 | convolution fusion | flops 1610612736 | bytes 10747904 | tf_op jit(solution)/shard_map/dot_general | solution.py:38
  349.2 9.2 %collective-permute-done.58 = bf16[96,2048]{1,0:T(8,128)(2,1)S(1)} collective-permute-done((bf16[96,2048]{1,0:T(8,128)(2,1)S(1)}, bf16[96,2048]{1,0:T(8,128)(2,1)S(1)}, u32[]{:S(2)}, u32[]{:S(2)}) %collective-permute-start.58) | collective-permute-done | bytes 393248 | tf_op jit(solution)/shard_map/ppermute | solution.py:51
  370.0 9.6 %attend_back.1 = (bf16[4,3,64,768]{3,2,1,0:T(8,128)(2,1)}, bf16[4,3,64,768]{3,2,1,0:T(8,128)(2,1)}) custom-call(s32[512,1]{1,0:T(8,128)} %copy.74.pq, s32[1,512]{1,0:T(1,128)} %bitcast.328, s32[3,512,1]{2,1,0:T(8,128)} %copy.75.lq, s32[3,1,512]{2,1,0:T(1,128)} %broadcast_in_dim.92.lk, bf16[4,3,64,768]{3,2,1,0:T(8,128)(2,1)} %bitcast.293, ...), custom_call_target="tpu_custom_call" | custom-call | flops 2013265920 | bytes 5505024 | tf_op jit(solution)/shard_map/attend_back/pallas_call | solution.py:458
  409.8 7.0 %collective-permute-done.62 = bf16[96,2048]{1,0:T(8,128)(2,1)S(1)} collective-permute-done((bf16[96,2048]{1,0:T(8,128)(2,1)S(1)}, bf16[96,2048]{1,0:T(8,128)(2,1)S(1)}, u32[]{:S(2)}, u32[]{:S(2)}) %collective-permute-start.62) | collective-permute-done | bytes 393248 | tf_op jit(solution)/shard_map/ppermute | solution.py:51
  434.6 5.1 %collective-permute-done.75 = bf16[1,48,1792]{2,1,0:T(8,128)(2,1)S(1)} collective-permute-done((bf16[1,48,1792]{2,1,0:T(8,128)(2,1)S(1)}, bf16[1,48,1792]{2,1,0:T(8,128)(2,1)S(1)}, u32[]{:S(2)}, u32[]{:S(2)}) %collective-permute-start.75) | collective-permute-done | bytes 172064 | tf_op jit(solution)/shard_map/ppermute | solution.py:51
  446.2 4.5 norm_back.3
  450.7 12.2 %collective-permute-done.76 = bf16[2,48,1792]{2,1,0:T(8,128)(2,1)S(1)} collective-permute-done((bf16[2,48,1792]{2,1,0:T(8,128)(2,1)}, bf16[2,48,1792]{2,1,0:T(8,128)(2,1)S(1)}, u32[]{:S(2)}, u32[]{:S(2)}) %collective-permute-start.76) | collective-permute-done | bytes 344096 | tf_op jit(solution)/shard_map/ppermute | solution.py:51
  (610 shorter events, 276.2 us)
Async XLA Ops:
  8.7 24.1 %collective-permute-start.5 = (bf16[128,1536]{1,0:T(8,128)(2,1)}, bf16[128,1536]{1,0:T(8,128)(2,1)}, u32[]{:S(2)}, u32[]{:S(2)}) collective-permute-start(bf16[128,1536]{1,0:T(8,128)(2,1)} %get-tuple-element.110), channel_id=1, source_target_pairs={{0,16},{4,20},{8,24},{12,28},{16,0},{20,4},{24,8},{28,12},{1,17},{... | collective-permute-start | bytes 1179656 | tf_op jit(solution)/shard_map/ppermute | solution.py:51
  10.3 24.2 %collective-permute-start.6 = (bf16[128,1536]{1,0:T(8,128)(2,1)}, bf16[128,1536]{1,0:T(8,128)(2,1)}, u32[]{:S(2)}, u32[]{:S(2)}) collective-permute-start(bf16[128,1536]{1,0:T(8,128)(2,1)} %get-tuple-element.111), channel_id=1, source_target_pairs={{0,24},{4,28},{8,16},{12,20},{16,8},{20,12},{24,0},{28,4},{1,25},{... | collective-permute-start | bytes 1179656 | tf_op jit(solution)/shard_map/ppermute | solution.py:51
  18.9 39.4 %collective-permute-start.15 = (bf16[128,1536]{1,0:T(8,128)(2,1)S(1)}, bf16[128,1536]{1,0:T(8,128)(2,1)}, u32[]{:S(2)}, u32[]{:S(2)}) collective-permute-start(bf16[128,1536]{1,0:T(8,128)(2,1)S(1)} %collective-permute-done.4.refs_1_), channel_id=1, source_target_pairs={{0,4},{4,0},{8,12},{12,8},{16,20},{20,16},{24,28},{28,24},{1,5},{5... | collective-permute-start | bytes 1179656 | tf_op jit(solution)/shard_map/ppermute | solution.py:51
  32.9 27.9 %collective-permute-start.11 = (bf16[128,1536]{1,0:T(8,128)(2,1)S(1)}, bf16[128,1536]{1,0:T(8,128)(2,1)S(1)}, u32[]{:S(2)}, u32[]{:S(2)}) collective-permute-start(bf16[128,1536]{1,0:T(8,128)(2,1)S(1)} %collective-permute-done.4.refs_1_), channel_id=1, source_target_pairs={{0,1},{1,0},{2,3},{3,2},{4,5},{5,4},{6,7},{7,6},{8,9},{9,8},{10,11... | collective-permute-start | bytes 1179656 | tf_op jit(solution)/shard_map/ppermute | solution.py:51
  34.5 26.8 %collective-permute-start.16 = (bf16[128,1536]{1,0:T(8,128)(2,1)}, bf16[128,1536]{1,0:T(8,128)(2,1)S(1)}, u32[]{:S(2)}, u32[]{:S(2)}) collective-permute-start(bf16[128,1536]{1,0:T(8,128)(2,1)} %collective-permute-done.5.refs_2_), channel_id=1, source_target_pairs={{0,4},{4,0},{8,12},{12,8},{16,20},{20,16},{24,28},{28,24},{1,5},{5... | collective-permute-start | bytes 1179656 | tf_op jit(solution)/shard_map/ppermute | solution.py:51
  101.2 35.1 %collective-permute-start.26 = (bf16[768,768]{1,0:T(8,128)(2,1)}, bf16[768,768]{1,0:T(8,128)(2,1)}, u32[]{:S(2)}, u32[]{:S(2)}) collective-permute-start(bf16[768,768]{1,0:T(8,128)(2,1)} %add_convert_fusion.1), channel_id=1, source_target_pairs={{0,4},{4,0},{8,12},{12,8},{16,20},{20,16},{24,28},{28,24},{1,5},{5... | collective-permute-start | bytes 3538952 | tf_op jit(solution)/shard_map/ppermute | solution.py:51
  111.2 25.1 %collective-permute-start.24 = (bf16[128,2048]{1,0:T(8,128)(2,1)}, bf16[128,2048]{1,0:T(8,128)(2,1)}, u32[]{:S(2)}, u32[]{:S(2)}) collective-permute-start(bf16[128,2048]{1,0:T(8,128)(2,1)} %get-tuple-element.135), channel_id=1, source_target_pairs={{0,16},{4,20},{8,24},{12,28},{16,0},{20,4},{24,8},{28,12},{1,17},{... | collective-permute-start | bytes 1572872 | tf_op jit(solution)/shard_map/ppermute | solution.py:51
  111.7 24.6 %collective-permute-start.25 = (bf16[128,2048]{1,0:T(8,128)(2,1)}, bf16[128,2048]{1,0:T(8,128)(2,1)}, u32[]{:S(2)}, u32[]{:S(2)}) collective-permute-start(bf16[128,2048]{1,0:T(8,128)(2,1)} %get-tuple-element.136), channel_id=1, source_target_pairs={{0,24},{4,28},{8,16},{12,20},{16,8},{20,12},{24,0},{28,4},{1,25},{... | collective-permute-start | bytes 1572872 | tf_op jit(solution)/shard_map/ppermute | solution.py:51
  146.3 20.1 %collective-permute-start.29 = (bf16[192,2048]{1,0:T(8,128)(2,1)}, bf16[192,2048]{1,0:T(8,128)(2,1)S(1)}, u32[]{:S(2)}, u32[]{:S(2)}) collective-permute-start(bf16[192,2048]{1,0:T(8,128)(2,1)} %bitcast.269), channel_id=1, source_target_pairs={{0,16},{4,20},{8,24},{12,28},{16,0},{20,4},{24,8},{28,12},{1,17},{... | collective-permute-start | bytes 2359304 | tf_op jit(solution)/shard_map/ppermute | solution.py:51
  147.5 20.6 %collective-permute-start.28 = (bf16[192,2048]{1,0:T(8,128)(2,1)}, bf16[192,2048]{1,0:T(8,128)(2,1)S(1)}, u32[]{:S(2)}, u32[]{:S(2)}) collective-permute-start(bf16[192,2048]{1,0:T(8,128)(2,1)} %bitcast.270), channel_id=1, source_target_pairs={{0,8},{4,12},{8,0},{12,4},{16,24},{20,28},{24,16},{28,20},{1,9},{5... | collective-permute-start | bytes 2359304 | tf_op jit(solution)/shard_map/ppermute | solution.py:51
  153.4 57.4 %collective-permute-start.40 = (bf16[128,2048]{1,0:T(8,128)(2,1)}, bf16[128,2048]{1,0:T(8,128)(2,1)}, u32[]{:S(2)}, u32[]{:S(2)}) collective-permute-start(bf16[128,2048]{1,0:T(8,128)(2,1)} %collective-permute-done.23.refs_1_), channel_id=1, source_target_pairs={{0,1},{1,0},{2,3},{3,2},{4,5},{5,4},{6,7},{7,6},{8,9},{9,8},{10,11... | collective-permute-start | bytes 1572872 | tf_op jit(solution)/shard_map/ppermute | solution.py:51
  153.9 56.9 %collective-permute-start.41 = (bf16[128,2048]{1,0:T(8,128)(2,1)}, bf16[128,2048]{1,0:T(8,128)(2,1)}, u32[]{:S(2)}, u32[]{:S(2)}) collective-permute-start(bf16[128,2048]{1,0:T(8,128)(2,1)} %collective-permute-done.24.refs_2_), channel_id=1, source_target_pairs={{0,1},{1,0},{2,3},{3,2},{4,5},{5,4},{6,7},{7,6},{8,9},{9,8},{10,11... | collective-permute-start | bytes 1572872 | tf_op jit(solution)/shard_map/ppermute | solution.py:51
  155.5 20.3 %collective-permute-start.33 = (bf16[96,2048]{1,0:T(8,128)(2,1)S(1)}, bf16[96,2048]{1,0:T(8,128)(2,1)S(1)}, u32[]{:S(2)}, u32[]{:S(2)}) collective-permute-start(bf16[96,2048]{1,0:T(8,128)(2,1)S(1)} %get-tuple-element.228), channel_id=1, source_target_pairs={{0,8},{4,12},{8,0},{12,4},{16,24},{20,28},{24,16},{28,20},{1,9},{5... | collective-permute-start | bytes 1179656 | tf_op jit(solution)/shard_map/ppermute | solution.py:51
  166.4 44.4 %collective-permute-start.42 = (bf16[128,2048]{1,0:T(8,128)(2,1)}, bf16[128,2048]{1,0:T(8,128)(2,1)}, u32[]{:S(2)}, u32[]{:S(2)}) collective-permute-start(bf16[128,2048]{1,0:T(8,128)(2,1)} %collective-permute-done.25.refs_3_), channel_id=1, source_target_pairs={{0,1},{1,0},{2,3},{3,2},{4,5},{5,4},{6,7},{7,6},{8,9},{9,8},{10,11... | collective-permute-start | bytes 1572872 | tf_op jit(solution)/shard_map/ppermute | solution.py:51
  308.6 71.0 %collective-permute-start.82 = (bf16[2,48,2048]{2,1,0:T(8,128)(2,1)}, bf16[2,48,2048]{2,1,0:T(8,128)(2,1)}, u32[]{:S(2)}, u32[]{:S(2)}) collective-permute-start(bf16[2,48,2048]{2,1,0:T(8,128)(2,1)} %pad_maximum_fusion.15), channel_id=1, source_target_pairs={{0,2},{1,3},{2,0},{3,1},{4,6},{5,7},{6,4},{7,5},{8,10},{9,11},{10,... | collective-permute-start | bytes 1179656 | tf_op jit(solution)/shard_map/ppermute | solution.py:51
  324.6 22.3 %collective-permute-start.57 = (bf16[192,2048]{1,0:T(8,128)(2,1)}, bf16[192,2048]{1,0:T(8,128)(2,1)S(1)}, u32[]{:S(2)}, u32[]{:S(2)}) collective-permute-start(bf16[192,2048]{1,0:T(8,128)(2,1)} %get-tuple-element.167), channel_id=1, source_target_pairs={{0,8},{4,12},{8,0},{12,4},{16,24},{20,28},{24,16},{28,20},{1,9},{5... | collective-permute-start | bytes 2359304 | tf_op jit(solution)/shard_map/ppermute | solution.py:51
  325.5 22.4 %collective-permute-start.55 = (bf16[192,2048]{1,0:T(8,128)(2,1)}, bf16[192,2048]{1,0:T(8,128)(2,1)S(1)}, u32[]{:S(2)}, u32[]{:S(2)}) collective-permute-start(bf16[192,2048]{1,0:T(8,128)(2,1)} %get-tuple-element.167), channel_id=1, source_target_pairs={{0,16},{4,20},{8,24},{12,28},{16,0},{20,4},{24,8},{28,12},{1,17},{... | collective-permute-start | bytes 2359304 | tf_op jit(solution)/shard_map/ppermute | solution.py:51
  386.2 43.7 %collective-permute-start.66 = (bf16[192,2304]{1,0:T(8,128)(2,1)}, bf16[192,2304]{1,0:T(8,128)(2,1)}, u32[]{:S(2)}, u32[]{:S(2)}) collective-permute-start(bf16[192,2304]{1,0:T(8,128)(2,1)} %pad_maximum_fusion.3), channel_id=1, source_target_pairs={{0,8},{4,12},{8,0},{12,4},{16,24},{20,28},{24,16},{28,20},{1,9},{5... | collective-permute-start | bytes 2654216 | tf_op jit(solution)/shard_map/ppermute | solution.py:51
  388.9 41.1 %collective-permute-start.68 = (bf16[192,2304]{1,0:T(8,128)(2,1)}, bf16[192,2304]{1,0:T(8,128)(2,1)}, u32[]{:S(2)}, u32[]{:S(2)}) collective-permute-start(bf16[192,2304]{1,0:T(8,128)(2,1)} %pad_maximum_fusion.4), channel_id=1, source_target_pairs={{0,16},{4,20},{8,24},{12,28},{16,0},{20,4},{24,8},{28,12},{1,17},{... | collective-permute-start | bytes 2654216 | tf_op jit(solution)/shard_map/ppermute | solution.py:51
  399.4 20.7 %collective-permute-start.61 = (bf16[96,2048]{1,0:T(8,128)(2,1)S(1)}, bf16[96,2048]{1,0:T(8,128)(2,1)S(1)}, u32[]{:S(2)}, u32[]{:S(2)}) collective-permute-start(bf16[96,2048]{1,0:T(8,128)(2,1)S(1)} %get-tuple-element.215), channel_id=1, source_target_pairs={{0,16},{4,20},{8,24},{12,28},{16,0},{20,4},{24,8},{28,12},{1,17},{... | collective-permute-start | bytes 1179656 | tf_op jit(solution)/shard_map/ppermute | solution.py:51
  425.2 21.0 %collective-permute-start.69 = (bf16[192,2048]{1,0:T(8,128)(2,1)}, bf16[192,2048]{1,0:T(8,128)(2,1)}, u32[]{:S(2)}, u32[]{:S(2)}) collective-permute-start(bf16[192,2048]{1,0:T(8,128)(2,1)} %pad_maximum_fusion.9), channel_id=1, source_target_pairs={{0,8},{4,12},{8,0},{12,4},{16,24},{20,28},{24,16},{28,20},{1,9},{5... | collective-permute-start | bytes 2359304 | tf_op jit(solution)/shard_map/ppermute | solution.py:51
  425.7 20.5 %collective-permute-start.70 = (bf16[192,2048]{1,0:T(8,128)(2,1)}, bf16[192,2048]{1,0:T(8,128)(2,1)}, u32[]{:S(2)}, u32[]{:S(2)}) collective-permute-start(bf16[192,2048]{1,0:T(8,128)(2,1)} %pad_maximum_fusion.10), channel_id=1, source_target_pairs={{0,16},{4,20},{8,24},{12,28},{16,0},{20,4},{24,8},{28,12},{1,17},{... | collective-permute-start | bytes 2359304 | tf_op jit(solution)/shard_map/ppermute | solution.py:51
  440.5 22.4 %collective-permute-start.76 = (bf16[2,48,1792]{2,1,0:T(8,128)(2,1)}, bf16[2,48,1792]{2,1,0:T(8,128)(2,1)S(1)}, u32[]{:S(2)}, u32[]{:S(2)}) collective-permute-start(bf16[2,48,1792]{2,1,0:T(8,128)(2,1)} %pad_maximum_fusion.16), channel_id=1, source_target_pairs={{0,2},{1,3},{2,0},{3,1},{4,6},{5,7},{6,4},{7,5},{8,10},{9,11},{10,... | collective-permute-start | bytes 1032200 | tf_op jit(solution)/shard_map/ppermute | solution.py:51
  445.8 22.9 %collective-permute-start.79 = (bf16[2,48,768]{2,1,0:T(8,128)(2,1)S(1)}, bf16[2,48,768]{2,1,0:T(8,128)(2,1)S(1)}, u32[]{:S(2)}, u32[]{:S(2)}) collective-permute-start(bf16[2,48,768]{2,1,0:T(8,128)(2,1)S(1)} %pad_maximum_fusion.23), channel_id=1, source_target_pairs={{0,2},{1,3},{2,0},{3,1},{4,6},{5,7},{6,4},{7,5},{8,10},{9,11},{10,... | collective-permute-start | bytes 442376 | tf_op jit(solution)/shard_map/ppermute | solution.py:51
  (164 other events, 2994.4 us)

commit v7 on v6

--- a/solution.py
+++ b/solution.py
@@ -107,13 +107,10 @@
     return [parts[0]] + [swap(b, "shard", bit) for b, bit in zip(blocks, bits)], blocks
 
 
-def gather_blocks(value, axis, bits, gates=None):
+def gather_blocks(value, axis, bits):
     current = value[None]
     for bit in bits:
-        there = swap(current, axis, bit)
-        if gates and bit in gates:
-            there = after(there, *gates[bit])
-        current = jnp.concatenate([current, there], 0)
+        current = jnp.concatenate([current, swap(current, axis, bit)], 0)
     return current
 
 
@@ -342,6 +339,36 @@
         ),
         name=name,
     )(*order)
+
+
+def sum_kernel(place, *refs, blocks):
+    gathered, outs = refs[:blocks], refs[blocks:]
+    start = 0
+    for out in outs:
+        width = out.shape[1]
+        total, row = None, 0
+        for ref in gathered:
+            for g in range(ref.shape[0]):
+                rows = ref.shape[1]
+                term = t_mm(place[row : row + rows], ref[g, :, start : start + width])
+                total = term if total is None else total + term
+                row += rows
+        out[...] = total
+        start += width
+
+
+def sum_blocks(place, gathered, widths):
+    total = sum(widths)
+    return pl.pallas_call(
+        functools.partial(sum_kernel, blocks=len(gathered)),
+        out_shape=[jax.ShapeDtypeStruct((place.shape[1], w), F32) for w in widths],
+        in_specs=[pl.BlockSpec(memory_space=pltpu.VMEM)] * (1 + len(gathered)),
+        out_specs=[pl.BlockSpec(memory_space=pltpu.VMEM)] * len(widths),
+        cost_estimate=pl.CostEstimate(
+            flops=2 * place.size * total, bytes_accessed=(2 * place.shape[0] + 4 * place.shape[1]) * total, transcendentals=0
+        ),
+        name="sum_blocks",
+    )(place, *gathered)
 
 
 def seen(pos_q, pos_k, lab_q, lab_k):
@@ -542,6 +569,7 @@
     w_down_other = swap(w_down, "shard", 1)
     pieces_qkv = cut_pieces(at, [w_query, w_key, w_value], span, chips, True)
     turned = exchange(pieces_qkv)
+    near_up = exchange(cut_pieces(at, [after(w_up, *pieces_qkv)], ff_part, chips, True))
 
     narrow = [out_query, out_key, out_value, in_attn, out_expand, in_reduce]
     edges = np.cumsum([0] + [n.shape[2] for n in narrow])
@@ -561,20 +589,19 @@
         (starts, b_query, b_value, b_up, me, chosen, packed), normed
     )
     vectors = after(jnp.stack([b_out, ln2_gain, ln2_bias, ln1_gain]), normed).astype(F32)
-    hidden_block = after(normed, packed_other, near_one, *turned[1:])
+    hidden_block = after(normed, packed_other, near_one, *turned[1:], *near_up[1:])
     hidden_one, one_first, one_last = gather_rows(hidden_block, bits)
 
     turned[0] = after(turned[0], *one_first)
     w_qkv_mine, w_qkv_other = place_weights(
         at, both_cores(turned + halves_over_rep(turned[1:])), chips, 3 * span, False
     )
+    far_up = halves_over_rep(near_up[1:])
     w_out_late, w_down_late = after((w_out, w_down), normed)
     w_out_chip = jnp.concatenate([w_out_late, w_out_other], 0)
     w_down_chip = jnp.concatenate([w_down_late, w_down_other], 0)
-    hidden_one = after(hidden_one, w_out_chip, w_down_chip)
+    hidden_one = after(hidden_one, w_out_chip, w_down_chip, *far_up)
     cot_mine = cotangent[0].reshape(block, wide)
-    cut_up = cut_pieces(at, [after(w_up, *one_first)], ff_part, chips, True)
-    near_up = exchange(after(tuple(cut_up), one_last))
     near = after(jnp.concatenate([mine[None], near_one], 0), *one_first)
     for bit in bits[1:]:
         near = jnp.concatenate([near, swap(near, "shard", bit)], 0)
@@ -632,6 +659,7 @@
                 products = [(after(v, parts[2 * i]), w, main) for v, w, main in products]
         return parts
 
+    hidden_one = after(hidden_one, where, out_qkv_mine, out_qkv_other, in_att, out_exp, in_red)
     low_qkv = keep_own(mm_t(hidden_one, in_qkv), 3)
     qkv_away = (
         mm(hidden_one, w_qkv_other) + mm(low_qkv, out_qkv_other) + b_qkv_of(me ^ 1)
@@ -640,12 +668,13 @@
     qkv_own = by_chip(
         (mm(hidden_one, w_qkv_mine) + mm(low_qkv, out_qkv_mine) + b_qkv_of(me)).astype(BF16)
     )
-    qkv_own = after(qkv_own, *near_up[1:])
     att_own, att_away, lse = attend(where, qkv_own, qkv_other, heads)
-    cot_pieces, _, _ = gather_rows(after(cot_mine, att_own), bits, apart=True)
     attended = jnp.concatenate([flat(att_own), swap(flat(att_away), "shard", 1)], 1)
     low_att = keep_own(mm_t(attended, in_att))
     parts = block_products([(attended, w_out_chip, mm)], low_att, out_att)
+    cot_pieces, _, _ = gather_rows(
+        after(cot_mine, one_last), bits, (parts[2 * (chips - 1)],), apart=True
+    )
     terms, relayed = scatter_rows(parts, bits)
     cot = jnp.concatenate(after(cot_pieces, *relayed), 0)
     glow_red = keep_own(mm_t(cot, out_red))
@@ -654,19 +683,8 @@
     residual, hidden_block = row_call(
         norm_kernel, [rows_in, vectors] + terms, block, wide, [F32, BF16], "norm"
     )
-    far_up = halves_over_rep(after(tuple(near_up[1:]), parts[2 * (chips - 1)]))
     pieces_up = after((*near_up, *far_up), hidden_block)
     hidden_two, _, _ = gather_rows(hidden_block, bits)
-
-    rep_bits = bits_of(lax.axis_size("rep"))
-    mark = (after(chosen, hidden_block)[:, None] == jnp.arange(ADAPTERS, dtype=jnp.int32)[None, :]).astype(BF16)
-    marks = gather_blocks(jnp.pad(mark, ((0, 16 - count), (0, 128 - ADAPTERS))), "rep", rep_bits)
-    groups = marks.shape[0]
-    marks = marks[:, :count, :ADAPTERS].reshape(groups * count, 1, ADAPTERS, 1)
-    place = (marks * jnp.eye(rank, dtype=BF16)[None, :, None, :]).reshape(
-        groups * count * rank, ADAPTERS * rank
-    )
-
 
     (w_up_chip,) = place_weights(at, both_cores(pieces_up), chips, ff_part, True)
     hidden_two = after(hidden_two, grad_act)
@@ -688,6 +706,16 @@
     )
     grad_branch, _, branch_last = gather_rows(grad_block, bits)
 
+    rep_bits = bits_of(lax.axis_size("rep"))
+    mark = (after(chosen, grad_block)[:, None] == jnp.arange(ADAPTERS, dtype=jnp.int32)[None, :]).astype(BF16)
+    marks = gather_blocks(jnp.pad(mark, ((0, 16 - count), (0, 128 - ADAPTERS))), "rep", rep_bits)
+    groups = marks.shape[0]
+    marks = marks[:, :count, :ADAPTERS].reshape(groups * count, 1, ADAPTERS, 1)
+    place = (marks * jnp.eye(rank, dtype=BF16)[None, :, None, :]).reshape(
+        groups * count * rank, ADAPTERS * rank
+    )
+
+
     act_late = after(act, grad_block)
     low_red = keep_own(mm_t(act_late, in_red))
     down_parts = block_products([(act_late, w_down_chip, mm)], low_red, out_red)
@@ -729,30 +757,32 @@
             current = current + (there if i else after(there, *gate)).astype(F32)
         return current[0], away
 
-    def over_groups(terms, gates=None):
+    def over_groups(terms, hold=()):
         widths = [t.shape[1] for t in terms]
         data = jnp.concatenate([t.astype(BF16) for t in terms], 1)
-        taken = gather_blocks(data, "rep", rep_bits, gates).reshape(groups * count * rank, -1)
-        outs, start = [], 0
-        for width in widths:
-            out = t_mm(place, taken[:, start : start + width])
-            outs.append(out.reshape(ADAPTERS, rank, width))
-            start += width
-        return outs
+        gathered, current = [data[None]], data[None]
+        for bit in rep_bits:
+            if hold and bit == rep_bits[-1]:
+                current = after(current, *hold)
+            there = swap(current, "rep", bit)
+            gathered.append(there)
+            if bit != rep_bits[-1]:
+                current = jnp.concatenate([current, there], 0)
+        return [out.reshape(ADAPTERS, rank, -1) for out in sum_blocks(place, gathered, widths)]
 
     def halves(value):
         middle = value.shape[1] // 2
         return value[:, :middle], value[:, middle:]
 
     glow_late, low_late = after((glow_exp, low_exp), grad_block)
-    act_mid, grad_mid, low_mid, glow_mid = after((act, grad_pre, low_exp, glow_red), *grad_sent)
+    act_mid, grad_mid, low_mid, glow_mid = after((act, grad_pre, low_exp, glow_red), grad_block)
     red_own, red_away = halves(t_mm(glow_mid, act_mid))
     exp_own, exp_away = halves(t_mm(low_mid, grad_mid))
     local = sum_cores(
         jnp.concatenate([red_own, exp_own], 1), jnp.concatenate([red_away, exp_away], 1)
     )
     s_in_red, s_out_exp = over_groups(
-        [local[:, :ff_part], local[:, ff_part:]], {rep_bits[-1]: (grad_away,)}
+        [local[:, :ff_part], local[:, ff_part:]]
     )
 
     near_first = core_columns(
@@ -787,6 +817,7 @@
 
     terms, relayed = scatter_rows(parts, bits, between=hop)
     second = aside["second"]
+    riders[0] = after(riders[0], s_in_red, s_out_exp)
     down, _ = scatter_rows(riders, bits, (grad_away,))
     down[0] = after(down[0], *relayed)
     first = sum(t[:tall, wide:].astype(F32) for t in down).reshape(2, count * rank, slice_wide)
@@ -804,13 +835,12 @@
     )
     out_att_sum = second[count * 3 * rank :]
     second = second[: count * 3 * rank].reshape(count, 3, rank, slice_wide)
-    ends = {rep_bits[-1]: (input_rows,)}
-    s_in_att, s_in_exp, s_out_red = over_groups([att_side, first[0], first[1]], ends)
+    s_in_att, s_in_exp, s_out_red = over_groups([att_side, first[0], first[1]])
     late = over_groups(
         [second[:, t].reshape(count * rank, slice_wide) for t in range(3)]
         + [outer[:, t * span : (t + 1) * span] for t in range(3)]
         + [out_att_sum],
-        ends,
+        terms[1:],
     )
     s_out_att = late.pop()
     shape = (1, count, rows, wide)

time: 478 us -> 523 us (1.094)
  local copies, waits for them, and re-layouts: 50.6 us -> 71.4 us
  waiting for transfers between devices: 145 us -> 153 us
  Pallas kernels: 58 us -> 65 us
    unnamed x235 -> x263, local copies, waits for them, and re-layouts: 25.7 us -> 37.8 us
    ppermute x83, waiting for transfers between devices: 145 us -> 153 us  [swap(): return lax.ppermute(value, axis, [(i, i ^ mask) for i in range(size)])]
    dot_general x32, matrix products: 50.7 us -> 58.9 us  [mm(): lax.dot_general(a, b, (((1,), (0,)), ((), ())), preferred_element_type=F32)]
    pallas_call x0 -> x3, Pallas kernels: none -> 7.43 us  [sum_blocks(): pl.pallas_call(functools.partial(sum_kernel, blocks=len(gathered)), out_s...]
    dot_general x21 -> x9, matrix products: 17.8 us -> 11.5 us  [t_mm(): lax.dot_general(a, b, (((0,), (0,)), ((), ())), preferred_element_type=F32)]
  transfers between devices with their start and end apart: 83 -> 83, of which waited for: 32 -> 28; matrix products, arithmetic and copies ran while one was open for 29% -> 31% of each run, Pallas kernels for 10% -> 8%
where the time goes in v7:
time: 523 us; the launch traced here: 516 us
  waiting for transfers between devices  153 us (29%)
  matrix products  121 us (23%)
  local copies, waits for them, and re-layouts  71.4 us (14%)
  starting transfers between devices  69.9 us (13%)
  Pallas kernels  65 us (12%)
  other arithmetic  30.8 us (6%)
  between operations  5.24 us (1%)
    ppermute x83, waiting for transfers between devices, swap(): return lax.ppermute(value, axis, [(i, i ^ mask) for i in range(size)])  153 us
    ppermute x83, starting transfers between devices, swap(): return lax.ppermute(value, axis, [(i, i ^ mask) for i in range(size)])  69.9 us
    dot_general x32, matrix products, mm(): lax.dot_general(a, b, (((1,), (0,)), ((), ())), preferred_element_type=F32)  58.9 us
    dot_general x23, matrix products, mm_t(): lax.dot_general(a, b, (((1,), (1,)), ((), ())), preferred_element_type=F32)  50.3 us
    unnamed x263, local copies, waits for them, and re-layouts  37.8 us
    pallas_call x2, Pallas kernels, place_weights(): pl.pallas_call(functools.partial(place_kernel, count=count, width=width,...  14.1 us
    pallas_call x3, Pallas kernels, row_call(): pl.pallas_call(kernel, out_shape=[jax.ShapeDtypeStruct((rows, wide), d) f...  13.2 us
    dot_general x9, matrix products, t_mm(): lax.dot_general(a, b, (((0,), (0,)), ((), ())), preferred_element_type=F32)  11.5 us
  transfers between devices with their start and end apart: 83, of which 28 were waited for; matrix products, arithmetic and copies ran while one was open for 31% of the time, Pallas kernels for 8%

profile of v7, /device:TPU:0, one launch (start us, length us, event | category | flops | bytes accessed | tf_op | source)
XLA Modules:
  0.0 516.3 jit_solution(16729517295587121714)
XLA Ops:
  40.7 9.2 %collective-permute-done.8.refs_2_ = bf16[128,2048]{1,0:T(8,128)(2,1)} collective-permute-done((bf16[128,2048]{1,0:T(8,128)(2,1)}, bf16[128,2048]{1,0:T(8,128)(2,1)}, u32[]{:S(2)}, u32[]{:S(2)}) %collective-permute-start.8) | collective-permute-done | bytes 524320 | tf_op jit(solution)/shard_map/ppermute | solution.py:51
  61.4 9.9 %collective-permute-done.10 = bf16[192,2048]{1,0:T(8,128)(2,1)S(1)} collective-permute-done((bf16[192,2048]{1,0:T(8,128)(2,1)S(1)}, bf16[192,2048]{1,0:T(8,128)(2,1)S(1)}, u32[]{:S(2)}, u32[]{:S(2)}) %collective-permute-start.10) | collective-permute-done | bytes 786464 | tf_op jit(solution)/shard_map/ppermute | solution.py:51
  80.5 7.0 %collective-permute-done.14.refs_4_ = bf16[128,2048]{1,0:T(8,128)(2,1)S(1)} collective-permute-done((bf16[128,2048]{1,0:T(8,128)(2,1)}, bf16[128,2048]{1,0:T(8,128)(2,1)S(1)}, u32[]{:S(2)}, u32[]{:S(2)}) %collective-permute-start.14) | collective-permute-done | bytes 524320 | tf_op jit(solution)/shard_map/ppermute | solution.py:51
  89.1 9.6 %collective-permute-done.15.refs_5_ = bf16[128,2048]{1,0:T(8,128)(2,1)S(1)} collective-permute-done((bf16[128,2048]{1,0:T(8,128)(2,1)}, bf16[128,2048]{1,0:T(8,128)(2,1)S(1)}, u32[]{:S(2)}, u32[]{:S(2)}) %collective-permute-start.15) | collective-permute-done | bytes 524320 | tf_op jit(solution)/shard_map/ppermute | solution.py:51
  99.7 8.6 %collective-permute-done.16.refs_6_ = bf16[128,2048]{1,0:T(8,128)(2,1)S(1)} collective-permute-done((bf16[128,2048]{1,0:T(8,128)(2,1)S(1)}, bf16[128,2048]{1,0:T(8,128)(2,1)S(1)}, u32[]{:S(2)}, u32[]{:S(2)}) %collective-permute-start.16) | collective-permute-done | bytes 524320 | tf_op jit(solution)/shard_map/ppermute | solution.py:51
  113.1 6.5 %place_weights.2 = (bf16[2048,768]{1,0:T(8,128)(2,1)}, bf16[2048,768]{1,0:T(8,128)(2,1)}) custom-call(s32[2]{0:T(128)} %pad_add_fusion.1.at_ref, bf16[256,1536]{1,0:T(8,128)(2,1)} %get-tuple-element.135.refs_0_, bf16[128,1536]{1,0:T(8,128)(2,1)} %collective-permute-done.4.refs_1_, bf16[128,1536]{1,0:T(8,128)(2,1)} %collective-permute-done.5.refs_2_, ...), custom_call_target="tpu_custom_call" | custom-call | bytes 12582912 | tf_op jit(solution)/shard_map/place_weights/pallas_call | solution.py:205
  128.4 5.5 %add_convert_fusion.1 = bf16[768,768]{1,0:T(8,128)(2,1)} fusion(f32[768,768]{1,0:T(8,128)S(1)} %fusion.197, bf16[768,2048]{1,0:T(8,128)(2,1)} %constant_dynamic-update-slice_fusion, bf16[2048,768]{1,0:T(8,128)(2,1)S(1)} %copy-done, f32[768]{0:T(1024)S(1)} %get-tuple-element.281), kind=kOutput, calls=%fused_computation.64 | convolution fusion | flops 2417688576 | bytes 9833472 | tf_op jit(solution)/shard_map/dot_general | solution.py:38
  138.6 6.5 %add_convert_fusion.2 = bf16[768,768]{1,0:T(8,128)(2,1)} fusion(f32[768,768]{1,0:T(8,128)S(1)} %fusion.196, bf16[768,2048]{1,0:T(8,128)(2,1)} %constant_dynamic-update-slice_fusion, bf16[2048,768]{1,0:T(8,128)(2,1)} %get-tuple-element.136, f32[768]{0:T(1024)S(1)} %get-tuple-element.282), kind=kOutput, calls=%fused_computation.65 | convolution fusion | flops 2417688576 | bytes 9833472 | tf_op jit(solution)/shard_map/dot_general | solution.py:38
  145.1 7.5 %attend.1 = (bf16[4,3,64,256]{3,2,1,0:T(8,128)(2,1)}, bf16[4,3,64,256]{3,2,1,0:T(8,128)(2,1)}, f32[3,512,2]{2,1,0:T(8,128)}) custom-call(s32[512,1]{1,0:T(8,128)} %copy.67.pq, s32[1,512]{1,0:T(1,128)} %bitcast.261, s32[3,512,1]{2,1,0:T(8,128)} %copy.68.lq, s32[3,1,512]{2,1,0:T(1,128)} %broadcast_in_dim.95.lk, bf16[4,3,64,768]{3,2,1,0:T(8,128)(2,1)} %bitcast.230, ...), custom_call_target="tpu_custom_call" | custom-call | flops 805306368 | bytes 3145728 | tf_op jit(solution)/shard_map/attend/pallas_call | solution.py:428
  166.2 10.4 %collective-permute-done.32 = bf16[192,2048]{1,0:T(8,128)(2,1)S(1)} collective-permute-done((bf16[192,2048]{1,0:T(8,128)(2,1)}, bf16[192,2048]{1,0:T(8,128)(2,1)S(1)}, u32[]{:S(2)}, u32[]{:S(2)}) %collective-permute-start.32) | collective-permute-done | bytes 786464 | tf_op jit(solution)/shard_map/ppermute | solution.py:51
  181.1 5.5 %collective-permute-done.36 = bf16[96,2048]{1,0:T(8,128)(2,1)S(1)} collective-permute-done((bf16[96,2048]{1,0:T(8,128)(2,1)S(1)}, bf16[96,2048]{1,0:T(8,128)(2,1)S(1)}, u32[]{:S(2)}, u32[]{:S(2)}) %collective-permute-start.36) | collective-permute-done | bytes 393248 | tf_op jit(solution)/shard_map/ppermute | solution.py:51
  189.1 5.9 %collective-permute-done.34 = bf16[96,2048]{1,0:T(8,128)(2,1)S(1)} collective-permute-done((bf16[96,2048]{1,0:T(8,128)(2,1)S(1)}, bf16[96,2048]{1,0:T(8,128)(2,1)S(1)}, u32[]{:S(2)}, u32[]{:S(2)}) %collective-permute-start.34) | collective-permute-done | bytes 393248 | tf_op jit(solution)/shard_map/ppermute | solution.py:51
  197.4 10.3 %add_convert_fusion = bf16[768,2048]{1,0:T(8,128)(2,1)} fusion(f32[768,2048]{1,0:T(8,128)S(1)} %fusion.179, bf16[768,2048]{1,0:T(8,128)(2,1)S(1)} %constant_dynamic-update-slice_fusion.9, bf16[2048,2048]{1,0:T(8,128)(2,1)} %copy-done.33), kind=kOutput, calls=%fused_computation.10 | convolution fusion | flops 6445596672 | bytes 20971520 | tf_op jit(solution)/shard_map/dot_general | solution.py:42
  219.3 15.9 %collective-permute-done.39 = bf16[192,2048]{1,0:T(8,128)(2,1)} collective-permute-done((bf16[192,2048]{1,0:T(8,128)(2,1)}, bf16[192,2048]{1,0:T(8,128)(2,1)}, u32[]{:S(2)}, u32[]{:S(2)}) %collective-permute-start.39) | collective-permute-done | bytes 786464 | tf_op jit(solution)/shard_map/ppermute | solution.py:51
  247.6 7.6 %place_weights.3 = bf16[2048,2048]{1,0:T(8,128)(2,1)} custom-call(s32[2]{0:T(128)} %pad_add_fusion.1.at_ref, bf16[256,2048]{1,0:T(8,128)(2,1)} %get-tuple-element.158.refs_0_, bf16[128,2048]{1,0:T(8,128)(2,1)} %collective-permute-done.7.refs_1_, bf16[128,2048]{1,0:T(8,128)(2,1)} %collective-permute-done.8.refs_2_, bf16[128,2048]{1,0:T(8,128)(2,1)} %copy-done.52, ...), custom_call_target="tpu_custom_call" | custom-call | bytes 16777216 | tf_op jit(solution)/shard_map/place_weights/pallas_call | solution.py:205
  264.2 13.3 %multiply_convert_fusion = (bf16[768,2048]{1,0:T(8,128)(2,1)}, bf16[768,2048]{1,0:T(8,128)(2,1)S(1)}) fusion(bf16[768,2048]{1,0:T(8,128)(2,1)} %add_convert_fusion, f32[2048]{0:T(1024)S(1)} %maximum_convert_fusion, f32[768,2048]{1,0:T(8,128)S(1)} %fusion.180, bf16[768,2048]{1,0:T(8,128)(2,1)} %constant_dynamic-update-slice_fusion.14, ...), kind=kOutput, calls=%fused_computation.7 | convolution fusion | flops 6466043904 | bytes 27271168 | tf_op jit(solution)/shard_map/dot_general | solution.py:38
  291.7 7.1 %collective-permute-done.52 = bf16[96,2048]{1,0:T(8,128)(2,1)S(1)} collective-permute-done((bf16[96,2048]{1,0:T(8,128)(2,1)S(1)}, bf16[96,2048]{1,0:T(8,128)(2,1)S(1)}, u32[]{:S(2)}, u32[]{:S(2)}) %collective-permute-start.52) | collective-permute-done | bytes 393248 | tf_op jit(solution)/shard_map/ppermute | solution.py:51
  306.4 11.1 %collective-permute-done.53.refs_2_ = bf16[192,2048]{1,0:T(8,128)(2,1)} collective-permute-done((bf16[192,2048]{1,0:T(8,128)(2,1)S(1)}, bf16[192,2048]{1,0:T(8,128)(2,1)}, u32[]{:S(2)}, u32[]{:S(2)}) %collective-permute-start.53) | collective-permute-done | bytes 786464 | tf_op jit(solution)/shard_map/ppermute | solution.py:51
  328.7 5.6 %fusion.53 = f32[192,2048]{1,0:T(8,128)S(1)} fusion(bf16[2048,2048]{1,0:T(8,128)(2,1)} %copy-done.33, bf16[768,2048]{1,0:T(8,128)(2,1)} %get-tuple-element.177), kind=kOutput, calls=%fused_computation.144 | convolution fusion | flops 1610612736 | bytes 10747904 | tf_op jit(solution)/shard_map/dot_general | solution.py:38
  337.6 5.4 %fusion.51 = f32[192,2048]{1,0:T(8,128)S(1)} fusion(bf16[2048,2048]{1,0:T(8,128)(2,1)} %copy-done.33, bf16[768,2048]{1,0:T(8,128)(2,1)S(1)} %copy-done.28), kind=kOutput, calls=%fused_computation.142 | convolution fusion | flops 1610612736 | bytes 10747904 | tf_op jit(solution)/shard_map/dot_general | solution.py:38
  382.3 10.4 %collective-permute-done.61.refs_2_ = bf16[2,48,2048]{2,1,0:T(8,128)(2,1)} collective-permute-done((bf16[2,48,2048]{2,1,0:T(8,128)(2,1)S(1)}, bf16[2,48,2048]{2,1,0:T(8,128)(2,1)}, u32[]{:S(2)}, u32[]{:S(2)}) %collective-permute-start.61) | collective-permute-done | bytes 393248 | tf_op jit(solution)/shard_map/ppermute | solution.py:51
  415.2 9.7 %attend_back.1 = (bf16[4,3,64,768]{3,2,1,0:T(8,128)(2,1)}, bf16[4,3,64,768]{3,2,1,0:T(8,128)(2,1)}) custom-call(s32[512,1]{1,0:T(8,128)} %copy.67.pq, s32[1,512]{1,0:T(1,128)} %bitcast.262, s32[3,512,1]{2,1,0:T(8,128)} %copy.68.lq, s32[3,1,512]{2,1,0:T(1,128)} %broadcast_in_dim.95.lk, bf16[4,3,64,768]{3,2,1,0:T(8,128)(2,1)} %bitcast.231, ...), custom_call_target="tpu_custom_call" | custom-call | flops 2013265920 | bytes 5505024 | tf_op jit(solution)/shard_map/attend_back/pallas_call | solution.py:485
  450.3 7.7 %collective-permute-done.67 = bf16[96,2048]{1,0:T(8,128)(2,1)S(1)} collective-permute-done((bf16[96,2048]{1,0:T(8,128)(2,1)S(1)}, bf16[96,2048]{1,0:T(8,128)(2,1)S(1)}, u32[]{:S(2)}, u32[]{:S(2)}) %collective-permute-start.67) | collective-permute-done | bytes 393248 | tf_op jit(solution)/shard_map/ppermute | solution.py:51
  492.6 12.9 %collective-permute-done.82.refs_2_ = bf16[2,48,768]{2,1,0:T(8,128)(2,1)S(1)} collective-permute-done((bf16[2,48,768]{2,1,0:T(8,128)(2,1)S(1)}, bf16[2,48,768]{2,1,0:T(8,128)(2,1)S(1)}, u32[]{:S(2)}, u32[]{:S(2)}) %collective-permute-start.82) | collective-permute-done | bytes 147488 | tf_op jit(solution)/shard_map/ppermute | solution.py:51
  (625 shorter events, 302.0 us)
Async XLA Ops:
  5.7 23.7 %collective-permute-start.4 = (bf16[128,1536]{1,0:T(8,128)(2,1)}, bf16[128,1536]{1,0:T(8,128)(2,1)}, u32[]{:S(2)}, u32[]{:S(2)}) collective-permute-start(bf16[128,1536]{1,0:T(8,128)(2,1)} %get-tuple-element.115), channel_id=1, source_target_pairs={{0,8},{4,12},{8,0},{12,4},{16,24},{20,28},{24,16},{28,20},{1,9},{5... | collective-permute-start | bytes 1179656 | tf_op jit(solution)/shard_map/ppermute | solution.py:51
  8.6 23.2 %collective-permute-start.5 = (bf16[128,1536]{1,0:T(8,128)(2,1)}, bf16[128,1536]{1,0:T(8,128)(2,1)}, u32[]{:S(2)}, u32[]{:S(2)}) collective-permute-start(bf16[128,1536]{1,0:T(8,128)(2,1)} %get-tuple-element.116), channel_id=1, source_target_pairs={{0,16},{4,20},{8,24},{12,28},{16,0},{20,4},{24,8},{28,12},{1,17},{... | collective-permute-start | bytes 1179656 | tf_op jit(solution)/shard_map/ppermute | solution.py:51
  10.1 24.7 %collective-permute-start.6 = (bf16[128,1536]{1,0:T(8,128)(2,1)}, bf16[128,1536]{1,0:T(8,128)(2,1)}, u32[]{:S(2)}, u32[]{:S(2)}) collective-permute-start(bf16[128,1536]{1,0:T(8,128)(2,1)} %get-tuple-element.117), channel_id=1, source_target_pairs={{0,24},{4,28},{8,16},{12,20},{16,8},{20,12},{24,0},{28,4},{1,25},{... | collective-permute-start | bytes 1179656 | tf_op jit(solution)/shard_map/ppermute | solution.py:51
  16.7 21.9 %collective-permute-start.7 = (bf16[128,2048]{1,0:T(8,128)(2,1)}, bf16[128,2048]{1,0:T(8,128)(2,1)}, u32[]{:S(2)}, u32[]{:S(2)}) collective-permute-start(bf16[128,2048]{1,0:T(8,128)(2,1)} %get-tuple-element.126), channel_id=1, source_target_pairs={{0,8},{4,12},{8,0},{12,4},{16,24},{20,28},{24,16},{28,20},{1,9},{5... | collective-permute-start | bytes 1572872 | tf_op jit(solution)/shard_map/ppermute | solution.py:51
  18.7 31.2 %collective-permute-start.8 = (bf16[128,2048]{1,0:T(8,128)(2,1)}, bf16[128,2048]{1,0:T(8,128)(2,1)}, u32[]{:S(2)}, u32[]{:S(2)}) collective-permute-start(bf16[128,2048]{1,0:T(8,128)(2,1)} %get-tuple-element.127), channel_id=1, source_target_pairs={{0,16},{4,20},{8,24},{12,28},{16,0},{20,4},{24,8},{28,12},{1,17},{... | collective-permute-start | bytes 1572872 | tf_op jit(solution)/shard_map/ppermute | solution.py:51
  51.5 22.6 %collective-permute-start.19 = (bf16[128,1536]{1,0:T(8,128)(2,1)}, bf16[128,1536]{1,0:T(8,128)(2,1)S(1)}, u32[]{:S(2)}, u32[]{:S(2)}) collective-permute-start(bf16[128,1536]{1,0:T(8,128)(2,1)} %collective-permute-done.6.refs_3_), channel_id=1, source_target_pairs={{0,1},{1,0},{2,3},{3,2},{4,5},{5,4},{6,7},{7,6},{8,9},{9,8},{10,11... | collective-permute-start | bytes 1179656 | tf_op jit(solution)/shard_map/ppermute | solution.py:51
  74.1 24.6 %collective-permute-start.15 = (bf16[128,2048]{1,0:T(8,128)(2,1)}, bf16[128,2048]{1,0:T(8,128)(2,1)S(1)}, u32[]{:S(2)}, u32[]{:S(2)}) collective-permute-start(bf16[128,2048]{1,0:T(8,128)(2,1)} %collective-permute-done.8.refs_2_), channel_id=1, source_target_pairs={{0,1},{1,0},{2,3},{3,2},{4,5},{5,4},{6,7},{7,6},{8,9},{9,8},{10,11... | collective-permute-start | bytes 1572872 | tf_op jit(solution)/shard_map/ppermute | solution.py:51
  78.0 30.3 %collective-permute-start.16 = (bf16[128,2048]{1,0:T(8,128)(2,1)S(1)}, bf16[128,2048]{1,0:T(8,128)(2,1)S(1)}, u32[]{:S(2)}, u32[]{:S(2)}) collective-permute-start(bf16[128,2048]{1,0:T(8,128)(2,1)S(1)} %collective-permute-done.9.refs_3_), channel_id=1, source_target_pairs={{0,1},{1,0},{2,3},{3,2},{4,5},{5,4},{6,7},{7,6},{8,9},{9,8},{10,11... | collective-permute-start | bytes 1572872 | tf_op jit(solution)/shard_map/ppermute | solution.py:51
  79.7 28.6 %collective-permute-start.12 = (bf16[96,2048]{1,0:T(8,128)(2,1)S(1)}, bf16[96,2048]{1,0:T(8,128)(2,1)S(1)}, u32[]{:S(2)}, u32[]{:S(2)}) collective-permute-start(bf16[96,2048]{1,0:T(8,128)(2,1)S(1)} %slice.514), channel_id=1, source_target_pairs={{0,16},{4,20},{8,24},{12,28},{16,0},{20,4},{24,8},{28,12},{1,17},{... | collective-permute-start | bytes 1179656 | tf_op jit(solution)/shard_map/ppermute | solution.py:51
  87.5 21.4 %collective-permute-start.13 = (bf16[96,2048]{1,0:T(8,128)(2,1)S(1)}, bf16[96,2048]{1,0:T(8,128)(2,1)S(1)}, u32[]{:S(2)}, u32[]{:S(2)}) collective-permute-start(bf16[96,2048]{1,0:T(8,128)(2,1)S(1)} %slice.515), channel_id=1, source_target_pairs={{0,8},{4,12},{8,0},{12,4},{16,24},{20,28},{24,16},{28,20},{1,9},{5... | collective-permute-start | bytes 1179656 | tf_op jit(solution)/shard_map/ppermute | solution.py:51
  89.0 23.2 %collective-permute-start.20 = (bf16[256,1536]{1,0:T(8,128)(2,1)S(1)}, bf16[256,1536]{1,0:T(8,128)(2,1)S(1)}, u32[]{:S(2)}, u32[]{:S(2)}) collective-permute-start(bf16[256,1536]{1,0:T(8,128)(2,1)S(1)} %copy-done.48), channel_id=1, source_target_pairs={{0,4},{4,0},{8,12},{12,8},{16,20},{20,16},{24,28},{28,24},{1,5},{5... | collective-permute-start | bytes 2359304 | tf_op jit(solution)/shard_map/ppermute | solution.py:51
  163.5 23.1 %collective-permute-start.36 = (bf16[96,2048]{1,0:T(8,128)(2,1)S(1)}, bf16[96,2048]{1,0:T(8,128)(2,1)S(1)}, u32[]{:S(2)}, u32[]{:S(2)}) collective-permute-start(bf16[96,2048]{1,0:T(8,128)(2,1)S(1)} %get-tuple-element.240), channel_id=1, source_target_pairs={{0,8},{4,12},{8,0},{12,4},{16,24},{20,28},{24,16},{28,20},{1,9},{5... | collective-permute-start | bytes 1179656 | tf_op jit(solution)/shard_map/ppermute | solution.py:51
  165.6 21.8 %collective-permute-start.35 = (bf16[96,2048]{1,0:T(8,128)(2,1)S(1)}, bf16[96,2048]{1,0:T(8,128)(2,1)S(1)}, u32[]{:S(2)}, u32[]{:S(2)}) collective-permute-start(bf16[96,2048]{1,0:T(8,128)(2,1)S(1)} %get-tuple-element.241), channel_id=1, source_target_pairs={{0,16},{4,20},{8,24},{12,28},{16,0},{20,4},{24,8},{28,12},{1,17},{... | collective-permute-start | bytes 1179656 | tf_op jit(solution)/shard_map/ppermute | solution.py:51
  186.8 23.3 %collective-permute-start.38 = (bf16[192,2048]{1,0:T(8,128)(2,1)S(1)}, bf16[192,2048]{1,0:T(8,128)(2,1)}, u32[]{:S(2)}, u32[]{:S(2)}) collective-permute-start(bf16[192,2048]{1,0:T(8,128)(2,1)S(1)} %pad_maximum_fusion.6), channel_id=1, source_target_pairs={{0,16},{4,20},{8,24},{12,28},{16,0},{20,4},{24,8},{28,12},{1,17},{... | collective-permute-start | bytes 2359304 | tf_op jit(solution)/shard_map/ppermute | solution.py:51
  187.6 23.7 %collective-permute-start.37 = (bf16[192,2048]{1,0:T(8,128)(2,1)S(1)}, bf16[192,2048]{1,0:T(8,128)(2,1)}, u32[]{:S(2)}, u32[]{:S(2)}) collective-permute-start(bf16[192,2048]{1,0:T(8,128)(2,1)S(1)} %pad_maximum_fusion.5), channel_id=1, source_target_pairs={{0,8},{4,12},{8,0},{12,4},{16,24},{20,28},{24,16},{28,20},{1,9},{5... | collective-permute-start | bytes 2359304 | tf_op jit(solution)/shard_map/ppermute | solution.py:51
  217.0 30.6 %collective-permute-start.43 = (bf16[256,2048]{1,0:T(8,128)(2,1)}, bf16[256,2048]{1,0:T(8,128)(2,1)}, u32[]{:S(2)}, u32[]{:S(2)}) collective-permute-start(bf16[256,2048]{1,0:T(8,128)(2,1)} %get-tuple-element.158.refs_0_), channel_id=1, source_target_pairs={{0,4},{4,0},{8,12},{12,8},{16,20},{20,16},{24,28},{28,24},{1,5},{5... | collective-permute-start | bytes 3145736 | tf_op jit(solution)/shard_map/ppermute | solution.py:51
  217.5 24.6 %collective-permute-start.46 = (bf16[128,2048]{1,0:T(8,128)(2,1)}, bf16[128,2048]{1,0:T(8,128)(2,1)}, u32[]{:S(2)}, u32[]{:S(2)}) collective-permute-start(bf16[128,2048]{1,0:T(8,128)(2,1)} %copy-done.52), channel_id=1, source_target_pairs={{0,4},{4,0},{8,12},{12,8},{16,20},{20,16},{24,28},{28,24},{1,5},{5... | collective-permute-start | bytes 1572872 | tf_op jit(solution)/shard_map/ppermute | solution.py:51
  219.2 25.5 %collective-permute-start.47 = (bf16[128,2048]{1,0:T(8,128)(2,1)}, bf16[128,2048]{1,0:T(8,128)(2,1)}, u32[]{:S(2)}, u32[]{:S(2)}) collective-permute-start(bf16[128,2048]{1,0:T(8,128)(2,1)} %copy-done.53), channel_id=1, source_target_pairs={{0,4},{4,0},{8,12},{12,8},{16,20},{20,16},{24,28},{28,24},{1,5},{5... | collective-permute-start | bytes 1572872 | tf_op jit(solution)/shard_map/ppermute | solution.py:51
  326.6 50.1 %collective-permute-start.62 = (bf16[192,2048]{1,0:T(8,128)(2,1)}, bf16[192,2048]{1,0:T(8,128)(2,1)}, u32[]{:S(2)}, u32[]{:S(2)}) collective-permute-start(bf16[192,2048]{1,0:T(8,128)(2,1)} %get-tuple-element.168), channel_id=1, source_target_pairs={{0,8},{4,12},{8,0},{12,4},{16,24},{20,28},{24,16},{28,20},{1,9},{5... | collective-permute-start | bytes 2359304 | tf_op jit(solution)/shard_map/ppermute | solution.py:51
  328.1 51.8 %collective-permute-start.55 = (bf16[192,2048]{1,0:T(8,128)(2,1)}, bf16[192,2048]{1,0:T(8,128)(2,1)}, u32[]{:S(2)}, u32[]{:S(2)}) collective-permute-start(bf16[192,2048]{1,0:T(8,128)(2,1)} %get-tuple-element.168), channel_id=1, source_target_pairs={{0,16},{4,20},{8,24},{12,28},{16,0},{20,4},{24,8},{28,12},{1,17},{... | collective-permute-start | bytes 2359304 | tf_op jit(solution)/shard_map/ppermute | solution.py:51
  427.5 41.2 %collective-permute-start.71 = (bf16[192,2304]{1,0:T(8,128)(2,1)S(1)}, bf16[192,2304]{1,0:T(8,128)(2,1)S(1)}, u32[]{:S(2)}, u32[]{:S(2)}) collective-permute-start(bf16[192,2304]{1,0:T(8,128)(2,1)S(1)} %pad_maximum_fusion.3), channel_id=1, source_target_pairs={{0,8},{4,12},{8,0},{12,4},{16,24},{20,28},{24,16},{28,20},{1,9},{5... | collective-permute-start | bytes 2654216 | tf_op jit(solution)/shard_map/ppermute | solution.py:51
  430.3 38.4 %collective-permute-start.73 = (bf16[192,2304]{1,0:T(8,128)(2,1)S(1)}, bf16[192,2304]{1,0:T(8,128)(2,1)S(1)}, u32[]{:S(2)}, u32[]{:S(2)}) collective-permute-start(bf16[192,2304]{1,0:T(8,128)(2,1)S(1)} %pad_maximum_fusion.4), channel_id=1, source_target_pairs={{0,16},{4,20},{8,24},{12,28},{16,0},{20,4},{24,8},{28,12},{1,17},{... | collective-permute-start | bytes 2654216 | tf_op jit(solution)/shard_map/ppermute | solution.py:51
  466.7 22.5 %collective-permute-start.74 = (bf16[192,2048]{1,0:T(8,128)(2,1)}, bf16[192,2048]{1,0:T(8,128)(2,1)}, u32[]{:S(2)}, u32[]{:S(2)}) collective-permute-start(bf16[192,2048]{1,0:T(8,128)(2,1)} %pad_maximum_fusion.9), channel_id=1, source_target_pairs={{0,8},{4,12},{8,0},{12,4},{16,24},{20,28},{24,16},{28,20},{1,9},{5... | collective-permute-start | bytes 2359304 | tf_op jit(solution)/shard_map/ppermute | solution.py:51
  489.2 23.6 %collective-permute-start.79 = (bf16[2,48,1792]{2,1,0:T(8,128)(2,1)S(1)}, bf16[2,48,1792]{2,1,0:T(8,128)(2,1)S(1)}, u32[]{:S(2)}, u32[]{:S(2)}) collective-permute-start(bf16[2,48,1792]{2,1,0:T(8,128)(2,1)S(1)} %pad_maximum_fusion.14), channel_id=1, source_target_pairs={{0,2},{1,3},{2,0},{3,1},{4,6},{5,7},{6,4},{7,5},{8,10},{9,11},{10,... | collective-permute-start | bytes 1032200 | tf_op jit(solution)/shard_map/ppermute | solution.py:51
  (178 other events, 2869.9 us)

commit v8 on v7

--- a/solution.py
+++ b/solution.py
@@ -107,10 +107,13 @@
     return [parts[0]] + [swap(b, "shard", bit) for b, bit in zip(blocks, bits)], blocks
 
 
-def gather_blocks(value, axis, bits):
+def gather_blocks(value, axis, bits, gates=None):
     current = value[None]
     for bit in bits:
-        current = jnp.concatenate([current, swap(current, axis, bit)], 0)
+        there = swap(current, axis, bit)
+        if gates and bit in gates:
+            there = after(there, *gates[bit])
+        current = jnp.concatenate([current, there], 0)
     return current
 
 
@@ -335,13 +338,13 @@
         in_specs=[pl.BlockSpec(memory_space=pltpu.VMEM)] * len(order),
         out_specs=[pl.BlockSpec(memory_space=pltpu.VMEM)] * len(dtypes),
         cost_estimate=pl.CostEstimate(
-            flops=20 * rows * wide, bytes_accessed=16 * rows * wide, transcendentals=0
+            flops=20 * rows * wide, bytes_accessed=200 * rows * wide, transcendentals=0
         ),
         name=name,
     )(*order)
 
 
-def sum_kernel(place, *refs, blocks):
+def sum_kernel(place, *refs, blocks, rows):
     gathered, outs = refs[:blocks], refs[blocks:]
     start = 0
     for out in outs:
@@ -349,18 +352,17 @@
         total, row = None, 0
         for ref in gathered:
             for g in range(ref.shape[0]):
-                rows = ref.shape[1]
-                term = t_mm(place[row : row + rows], ref[g, :, start : start + width])
+                term = t_mm(place[row : row + rows], ref[g, :rows, start : start + width])
                 total = term if total is None else total + term
                 row += rows
         out[...] = total
         start += width
 
 
-def sum_blocks(place, gathered, widths):
+def sum_blocks(place, gathered, rows, widths):
     total = sum(widths)
     return pl.pallas_call(
-        functools.partial(sum_kernel, blocks=len(gathered)),
+        functools.partial(sum_kernel, blocks=len(gathered), rows=rows),
         out_shape=[jax.ShapeDtypeStruct((place.shape[1], w), F32) for w in widths],
         in_specs=[pl.BlockSpec(memory_space=pltpu.VMEM)] * (1 + len(gathered)),
         out_specs=[pl.BlockSpec(memory_space=pltpu.VMEM)] * len(widths),
@@ -549,9 +551,9 @@
     chosen = adapter_pick[0]
     starts = piece_start[0]
 
-    def keep_own(value, terms=1):
+    def keep_own(value):
         of_row = lax.broadcasted_iota(jnp.int32, value.shape, 0) // rows % count
-        of_col = lax.broadcasted_iota(jnp.int32, value.shape, 1) // (terms * rank)
+        of_col = lax.broadcasted_iota(jnp.int32, value.shape, 1) // rank % count
         return jnp.where(of_row == of_col, value, 0.0).astype(BF16)
 
     chip = me // 2
@@ -596,11 +598,10 @@
     w_qkv_mine, w_qkv_other = place_weights(
         at, both_cores(turned + halves_over_rep(turned[1:])), chips, 3 * span, False
     )
-    far_up = halves_over_rep(near_up[1:])
     w_out_late, w_down_late = after((w_out, w_down), normed)
     w_out_chip = jnp.concatenate([w_out_late, w_out_other], 0)
     w_down_chip = jnp.concatenate([w_down_late, w_down_other], 0)
-    hidden_one = after(hidden_one, w_out_chip, w_down_chip, *far_up)
+    hidden_one = after(hidden_one, w_out_chip, w_down_chip)
     cot_mine = cotangent[0].reshape(block, wide)
     near = after(jnp.concatenate([mine[None], near_one], 0), *one_first)
     for bit in bits[1:]:
@@ -614,15 +615,15 @@
     where = (positions[:, None], positions[None, :], labels[:, :, None], labels[:, None, :])
 
     whole = place_columns(me_arr, stacked, subsets(order)).reshape(6, count, rank, wide)
-    in_qkv = jnp.swapaxes(whole[:3], 0, 1).reshape(count * 3 * rank, wide)
+    in_qkv = whole[:3].reshape(3 * count * rank, wide)
     in_exp, out_att, out_red = (whole[3 + i].reshape(count * rank, wide) for i in range(3))
 
     def unpack(table, i):
         return table[:, edges[i] : edges[i + 1]]
 
     def out_qkv_of(table):
-        stacked = jnp.stack([unpack(table, t).reshape(count, rank, span) for t in range(3)], 1)
-        spread = stacked[:, :, :, None, :] * jnp.eye(3, dtype=BF16)[None, :, None, :, None]
+        stacked = jnp.stack([unpack(table, t) for t in range(3)])
+        spread = stacked[:, :, None, :] * jnp.eye(3, dtype=BF16)[:, None, :, None]
         return spread.reshape(count * 3 * rank, 3 * span)
 
     out_qkv_mine, out_qkv_other = out_qkv_of(packed), out_qkv_of(packed_other)
@@ -659,8 +660,7 @@
                 products = [(after(v, parts[2 * i]), w, main) for v, w, main in products]
         return parts
 
-    hidden_one = after(hidden_one, where, out_qkv_mine, out_qkv_other, in_att, out_exp, in_red)
-    low_qkv = keep_own(mm_t(hidden_one, in_qkv), 3)
+    low_qkv = keep_own(mm_t(hidden_one, in_qkv))
     qkv_away = (
         mm(hidden_one, w_qkv_other) + mm(low_qkv, out_qkv_other) + b_qkv_of(me ^ 1)
     ).astype(BF16)
@@ -669,12 +669,10 @@
         (mm(hidden_one, w_qkv_mine) + mm(low_qkv, out_qkv_mine) + b_qkv_of(me)).astype(BF16)
     )
     att_own, att_away, lse = attend(where, qkv_own, qkv_other, heads)
+    cot_pieces, _, _ = gather_rows(after(cot_mine, att_own), bits, apart=True)
     attended = jnp.concatenate([flat(att_own), swap(flat(att_away), "shard", 1)], 1)
     low_att = keep_own(mm_t(attended, in_att))
     parts = block_products([(attended, w_out_chip, mm)], low_att, out_att)
-    cot_pieces, _, _ = gather_rows(
-        after(cot_mine, one_last), bits, (parts[2 * (chips - 1)],), apart=True
-    )
     terms, relayed = scatter_rows(parts, bits)
     cot = jnp.concatenate(after(cot_pieces, *relayed), 0)
     glow_red = keep_own(mm_t(cot, out_red))
@@ -683,6 +681,7 @@
     residual, hidden_block = row_call(
         norm_kernel, [rows_in, vectors] + terms, block, wide, [F32, BF16], "norm"
     )
+    far_up = halves_over_rep(after(tuple(near_up[1:]), *relayed))
     pieces_up = after((*near_up, *far_up), hidden_block)
     hidden_two, _, _ = gather_rows(hidden_block, bits)
 
@@ -706,16 +705,6 @@
     )
     grad_branch, _, branch_last = gather_rows(grad_block, bits)
 
-    rep_bits = bits_of(lax.axis_size("rep"))
-    mark = (after(chosen, grad_block)[:, None] == jnp.arange(ADAPTERS, dtype=jnp.int32)[None, :]).astype(BF16)
-    marks = gather_blocks(jnp.pad(mark, ((0, 16 - count), (0, 128 - ADAPTERS))), "rep", rep_bits)
-    groups = marks.shape[0]
-    marks = marks[:, :count, :ADAPTERS].reshape(groups * count, 1, ADAPTERS, 1)
-    place = (marks * jnp.eye(rank, dtype=BF16)[None, :, None, :]).reshape(
-        groups * count * rank, ADAPTERS * rank
-    )
-
-
     act_late = after(act, grad_block)
     low_red = keep_own(mm_t(act_late, in_red))
     down_parts = block_products([(act_late, w_down_chip, mm)], low_red, out_red)
@@ -726,7 +715,7 @@
     grad_own, grad_away = attend_back(where, qkv_own, qkv_other, lse, ga_own, ga_other, heads)
     grad_own = flat(grad_own)
     grad_other = swap(flat(grad_away), "shard", 1)
-    glow_qkv = keep_own(mm_t(grad_own, out_qkv_mine) + mm_t(grad_other, out_qkv_other), 3)
+    glow_qkv = keep_own(mm_t(grad_own, out_qkv_mine) + mm_t(grad_other, out_qkv_other))
     def sum_cores(own, away):
         return own + swap(away.astype(BF16), "shard", 1).astype(F32)
 
@@ -757,33 +746,47 @@
             current = current + (there if i else after(there, *gate)).astype(F32)
         return current[0], away
 
-    def over_groups(terms, hold=()):
-        widths = [t.shape[1] for t in terms]
-        data = jnp.concatenate([t.astype(BF16) for t in terms], 1)
-        gathered, current = [data[None]], data[None]
+    rep_bits = bits_of(lax.axis_size("rep"))
+
+    def over_rep(terms, extra=(), gates=None):
+        current = jnp.concatenate([t.astype(BF16) for t in terms], 1)
+        current = jnp.concatenate([current, *extra], 0)[None]
+        gathered = [current]
         for bit in rep_bits:
-            if hold and bit == rep_bits[-1]:
-                current = after(current, *hold)
             there = swap(current, "rep", bit)
+            if gates and bit in gates:
+                there = after(there, *gates[bit])
             gathered.append(there)
             if bit != rep_bits[-1]:
                 current = jnp.concatenate([current, there], 0)
-        return [out.reshape(ADAPTERS, rank, -1) for out in sum_blocks(place, gathered, widths)]
+        return gathered
+
+    def over_groups(terms, place, gathered):
+        widths = [t.shape[1] for t in terms]
+        outs = sum_blocks(place, gathered, count * rank, widths)
+        return [out.reshape(ADAPTERS, rank, -1) for out in outs]
 
     def halves(value):
         middle = value.shape[1] // 2
         return value[:, :middle], value[:, middle:]
 
     glow_late, low_late = after((glow_exp, low_exp), grad_block)
-    act_mid, grad_mid, low_mid, glow_mid = after((act, grad_pre, low_exp, glow_red), grad_block)
+    act_mid, grad_mid, low_mid, glow_mid = after((act, grad_pre, low_exp, glow_red), *grad_sent)
     red_own, red_away = halves(t_mm(glow_mid, act_mid))
     exp_own, exp_away = halves(t_mm(low_mid, grad_mid))
     local = sum_cores(
         jnp.concatenate([red_own, exp_own], 1), jnp.concatenate([red_away, exp_away], 1)
     )
-    s_in_red, s_out_exp = over_groups(
-        [local[:, :ff_part], local[:, ff_part:]]
-    )
+    mark = (chosen[:, None] == jnp.arange(ADAPTERS, dtype=jnp.int32)[None, :]).astype(BF16)
+    mark = jnp.pad(mark, ((0, 16 - count), (0, local.shape[1] - ADAPTERS)))
+    sums = [local[:, :ff_part], local[:, ff_part:]]
+    gathered = over_rep(sums, [mark], {rep_bits[-1]: (grad_away,)})
+    marks = jnp.concatenate(
+        [g[:, count * rank : count * rank + count, :ADAPTERS] for g in gathered], 0
+    )
+    place = marks.reshape(-1, 1, ADAPTERS, 1) * jnp.eye(rank, dtype=BF16)[None, :, None, :]
+    place = place.reshape(-1, ADAPTERS * rank)
+    s_in_red, s_out_exp = over_groups(sums, place, gathered)
 
     near_first = core_columns(
         jnp.concatenate([t_mm(glow_late, hidden_two), t_mm(low_red, cot)], 0)
@@ -800,9 +803,9 @@
     in_terms = jnp.concatenate([t_mm(glow_last, hidden_one), t_mm(low_att, grad_branch)], 0)
 
     def own_terms(full):
-        full = full.reshape(count, 3, rank, 3, span)
+        height = count * rank
         return jnp.concatenate(
-            [full[:, t, :, t].reshape(count * rank, span) for t in range(3)], 1
+            [full[t * height : (t + 1) * height, t * span : (t + 1) * span] for t in range(3)], 1
         )
 
     near_second = core_columns(in_terms)
@@ -817,7 +820,6 @@
 
     terms, relayed = scatter_rows(parts, bits, between=hop)
     second = aside["second"]
-    riders[0] = after(riders[0], s_in_red, s_out_exp)
     down, _ = scatter_rows(riders, bits, (grad_away,))
     down[0] = after(down[0], *relayed)
     first = sum(t[:tall, wide:].astype(F32) for t in down).reshape(2, count * rank, slice_wide)
@@ -834,14 +836,13 @@
         "norm_back",
     )
     out_att_sum = second[count * 3 * rank :]
-    second = second[: count * 3 * rank].reshape(count, 3, rank, slice_wide)
-    s_in_att, s_in_exp, s_out_red = over_groups([att_side, first[0], first[1]])
-    late = over_groups(
-        [second[:, t].reshape(count * rank, slice_wide) for t in range(3)]
-        + [outer[:, t * span : (t + 1) * span] for t in range(3)]
-        + [out_att_sum],
-        terms[1:],
-    )
+    second = second[: count * 3 * rank].reshape(3, count * rank, slice_wide)
+    sums = [att_side, first[0], first[1]]
+    ends = {rep_bits[-1]: (input_rows,)}
+    s_in_att, s_in_exp, s_out_red = over_groups(sums, place, over_rep(sums, (), ends))
+    sums = [second[t] for t in range(3)]
+    sums += [outer[:, t * span : (t + 1) * span] for t in range(3)] + [out_att_sum]
+    late = over_groups(sums, place, over_rep(sums, (), ends))
     s_out_att = late.pop()
     shape = (1, count, rows, wide)
     return (

time: 523 us -> 473 us (0.904)
  local copies, waits for them, and re-layouts: 71.4 us -> 46.8 us
  waiting for transfers between devices: 153 us -> 139 us
  other arithmetic: 30.8 us -> 24 us
    ppermute x83 -> x81, waiting for transfers between devices: 153 us -> 139 us  [swap(): return lax.ppermute(value, axis, [(i, i ^ mask) for i in range(size)])]
    unnamed x263 -> x297, local copies, waits for them, and re-layouts: 37.8 us -> 24.8 us
    slice x8, local copies, waits for them, and re-layouts: 7.19 us -> 1.74 us  [gather_rows(): upper[bit], lower[bit] = (there[:half], there[half:])]
    ppermute x83 -> x81, starting transfers between devices: 69.9 us -> 69.8 us  [swap(): return lax.ppermute(value, axis, [(i, i ^ mask) for i in range(size)])]
  transfers between devices with their start and end apart: 83 -> 81, of which waited for: 28 -> 32; matrix products, arithmetic and copies ran while one was open for 31% -> 29% of each run, Pallas kernels for 8% -> 11%
where the time goes in v8:
time: 473 us; the launch traced here: 467 us
  waiting for transfers between devices  139 us (29%)
  matrix products  117 us (25%)
  starting transfers between devices  69.8 us (15%)
  Pallas kernels  65.2 us (14%)
  local copies, waits for them, and re-layouts  46.8 us (10%)
  other arithmetic  24 us (5%)
  between operations  5.52 us (1%)
    ppermute x81, waiting for transfers between devices, swap(): return lax.ppermute(value, axis, [(i, i ^ mask) for i in range(size)])  139 us
    ppermute x81, starting transfers between devices, swap(): return lax.ppermute(value, axis, [(i, i ^ mask) for i in range(size)])  69.8 us
    dot_general x32, matrix products, mm(): lax.dot_general(a, b, (((1,), (0,)), ((), ())), preferred_element_type=F32)  56 us
    dot_general x23, matrix products, mm_t(): lax.dot_general(a, b, (((1,), (1,)), ((), ())), preferred_element_type=F32)  52.9 us
    unnamed x297, local copies, waits for them, and re-layouts  24.8 us
    pallas_call x2, Pallas kernels, place_weights(): pl.pallas_call(functools.partial(place_kernel, count=count, width=width,...  14.1 us
    pallas_call x3, Pallas kernels, row_call(): pl.pallas_call(kernel, out_shape=[jax.ShapeDtypeStruct((rows, wide), d) f...  13.2 us
    pallas_call x1, Pallas kernels, attend_back(): pl.pallas_call(functools.partial(attend_back_kernel, heads=heads, factor=...  9.69 us
  transfers between devices with their start and end apart: 81, of which 32 were waited for; matrix products, arithmetic and copies ran while one was open for 29% of the time, Pallas kernels for 11%

profile of v8, /device:TPU:0, one launch (start us, length us, event | category | flops | bytes accessed | tf_op | source)
XLA Modules:
  0.0 467.0 jit_solution(1550229081924394866)
XLA Ops:
  40.7 9.2 %collective-permute-done.8.refs_2_ = bf16[128,2048]{1,0:T(8,128)(2,1)} collective-permute-done((bf16[128,2048]{1,0:T(8,128)(2,1)}, bf16[128,2048]{1,0:T(8,128)(2,1)}, u32[]{:S(2)}, u32[]{:S(2)}) %collective-permute-start.8) | collective-permute-done | bytes 524320 | tf_op jit(solution)/shard_map/ppermute | solution.py:51
  58.2 13.0 %collective-permute-done.10 = bf16[192,2048]{1,0:T(8,128)(2,1)S(1)} collective-permute-done((bf16[192,2048]{1,0:T(8,128)(2,1)S(1)}, bf16[192,2048]{1,0:T(8,128)(2,1)S(1)}, u32[]{:S(2)}, u32[]{:S(2)}) %collective-permute-start.10) | collective-permute-done | bytes 786464 | tf_op jit(solution)/shard_map/ppermute | solution.py:51
  79.8 5.1 %collective-permute-done.24 = bf16[2,288,256]{2,1,0:T(8,128)(2,1)S(1)} collective-permute-done((bf16[2,288,256]{2,1,0:T(8,128)(2,1)S(1)}, bf16[2,288,256]{2,1,0:T(8,128)(2,1)S(1)}, u32[]{:S(2)}, u32[]{:S(2)}) %collective-permute-start.24) | collective-permute-done | bytes 294944 | tf_op jit(solution)/shard_map/ppermute | solution.py:51
  86.5 6.3 %collective-permute-done.12 = bf16[96,2048]{1,0:T(8,128)(2,1)S(1)} collective-permute-done((bf16[96,2048]{1,0:T(8,128)(2,1)S(1)}, bf16[96,2048]{1,0:T(8,128)(2,1)S(1)}, u32[]{:S(2)}, u32[]{:S(2)}) %collective-permute-start.12) | collective-permute-done | bytes 393248 | tf_op jit(solution)/shard_map/ppermute | solution.py:51
  96.2 6.5 %place_weights.2 = (bf16[2048,768]{1,0:T(8,128)(2,1)}, bf16[2048,768]{1,0:T(8,128)(2,1)}) custom-call(s32[2]{0:T(128)} %pad_add_fusion.1.at_ref, bf16[256,1536]{1,0:T(8,128)(2,1)} %get-tuple-element.133.refs_0_, bf16[128,1536]{1,0:T(8,128)(2,1)} %collective-permute-done.4.refs_1_, bf16[128,1536]{1,0:T(8,128)(2,1)} %collective-permute-done.5.refs_2_, ...), custom_call_target="tpu_custom_call" | custom-call | bytes 12582912 | tf_op jit(solution)/shard_map/place_weights/pallas_call | solution.py:208
  120.7 5.6 %add_convert_fusion.2 = bf16[768,768]{1,0:T(8,128)(2,1)} fusion(f32[768,768]{1,0:T(8,128)S(1)} %fusion.209, bf16[768,2048]{1,0:T(8,128)(2,1)} %copy-done.11, bf16[2048,768]{1,0:T(8,128)(2,1)S(1)} %copy-done.1, f32[768]{0:T(1024)S(1)} %get-tuple-element.279), kind=kOutput, calls=%fused_computation.65 | convolution fusion | flops 2417688576 | bytes 9833472 | tf_op jit(solution)/shard_map/dot_general | solution.py:38
  126.3 7.6 %attend.1 = (bf16[4,3,64,256]{3,2,1,0:T(8,128)(2,1)}, bf16[4,3,64,256]{3,2,1,0:T(8,128)(2,1)}, f32[3,512,2]{2,1,0:T(8,128)}) custom-call(s32[512,1]{1,0:T(8,128)} %copy.49.pq, s32[1,512]{1,0:T(1,128)} %bitcast.236, s32[3,512,1]{2,1,0:T(8,128)} %copy.50.lq, s32[3,1,512]{2,1,0:T(1,128)} %broadcast_in_dim.86.lk, bf16[4,3,64,768]{3,2,1,0:T(8,128)(2,1)} %bitcast.221, ...), custom_call_target="tpu_custom_call" | custom-call | flops 805306368 | bytes 3145728 | tf_op jit(solution)/shard_map/attend/pallas_call | solution.py:430
  158.4 6.2 %collective-permute-done.33 = bf16[96,2048]{1,0:T(8,128)(2,1)S(1)} collective-permute-done((bf16[96,2048]{1,0:T(8,128)(2,1)S(1)}, bf16[96,2048]{1,0:T(8,128)(2,1)S(1)}, u32[]{:S(2)}, u32[]{:S(2)}) %collective-permute-start.33) | collective-permute-done | bytes 393248 | tf_op jit(solution)/shard_map/ppermute | solution.py:51
  168.7 4.9 %collective-permute-done.30 = bf16[96,2048]{1,0:T(8,128)(2,1)S(1)} collective-permute-done((bf16[96,2048]{1,0:T(8,128)(2,1)S(1)}, bf16[96,2048]{1,0:T(8,128)(2,1)S(1)}, u32[]{:S(2)}, u32[]{:S(2)}) %collective-permute-start.30) | collective-permute-done | bytes 393248 | tf_op jit(solution)/shard_map/ppermute | solution.py:51
  178.7 10.3 %add_convert_fusion = bf16[768,2048]{1,0:T(8,128)(2,1)} fusion(f32[768,2048]{1,0:T(8,128)S(1)} %fusion.121, bf16[768,2048]{1,0:T(8,128)(2,1)S(1)} %constant_dynamic-update-slice_fusion.9, bf16[2048,2048]{1,0:T(8,128)(2,1)} %copy-done.27), kind=kOutput, calls=%fused_computation.10 | convolution fusion | flops 6445596672 | bytes 20971520 | tf_op jit(solution)/shard_map/dot_general | solution.py:42
  193.5 8.1 %collective-permute-done.42.refs_6_ = bf16[128,2048]{1,0:T(8,128)(2,1)} collective-permute-done((bf16[128,2048]{1,0:T(8,128)(2,1)}, bf16[128,2048]{1,0:T(8,128)(2,1)}, u32[]{:S(2)}, u32[]{:S(2)}) %collective-permute-start.42) | collective-permute-done | bytes 524320 | tf_op jit(solution)/shard_map/ppermute | solution.py:51
  207.0 15.3 %collective-permute-done.36 = bf16[192,2048]{1,0:T(8,128)(2,1)S(1)} collective-permute-done((bf16[192,2048]{1,0:T(8,128)(2,1)}, bf16[192,2048]{1,0:T(8,128)(2,1)S(1)}, u32[]{:S(2)}, u32[]{:S(2)}) %collective-permute-start.36) | collective-permute-done | bytes 786464 | tf_op jit(solution)/shard_map/ppermute | solution.py:51
  232.3 7.6 %place_weights.3 = bf16[2048,2048]{1,0:T(8,128)(2,1)} custom-call(s32[2]{0:T(128)} %pad_add_fusion.1.at_ref, bf16[256,2048]{1,0:T(8,128)(2,1)} %get-tuple-element.158.refs_0_, bf16[128,2048]{1,0:T(8,128)(2,1)} %collective-permute-done.7.refs_1_, bf16[128,2048]{1,0:T(8,128)(2,1)} %collective-permute-done.8.refs_2_, ...), custom_call_target="tpu_custom_call" | custom-call | bytes 16777216 | tf_op jit(solution)/shard_map/place_weights/pallas_call | solution.py:208
  249.5 11.5 %multiply_convert_fusion = (bf16[768,2048]{1,0:T(8,128)(2,1)S(1)}, bf16[768,2048]{1,0:T(8,128)(2,1)S(1)}) fusion(bf16[768,2048]{1,0:T(8,128)(2,1)} %add_convert_fusion, f32[2048]{0:T(1024)} %maximum_convert_fusion, f32[768,2048]{1,0:T(8,128)S(1)} %fusion.120, bf16[768,2048]{1,0:T(8,128)(2,1)} %constant_dynamic-update-slice_fusion.14, ...), kind=kOutput, calls=%fused_computation.7 | convolution fusion | flops 6466043904 | bytes 27271168 | tf_op jit(solution)/shard_map/dot_general | solution.py:38
  275.3 7.4 %collective-permute-done.52 = bf16[96,2048]{1,0:T(8,128)(2,1)S(1)} collective-permute-done((bf16[96,2048]{1,0:T(8,128)(2,1)S(1)}, bf16[96,2048]{1,0:T(8,128)(2,1)S(1)}, u32[]{:S(2)}, u32[]{:S(2)}) %collective-permute-start.52) | collective-permute-done | bytes 393248 | tf_op jit(solution)/shard_map/ppermute | solution.py:51
  294.5 4.8 %collective-permute-done.72.refs_1_ = bf16[1,64,2048]{2,1,0:T(8,128)(2,1)S(1)} collective-permute-done((bf16[1,64,2048]{2,1,0:T(8,128)(2,1)S(1)}, bf16[1,64,2048]{2,1,0:T(8,128)(2,1)S(1)}, u32[]{:S(2)}, u32[]{:S(2)}) %collective-permute-start.72) | collective-permute-done | bytes 262176 | tf_op jit(solution)/shard_map/ppermute | solution.py:51
  303.6 5.3 %collective-permute-done.53.refs_2_ = bf16[192,2048]{1,0:T(8,128)(2,1)} collective-permute-done((bf16[192,2048]{1,0:T(8,128)(2,1)S(1)}, bf16[192,2048]{1,0:T(8,128)(2,1)}, u32[]{:S(2)}, u32[]{:S(2)}) %collective-permute-start.53) | collective-permute-done | bytes 786464 | tf_op jit(solution)/shard_map/ppermute | solution.py:51
  310.1 5.0 %norm_back.2 = (f32[192,2048]{1,0:T(8,128)}, bf16[192,2048]{1,0:T(8,128)(2,1)}) custom-call(f32[192,2048]{1,0:T(8,128)} %get-tuple-element.151.values, f32[4,2048]{1,0:T(4,128)} %convert_element_type.313.vectors, bf16[192,2048]{1,0:T(8,128)(2,1)} %bitcast.210, bf16[192,2048]{1,0:T(8,128)(2,1)} %fusion.15.refs_0_, ...), custom_call_target="tpu_custom_call" | custom-call | flops 7864320 | bytes 78643200 | tf_op jit(solution)/shard_map/norm_back/pallas_call | solution.py:335
  316.7 5.4 %fusion.53 = f32[192,2048]{1,0:T(8,128)S(1)} fusion(bf16[2048,2048]{1,0:T(8,128)(2,1)} %copy-done.27, bf16[768,2048]{1,0:T(8,128)(2,1)} %copy-done.24), kind=kOutput, calls=%fused_computation.144 | convolution fusion | flops 1610612736 | bytes 10747904 | tf_op jit(solution)/shard_map/dot_general | solution.py:38
  325.2 5.3 %fusion.51 = f32[192,2048]{1,0:T(8,128)S(1)} fusion(bf16[2048,2048]{1,0:T(8,128)(2,1)} %copy-done.27, bf16[768,2048]{1,0:T(8,128)(2,1)S(1)} %copy-done.25), kind=kOutput, calls=%fused_computation.142 | convolution fusion | flops 1610612736 | bytes 10747904 | tf_op jit(solution)/shard_map/dot_general | solution.py:38
  343.4 8.7 %collective-permute-done.58 = bf16[96,2048]{1,0:T(8,128)(2,1)S(1)} collective-permute-done((bf16[96,2048]{1,0:T(8,128)(2,1)S(1)}, bf16[96,2048]{1,0:T(8,128)(2,1)S(1)}, u32[]{:S(2)}, u32[]{:S(2)}) %collective-permute-start.58) | collective-permute-done | bytes 393248 | tf_op jit(solution)/shard_map/ppermute | solution.py:51
  365.6 9.7 %attend_back.1 = (bf16[4,3,64,768]{3,2,1,0:T(8,128)(2,1)}, bf16[4,3,64,768]{3,2,1,0:T(8,128)(2,1)}) custom-call(s32[512,1]{1,0:T(8,128)} %copy.49.pq, s32[1,512]{1,0:T(1,128)} %bitcast.237, s32[3,512,1]{2,1,0:T(8,128)} %copy.50.lq, s32[3,1,512]{2,1,0:T(1,128)} %broadcast_in_dim.86.lk, bf16[4,3,64,768]{3,2,1,0:T(8,128)(2,1)} %bitcast.222, ...), custom_call_target="tpu_custom_call" | custom-call | flops 2013265920 | bytes 5505024 | tf_op jit(solution)/shard_map/attend_back/pallas_call | solution.py:487
  417.1 5.4 %collective-permute-done.61 = bf16[96,2048]{1,0:T(8,128)(2,1)S(1)} collective-permute-done((bf16[96,2048]{1,0:T(8,128)(2,1)S(1)}, bf16[96,2048]{1,0:T(8,128)(2,1)S(1)}, u32[]{:S(2)}, u32[]{:S(2)}) %collective-permute-start.61) | collective-permute-done | bytes 393248 | tf_op jit(solution)/shard_map/ppermute | solution.py:51
  442.2 12.6 %collective-permute-done.69.refs_1_ = bf16[192,2048]{1,0:T(8,128)(2,1)S(1)} collective-permute-done((bf16[192,2048]{1,0:T(8,128)(2,1)S(1)}, bf16[192,2048]{1,0:T(8,128)(2,1)S(1)}, u32[]{:S(2)}, u32[]{:S(2)}) %collective-permute-start.69) | collective-permute-done | bytes 786464 | tf_op jit(solution)/shard_map/ppermute | solution.py:51
  (651 shorter events, 274.7 us)
Async XLA Ops:
  5.6 24.8 %collective-permute-start.4 = (bf16[128,1536]{1,0:T(8,128)(2,1)}, bf16[128,1536]{1,0:T(8,128)(2,1)}, u32[]{:S(2)}, u32[]{:S(2)}) collective-permute-start(bf16[128,1536]{1,0:T(8,128)(2,1)} %get-tuple-element.115), channel_id=1, source_target_pairs={{0,8},{4,12},{8,0},{12,4},{16,24},{20,28},{24,16},{28,20},{1,9},{5... | collective-permute-start | bytes 1179656 | tf_op jit(solution)/shard_map/ppermute | solution.py:51
  8.6 22.5 %collective-permute-start.5 = (bf16[128,1536]{1,0:T(8,128)(2,1)}, bf16[128,1536]{1,0:T(8,128)(2,1)}, u32[]{:S(2)}, u32[]{:S(2)}) collective-permute-start(bf16[128,1536]{1,0:T(8,128)(2,1)} %get-tuple-element.116), channel_id=1, source_target_pairs={{0,16},{4,20},{8,24},{12,28},{16,0},{20,4},{24,8},{28,12},{1,17},{... | collective-permute-start | bytes 1179656 | tf_op jit(solution)/shard_map/ppermute | solution.py:51
  15.6 23.0 %collective-permute-start.7 = (bf16[128,2048]{1,0:T(8,128)(2,1)}, bf16[128,2048]{1,0:T(8,128)(2,1)}, u32[]{:S(2)}, u32[]{:S(2)}) collective-permute-start(bf16[128,2048]{1,0:T(8,128)(2,1)} %get-tuple-element.126), channel_id=1, source_target_pairs={{0,8},{4,12},{8,0},{12,4},{16,24},{20,28},{24,16},{28,20},{1,9},{5... | collective-permute-start | bytes 1572872 | tf_op jit(solution)/shard_map/ppermute | solution.py:51
  17.6 32.3 %collective-permute-start.8 = (bf16[128,2048]{1,0:T(8,128)(2,1)}, bf16[128,2048]{1,0:T(8,128)(2,1)}, u32[]{:S(2)}, u32[]{:S(2)}) collective-permute-start(bf16[128,2048]{1,0:T(8,128)(2,1)} %get-tuple-element.127), channel_id=1, source_target_pairs={{0,16},{4,20},{8,24},{12,28},{16,0},{20,4},{24,8},{28,12},{1,17},{... | collective-permute-start | bytes 1572872 | tf_op jit(solution)/shard_map/ppermute | solution.py:51
  31.1 21.8 %collective-permute-start.2 = (bf16[48,3072]{1,0:T(8,128)(2,1)S(1)}, bf16[48,3072]{1,0:T(8,128)(2,1)S(1)}, u32[]{:S(2)}, u32[]{:S(2)}) collective-permute-start(bf16[48,3072]{1,0:T(8,128)(2,1)S(1)} %copy-done.75), channel_id=1, source_target_pairs={{0,4},{4,0},{8,12},{12,8},{16,20},{20,16},{24,28},{28,24},{1,5},{5... | collective-permute-start | bytes 884744 | tf_op jit(solution)/shard_map/ppermute | solution.py:51
  31.1 21.8 %collective-permute-start.3 = (bf16[1,288,256]{2,1,0:T(8,128)(2,1)S(1)}, bf16[1,288,256]{2,1,0:T(8,128)(2,1)S(1)}, u32[]{:S(2)}, u32[]{:S(2)}) collective-permute-start(bf16[1,288,256]{2,1,0:T(8,128)(2,1)S(1)} %bitcast.233), channel_id=1, source_target_pairs={{0,8},{4,12},{8,0},{12,4},{16,24},{20,28},{24,16},{28,20},{1,9},{5... | collective-permute-start | bytes 442376 | tf_op jit(solution)/shard_map/ppermute | solution.py:51
  38.6 36.5 %collective-permute-start.14 = (bf16[128,1536]{1,0:T(8,128)(2,1)}, bf16[128,1536]{1,0:T(8,128)(2,1)S(1)}, u32[]{:S(2)}, u32[]{:S(2)}) collective-permute-start(bf16[128,1536]{1,0:T(8,128)(2,1)} %collective-permute-done.4.refs_1_), channel_id=1, source_target_pairs={{0,1},{1,0},{2,3},{3,2},{4,5},{5,4},{6,7},{7,6},{8,9},{9,8},{10,11... | collective-permute-start | bytes 1179656 | tf_op jit(solution)/shard_map/ppermute | solution.py:51
  49.9 28.5 %collective-permute-start.15 = (bf16[128,1536]{1,0:T(8,128)(2,1)}, bf16[128,1536]{1,0:T(8,128)(2,1)S(1)}, u32[]{:S(2)}, u32[]{:S(2)}) collective-permute-start(bf16[128,1536]{1,0:T(8,128)(2,1)} %collective-permute-done.5.refs_2_), channel_id=1, source_target_pairs={{0,1},{1,0},{2,3},{3,2},{4,5},{5,4},{6,7},{7,6},{8,9},{9,8},{10,11... | collective-permute-start | bytes 1179656 | tf_op jit(solution)/shard_map/ppermute | solution.py:51
  51.5 27.2 %collective-permute-start.16 = (bf16[128,1536]{1,0:T(8,128)(2,1)}, bf16[128,1536]{1,0:T(8,128)(2,1)S(1)}, u32[]{:S(2)}, u32[]{:S(2)}) collective-permute-start(bf16[128,1536]{1,0:T(8,128)(2,1)} %collective-permute-done.6.refs_3_), channel_id=1, source_target_pairs={{0,1},{1,0},{2,3},{3,2},{4,5},{5,4},{6,7},{7,6},{8,9},{9,8},{10,11... | collective-permute-start | bytes 1179656 | tf_op jit(solution)/shard_map/ppermute | solution.py:51
  164.8 24.6 %collective-permute-start.35 = (bf16[192,2048]{1,0:T(8,128)(2,1)S(1)}, bf16[192,2048]{1,0:T(8,128)(2,1)}, u32[]{:S(2)}, u32[]{:S(2)}) collective-permute-start(bf16[192,2048]{1,0:T(8,128)(2,1)S(1)} %pad_maximum_fusion.6), channel_id=1, source_target_pairs={{0,16},{4,20},{8,24},{12,28},{16,0},{20,4},{24,8},{28,12},{1,17},{... | collective-permute-start | bytes 2359304 | tf_op jit(solution)/shard_map/ppermute | solution.py:51
  166.5 22.9 %collective-permute-start.34 = (bf16[192,2048]{1,0:T(8,128)(2,1)S(1)}, bf16[192,2048]{1,0:T(8,128)(2,1)}, u32[]{:S(2)}, u32[]{:S(2)}) collective-permute-start(bf16[192,2048]{1,0:T(8,128)(2,1)S(1)} %pad_maximum_fusion.5), channel_id=1, source_target_pairs={{0,8},{4,12},{8,0},{12,4},{16,24},{20,28},{24,16},{28,20},{1,9},{5... | collective-permute-start | bytes 2359304 | tf_op jit(solution)/shard_map/ppermute | solution.py:51
  167.1 26.0 %collective-permute-start.40 = (bf16[128,2048]{1,0:T(8,128)(2,1)}, bf16[128,2048]{1,0:T(8,128)(2,1)}, u32[]{:S(2)}, u32[]{:S(2)}) collective-permute-start(bf16[128,2048]{1,0:T(8,128)(2,1)} %collective-permute-done.7.refs_1_), channel_id=1, source_target_pairs={{0,1},{1,0},{2,3},{3,2},{4,5},{5,4},{6,7},{7,6},{8,9},{9,8},{10,11... | collective-permute-start | bytes 1572872 | tf_op jit(solution)/shard_map/ppermute | solution.py:51
  175.1 26.4 %collective-permute-start.42 = (bf16[128,2048]{1,0:T(8,128)(2,1)}, bf16[128,2048]{1,0:T(8,128)(2,1)}, u32[]{:S(2)}, u32[]{:S(2)}) collective-permute-start(bf16[128,2048]{1,0:T(8,128)(2,1)} %collective-permute-done.9.refs_3_), channel_id=1, source_target_pairs={{0,1},{1,0},{2,3},{3,2},{4,5},{5,4},{6,7},{7,6},{8,9},{9,8},{10,11... | collective-permute-start | bytes 1572872 | tf_op jit(solution)/shard_map/ppermute | solution.py:51
  204.2 28.1 %collective-permute-start.43 = (bf16[256,2048]{1,0:T(8,128)(2,1)}, bf16[256,2048]{1,0:T(8,128)(2,1)}, u32[]{:S(2)}, u32[]{:S(2)}) collective-permute-start(bf16[256,2048]{1,0:T(8,128)(2,1)} %get-tuple-element.158.refs_0_), channel_id=1, source_target_pairs={{0,4},{4,0},{8,12},{12,8},{16,20},{20,16},{24,28},{28,24},{1,5},{5... | collective-permute-start | bytes 3145736 | tf_op jit(solution)/shard_map/ppermute | solution.py:51
  204.7 22.4 %collective-permute-start.46 = (bf16[128,2048]{1,0:T(8,128)(2,1)}, bf16[128,2048]{1,0:T(8,128)(2,1)S(1)}, u32[]{:S(2)}, u32[]{:S(2)}) collective-permute-start(bf16[128,2048]{1,0:T(8,128)(2,1)} %collective-permute-done.9.refs_3_), channel_id=1, source_target_pairs={{0,4},{4,0},{8,12},{12,8},{16,20},{20,16},{24,28},{28,24},{1,5},{5... | collective-permute-start | bytes 1572872 | tf_op jit(solution)/shard_map/ppermute | solution.py:51
  206.3 22.4 %collective-permute-start.47 = (bf16[128,2048]{1,0:T(8,128)(2,1)}, bf16[128,2048]{1,0:T(8,128)(2,1)S(1)}, u32[]{:S(2)}, u32[]{:S(2)}) collective-permute-start(bf16[128,2048]{1,0:T(8,128)(2,1)} %collective-permute-done.40.refs_4_), channel_id=1, source_target_pairs={{0,4},{4,0},{8,12},{12,8},{16,20},{20,16},{24,28},{28,24},{1,5},{5... | collective-permute-start | bytes 1572872 | tf_op jit(solution)/shard_map/ppermute | solution.py:51
  300.5 74.8 %collective-permute-start.73 = (bf16[2,64,2048]{2,1,0:T(8,128)(2,1)}, bf16[2,64,2048]{2,1,0:T(8,128)(2,1)}, u32[]{:S(2)}, u32[]{:S(2)}) collective-permute-start(bf16[2,64,2048]{2,1,0:T(8,128)(2,1)} %pad_maximum_fusion.12), channel_id=1, source_target_pairs={{0,2},{1,3},{2,0},{3,1},{4,6},{5,7},{6,4},{7,5},{8,10},{9,11},{10,... | collective-permute-start | bytes 1572872 | tf_op jit(solution)/shard_map/ppermute | solution.py:51
  315.1 25.3 %collective-permute-start.57 = (bf16[192,2048]{1,0:T(8,128)(2,1)}, bf16[192,2048]{1,0:T(8,128)(2,1)S(1)}, u32[]{:S(2)}, u32[]{:S(2)}) collective-permute-start(bf16[192,2048]{1,0:T(8,128)(2,1)} %get-tuple-element.168), channel_id=1, source_target_pairs={{0,8},{4,12},{8,0},{12,4},{16,24},{20,28},{24,16},{28,20},{1,9},{5... | collective-permute-start | bytes 2359304 | tf_op jit(solution)/shard_map/ppermute | solution.py:51
  315.8 25.9 %collective-permute-start.55 = (bf16[192,2048]{1,0:T(8,128)(2,1)}, bf16[192,2048]{1,0:T(8,128)(2,1)S(1)}, u32[]{:S(2)}, u32[]{:S(2)}) collective-permute-start(bf16[192,2048]{1,0:T(8,128)(2,1)} %get-tuple-element.168), channel_id=1, source_target_pairs={{0,16},{4,20},{8,24},{12,28},{16,0},{20,4},{24,8},{28,12},{1,17},{... | collective-permute-start | bytes 2359304 | tf_op jit(solution)/shard_map/ppermute | solution.py:51
  361.3 22.6 %collective-permute-start.65 = (bf16[96,2304]{1,0:T(8,128)(2,1)}, bf16[96,2304]{1,0:T(8,128)(2,1)}, u32[]{:S(2)}, u32[]{:S(2)}) collective-permute-start(bf16[96,2304]{1,0:T(8,128)(2,1)} %get-tuple-element.224), channel_id=1, source_target_pairs={{0,16},{4,20},{8,24},{12,28},{16,0},{20,4},{24,8},{28,12},{1,17},{... | collective-permute-start | bytes 1327112 | tf_op jit(solution)/shard_map/ppermute | solution.py:51
  363.1 24.3 %collective-permute-start.67 = (bf16[96,2304]{1,0:T(8,128)(2,1)}, bf16[96,2304]{1,0:T(8,128)(2,1)}, u32[]{:S(2)}, u32[]{:S(2)}) collective-permute-start(bf16[96,2304]{1,0:T(8,128)(2,1)} %get-tuple-element.225), channel_id=1, source_target_pairs={{0,8},{4,12},{8,0},{12,4},{16,24},{20,28},{24,16},{28,20},{1,9},{5... | collective-permute-start | bytes 1327112 | tf_op jit(solution)/shard_map/ppermute | solution.py:51
  386.4 40.2 %collective-permute-start.66 = (bf16[192,2304]{1,0:T(8,128)(2,1)S(1)}, bf16[192,2304]{1,0:T(8,128)(2,1)S(1)}, u32[]{:S(2)}, u32[]{:S(2)}) collective-permute-start(bf16[192,2304]{1,0:T(8,128)(2,1)S(1)} %pad_maximum_fusion.3), channel_id=1, source_target_pairs={{0,8},{4,12},{8,0},{12,4},{16,24},{20,28},{24,16},{28,20},{1,9},{5... | collective-permute-start | bytes 2654216 | tf_op jit(solution)/shard_map/ppermute | solution.py:51
  388.7 37.9 %collective-permute-start.68 = (bf16[192,2304]{1,0:T(8,128)(2,1)S(1)}, bf16[192,2304]{1,0:T(8,128)(2,1)S(1)}, u32[]{:S(2)}, u32[]{:S(2)}) collective-permute-start(bf16[192,2304]{1,0:T(8,128)(2,1)S(1)} %pad_maximum_fusion.4), channel_id=1, source_target_pairs={{0,16},{4,20},{8,24},{12,28},{16,0},{20,4},{24,8},{28,12},{1,17},{... | collective-permute-start | bytes 2654216 | tf_op jit(solution)/shard_map/ppermute | solution.py:51
  437.3 24.0 %collective-permute-start.80 = (bf16[2,48,768]{2,1,0:T(8,128)(2,1)S(1)}, bf16[2,48,768]{2,1,0:T(8,128)(2,1)S(1)}, u32[]{:S(2)}, u32[]{:S(2)}) collective-permute-start(bf16[2,48,768]{2,1,0:T(8,128)(2,1)S(1)} %pad_maximum_fusion.20), channel_id=1, source_target_pairs={{0,2},{1,3},{2,0},{3,1},{4,6},{5,7},{6,4},{7,5},{8,10},{9,11},{10,... | collective-permute-start | bytes 442376 | tf_op jit(solution)/shard_map/ppermute | solution.py:51
  (195 other events, 2594.5 us)

commit v9 on v8

--- a/solution.py
+++ b/solution.py
@@ -165,24 +165,24 @@
 
 
 def place_kernel(at_ref, *refs, count, width, rows, joined):
-    each = (len(refs) - 1 - (1 if joined else 2)) // 2
-    pieces, outs, sems = refs[: 2 * each], refs[2 * each : -1], refs[-1]
+    pieces, outs, sems = refs[:6], refs[6:-1], refs[-1]
     me, part = at_ref[0], at_ref[1]
+    half = rows // 2
 
     def copies(core):
         made = []
         for side in range(2):
-            for j in range(each):
-                i, second = (j, 0) if j < count else (j - count + 1, 1)
-                piece = pieces[side * each + j]
-                height = piece.shape[0]
-                row = (me ^ (2 * i) ^ side) * rows
-                if height < rows:
-                    row = row + (part ^ second) * height
-                row = pl.multiple_of(row, height)
+            parts = [(pieces[3 * side], 0, rows, 0, 0)]
+            for second in range(2):
+                parts += [
+                    (pieces[3 * side + 1 + second], (i - 1) * half, half, i, part ^ second)
+                    for i in range(1, count)
+                ]
+            for piece, first, height, i, which in parts:
+                row = pl.multiple_of((me ^ (2 * i) ^ side) * rows + which * half, half)
                 for k in range(2):
                     own = k ^ core
-                    source = piece.at[:, pl.ds(k * width, width)]
+                    source = piece.at[pl.ds(first, height), pl.ds(k * width, width)]
                     if joined:
                         target = outs[0].at[pl.ds(row, height), pl.ds(own * width, width)]
                     else:
@@ -211,7 +211,7 @@
         in_specs=[pl.BlockSpec(memory_space=pltpu.SMEM)]
         + [pl.BlockSpec(memory_space=pl.ANY)] * len(pieces),
         out_specs=[pl.BlockSpec(memory_space=pltpu.VMEM)] * len(shapes),
-        scratch_shapes=[pltpu.SemaphoreType.DMA((2 * len(pieces),))],
+        scratch_shapes=[pltpu.SemaphoreType.DMA((8 * count - 4,))],
         cost_estimate=pl.CostEstimate(
             flops=0, bytes_accessed=16 * rows * count * width, transcendentals=0
         ),
@@ -561,8 +561,9 @@
     def exchange(pieces):
         return [pieces[0]] + [swap(p, "shard", 2 * i) for i, p in enumerate(pieces) if i]
 
-    def halves_over_rep(pieces):
-        return [swap(piece, "rep", 1) for piece in pieces]
+    def with_halves(pieces):
+        near = jnp.concatenate(pieces[1:], 0)
+        return [pieces[0], near, swap(near, "rep", 1)]
 
     def both_cores(own):
         return list(own) + [swap(piece, "shard", 1) for piece in own]
@@ -596,7 +597,7 @@
 
     turned[0] = after(turned[0], *one_first)
     w_qkv_mine, w_qkv_other = place_weights(
-        at, both_cores(turned + halves_over_rep(turned[1:])), chips, 3 * span, False
+        at, both_cores(with_halves(turned)), chips, 3 * span, False
     )
     w_out_late, w_down_late = after((w_out, w_down), normed)
     w_out_chip = jnp.concatenate([w_out_late, w_out_other], 0)
@@ -669,6 +670,8 @@
         (mm(hidden_one, w_qkv_mine) + mm(low_qkv, out_qkv_mine) + b_qkv_of(me)).astype(BF16)
     )
     att_own, att_away, lse = attend(where, qkv_own, qkv_other, heads)
+    near_up[1:] = after(tuple(near_up[1:]), att_own)
+    halves_up = with_halves(near_up)
     cot_pieces, _, _ = gather_rows(after(cot_mine, att_own), bits, apart=True)
     attended = jnp.concatenate([flat(att_own), swap(flat(att_away), "shard", 1)], 1)
     low_att = keep_own(mm_t(attended, in_att))
@@ -681,8 +684,7 @@
     residual, hidden_block = row_call(
         norm_kernel, [rows_in, vectors] + terms, block, wide, [F32, BF16], "norm"
     )
-    far_up = halves_over_rep(after(tuple(near_up[1:]), *relayed))
-    pieces_up = after((*near_up, *far_up), hidden_block)
+    pieces_up = after(tuple(halves_up), hidden_block)
     hidden_two, _, _ = gather_rows(hidden_block, bits)
 
     (w_up_chip,) = place_weights(at, both_cores(pieces_up), chips, ff_part, True)
@@ -694,7 +696,17 @@
     slope = share + pre * (jnp.exp(-0.5 * pre * pre) * np.float32((2 * np.pi) ** -0.5))
     grad_pre = (slope * grad_act.astype(F32)).astype(BF16)
     glow_exp = keep_own(mm_t(grad_pre, out_exp))
-    terms, grad_sent = scatter_rows(block_products([(grad_pre, w_up_chip, mm_t)], glow_exp, in_exp), bits)
+    parts = block_products([(grad_pre, w_up_chip, mm_t)], glow_exp, in_exp)
+    far = 2 * (chips - 1)
+
+    def halves(value):
+        middle = value.shape[1] // 2
+        return value[:, :middle], value[:, middle:]
+
+    act_mid, grad_mid, low_mid, glow_mid = after((act, grad_pre, low_exp, glow_red), parts[far])
+    red_own, red_away = halves(t_mm(glow_mid, act_mid))
+    exp_own, exp_away = halves(t_mm(low_mid, grad_mid))
+    terms, _ = scatter_rows(parts, bits, (parts[0], red_own, exp_own))
     grad_residual, grad_block = row_call(
         functools.partial(norm_back_kernel, outs=2, row=1),
         [residual, vectors, cot_mine] + terms,
@@ -703,7 +715,7 @@
         [F32, BF16],
         "norm_back",
     )
-    grad_branch, _, branch_last = gather_rows(grad_block, bits)
+    grad_branch, branch_first, branch_last = gather_rows(grad_block, bits)
 
     act_late = after(act, grad_block)
     low_red = keep_own(mm_t(act_late, in_red))
@@ -766,30 +778,12 @@
         outs = sum_blocks(place, gathered, count * rank, widths)
         return [out.reshape(ADAPTERS, rank, -1) for out in outs]
 
-    def halves(value):
-        middle = value.shape[1] // 2
-        return value[:, :middle], value[:, middle:]
-
-    glow_late, low_late = after((glow_exp, low_exp), grad_block)
-    act_mid, grad_mid, low_mid, glow_mid = after((act, grad_pre, low_exp, glow_red), *grad_sent)
-    red_own, red_away = halves(t_mm(glow_mid, act_mid))
-    exp_own, exp_away = halves(t_mm(low_mid, grad_mid))
     local = sum_cores(
         jnp.concatenate([red_own, exp_own], 1), jnp.concatenate([red_away, exp_away], 1)
     )
-    mark = (chosen[:, None] == jnp.arange(ADAPTERS, dtype=jnp.int32)[None, :]).astype(BF16)
-    mark = jnp.pad(mark, ((0, 16 - count), (0, local.shape[1] - ADAPTERS)))
-    sums = [local[:, :ff_part], local[:, ff_part:]]
-    gathered = over_rep(sums, [mark], {rep_bits[-1]: (grad_away,)})
-    marks = jnp.concatenate(
-        [g[:, count * rank : count * rank + count, :ADAPTERS] for g in gathered], 0
-    )
-    place = marks.reshape(-1, 1, ADAPTERS, 1) * jnp.eye(rank, dtype=BF16)[None, :, None, :]
-    place = place.reshape(-1, ADAPTERS * rank)
-    s_in_red, s_out_exp = over_groups(sums, place, gathered)
-
+    glow_late, low_late = after((glow_exp, low_red), *branch_first)
     near_first = core_columns(
-        jnp.concatenate([t_mm(glow_late, hidden_two), t_mm(low_red, cot)], 0)
+        jnp.concatenate([t_mm(glow_late, hidden_two), t_mm(low_late, cot)], 0)
     ).astype(BF16)
     tall = near_first.shape[1]
     riders = {}
@@ -812,21 +806,34 @@
     products = [(grad_own, w_qkv_mine, mm_t), (grad_other, w_qkv_other, mm_t)]
     parts = block_products(products, after(glow_qkv, in_terms), in_qkv)
     far_part = parts[2 * (chips - 1)]
+    mark = (chosen[:, None] == jnp.arange(ADAPTERS, dtype=jnp.int32)[None, :]).astype(BF16)
+    mark = jnp.pad(mark, ((0, 16 - count), (0, local.shape[1] - ADAPTERS)))
+    sums = [local[:, :ff_part], local[:, ff_part:]]
+    gathered = over_rep(sums, [mark], {rep_bits[-1]: (far_part,)})
+    marks = jnp.concatenate(
+        [g[:, count * rank : count * rank + count, :ADAPTERS] for g in gathered], 0
+    )
+    place = marks.reshape(-1, 1, ADAPTERS, 1) * jnp.eye(rank, dtype=BF16)[None, :, None, :]
+    place = place.reshape(-1, ADAPTERS * rank)
+    s_in_red, s_out_exp = over_groups(sums, place, gathered)
+
+    own_last, other_last = after((grad_own, grad_other), far_part)
+    outer_own = own_terms(t_mm(low_qkv, own_last))
+    outer_away = own_terms(t_mm(low_qkv, other_last))
     aside = {}
 
     def hop(relayed):
         aside["second"], sent = sum_chips(after(near_second, far_part), *relayed)
         return sent
 
-    terms, relayed = scatter_rows(parts, bits, between=hop)
+    terms, relayed = scatter_rows(parts, bits, (parts[0], outer_own, outer_away), hop)
+    outer = sum_cores(outer_own, after(outer_away, *relayed))
     second = aside["second"]
     down, _ = scatter_rows(riders, bits, (grad_away,))
     down[0] = after(down[0], *relayed)
     first = sum(t[:tall, wide:].astype(F32) for t in down).reshape(2, count * rank, slice_wide)
     layer_rows = residual + b_down.astype(F32) + sum(t[:, :wide].astype(F32) for t in down)
 
-    own_last, other_last = after((grad_own, grad_other), *relayed)
-    outer = sum_cores(own_terms(t_mm(low_qkv, own_last)), own_terms(t_mm(low_qkv, other_last)))
     (input_rows,) = row_call(
         functools.partial(norm_back_kernel, outs=1, row=3),
         [rows_in, vectors, grad_residual] + terms,

time: 473 us -> 464 us (0.981)
  waiting for transfers between devices: 139 us -> 110 us
  other arithmetic: 24 us -> 35.4 us
  matrix products: 117 us -> 124 us
  starting transfers between devices: 69.8 us -> 64.7 us
  local copies, waits for them, and re-layouts: 46.8 us -> 51.7 us
    ppermute x81 -> x69, waiting for transfers between devices: 139 us -> 110 us  [swap(): return lax.ppermute(value, axis, [(i, i ^ mask) for i in range(size)])]
    dot_general x32, matrix products: 56 us -> 69.1 us  [mm(): lax.dot_general(a, b, (((1,), (0,)), ((), ())), preferred_element_type=F32)]
    ppermute x81 -> x69, starting transfers between devices: 69.8 us -> 64.7 us  [swap(): return lax.ppermute(value, axis, [(i, i ^ mask) for i in range(size)])]
    unnamed x297 -> x273, local copies, waits for them, and re-layouts: 24.8 us -> 27.7 us
  transfers between devices with their start and end apart: 81 -> 69, of which waited for: 32 -> 27; matrix products, arithmetic and copies ran while one was open for 29% -> 36% of each run, Pallas kernels for 11% -> 9%
where the time goes in v9:
time: 464 us; the launch traced here: 457 us
  matrix products  124 us (27%)
  waiting for transfers between devices  110 us (24%)
  Pallas kernels  65.2 us (14%)
  starting transfers between devices  64.7 us (14%)
  local copies, waits for them, and re-layouts  51.7 us (11%)
  other arithmetic  35.4 us (8%)
  between operations  5.29 us (1%)
    ppermute x69, waiting for transfers between devices, swap(): return lax.ppermute(value, axis, [(i, i ^ mask) for i in range(size)])  110 us
    dot_general x32, matrix products, mm(): lax.dot_general(a, b, (((1,), (0,)), ((), ())), preferred_element_type=F32)  69.1 us
    ppermute x69, starting transfers between devices, swap(): return lax.ppermute(value, axis, [(i, i ^ mask) for i in range(size)])  64.7 us
    dot_general x23, matrix products, mm_t(): lax.dot_general(a, b, (((1,), (1,)), ((), ())), preferred_element_type=F32)  49.1 us
    unnamed x273, local copies, waits for them, and re-layouts  27.7 us
    pallas_call x2, Pallas kernels, place_weights(): pl.pallas_call(functools.partial(place_kernel, count=count, width=width,...  14.4 us
    pallas_call x3, Pallas kernels, row_call(): pl.pallas_call(kernel, out_shape=[jax.ShapeDtypeStruct((rows, wide), d) f...  13.3 us
    pallas_call x1, Pallas kernels, attend_back(): pl.pallas_call(functools.partial(attend_back_kernel, heads=heads, factor=...  9.67 us
  transfers between devices with their start and end apart: 69, of which 27 were waited for; matrix products, arithmetic and copies ran while one was open for 36% of the time, Pallas kernels for 9%

profile of v9, /device:TPU:0, one launch (start us, length us, event | category | flops | bytes accessed | tf_op | source)
XLA Modules:
  0.0 456.9 jit_solution(4942919437801071001)
XLA Ops:
  40.5 4.8 %constant_dynamic-update-slice_fusion.8 = bf16[2048,2048]{1,0:T(8,128)(2,1)} fusion(bf16[1024,2048]{1,0:T(8,128)(2,1)} %param.47), kind=kLoop, calls=%fused_computation.292 | loop fusion | bytes 8388608
  50.8 4.8 %constant_dynamic-update-slice_fusion.7 = bf16[2048,2048]{1,0:T(8,128)(2,1)} fusion(bf16[2048,2048]{1,0:T(8,128)(2,1)} %constant_dynamic-update-slice_fusion.8, bf16[1024,2048]{1,0:T(8,128)(2,1)} %collective-permute-done.1), kind=kLoop, calls=%fused_computation.291 | loop fusion | bytes 8388608 | tf_op jit(solution)/shard_map/concatenate | solution.py:604
  71.4 13.5 %collective-permute-done.10 = bf16[192,2048]{1,0:T(8,128)(2,1)S(1)} collective-permute-done((bf16[192,2048]{1,0:T(8,128)(2,1)}, bf16[192,2048]{1,0:T(8,128)(2,1)S(1)}, u32[]{:S(2)}, u32[]{:S(2)}) %collective-permute-start.10) | collective-permute-done | bytes 786464 | tf_op jit(solution)/shard_map/ppermute | solution.py:51
  96.1 5.8 %collective-permute-done.12 = bf16[96,2048]{1,0:T(8,128)(2,1)S(1)} collective-permute-done((bf16[96,2048]{1,0:T(8,128)(2,1)S(1)}, bf16[96,2048]{1,0:T(8,128)(2,1)S(1)}, u32[]{:S(2)}, u32[]{:S(2)}) %collective-permute-start.12) | collective-permute-done | bytes 393248 | tf_op jit(solution)/shard_map/ppermute | solution.py:51
  102.1 6.9 %place_weights.2 = (bf16[2048,768]{1,0:T(8,128)(2,1)}, bf16[2048,768]{1,0:T(8,128)(2,1)}) custom-call(s32[2]{0:T(128)} %pad_add_fusion.1.at_ref, bf16[256,1536]{1,0:T(8,128)(2,1)} %get-tuple-element.135.refs_0_, bf16[384,1536]{1,0:T(8,128)(2,1)} %constant_dynamic-update-slice_fusion.9.refs_1_, bf16[384,1536]{1,0:T(8,128)(2,1)} %collective-permute-done.14.refs_2_, ...), custom_call_target="tpu_custom_call" | custom-call | bytes 12582912 | tf_op jit(solution)/shard_map/place_weights/pallas_call | solution.py:208
  126.5 7.3 %attend.1 = (bf16[4,3,64,256]{3,2,1,0:T(8,128)(2,1)}, bf16[4,3,64,256]{3,2,1,0:T(8,128)(2,1)}, f32[3,512,2]{2,1,0:T(8,128)}) custom-call(s32[512,1]{1,0:T(8,128)} %copy.49.pq, s32[1,512]{1,0:T(1,128)} %bitcast.232, s32[3,512,1]{2,1,0:T(8,128)} %copy.50.lq, s32[3,1,512]{2,1,0:T(1,128)} %broadcast_in_dim.86.lk, bf16[4,3,64,768]{3,2,1,0:T(8,128)(2,1)} %bitcast.217, ...), custom_call_target="tpu_custom_call" | custom-call | flops 805306368 | bytes 3145728 | tf_op jit(solution)/shard_map/attend/pallas_call | solution.py:430
  159.3 5.5 %collective-permute-done.27 = bf16[96,2048]{1,0:T(8,128)(2,1)S(1)} collective-permute-done((bf16[96,2048]{1,0:T(8,128)(2,1)S(1)}, bf16[96,2048]{1,0:T(8,128)(2,1)S(1)}, u32[]{:S(2)}, u32[]{:S(2)}) %collective-permute-start.27) | collective-permute-done | bytes 393248 | tf_op jit(solution)/shard_map/ppermute | solution.py:51
  168.0 6.7 %collective-permute-done.24 = bf16[96,2048]{1,0:T(8,128)(2,1)S(1)} collective-permute-done((bf16[96,2048]{1,0:T(8,128)(2,1)S(1)}, bf16[96,2048]{1,0:T(8,128)(2,1)S(1)}, u32[]{:S(2)}, u32[]{:S(2)}) %collective-permute-start.24) | collective-permute-done | bytes 393248 | tf_op jit(solution)/shard_map/ppermute | solution.py:51
  177.2 10.8 %add_convert_fusion = bf16[768,2048]{1,0:T(8,128)(2,1)} fusion(f32[768,2048]{1,0:T(8,128)S(1)} %fusion.120, bf16[768,2048]{1,0:T(8,128)(2,1)S(1)} %constant_dynamic-update-slice_fusion.12, bf16[2048,2048]{1,0:T(8,128)(2,1)} %constant_dynamic-update-slice_fusion.7), kind=kOutput, calls=%fused_computation.10 | convolution fusion | flops 6445596672 | bytes 20971520 | tf_op jit(solution)/shard_map/dot_general | solution.py:42
  198.6 15.0 %collective-permute-done.30 = bf16[192,2048]{1,0:T(8,128)(2,1)S(1)} collective-permute-done((bf16[192,2048]{1,0:T(8,128)(2,1)}, bf16[192,2048]{1,0:T(8,128)(2,1)S(1)}, u32[]{:S(2)}, u32[]{:S(2)}) %collective-permute-start.30) | collective-permute-done | bytes 786464 | tf_op jit(solution)/shard_map/ppermute | solution.py:51
  216.0 7.2 %collective-permute-done.32 = bf16[96,2048]{1,0:T(8,128)(2,1)S(1)} collective-permute-done((bf16[96,2048]{1,0:T(8,128)(2,1)S(1)}, bf16[96,2048]{1,0:T(8,128)(2,1)S(1)}, u32[]{:S(2)}, u32[]{:S(2)}) %collective-permute-start.32) | collective-permute-done | bytes 393248 | tf_op jit(solution)/shard_map/ppermute | solution.py:51
  230.3 7.5 %place_weights.3 = bf16[2048,2048]{1,0:T(8,128)(2,1)} custom-call(s32[2]{0:T(128)} %pad_add_fusion.1.at_ref, bf16[256,2048]{1,0:T(8,128)(2,1)} %get-tuple-element.160.refs_0_, bf16[384,2048]{1,0:T(8,128)(2,1)} %constant_dynamic-update-slice_fusion.22.refs_1_, bf16[384,2048]{1,0:T(8,128)(2,1)} %collective-permute-done.34.refs_2_, ...), custom_call_target="tpu_custom_call" | custom-call | bytes 16777216 | tf_op jit(solution)/shard_map/place_weights/pallas_call | solution.py:208
  237.9 14.8 %multiply_convert_fusion = (bf16[768,2048]{1,0:T(8,128)(2,1)S(1)}, bf16[768,2048]{1,0:T(8,128)(2,1)S(1)}) fusion(bf16[768,2048]{1,0:T(8,128)(2,1)} %add_convert_fusion, f32[2048]{0:T(1024)S(1)} %maximum_convert_fusion, f32[768,2048]{1,0:T(8,128)} %fusion.119, bf16[768,2048]{1,0:T(8,128)(2,1)} %copy-done.20, bf16[2048,2048]{1,0:T(8,128)(2,1)} %place_weights.3), kind=kOutput, calls=%fused_computation.7 | convolution fusion | flops 6466043904 | bytes 27271168 | tf_op jit(solution)/shard_map/dot_general | solution.py:38
  272.5 6.7 %collective-permute-done.40 = bf16[96,2048]{1,0:T(8,128)(2,1)S(1)} collective-permute-done((bf16[96,2048]{1,0:T(8,128)(2,1)S(1)}, bf16[96,2048]{1,0:T(8,128)(2,1)S(1)}, u32[]{:S(2)}, u32[]{:S(2)}) %collective-permute-start.40) | collective-permute-done | bytes 393248 | tf_op jit(solution)/shard_map/ppermute | solution.py:51
  285.8 5.5 %collective-permute-done.60.refs_1_ = bf16[1,64,2048]{2,1,0:T(8,128)(2,1)} collective-permute-done((bf16[1,64,2048]{2,1,0:T(8,128)(2,1)S(1)}, bf16[1,64,2048]{2,1,0:T(8,128)(2,1)}, u32[]{:S(2)}, u32[]{:S(2)}) %collective-permute-start.60) | collective-permute-done | bytes 262176 | tf_op jit(solution)/shard_map/ppermute | solution.py:51
  301.4 5.1 %norm_back.2 = (f32[192,2048]{1,0:T(8,128)}, bf16[192,2048]{1,0:T(8,128)(2,1)}) custom-call(f32[192,2048]{1,0:T(8,128)} %get-tuple-element.153.values, f32[4,2048]{1,0:T(4,128)} %convert_element_type.315.vectors, bf16[192,2048]{1,0:T(8,128)(2,1)} %bitcast.208, bf16[192,2048]{1,0:T(8,128)(2,1)} %fusion.15.refs_0_, ...), custom_call_target="tpu_custom_call" | custom-call | flops 7864320 | bytes 78643200 | tf_op jit(solution)/shard_map/norm_back/pallas_call | solution.py:335
  309.9 5.4 %fusion.53 = f32[192,2048]{1,0:T(8,128)S(1)} fusion(bf16[2048,2048]{1,0:T(8,128)(2,1)} %constant_dynamic-update-slice_fusion.7, bf16[768,2048]{1,0:T(8,128)(2,1)} %copy-done.33), kind=kOutput, calls=%fused_computation.143 | convolution fusion | flops 1610612736 | bytes 10747904 | tf_op jit(solution)/shard_map/dot_general | solution.py:38
  317.1 5.2 %fusion.51 = f32[192,2048]{1,0:T(8,128)S(1)} fusion(bf16[2048,2048]{1,0:T(8,128)(2,1)} %constant_dynamic-update-slice_fusion.7, bf16[768,2048]{1,0:T(8,128)(2,1)S(1)} %copy-done.34), kind=kOutput, calls=%fused_computation.141 | convolution fusion | flops 1610612736 | bytes 10747904 | tf_op jit(solution)/shard_map/dot_general | solution.py:38
  322.3 5.2 %fusion.49 = f32[192,2048]{1,0:T(8,128)S(1)} fusion(bf16[2048,2048]{1,0:T(8,128)(2,1)} %constant_dynamic-update-slice_fusion.7, bf16[768,2048]{1,0:T(8,128)(2,1)S(1)} %copy-done.34), kind=kOutput, calls=%fused_computation.137 | convolution fusion | flops 1610612736 | bytes 10747904 | tf_op jit(solution)/shard_map/dot_general | solution.py:38
  328.4 5.2 %fusion.47 = f32[192,2048]{1,0:T(8,128)S(1)} fusion(bf16[2048,2048]{1,0:T(8,128)(2,1)} %constant_dynamic-update-slice_fusion.7, bf16[768,2048]{1,0:T(8,128)(2,1)S(1)} %copy-done.34), kind=kOutput, calls=%fused_computation.135 | convolution fusion | flops 1610612736 | bytes 10747904 | tf_op jit(solution)/shard_map/dot_general | solution.py:38
  356.4 9.7 %attend_back.1 = (bf16[4,3,64,768]{3,2,1,0:T(8,128)(2,1)}, bf16[4,3,64,768]{3,2,1,0:T(8,128)(2,1)}) custom-call(s32[512,1]{1,0:T(8,128)} %copy.49.pq, s32[1,512]{1,0:T(1,128)} %bitcast.233, s32[3,512,1]{2,1,0:T(8,128)} %copy.50.lq, s32[3,1,512]{2,1,0:T(1,128)} %broadcast_in_dim.86.lk, bf16[4,3,64,768]{3,2,1,0:T(8,128)(2,1)} %bitcast.218, ...), custom_call_target="tpu_custom_call" | custom-call | flops 2013265920 | bytes 5505024 | tf_op jit(solution)/shard_map/attend_back/pallas_call | solution.py:487
  405.6 6.2 %collective-permute-done.50 = bf16[96,2048]{1,0:T(8,128)(2,1)S(1)} collective-permute-done((bf16[96,2048]{1,0:T(8,128)(2,1)S(1)}, bf16[96,2048]{1,0:T(8,128)(2,1)S(1)}, u32[]{:S(2)}, u32[]{:S(2)}) %collective-permute-start.50) | collective-permute-done | bytes 393248 | tf_op jit(solution)/shard_map/ppermute | solution.py:51
  434.8 10.9 %collective-permute-done.57.refs_1_ = bf16[192,2048]{1,0:T(8,128)(2,1)S(1)} collective-permute-done((bf16[192,2048]{1,0:T(8,128)(2,1)}, bf16[192,2048]{1,0:T(8,128)(2,1)S(1)}, u32[]{:S(2)}, u32[]{:S(2)}) %collective-permute-start.57) | collective-permute-done | bytes 786464 | tf_op jit(solution)/shard_map/ppermute | solution.py:51
  447.4 4.5 norm_back.3
  (607 shorter events, 271.3 us)
Async XLA Ops:
  0.7 35.1 %collective-permute-start.1 = (bf16[1024,2048]{1,0:T(8,128)(2,1)}, bf16[1024,2048]{1,0:T(8,128)(2,1)}, u32[]{:S(2)}, u32[]{:S(2)}) collective-permute-start(bf16[1024,2048]{1,0:T(8,128)(2,1)} %param.47), channel_id=1, source_target_pairs={{0,4},{4,0},{8,12},{12,8},{16,20},{20,16},{24,28},{28,24},{1,5},{5... | collective-permute-start | bytes 12582920 | tf_op jit(solution)/shard_map/ppermute | solution.py:51
  1.3 31.8 %collective-permute-start = (bf16[256,2048]{1,0:T(8,128)(2,1)}, bf16[256,2048]{1,0:T(8,128)(2,1)S(1)}, u32[]{:S(2)}, u32[]{:S(2)}) collective-permute-start(bf16[256,2048]{1,0:T(8,128)(2,1)} %param.41), channel_id=1, source_target_pairs={{0,4},{4,0},{8,12},{12,8},{16,20},{20,16},{24,28},{28,24},{1,5},{5... | collective-permute-start | bytes 3145736 | tf_op jit(solution)/shard_map/ppermute | solution.py:51
  10.2 22.0 %collective-permute-start.6 = (bf16[128,1536]{1,0:T(8,128)(2,1)}, bf16[128,1536]{1,0:T(8,128)(2,1)S(1)}, u32[]{:S(2)}, u32[]{:S(2)}) collective-permute-start(bf16[128,1536]{1,0:T(8,128)(2,1)} %get-tuple-element.119), channel_id=1, source_target_pairs={{0,24},{4,28},{8,16},{12,20},{16,8},{20,12},{24,0},{28,4},{1,25},{... | collective-permute-start | bytes 1179656 | tf_op jit(solution)/shard_map/ppermute | solution.py:51
  19.6 38.6 %collective-permute-start.7 = (bf16[128,2048]{1,0:T(8,128)(2,1)}, bf16[128,2048]{1,0:T(8,128)(2,1)S(1)}, u32[]{:S(2)}, u32[]{:S(2)}) collective-permute-start(bf16[128,2048]{1,0:T(8,128)(2,1)} %get-tuple-element.128), channel_id=1, source_target_pairs={{0,8},{4,12},{8,0},{12,4},{16,24},{20,28},{24,16},{28,20},{1,9},{5... | collective-permute-start | bytes 1572872 | tf_op jit(solution)/shard_map/ppermute | solution.py:51
  28.2 36.3 %collective-permute-start.8 = (bf16[128,2048]{1,0:T(8,128)(2,1)}, bf16[128,2048]{1,0:T(8,128)(2,1)S(1)}, u32[]{:S(2)}, u32[]{:S(2)}) collective-permute-start(bf16[128,2048]{1,0:T(8,128)(2,1)} %get-tuple-element.129), channel_id=1, source_target_pairs={{0,16},{4,20},{8,24},{12,28},{16,0},{20,4},{24,8},{28,12},{1,17},{... | collective-permute-start | bytes 1572872 | tf_op jit(solution)/shard_map/ppermute | solution.py:51
  32.2 32.8 %collective-permute-start.9 = (bf16[128,2048]{1,0:T(8,128)(2,1)}, bf16[128,2048]{1,0:T(8,128)(2,1)}, u32[]{:S(2)}, u32[]{:S(2)}) collective-permute-start(bf16[128,2048]{1,0:T(8,128)(2,1)} %get-tuple-element.130), channel_id=1, source_target_pairs={{0,24},{4,28},{8,16},{12,20},{16,8},{20,12},{24,0},{28,4},{1,25},{... | collective-permute-start | bytes 1572872 | tf_op jit(solution)/shard_map/ppermute | solution.py:51
  33.0 31.6 %collective-permute-start.14 = (bf16[384,1536]{1,0:T(8,128)(2,1)}, bf16[384,1536]{1,0:T(8,128)(2,1)}, u32[]{:S(2)}, u32[]{:S(2)}) collective-permute-start(bf16[384,1536]{1,0:T(8,128)(2,1)} %constant_dynamic-update-slice_fusion.9.refs_1_), channel_id=1, source_target_pairs={{0,1},{1,0},{2,3},{3,2},{4,5},{5,4},{6,7},{7,6},{8,9},{9,8},{10,11... | collective-permute-start | bytes 3538952 | tf_op jit(solution)/shard_map/ppermute | solution.py:51
  39.2 25.8 %collective-permute-start.2 = (bf16[48,3072]{1,0:T(8,128)(2,1)}, bf16[48,3072]{1,0:T(8,128)(2,1)S(1)}, u32[]{:S(2)}, u32[]{:S(2)}) collective-permute-start(bf16[48,3072]{1,0:T(8,128)(2,1)} %get-tuple-element.138), channel_id=1, source_target_pairs={{0,4},{4,0},{8,12},{12,8},{16,20},{20,16},{24,28},{28,24},{1,5},{5... | collective-permute-start | bytes 884744 | tf_op jit(solution)/shard_map/ppermute | solution.py:51
  64.5 37.6 %collective-permute-start.16 = (bf16[384,1536]{1,0:T(8,128)(2,1)}, bf16[384,1536]{1,0:T(8,128)(2,1)}, u32[]{:S(2)}, u32[]{:S(2)}) collective-permute-start(bf16[384,1536]{1,0:T(8,128)(2,1)} %constant_dynamic-update-slice_fusion.9.refs_1_), channel_id=1, source_target_pairs={{0,4},{4,0},{8,12},{12,8},{16,20},{20,16},{24,28},{28,24},{1,5},{5... | collective-permute-start | bytes 3538952 | tf_op jit(solution)/shard_map/ppermute | solution.py:51
  64.7 37.4 %collective-permute-start.17 = (bf16[384,1536]{1,0:T(8,128)(2,1)}, bf16[384,1536]{1,0:T(8,128)(2,1)}, u32[]{:S(2)}, u32[]{:S(2)}) collective-permute-start(bf16[384,1536]{1,0:T(8,128)(2,1)} %collective-permute-done.14.refs_2_), channel_id=1, source_target_pairs={{0,4},{4,0},{8,12},{12,8},{16,20},{20,16},{24,28},{28,24},{1,5},{5... | collective-permute-start | bytes 3538952 | tf_op jit(solution)/shard_map/ppermute | solution.py:51
  133.8 22.2 %collective-permute-start.22 = (bf16[192,2048]{1,0:T(8,128)(2,1)}, bf16[192,2048]{1,0:T(8,128)(2,1)S(1)}, u32[]{:S(2)}, u32[]{:S(2)}) collective-permute-start(bf16[192,2048]{1,0:T(8,128)(2,1)} %bitcast.206), channel_id=1, source_target_pairs={{0,8},{4,12},{8,0},{12,4},{16,24},{20,28},{24,16},{28,20},{1,9},{5... | collective-permute-start | bytes 2359304 | tf_op jit(solution)/shard_map/ppermute | solution.py:51
  135.7 22.1 %collective-permute-start.23 = (bf16[192,2048]{1,0:T(8,128)(2,1)}, bf16[192,2048]{1,0:T(8,128)(2,1)S(1)}, u32[]{:S(2)}, u32[]{:S(2)}) collective-permute-start(bf16[192,2048]{1,0:T(8,128)(2,1)} %bitcast.207), channel_id=1, source_target_pairs={{0,16},{4,20},{8,24},{12,28},{16,0},{20,4},{24,8},{28,12},{1,17},{... | collective-permute-start | bytes 2359304 | tf_op jit(solution)/shard_map/ppermute | solution.py:51
  142.9 53.9 %collective-permute-start.34 = (bf16[384,2048]{1,0:T(8,128)(2,1)}, bf16[384,2048]{1,0:T(8,128)(2,1)}, u32[]{:S(2)}, u32[]{:S(2)}) collective-permute-start(bf16[384,2048]{1,0:T(8,128)(2,1)} %constant_dynamic-update-slice_fusion.22.refs_1_), channel_id=1, source_target_pairs={{0,1},{1,0},{2,3},{3,2},{4,5},{5,4},{6,7},{7,6},{8,9},{9,8},{10,11... | collective-permute-start | bytes 4718600 | tf_op jit(solution)/shard_map/ppermute | solution.py:51
  165.0 26.0 %collective-permute-start.29 = (bf16[192,2048]{1,0:T(8,128)(2,1)S(1)}, bf16[192,2048]{1,0:T(8,128)(2,1)}, u32[]{:S(2)}, u32[]{:S(2)}) collective-permute-start(bf16[192,2048]{1,0:T(8,128)(2,1)S(1)} %pad_maximum_fusion.6), channel_id=1, source_target_pairs={{0,16},{4,20},{8,24},{12,28},{16,0},{20,4},{24,8},{28,12},{1,17},{... | collective-permute-start | bytes 2359304 | tf_op jit(solution)/shard_map/ppermute | solution.py:51
  166.5 24.4 %collective-permute-start.28 = (bf16[192,2048]{1,0:T(8,128)(2,1)S(1)}, bf16[192,2048]{1,0:T(8,128)(2,1)}, u32[]{:S(2)}, u32[]{:S(2)}) collective-permute-start(bf16[192,2048]{1,0:T(8,128)(2,1)S(1)} %pad_maximum_fusion.5), channel_id=1, source_target_pairs={{0,8},{4,12},{8,0},{12,4},{16,24},{20,28},{24,16},{28,20},{1,9},{5... | collective-permute-start | bytes 2359304 | tf_op jit(solution)/shard_map/ppermute | solution.py:51
  196.8 33.5 %collective-permute-start.36 = (bf16[384,2048]{1,0:T(8,128)(2,1)}, bf16[384,2048]{1,0:T(8,128)(2,1)}, u32[]{:S(2)}, u32[]{:S(2)}) collective-permute-start(bf16[384,2048]{1,0:T(8,128)(2,1)} %constant_dynamic-update-slice_fusion.22.refs_1_), channel_id=1, source_target_pairs={{0,4},{4,0},{8,12},{12,8},{16,20},{20,16},{24,28},{28,24},{1,5},{5... | collective-permute-start | bytes 4718600 | tf_op jit(solution)/shard_map/ppermute | solution.py:51
  196.9 33.5 %collective-permute-start.37 = (bf16[384,2048]{1,0:T(8,128)(2,1)}, bf16[384,2048]{1,0:T(8,128)(2,1)}, u32[]{:S(2)}, u32[]{:S(2)}) collective-permute-start(bf16[384,2048]{1,0:T(8,128)(2,1)} %collective-permute-done.34.refs_2_), channel_id=1, source_target_pairs={{0,4},{4,0},{8,12},{12,8},{16,20},{20,16},{24,28},{28,24},{1,5},{5... | collective-permute-start | bytes 4718600 | tf_op jit(solution)/shard_map/ppermute | solution.py:51
  197.4 32.9 %collective-permute-start.35 = (bf16[256,2048]{1,0:T(8,128)(2,1)}, bf16[256,2048]{1,0:T(8,128)(2,1)}, u32[]{:S(2)}, u32[]{:S(2)}) collective-permute-start(bf16[256,2048]{1,0:T(8,128)(2,1)} %get-tuple-element.160.refs_0_), channel_id=1, source_target_pairs={{0,4},{4,0},{8,12},{12,8},{16,20},{20,16},{24,28},{28,24},{1,5},{5... | collective-permute-start | bytes 3145736 | tf_op jit(solution)/shard_map/ppermute | solution.py:51
  293.5 95.2 %collective-permute-start.61 = (bf16[2,64,2048]{2,1,0:T(8,128)(2,1)}, bf16[2,64,2048]{2,1,0:T(8,128)(2,1)}, u32[]{:S(2)}, u32[]{:S(2)}) collective-permute-start(bf16[2,64,2048]{2,1,0:T(8,128)(2,1)} %pad_maximum_fusion.12), channel_id=1, source_target_pairs={{0,2},{1,3},{2,0},{3,1},{4,6},{5,7},{6,4},{7,5},{8,10},{9,11},{10,... | collective-permute-start | bytes 1572872 | tf_op jit(solution)/shard_map/ppermute | solution.py:51
  307.7 26.3 %collective-permute-start.42 = (bf16[192,2048]{1,0:T(8,128)(2,1)}, bf16[192,2048]{1,0:T(8,128)(2,1)S(1)}, u32[]{:S(2)}, u32[]{:S(2)}) collective-permute-start(bf16[192,2048]{1,0:T(8,128)(2,1)} %get-tuple-element.172), channel_id=1, source_target_pairs={{0,8},{4,12},{8,0},{12,4},{16,24},{20,28},{24,16},{28,20},{1,9},{5... | collective-permute-start | bytes 2359304 | tf_op jit(solution)/shard_map/ppermute | solution.py:51
  309.3 26.3 %collective-permute-start.43 = (bf16[192,2048]{1,0:T(8,128)(2,1)}, bf16[192,2048]{1,0:T(8,128)(2,1)S(1)}, u32[]{:S(2)}, u32[]{:S(2)}) collective-permute-start(bf16[192,2048]{1,0:T(8,128)(2,1)} %get-tuple-element.172), channel_id=1, source_target_pairs={{0,16},{4,20},{8,24},{12,28},{16,0},{20,4},{24,8},{28,12},{1,17},{... | collective-permute-start | bytes 2359304 | tf_op jit(solution)/shard_map/ppermute | solution.py:51
  369.5 48.5 %collective-permute-start.54 = (bf16[192,2304]{1,0:T(8,128)(2,1)}, bf16[192,2304]{1,0:T(8,128)(2,1)}, u32[]{:S(2)}, u32[]{:S(2)}) collective-permute-start(bf16[192,2304]{1,0:T(8,128)(2,1)} %pad_maximum_fusion.3), channel_id=1, source_target_pairs={{0,8},{4,12},{8,0},{12,4},{16,24},{20,28},{24,16},{28,20},{1,9},{5... | collective-permute-start | bytes 2654216 | tf_op jit(solution)/shard_map/ppermute | solution.py:51
  372.7 45.3 %collective-permute-start.56 = (bf16[192,2304]{1,0:T(8,128)(2,1)}, bf16[192,2304]{1,0:T(8,128)(2,1)}, u32[]{:S(2)}, u32[]{:S(2)}) collective-permute-start(bf16[192,2304]{1,0:T(8,128)(2,1)} %pad_maximum_fusion.4), channel_id=1, source_target_pairs={{0,16},{4,20},{8,24},{12,28},{16,0},{20,4},{24,8},{28,12},{1,17},{... | collective-permute-start | bytes 2654216 | tf_op jit(solution)/shard_map/ppermute | solution.py:51
  428.4 23.6 %collective-permute-start.68 = (bf16[2,48,768]{2,1,0:T(8,128)(2,1)S(1)}, bf16[2,48,768]{2,1,0:T(8,128)(2,1)}, u32[]{:S(2)}, u32[]{:S(2)}) collective-permute-start(bf16[2,48,768]{2,1,0:T(8,128)(2,1)S(1)} %pad_maximum_fusion.22), channel_id=1, source_target_pairs={{0,2},{1,3},{2,0},{3,1},{4,6},{5,7},{6,4},{7,5},{8,10},{9,11},{10,... | collective-permute-start | bytes 442376 | tf_op jit(solution)/shard_map/ppermute | solution.py:51
  (173 other events, 1346.7 us)

commit v10 on v9

--- a/solution.py
+++ b/solution.py
@@ -588,21 +588,22 @@
     rows_in = after(inputs[0].reshape(block, wide), mine)
     features = rows_in.astype(F32)
     normed = layer_norm(features, ln1_gain.astype(F32), ln1_bias.astype(F32)).astype(BF16)
-    starts, b_query, b_value, b_up, me_late, chosen, packed = after(
-        (starts, b_query, b_value, b_up, me, chosen, packed), normed
-    )
     vectors = after(jnp.stack([b_out, ln2_gain, ln2_bias, ln1_gain]), normed).astype(F32)
     hidden_block = after(normed, packed_other, near_one, *turned[1:], *near_up[1:])
+    starts, b_query, b_value, b_up, me_late, chosen, packed = after(
+        (starts, b_query, b_value, b_up, me, chosen, packed), hidden_block
+    )
     hidden_one, one_first, one_last = gather_rows(hidden_block, bits)
 
     turned[0] = after(turned[0], *one_first)
     w_qkv_mine, w_qkv_other = place_weights(
         at, both_cores(with_halves(turned)), chips, 3 * span, False
     )
-    w_out_late, w_down_late = after((w_out, w_down), normed)
+    w_out_late, w_down_late, *near_up = after((w_out, w_down, *near_up), hidden_block)
+    merged_up = jnp.concatenate(near_up[1:], 0)
     w_out_chip = jnp.concatenate([w_out_late, w_out_other], 0)
     w_down_chip = jnp.concatenate([w_down_late, w_down_other], 0)
-    hidden_one = after(hidden_one, w_out_chip, w_down_chip)
+    hidden_one = after(hidden_one, merged_up, w_out_chip, w_down_chip)
     cot_mine = cotangent[0].reshape(block, wide)
     near = after(jnp.concatenate([mine[None], near_one], 0), *one_first)
     for bit in bits[1:]:
@@ -670,8 +671,7 @@
         (mm(hidden_one, w_qkv_mine) + mm(low_qkv, out_qkv_mine) + b_qkv_of(me)).astype(BF16)
     )
     att_own, att_away, lse = attend(where, qkv_own, qkv_other, heads)
-    near_up[1:] = after(tuple(near_up[1:]), att_own)
-    halves_up = with_halves(near_up)
+    halves_up = [near_up[0], merged_up, swap(after(merged_up, att_own), "rep", 1)]
     cot_pieces, _, _ = gather_rows(after(cot_mine, att_own), bits, apart=True)
     attended = jnp.concatenate([flat(att_own), swap(flat(att_away), "shard", 1)], 1)
     low_att = keep_own(mm_t(attended, in_att))
@@ -685,10 +685,11 @@
         norm_kernel, [rows_in, vectors] + terms, block, wide, [F32, BF16], "norm"
     )
     pieces_up = after(tuple(halves_up), hidden_block)
-    hidden_two, _, _ = gather_rows(hidden_block, bits)
+    two_pieces, _, _ = gather_rows(hidden_block, bits, apart=True)
 
     (w_up_chip,) = place_weights(at, both_cores(pieces_up), chips, ff_part, True)
-    hidden_two = after(hidden_two, grad_act)
+    two_pieces[-2:] = after(tuple(two_pieces[-2:]), w_up_chip)
+    hidden_two = jnp.concatenate(two_pieces, 0)
     low_exp = keep_own(mm_t(hidden_two, in_exp))
     pre = mm(hidden_two, w_up_chip) + mm(low_exp, out_exp) + b_up_chip
     share = 0.5 * (1.0 + lax.erf(pre * np.float32(0.5**0.5)))
@@ -719,7 +720,8 @@
 
     act_late = after(act, grad_block)
     low_red = keep_own(mm_t(act_late, in_red))
-    down_parts = block_products([(act_late, w_down_chip, mm)], low_red, out_red)
+    down = (mm(act_late, w_down_chip) + mm(low_red, out_red)).astype(BF16)
+    down_parts = {2 * i: down[i * block : (i + 1) * block] for i in range(chips)}
     glow_att = keep_own(mm_t(grad_branch, out_att))
     grad_att = (mm_t(grad_branch, w_out_chip) + mm(glow_att, in_att)).astype(BF16)
     ga_own = by_chip(grad_att[:, :span])

time: 464 us -> 456 us (0.983)
  matrix products: 124 us -> 117 us
    dot_general x32 -> x26, matrix products: 69.1 us -> 56.6 us  [mm(): lax.dot_general(a, b, (((1,), (0,)), ((), ())), preferred_element_type=F32)]
    unnamed x273 -> x291, local copies, waits for them, and re-layouts: 27.7 us -> 28.7 us
  transfers between devices with their start and end apart: 69 -> 69, of which waited for: 27 -> 26; matrix products, arithmetic and copies ran while one was open for 36% -> 32% of each run, Pallas kernels for 9% -> 11%
where the time goes in v10:
time: 456 us; the launch traced here: 450 us
  matrix products  117 us (26%)
  waiting for transfers between devices  114 us (25%)
  Pallas kernels  65 us (14%)
  starting transfers between devices  61.7 us (14%)
  local copies, waits for them, and re-layouts  52.3 us (11%)
  other arithmetic  33.6 us (7%)
  between operations  5.82 us (1%)
    ppermute x69, waiting for transfers between devices, swap(): return lax.ppermute(value, axis, [(i, i ^ mask) for i in range(size)])  114 us
    ppermute x69, starting transfers between devices, swap(): return lax.ppermute(value, axis, [(i, i ^ mask) for i in range(size)])  61.7 us
    dot_general x26, matrix products, mm(): lax.dot_general(a, b, (((1,), (0,)), ((), ())), preferred_element_type=F32)  56.6 us
    dot_general x23, matrix products, mm_t(): lax.dot_general(a, b, (((1,), (1,)), ((), ())), preferred_element_type=F32)  52.3 us
    unnamed x291, local copies, waits for them, and re-layouts  28.7 us
    pallas_call x2, Pallas kernels, place_weights(): pl.pallas_call(functools.partial(place_kernel, count=count, width=width,...  14.1 us
    pallas_call x3, Pallas kernels, row_call(): pl.pallas_call(kernel, out_shape=[jax.ShapeDtypeStruct((rows, wide), d) f...  13.3 us
    pallas_call x1, Pallas kernels, attend_back(): pl.pallas_call(functools.partial(attend_back_kernel, heads=heads, factor=...  9.64 us
  transfers between devices with their start and end apart: 69, of which 26 were waited for; matrix products, arithmetic and copies ran while one was open for 32% of the time, Pallas kernels for 11%

profile of v10, /device:TPU:0, one launch (start us, length us, event | category | flops | bytes accessed | tf_op | source)
XLA Modules:
  0.0 449.7 jit_solution(175927867752874745)
XLA Ops:
  12.7 3.9 cut_pieces.3
  23.4 4.0 collective-permute-done.5
  40.6 11.8 %collective-permute-done.3 = bf16[1,288,256]{2,1,0:T(8,128)(2,1)S(1)} collective-permute-done((bf16[1,288,256]{2,1,0:T(8,128)(2,1)}, bf16[1,288,256]{2,1,0:T(8,128)(2,1)S(1)}, u32[]{:S(2)}, u32[]{:S(2)}) %collective-permute-start.3) | collective-permute-done | bytes 147488 | tf_op jit(solution)/shard_map/ppermute | solution.py:51
  53.5 6.0 %collective-permute-done.14.refs_2_ = bf16[384,1536]{1,0:T(8,128)(2,1)} collective-permute-done((bf16[384,1536]{1,0:T(8,128)(2,1)}, bf16[384,1536]{1,0:T(8,128)(2,1)}, u32[]{:S(2)}, u32[]{:S(2)}) %collective-permute-start.14) | collective-permute-done | bytes 1179680 | tf_op jit(solution)/shard_map/ppermute | solution.py:51
  85.4 5.2 %collective-permute-done.18 = bf16[2,288,256]{2,1,0:T(8,128)(2,1)S(1)} collective-permute-done((bf16[2,288,256]{2,1,0:T(8,128)(2,1)S(1)}, bf16[2,288,256]{2,1,0:T(8,128)(2,1)S(1)}, u32[]{:S(2)}, u32[]{:S(2)}) %collective-permute-start.18) | collective-permute-done | bytes 294944 | tf_op jit(solution)/shard_map/ppermute | solution.py:51
  91.5 5.9 %collective-permute-done.12 = bf16[96,2048]{1,0:T(8,128)(2,1)S(1)} collective-permute-done((bf16[96,2048]{1,0:T(8,128)(2,1)S(1)}, bf16[96,2048]{1,0:T(8,128)(2,1)S(1)}, u32[]{:S(2)}, u32[]{:S(2)}) %collective-permute-start.12) | collective-permute-done | bytes 393248 | tf_op jit(solution)/shard_map/ppermute | solution.py:51
  100.7 6.5 %place_weights.2 = (bf16[2048,768]{1,0:T(8,128)(2,1)}, bf16[2048,768]{1,0:T(8,128)(2,1)}) custom-call(s32[2]{0:T(128)} %pad_add_fusion.1.at_ref, bf16[256,1536]{1,0:T(8,128)(2,1)} %get-tuple-element.140.refs_0_, bf16[384,1536]{1,0:T(8,128)(2,1)} %constant_dynamic-update-slice_fusion.12.refs_1_, bf16[384,1536]{1,0:T(8,128)(2,1)} %collective-permute-done.14.refs_2_, ...), custom_call_target="tpu_custom_call" | custom-call | bytes 12582912 | tf_op jit(solution)/shard_map/place_weights/pallas_call | solution.py:208
  124.5 6.5 %add_convert_fusion.3 = bf16[768,768]{1,0:T(8,128)(2,1)} fusion(f32[768,768]{1,0:T(8,128)S(1)} %fusion.190, bf16[768,2048]{1,0:T(8,128)(2,1)} %copy-done.14, bf16[2048,768]{1,0:T(8,128)(2,1)} %get-tuple-element.141, f32[768]{0:T(1024)S(1)} %get-tuple-element.289), kind=kOutput, calls=%fused_computation.58 | convolution fusion | flops 2417688576 | bytes 9833472 | tf_op jit(solution)/shard_map/dot_general | solution.py:38
  131.0 7.5 %attend.1 = (bf16[4,3,64,256]{3,2,1,0:T(8,128)(2,1)}, bf16[4,3,64,256]{3,2,1,0:T(8,128)(2,1)}, f32[3,512,2]{2,1,0:T(8,128)}) custom-call(s32[512,1]{1,0:T(8,128)} %copy.49.pq, s32[1,512]{1,0:T(1,128)} %bitcast.233, s32[3,512,1]{2,1,0:T(8,128)} %copy.50.lq, s32[3,1,512]{2,1,0:T(1,128)} %broadcast_in_dim.87.lk, bf16[4,3,64,768]{3,2,1,0:T(8,128)(2,1)} %bitcast.218, ...), custom_call_target="tpu_custom_call" | custom-call | flops 805306368 | bytes 3145728 | tf_op jit(solution)/shard_map/attend/pallas_call | solution.py:430
  164.2 5.2 %collective-permute-done.27 = bf16[96,2048]{1,0:T(8,128)(2,1)S(1)} collective-permute-done((bf16[96,2048]{1,0:T(8,128)(2,1)S(1)}, bf16[96,2048]{1,0:T(8,128)(2,1)S(1)}, u32[]{:S(2)}, u32[]{:S(2)}) %collective-permute-start.27) | collective-permute-done | bytes 393248 | tf_op jit(solution)/shard_map/ppermute | solution.py:51
  173.0 6.2 %collective-permute-done.24 = bf16[96,2048]{1,0:T(8,128)(2,1)S(1)} collective-permute-done((bf16[96,2048]{1,0:T(8,128)(2,1)S(1)}, bf16[96,2048]{1,0:T(8,128)(2,1)S(1)}, u32[]{:S(2)}, u32[]{:S(2)}) %collective-permute-start.24) | collective-permute-done | bytes 393248 | tf_op jit(solution)/shard_map/ppermute | solution.py:51
  182.3 10.3 %add_convert_fusion.1 = bf16[768,2048]{1,0:T(8,128)(2,1)} fusion(f32[768,2048]{1,0:T(8,128)S(1)} %fusion.111, bf16[768,2048]{1,0:T(8,128)(2,1)S(1)} %constant_dynamic-update-slice_fusion.15, bf16[2048,2048]{1,0:T(8,128)(2,1)} %copy-done.32), kind=kOutput, calls=%fused_computation.11 | convolution fusion | flops 6445596672 | bytes 20971520 | tf_op jit(solution)/shard_map/dot_general | solution.py:42
  205.6 14.4 %collective-permute-done.30 = bf16[192,2048]{1,0:T(8,128)(2,1)S(1)} collective-permute-done((bf16[192,2048]{1,0:T(8,128)(2,1)}, bf16[192,2048]{1,0:T(8,128)(2,1)S(1)}, u32[]{:S(2)}, u32[]{:S(2)}) %collective-permute-start.30) | collective-permute-done | bytes 786464 | tf_op jit(solution)/shard_map/ppermute | solution.py:51
  226.1 7.6 %place_weights.3 = bf16[2048,2048]{1,0:T(8,128)(2,1)} custom-call(s32[2]{0:T(128)} %pad_add_fusion.1.at_ref, bf16[256,2048]{1,0:T(8,128)(2,1)} %get-tuple-element.162.refs_0_, bf16[384,2048]{1,0:T(8,128)(2,1)} %constant_dynamic-update-slice_fusion.5.refs_1_, bf16[384,2048]{1,0:T(8,128)(2,1)} %collective-permute-done.34.refs_2_, ...), custom_call_target="tpu_custom_call" | custom-call | bytes 16777216 | tf_op jit(solution)/shard_map/place_weights/pallas_call | solution.py:208
  243.3 11.5 %multiply_convert_fusion = (bf16[768,2048]{1,0:T(8,128)(2,1)S(1)}, bf16[768,2048]{1,0:T(8,128)(2,1)S(1)}) fusion(bf16[768,2048]{1,0:T(8,128)(2,1)} %add_convert_fusion.1, f32[2048]{0:T(1024)} %maximum_convert_fusion, f32[768,2048]{1,0:T(8,128)S(1)} %fusion.110, bf16[768,2048]{1,0:T(8,128)(2,1)} %constant_dynamic-update-slice_fusion.20, ...), kind=kOutput, calls=%fused_computation.8 | convolution fusion | flops 6466043904 | bytes 27271168 | tf_op jit(solution)/shard_map/dot_general | solution.py:38
  274.5 7.6 %collective-permute-done.40 = bf16[96,2048]{1,0:T(8,128)(2,1)S(1)} collective-permute-done((bf16[96,2048]{1,0:T(8,128)(2,1)S(1)}, bf16[96,2048]{1,0:T(8,128)(2,1)S(1)}, u32[]{:S(2)}, u32[]{:S(2)}) %collective-permute-start.40) | collective-permute-done | bytes 393248 | tf_op jit(solution)/shard_map/ppermute | solution.py:51
  287.2 6.0 %collective-permute-done.60.refs_1_ = bf16[1,64,2048]{2,1,0:T(8,128)(2,1)} collective-permute-done((bf16[1,64,2048]{2,1,0:T(8,128)(2,1)S(1)}, bf16[1,64,2048]{2,1,0:T(8,128)(2,1)}, u32[]{:S(2)}, u32[]{:S(2)}) %collective-permute-start.60) | collective-permute-done | bytes 262176 | tf_op jit(solution)/shard_map/ppermute | solution.py:51
  296.3 6.2 %collective-permute-done.41.refs_2_ = bf16[192,2048]{1,0:T(8,128)(2,1)} collective-permute-done((bf16[192,2048]{1,0:T(8,128)(2,1)}, bf16[192,2048]{1,0:T(8,128)(2,1)}, u32[]{:S(2)}, u32[]{:S(2)}) %collective-permute-start.41) | collective-permute-done | bytes 786464 | tf_op jit(solution)/shard_map/ppermute | solution.py:51
  303.6 5.0 %norm_back.2 = (f32[192,2048]{1,0:T(8,128)}, bf16[192,2048]{1,0:T(8,128)(2,1)}) custom-call(f32[192,2048]{1,0:T(8,128)} %get-tuple-element.158.values, f32[4,2048]{1,0:T(4,128)} %convert_element_type.306.vectors, bf16[192,2048]{1,0:T(8,128)(2,1)} %bitcast.209, bf16[192,2048]{1,0:T(8,128)(2,1)} %fusion.15.refs_0_, ...), custom_call_target="tpu_custom_call" | custom-call | flops 7864320 | bytes 78643200 | tf_op jit(solution)/shard_map/norm_back/pallas_call | solution.py:335
  316.7 9.2 %add_convert_fusion = bf16[768,2048]{1,0:T(8,128)(2,1)S(1)} fusion(f32[768,2048]{1,0:T(8,128)S(1)} %fusion.100, bf16[768,2048]{1,0:T(8,128)(2,1)S(1)} %copy-done.30, bf16[2048,2048]{1,0:T(8,128)(2,1)} %copy-done.32), kind=kOutput, calls=%fused_computation.7 | convolution fusion | flops 6445596672 | bytes 20971520 | tf_op jit(solution)/shard_map/dot_general | solution.py:38
  349.5 9.6 %attend_back.1 = (bf16[4,3,64,768]{3,2,1,0:T(8,128)(2,1)}, bf16[4,3,64,768]{3,2,1,0:T(8,128)(2,1)}) custom-call(s32[512,1]{1,0:T(8,128)} %copy.49.pq, s32[1,512]{1,0:T(1,128)} %bitcast.234, s32[3,512,1]{2,1,0:T(8,128)} %copy.50.lq, s32[3,1,512]{2,1,0:T(1,128)} %broadcast_in_dim.87.lk, bf16[4,3,64,768]{3,2,1,0:T(8,128)(2,1)} %bitcast.219, ...), custom_call_target="tpu_custom_call" | custom-call | flops 2013265920 | bytes 5505024 | tf_op jit(solution)/shard_map/attend_back/pallas_call | solution.py:487
  399.2 5.3 %collective-permute-done.50 = bf16[96,2048]{1,0:T(8,128)(2,1)S(1)} collective-permute-done((bf16[96,2048]{1,0:T(8,128)(2,1)S(1)}, bf16[96,2048]{1,0:T(8,128)(2,1)S(1)}, u32[]{:S(2)}, u32[]{:S(2)}) %collective-permute-start.50) | collective-permute-done | bytes 393248 | tf_op jit(solution)/shard_map/ppermute | solution.py:51
  427.1 11.3 %collective-permute-done.57.refs_1_ = bf16[192,2048]{1,0:T(8,128)(2,1)S(1)} collective-permute-done((bf16[192,2048]{1,0:T(8,128)(2,1)}, bf16[192,2048]{1,0:T(8,128)(2,1)S(1)}, u32[]{:S(2)}, u32[]{:S(2)}) %collective-permute-start.57) | collective-permute-done | bytes 786464 | tf_op jit(solution)/shard_map/ppermute | solution.py:51
  440.2 4.5 norm_back.3
  (619 shorter events, 266.7 us)
Async XLA Ops:
  0.7 35.0 %collective-permute-start.1 = (bf16[1024,2048]{1,0:T(8,128)(2,1)}, bf16[1024,2048]{1,0:T(8,128)(2,1)}, u32[]{:S(2)}, u32[]{:S(2)}) collective-permute-start(bf16[1024,2048]{1,0:T(8,128)(2,1)} %param.47), channel_id=1, source_target_pairs={{0,4},{4,0},{8,12},{12,8},{16,20},{20,16},{24,28},{28,24},{1,5},{5... | collective-permute-start | bytes 12582920 | tf_op jit(solution)/shard_map/ppermute | solution.py:51
  1.3 31.7 %collective-permute-start = (bf16[256,2048]{1,0:T(8,128)(2,1)}, bf16[256,2048]{1,0:T(8,128)(2,1)S(1)}, u32[]{:S(2)}, u32[]{:S(2)}) collective-permute-start(bf16[256,2048]{1,0:T(8,128)(2,1)} %param.41), channel_id=1, source_target_pairs={{0,4},{4,0},{8,12},{12,8},{16,20},{20,16},{24,28},{28,24},{1,5},{5... | collective-permute-start | bytes 3145736 | tf_op jit(solution)/shard_map/ppermute | solution.py:51
  10.1 22.0 %collective-permute-start.6 = (bf16[128,1536]{1,0:T(8,128)(2,1)}, bf16[128,1536]{1,0:T(8,128)(2,1)S(1)}, u32[]{:S(2)}, u32[]{:S(2)}) collective-permute-start(bf16[128,1536]{1,0:T(8,128)(2,1)} %get-tuple-element.120), channel_id=1, source_target_pairs={{0,24},{4,28},{8,16},{12,20},{16,8},{20,12},{24,0},{28,4},{1,25},{... | collective-permute-start | bytes 1179656 | tf_op jit(solution)/shard_map/ppermute | solution.py:51
  19.6 33.3 %collective-permute-start.7 = (bf16[128,2048]{1,0:T(8,128)(2,1)}, bf16[128,2048]{1,0:T(8,128)(2,1)S(1)}, u32[]{:S(2)}, u32[]{:S(2)}) collective-permute-start(bf16[128,2048]{1,0:T(8,128)(2,1)} %get-tuple-element.127), channel_id=1, source_target_pairs={{0,8},{4,12},{8,0},{12,4},{16,24},{20,28},{24,16},{28,20},{1,9},{5... | collective-permute-start | bytes 1572872 | tf_op jit(solution)/shard_map/ppermute | solution.py:51
  28.2 31.3 %collective-permute-start.8 = (bf16[128,2048]{1,0:T(8,128)(2,1)}, bf16[128,2048]{1,0:T(8,128)(2,1)S(1)}, u32[]{:S(2)}, u32[]{:S(2)}) collective-permute-start(bf16[128,2048]{1,0:T(8,128)(2,1)} %get-tuple-element.128), channel_id=1, source_target_pairs={{0,16},{4,20},{8,24},{12,28},{16,0},{20,4},{24,8},{28,12},{1,17},{... | collective-permute-start | bytes 1572872 | tf_op jit(solution)/shard_map/ppermute | solution.py:51
  32.2 27.3 %collective-permute-start.9 = (bf16[128,2048]{1,0:T(8,128)(2,1)}, bf16[128,2048]{1,0:T(8,128)(2,1)}, u32[]{:S(2)}, u32[]{:S(2)}) collective-permute-start(bf16[128,2048]{1,0:T(8,128)(2,1)} %get-tuple-element.129), channel_id=1, source_target_pairs={{0,24},{4,28},{8,16},{12,20},{16,8},{20,12},{24,0},{28,4},{1,25},{... | collective-permute-start | bytes 1572872 | tf_op jit(solution)/shard_map/ppermute | solution.py:51
  32.9 26.5 %collective-permute-start.14 = (bf16[384,1536]{1,0:T(8,128)(2,1)}, bf16[384,1536]{1,0:T(8,128)(2,1)}, u32[]{:S(2)}, u32[]{:S(2)}) collective-permute-start(bf16[384,1536]{1,0:T(8,128)(2,1)} %constant_dynamic-update-slice_fusion.12.refs_1_), channel_id=1, source_target_pairs={{0,1},{1,0},{2,3},{3,2},{4,5},{5,4},{6,7},{7,6},{8,9},{9,8},{10,11... | collective-permute-start | bytes 3538952 | tf_op jit(solution)/shard_map/ppermute | solution.py:51
  52.9 44.7 %collective-permute-start.16 = (bf16[384,1536]{1,0:T(8,128)(2,1)}, bf16[384,1536]{1,0:T(8,128)(2,1)S(1)}, u32[]{:S(2)}, u32[]{:S(2)}) collective-permute-start(bf16[384,1536]{1,0:T(8,128)(2,1)} %constant_dynamic-update-slice_fusion.12.refs_1_), channel_id=1, source_target_pairs={{0,4},{4,0},{8,12},{12,8},{16,20},{20,16},{24,28},{28,24},{1,5},{5... | collective-permute-start | bytes 3538952 | tf_op jit(solution)/shard_map/ppermute | solution.py:51
  59.5 40.1 %collective-permute-start.17 = (bf16[384,1536]{1,0:T(8,128)(2,1)}, bf16[384,1536]{1,0:T(8,128)(2,1)S(1)}, u32[]{:S(2)}, u32[]{:S(2)}) collective-permute-start(bf16[384,1536]{1,0:T(8,128)(2,1)} %collective-permute-done.14.refs_2_), channel_id=1, source_target_pairs={{0,4},{4,0},{8,12},{12,8},{16,20},{20,16},{24,28},{28,24},{1,5},{5... | collective-permute-start | bytes 3538952 | tf_op jit(solution)/shard_map/ppermute | solution.py:51
  59.5 20.0 %collective-permute-start.10 = (bf16[192,2048]{1,0:T(8,128)(2,1)S(1)}, bf16[192,2048]{1,0:T(8,128)(2,1)S(1)}, u32[]{:S(2)}, u32[]{:S(2)}) collective-permute-start(bf16[192,2048]{1,0:T(8,128)(2,1)S(1)} %fusion.27), channel_id=1, source_target_pairs={{0,8},{4,12},{8,0},{12,4},{16,24},{20,28},{24,16},{28,20},{1,9},{5... | collective-permute-start | bytes 2359304 | tf_op jit(solution)/shard_map/ppermute | solution.py:51
  140.4 20.7 %collective-permute-start.22 = (bf16[192,2048]{1,0:T(8,128)(2,1)}, bf16[192,2048]{1,0:T(8,128)(2,1)S(1)}, u32[]{:S(2)}, u32[]{:S(2)}) collective-permute-start(bf16[192,2048]{1,0:T(8,128)(2,1)} %bitcast.207), channel_id=1, source_target_pairs={{0,8},{4,12},{8,0},{12,4},{16,24},{20,28},{24,16},{28,20},{1,9},{5... | collective-permute-start | bytes 2359304 | tf_op jit(solution)/shard_map/ppermute | solution.py:51
  141.7 21.2 %collective-permute-start.23 = (bf16[192,2048]{1,0:T(8,128)(2,1)}, bf16[192,2048]{1,0:T(8,128)(2,1)S(1)}, u32[]{:S(2)}, u32[]{:S(2)}) collective-permute-start(bf16[192,2048]{1,0:T(8,128)(2,1)} %bitcast.208), channel_id=1, source_target_pairs={{0,16},{4,20},{8,24},{12,28},{16,0},{20,4},{24,8},{28,12},{1,17},{... | collective-permute-start | bytes 2359304 | tf_op jit(solution)/shard_map/ppermute | solution.py:51
  143.4 55.7 %collective-permute-start.34 = (bf16[384,2048]{1,0:T(8,128)(2,1)}, bf16[384,2048]{1,0:T(8,128)(2,1)}, u32[]{:S(2)}, u32[]{:S(2)}) collective-permute-start(bf16[384,2048]{1,0:T(8,128)(2,1)} %constant_dynamic-update-slice_fusion.5.refs_1_), channel_id=1, source_target_pairs={{0,1},{1,0},{2,3},{3,2},{4,5},{5,4},{6,7},{7,6},{8,9},{9,8},{10,11... | collective-permute-start | bytes 4718600 | tf_op jit(solution)/shard_map/ppermute | solution.py:51
  169.7 25.7 %collective-permute-start.29 = (bf16[192,2048]{1,0:T(8,128)(2,1)S(1)}, bf16[192,2048]{1,0:T(8,128)(2,1)}, u32[]{:S(2)}, u32[]{:S(2)}) collective-permute-start(bf16[192,2048]{1,0:T(8,128)(2,1)S(1)} %pad_maximum_fusion.6), channel_id=1, source_target_pairs={{0,16},{4,20},{8,24},{12,28},{16,0},{20,4},{24,8},{28,12},{1,17},{... | collective-permute-start | bytes 2359304 | tf_op jit(solution)/shard_map/ppermute | solution.py:51
  171.7 23.7 %collective-permute-start.28 = (bf16[192,2048]{1,0:T(8,128)(2,1)S(1)}, bf16[192,2048]{1,0:T(8,128)(2,1)}, u32[]{:S(2)}, u32[]{:S(2)}) collective-permute-start(bf16[192,2048]{1,0:T(8,128)(2,1)S(1)} %pad_maximum_fusion.5), channel_id=1, source_target_pairs={{0,8},{4,12},{8,0},{12,4},{16,24},{20,28},{24,16},{28,20},{1,9},{5... | collective-permute-start | bytes 2359304 | tf_op jit(solution)/shard_map/ppermute | solution.py:51
  199.1 27.0 %collective-permute-start.36 = (bf16[384,2048]{1,0:T(8,128)(2,1)}, bf16[384,2048]{1,0:T(8,128)(2,1)}, u32[]{:S(2)}, u32[]{:S(2)}) collective-permute-start(bf16[384,2048]{1,0:T(8,128)(2,1)} %constant_dynamic-update-slice_fusion.5.refs_1_), channel_id=1, source_target_pairs={{0,4},{4,0},{8,12},{12,8},{16,20},{20,16},{24,28},{28,24},{1,5},{5... | collective-permute-start | bytes 4718600 | tf_op jit(solution)/shard_map/ppermute | solution.py:51
  199.1 27.0 %collective-permute-start.37 = (bf16[384,2048]{1,0:T(8,128)(2,1)}, bf16[384,2048]{1,0:T(8,128)(2,1)}, u32[]{:S(2)}, u32[]{:S(2)}) collective-permute-start(bf16[384,2048]{1,0:T(8,128)(2,1)} %collective-permute-done.34.refs_2_), channel_id=1, source_target_pairs={{0,4},{4,0},{8,12},{12,8},{16,20},{20,16},{24,28},{28,24},{1,5},{5... | collective-permute-start | bytes 4718600 | tf_op jit(solution)/shard_map/ppermute | solution.py:51
  201.1 21.4 %collective-permute-start.31 = (bf16[192,2048]{1,0:T(8,128)(2,1)}, bf16[192,2048]{1,0:T(8,128)(2,1)S(1)}, u32[]{:S(2)}, u32[]{:S(2)}) collective-permute-start(bf16[192,2048]{1,0:T(8,128)(2,1)} %get-tuple-element.159), channel_id=1, source_target_pairs={{0,16},{4,20},{8,24},{12,28},{16,0},{20,4},{24,8},{28,12},{1,17},{... | collective-permute-start | bytes 2359304 | tf_op jit(solution)/shard_map/ppermute | solution.py:51
  202.9 23.2 %collective-permute-start.35 = (bf16[256,2048]{1,0:T(8,128)(2,1)}, bf16[256,2048]{1,0:T(8,128)(2,1)}, u32[]{:S(2)}, u32[]{:S(2)}) collective-permute-start(bf16[256,2048]{1,0:T(8,128)(2,1)} %get-tuple-element.162.refs_0_), channel_id=1, source_target_pairs={{0,4},{4,0},{8,12},{12,8},{16,20},{20,16},{24,28},{28,24},{1,5},{5... | collective-permute-start | bytes 3145736 | tf_op jit(solution)/shard_map/ppermute | solution.py:51
  295.1 86.6 %collective-permute-start.61 = (bf16[2,64,2048]{2,1,0:T(8,128)(2,1)}, bf16[2,64,2048]{2,1,0:T(8,128)(2,1)}, u32[]{:S(2)}, u32[]{:S(2)}) collective-permute-start(bf16[2,64,2048]{2,1,0:T(8,128)(2,1)} %pad_maximum_fusion.12), channel_id=1, source_target_pairs={{0,2},{1,3},{2,0},{3,1},{4,6},{5,7},{6,4},{7,5},{8,10},{9,11},{10,... | collective-permute-start | bytes 1572872 | tf_op jit(solution)/shard_map/ppermute | solution.py:51
  362.7 48.0 %collective-permute-start.54 = (bf16[192,2304]{1,0:T(8,128)(2,1)}, bf16[192,2304]{1,0:T(8,128)(2,1)}, u32[]{:S(2)}, u32[]{:S(2)}) collective-permute-start(bf16[192,2304]{1,0:T(8,128)(2,1)} %pad_maximum_fusion.3), channel_id=1, source_target_pairs={{0,8},{4,12},{8,0},{12,4},{16,24},{20,28},{24,16},{28,20},{1,9},{5... | collective-permute-start | bytes 2654216 | tf_op jit(solution)/shard_map/ppermute | solution.py:51
  366.1 44.6 %collective-permute-start.56 = (bf16[192,2304]{1,0:T(8,128)(2,1)}, bf16[192,2304]{1,0:T(8,128)(2,1)}, u32[]{:S(2)}, u32[]{:S(2)}) collective-permute-start(bf16[192,2304]{1,0:T(8,128)(2,1)} %pad_maximum_fusion.4), channel_id=1, source_target_pairs={{0,16},{4,20},{8,24},{12,28},{16,0},{20,4},{24,8},{28,12},{1,17},{... | collective-permute-start | bytes 2654216 | tf_op jit(solution)/shard_map/ppermute | solution.py:51
  420.6 24.1 %collective-permute-start.68 = (bf16[2,48,768]{2,1,0:T(8,128)(2,1)S(1)}, bf16[2,48,768]{2,1,0:T(8,128)(2,1)}, u32[]{:S(2)}, u32[]{:S(2)}) collective-permute-start(bf16[2,48,768]{2,1,0:T(8,128)(2,1)S(1)} %pad_maximum_fusion.22), channel_id=1, source_target_pairs={{0,2},{1,3},{2,0},{3,1},{4,6},{5,7},{6,4},{7,5},{8,10},{9,11},{10,... | collective-permute-start | bytes 442376 | tf_op jit(solution)/shard_map/ppermute | solution.py:51
  422.1 22.6 %collective-permute-start.65 = (bf16[2,48,1792]{2,1,0:T(8,128)(2,1)}, bf16[2,48,1792]{2,1,0:T(8,128)(2,1)S(1)}, u32[]{:S(2)}, u32[]{:S(2)}) collective-permute-start(bf16[2,48,1792]{2,1,0:T(8,128)(2,1)} %pad_maximum_fusion.14), channel_id=1, source_target_pairs={{0,2},{1,3},{2,0},{3,1},{4,6},{5,7},{6,4},{7,5},{8,10},{9,11},{10,... | collective-permute-start | bytes 1032200 | tf_op jit(solution)/shard_map/ppermute | solution.py:51
  (181 other events, 2045.6 us)

commit v11 on v10

--- a/solution.py
+++ b/solution.py
@@ -595,17 +595,15 @@
     )
     hidden_one, one_first, one_last = gather_rows(hidden_block, bits)
 
-    turned[0] = after(turned[0], *one_first)
-    w_qkv_mine, w_qkv_other = place_weights(
-        at, both_cores(with_halves(turned)), chips, 3 * span, False
-    )
+    halves_qkv = after(tuple(with_halves(turned)), *one_first)
+    w_qkv_mine, w_qkv_other = place_weights(at, both_cores(halves_qkv), chips, 3 * span, False)
     w_out_late, w_down_late, *near_up = after((w_out, w_down, *near_up), hidden_block)
     merged_up = jnp.concatenate(near_up[1:], 0)
     w_out_chip = jnp.concatenate([w_out_late, w_out_other], 0)
     w_down_chip = jnp.concatenate([w_down_late, w_down_other], 0)
     hidden_one = after(hidden_one, merged_up, w_out_chip, w_down_chip)
     cot_mine = cotangent[0].reshape(block, wide)
-    near = after(jnp.concatenate([mine[None], near_one], 0), *one_first)
+    near = after(jnp.concatenate([mine[None], near_one], 0), hidden_block)
     for bit in bits[1:]:
         near = jnp.concatenate([near, swap(near, "shard", bit)], 0)
     stacked = jnp.concatenate([near, swap(near, "shard", 1)], 0)

time: 456 us -> 452 us (level)
    unnamed x291 -> x295, local copies, waits for them, and re-layouts: 28.7 us -> 26.2 us
  transfers between devices with their start and end apart: 69 -> 69, of which waited for: 26 -> 25; matrix products, arithmetic and copies ran while one was open for 32% -> 34% of each run, Pallas kernels for 11% -> 10%
where the time goes in v11:
time: 452 us; the launch traced here: 445 us
  matrix products  118 us (26%)
  waiting for transfers between devices  110 us (24%)
  Pallas kernels  64.6 us (14%)
  starting transfers between devices  59.7 us (13%)
  local copies, waits for them, and re-layouts  52.4 us (12%)
  other arithmetic  34.1 us (8%)
  between operations  5.62 us (1%)
    ppermute x69, waiting for transfers between devices, swap(): return lax.ppermute(value, axis, [(i, i ^ mask) for i in range(size)])  110 us
    ppermute x69, starting transfers between devices, swap(): return lax.ppermute(value, axis, [(i, i ^ mask) for i in range(size)])  59.7 us
    dot_general x26, matrix products, mm(): lax.dot_general(a, b, (((1,), (0,)), ((), ())), preferred_element_type=F32)  56.2 us
    dot_general x23, matrix products, mm_t(): lax.dot_general(a, b, (((1,), (1,)), ((), ())), preferred_element_type=F32)  53.9 us
    unnamed x295, local copies, waits for them, and re-layouts  26.2 us
    pallas_call x2, Pallas kernels, place_weights(): pl.pallas_call(functools.partial(place_kernel, count=count, width=width,...  14 us
    pallas_call x3, Pallas kernels, row_call(): pl.pallas_call(kernel, out_shape=[jax.ShapeDtypeStruct((rows, wide), d) f...  13.3 us
    pallas_call x1, Pallas kernels, attend_back(): pl.pallas_call(functools.partial(attend_back_kernel, heads=heads, factor=...  9.71 us
  transfers between devices with their start and end apart: 69, of which 25 were waited for; matrix products, arithmetic and copies ran while one was open for 34% of the time, Pallas kernels for 10%

profile of v11, /device:TPU:0, one launch (start us, length us, event | category | flops | bytes accessed | tf_op | source)
XLA Modules:
  0.0 444.8 jit_solution(6038910597066157451)
XLA Ops:
  13.7 3.9 cut_pieces.3
  21.6 5.8 %collective-permute-done.5 = bf16[128,1536]{1,0:T(8,128)(2,1)S(1)} collective-permute-done((bf16[128,1536]{1,0:T(8,128)(2,1)}, bf16[128,1536]{1,0:T(8,128)(2,1)S(1)}, u32[]{:S(2)}, u32[]{:S(2)}) %collective-permute-start.5) | collective-permute-done | bytes 393248 | tf_op jit(solution)/shard_map/ppermute | solution.py:51
  38.4 13.9 %collective-permute-done.3 = bf16[1,288,256]{2,1,0:T(8,128)(2,1)S(1)} collective-permute-done((bf16[1,288,256]{2,1,0:T(8,128)(2,1)}, bf16[1,288,256]{2,1,0:T(8,128)(2,1)S(1)}, u32[]{:S(2)}, u32[]{:S(2)}) %collective-permute-start.3) | collective-permute-done | bytes 147488 | tf_op jit(solution)/shard_map/ppermute | solution.py:51
  75.3 5.9 %collective-permute-done.18 = bf16[2,288,256]{2,1,0:T(8,128)(2,1)S(1)} collective-permute-done((bf16[2,288,256]{2,1,0:T(8,128)(2,1)S(1)}, bf16[2,288,256]{2,1,0:T(8,128)(2,1)S(1)}, u32[]{:S(2)}, u32[]{:S(2)}) %collective-permute-start.18) | collective-permute-done | bytes 294944 | tf_op jit(solution)/shard_map/ppermute | solution.py:51
  90.0 4.4 %collective-permute-done.12 = bf16[96,2048]{1,0:T(8,128)(2,1)S(1)} collective-permute-done((bf16[96,2048]{1,0:T(8,128)(2,1)}, bf16[96,2048]{1,0:T(8,128)(2,1)S(1)}, u32[]{:S(2)}, u32[]{:S(2)}) %collective-permute-start.12) | collective-permute-done | bytes 393248 | tf_op jit(solution)/shard_map/ppermute | solution.py:51
  102.4 6.5 %place_weights.2 = (bf16[2048,768]{1,0:T(8,128)(2,1)}, bf16[2048,768]{1,0:T(8,128)(2,1)}) custom-call(s32[2]{0:T(128)} %pad_add_fusion.1.at_ref, bf16[256,1536]{1,0:T(8,128)(2,1)} %get-tuple-element.142.refs_0_, bf16[384,1536]{1,0:T(8,128)(2,1)} %constant_dynamic-update-slice_fusion.12.refs_1_, bf16[384,1536]{1,0:T(8,128)(2,1)} %collective-permute-done.14.refs_2_, ...), custom_call_target="tpu_custom_call" | custom-call | bytes 12582912 | tf_op jit(solution)/shard_map/place_weights/pallas_call | solution.py:208
  109.1 5.9 %add_convert_fusion.2 = bf16[768,768]{1,0:T(8,128)(2,1)} fusion(f32[768,768]{1,0:T(8,128)} %fusion.190, bf16[768,2048]{1,0:T(8,128)(2,1)S(1)} %constant_dynamic-update-slice_fusion, bf16[2048,768]{1,0:T(8,128)(2,1)} %get-tuple-element.150, f32[768]{0:T(1024)S(1)} %copy-done.108), kind=kOutput, calls=%fused_computation.57 | convolution fusion | flops 2417688576 | bytes 9833472 | tf_op jit(solution)/shard_map/dot_general | solution.py:38
  119.2 5.5 %add_convert_fusion.3 = bf16[768,768]{1,0:T(8,128)(2,1)} fusion(f32[768,768]{1,0:T(8,128)S(1)} %fusion.189, bf16[768,2048]{1,0:T(8,128)(2,1)} %copy-done.16, bf16[2048,768]{1,0:T(8,128)(2,1)S(1)} %copy-done.1, f32[768]{0:T(1024)S(1)} %copy-done.107), kind=kOutput, calls=%fused_computation.58 | convolution fusion | flops 2417688576 | bytes 9833472 | tf_op jit(solution)/shard_map/dot_general | solution.py:38
  124.7 7.1 %attend.1 = (bf16[4,3,64,256]{3,2,1,0:T(8,128)(2,1)}, bf16[4,3,64,256]{3,2,1,0:T(8,128)(2,1)}, f32[3,512,2]{2,1,0:T(8,128)}) custom-call(s32[512,1]{1,0:T(8,128)} %copy.49.pq, s32[1,512]{1,0:T(1,128)} %bitcast.232, s32[3,512,1]{2,1,0:T(8,128)} %copy.50.lq, s32[3,1,512]{2,1,0:T(1,128)} %broadcast_in_dim.87.lk, bf16[4,3,64,768]{3,2,1,0:T(8,128)(2,1)} %bitcast.218, ...), custom_call_target="tpu_custom_call" | custom-call | flops 805306368 | bytes 3145728 | tf_op jit(solution)/shard_map/attend/pallas_call | solution.py:430
  156.9 6.3 %collective-permute-done.27 = bf16[96,2048]{1,0:T(8,128)(2,1)S(1)} collective-permute-done((bf16[96,2048]{1,0:T(8,128)(2,1)S(1)}, bf16[96,2048]{1,0:T(8,128)(2,1)S(1)}, u32[]{:S(2)}, u32[]{:S(2)}) %collective-permute-start.27) | collective-permute-done | bytes 393248 | tf_op jit(solution)/shard_map/ppermute | solution.py:51
  165.5 6.7 %collective-permute-done.24 = bf16[96,2048]{1,0:T(8,128)(2,1)S(1)} collective-permute-done((bf16[96,2048]{1,0:T(8,128)(2,1)S(1)}, bf16[96,2048]{1,0:T(8,128)(2,1)S(1)}, u32[]{:S(2)}, u32[]{:S(2)}) %collective-permute-start.24) | collective-permute-done | bytes 393248 | tf_op jit(solution)/shard_map/ppermute | solution.py:51
  175.3 10.5 %add_convert_fusion.1 = bf16[768,2048]{1,0:T(8,128)(2,1)} fusion(f32[768,2048]{1,0:T(8,128)S(1)} %fusion.110, bf16[768,2048]{1,0:T(8,128)(2,1)S(1)} %constant_dynamic-update-slice_fusion.15, bf16[2048,2048]{1,0:T(8,128)(2,1)} %copy-done.35), kind=kOutput, calls=%fused_computation.11 | convolution fusion | flops 6445596672 | bytes 20971520 | tf_op jit(solution)/shard_map/dot_general | solution.py:42
  188.0 3.7 norm.1
  197.7 14.9 %collective-permute-done.30 = bf16[192,2048]{1,0:T(8,128)(2,1)S(1)} collective-permute-done((bf16[192,2048]{1,0:T(8,128)(2,1)}, bf16[192,2048]{1,0:T(8,128)(2,1)S(1)}, u32[]{:S(2)}, u32[]{:S(2)}) %collective-permute-start.30) | collective-permute-done | bytes 786464 | tf_op jit(solution)/shard_map/ppermute | solution.py:51
  218.2 7.5 %place_weights.3 = bf16[2048,2048]{1,0:T(8,128)(2,1)} custom-call(s32[2]{0:T(128)} %pad_add_fusion.1.at_ref, bf16[256,2048]{1,0:T(8,128)(2,1)} %get-tuple-element.166.refs_0_, bf16[384,2048]{1,0:T(8,128)(2,1)} %copy-done.33, bf16[384,2048]{1,0:T(8,128)(2,1)} %collective-permute-done.34.refs_2_, bf16[256,2048]{1,0:T(8,128)(2,1)} %collective-permute-done.35.refs_3_, ...), custom_call_target="tpu_custom_call" | custom-call | bytes 16777216 | tf_op jit(solution)/shard_map/place_weights/pallas_call | solution.py:208
  235.2 12.0 %multiply_convert_fusion = (bf16[768,2048]{1,0:T(8,128)(2,1)S(1)}, bf16[768,2048]{1,0:T(8,128)(2,1)S(1)}) fusion(bf16[768,2048]{1,0:T(8,128)(2,1)} %add_convert_fusion.1, f32[2048]{0:T(1024)} %maximum_convert_fusion, f32[768,2048]{1,0:T(8,128)S(1)} %fusion.109, bf16[768,2048]{1,0:T(8,128)(2,1)} %constant_dynamic-update-slice_fusion.20, ...), kind=kOutput, calls=%fused_computation.8 | convolution fusion | flops 6466043904 | bytes 27271168 | tf_op jit(solution)/shard_map/dot_general | solution.py:38
  267.5 6.9 %collective-permute-done.40 = bf16[96,2048]{1,0:T(8,128)(2,1)S(1)} collective-permute-done((bf16[96,2048]{1,0:T(8,128)(2,1)S(1)}, bf16[96,2048]{1,0:T(8,128)(2,1)S(1)}, u32[]{:S(2)}, u32[]{:S(2)}) %collective-permute-start.40) | collective-permute-done | bytes 393248 | tf_op jit(solution)/shard_map/ppermute | solution.py:51
  280.3 6.1 %collective-permute-done.60.refs_1_ = bf16[1,64,2048]{2,1,0:T(8,128)(2,1)} collective-permute-done((bf16[1,64,2048]{2,1,0:T(8,128)(2,1)S(1)}, bf16[1,64,2048]{2,1,0:T(8,128)(2,1)}, u32[]{:S(2)}, u32[]{:S(2)}) %collective-permute-start.60) | collective-permute-done | bytes 262176 | tf_op jit(solution)/shard_map/ppermute | solution.py:51
  297.2 5.0 %norm_back.2 = (f32[192,2048]{1,0:T(8,128)}, bf16[192,2048]{1,0:T(8,128)(2,1)}) custom-call(f32[192,2048]{1,0:T(8,128)} %get-tuple-element.162.values, f32[4,2048]{1,0:T(4,128)} %convert_element_type.306.vectors, bf16[192,2048]{1,0:T(8,128)(2,1)} %bitcast.209, bf16[192,2048]{1,0:T(8,128)(2,1)} %fusion.15.refs_0_, ...), custom_call_target="tpu_custom_call" | custom-call | flops 7864320 | bytes 78643200 | tf_op jit(solution)/shard_map/norm_back/pallas_call | solution.py:335
  308.6 9.2 %add_convert_fusion = bf16[768,2048]{1,0:T(8,128)(2,1)S(1)} fusion(f32[768,2048]{1,0:T(8,128)S(1)} %fusion.99, bf16[768,2048]{1,0:T(8,128)(2,1)S(1)} %copy-done.32, bf16[2048,2048]{1,0:T(8,128)(2,1)} %copy-done.35), kind=kOutput, calls=%fused_computation.7 | convolution fusion | flops 6445596672 | bytes 20971520 | tf_op jit(solution)/shard_map/dot_general | solution.py:38
  342.3 9.7 %attend_back.1 = (bf16[4,3,64,768]{3,2,1,0:T(8,128)(2,1)}, bf16[4,3,64,768]{3,2,1,0:T(8,128)(2,1)}) custom-call(s32[512,1]{1,0:T(8,128)} %copy.49.pq, s32[1,512]{1,0:T(1,128)} %bitcast.233, s32[3,512,1]{2,1,0:T(8,128)} %copy.50.lq, s32[3,1,512]{2,1,0:T(1,128)} %broadcast_in_dim.87.lk, bf16[4,3,64,768]{3,2,1,0:T(8,128)(2,1)} %bitcast.219, ...), custom_call_target="tpu_custom_call" | custom-call | flops 2013265920 | bytes 5505024 | tf_op jit(solution)/shard_map/attend_back/pallas_call | solution.py:487
  393.3 6.1 %collective-permute-done.50 = bf16[96,2048]{1,0:T(8,128)(2,1)S(1)} collective-permute-done((bf16[96,2048]{1,0:T(8,128)(2,1)S(1)}, bf16[96,2048]{1,0:T(8,128)(2,1)S(1)}, u32[]{:S(2)}, u32[]{:S(2)}) %collective-permute-start.50) | collective-permute-done | bytes 393248 | tf_op jit(solution)/shard_map/ppermute | solution.py:51
  422.5 10.7 %collective-permute-done.57.refs_1_ = bf16[192,2048]{1,0:T(8,128)(2,1)S(1)} collective-permute-done((bf16[192,2048]{1,0:T(8,128)(2,1)}, bf16[192,2048]{1,0:T(8,128)(2,1)S(1)}, u32[]{:S(2)}, u32[]{:S(2)}) %collective-permute-start.57) | collective-permute-done | bytes 786464 | tf_op jit(solution)/shard_map/ppermute | solution.py:51
  435.1 4.5 %norm_back.3 = bf16[192,2048]{1,0:T(8,128)(2,1)} custom-call(bf16[192,2048]{1,0:T(8,128)(2,1)} %bitcast.196, f32[4,2048]{1,0:T(4,128)} %convert_element_type.306.vectors, f32[192,2048]{1,0:T(8,128)} %get-tuple-element.206.base, bf16[192,2048]{1,0:T(8,128)(2,1)} %fusion.8.refs_0_, bf16[192,2048]{1,0:T(8,128)(2,1)} %copy-done.49, bf16[192,2048]{1,0:T(8,128)(2,1)} %copy-done.50), custom_call_target="tpu_custom_call" | custom-call | flops 7864320 | bytes 78643200 | tf_op jit(solution)/shard_map/norm_back/pallas_call | solution.py:335
  (623 shorter events, 260.3 us)
Async XLA Ops:
  0.7 32.2 %collective-permute-start.1 = (bf16[1024,2048]{1,0:T(8,128)(2,1)}, bf16[1024,2048]{1,0:T(8,128)(2,1)}, u32[]{:S(2)}, u32[]{:S(2)}) collective-permute-start(bf16[1024,2048]{1,0:T(8,128)(2,1)} %param.47), channel_id=1, source_target_pairs={{0,4},{4,0},{8,12},{12,8},{16,20},{20,16},{24,28},{28,24},{1,5},{5... | collective-permute-start | bytes 12582920 | tf_op jit(solution)/shard_map/ppermute | solution.py:51
  1.3 31.6 %collective-permute-start = (bf16[256,2048]{1,0:T(8,128)(2,1)}, bf16[256,2048]{1,0:T(8,128)(2,1)S(1)}, u32[]{:S(2)}, u32[]{:S(2)}) collective-permute-start(bf16[256,2048]{1,0:T(8,128)(2,1)} %param.41), channel_id=1, source_target_pairs={{0,4},{4,0},{8,12},{12,8},{16,20},{20,16},{24,28},{28,24},{1,5},{5... | collective-permute-start | bytes 3145736 | tf_op jit(solution)/shard_map/ppermute | solution.py:51
  10.1 22.0 %collective-permute-start.6 = (bf16[128,1536]{1,0:T(8,128)(2,1)}, bf16[128,1536]{1,0:T(8,128)(2,1)S(1)}, u32[]{:S(2)}, u32[]{:S(2)}) collective-permute-start(bf16[128,1536]{1,0:T(8,128)(2,1)} %get-tuple-element.122), channel_id=1, source_target_pairs={{0,24},{4,28},{8,16},{12,20},{16,8},{20,12},{24,0},{28,4},{1,25},{... | collective-permute-start | bytes 1179656 | tf_op jit(solution)/shard_map/ppermute | solution.py:51
  18.8 35.4 %collective-permute-start.7 = (bf16[128,2048]{1,0:T(8,128)(2,1)}, bf16[128,2048]{1,0:T(8,128)(2,1)S(1)}, u32[]{:S(2)}, u32[]{:S(2)}) collective-permute-start(bf16[128,2048]{1,0:T(8,128)(2,1)} %get-tuple-element.129), channel_id=1, source_target_pairs={{0,8},{4,12},{8,0},{12,4},{16,24},{20,28},{24,16},{28,20},{1,9},{5... | collective-permute-start | bytes 1572872 | tf_op jit(solution)/shard_map/ppermute | solution.py:51
  28.1 26.1 %collective-permute-start.8 = (bf16[128,2048]{1,0:T(8,128)(2,1)}, bf16[128,2048]{1,0:T(8,128)(2,1)S(1)}, u32[]{:S(2)}, u32[]{:S(2)}) collective-permute-start(bf16[128,2048]{1,0:T(8,128)(2,1)} %get-tuple-element.130), channel_id=1, source_target_pairs={{0,16},{4,20},{8,24},{12,28},{16,0},{20,4},{24,8},{28,12},{1,17},{... | collective-permute-start | bytes 1572872 | tf_op jit(solution)/shard_map/ppermute | solution.py:51
  32.1 22.1 %collective-permute-start.9 = (bf16[128,2048]{1,0:T(8,128)(2,1)}, bf16[128,2048]{1,0:T(8,128)(2,1)}, u32[]{:S(2)}, u32[]{:S(2)}) collective-permute-start(bf16[128,2048]{1,0:T(8,128)(2,1)} %get-tuple-element.131), channel_id=1, source_target_pairs={{0,24},{4,28},{8,16},{12,20},{16,8},{20,12},{24,0},{28,4},{1,25},{... | collective-permute-start | bytes 1572872 | tf_op jit(solution)/shard_map/ppermute | solution.py:51
  52.3 33.3 %collective-permute-start.14 = (bf16[384,1536]{1,0:T(8,128)(2,1)}, bf16[384,1536]{1,0:T(8,128)(2,1)}, u32[]{:S(2)}, u32[]{:S(2)}) collective-permute-start(bf16[384,1536]{1,0:T(8,128)(2,1)} %constant_dynamic-update-slice_fusion.12.refs_1_), channel_id=1, source_target_pairs={{0,1},{1,0},{2,3},{3,2},{4,5},{5,4},{6,7},{7,6},{8,9},{9,8},{10,11... | collective-permute-start | bytes 3538952 | tf_op jit(solution)/shard_map/ppermute | solution.py:51
  55.2 26.7 %collective-permute-start.10 = (bf16[192,2048]{1,0:T(8,128)(2,1)S(1)}, bf16[192,2048]{1,0:T(8,128)(2,1)S(1)}, u32[]{:S(2)}, u32[]{:S(2)}) collective-permute-start(bf16[192,2048]{1,0:T(8,128)(2,1)S(1)} %fusion.27), channel_id=1, source_target_pairs={{0,8},{4,12},{8,0},{12,4},{16,24},{20,28},{24,16},{28,20},{1,9},{5... | collective-permute-start | bytes 2359304 | tf_op jit(solution)/shard_map/ppermute | solution.py:51
  56.8 27.4 %collective-permute-start.11 = (bf16[192,2048]{1,0:T(8,128)(2,1)S(1)}, bf16[192,2048]{1,0:T(8,128)(2,1)S(1)}, u32[]{:S(2)}, u32[]{:S(2)}) collective-permute-start(bf16[192,2048]{1,0:T(8,128)(2,1)S(1)} %fusion.27), channel_id=1, source_target_pairs={{0,16},{4,20},{8,24},{12,28},{16,0},{20,4},{24,8},{28,12},{1,17},{... | collective-permute-start | bytes 2359304 | tf_op jit(solution)/shard_map/ppermute | solution.py:51
  59.7 21.6 %collective-permute-start.18 = (bf16[2,288,256]{2,1,0:T(8,128)(2,1)S(1)}, bf16[2,288,256]{2,1,0:T(8,128)(2,1)S(1)}, u32[]{:S(2)}, u32[]{:S(2)}) collective-permute-start(bf16[2,288,256]{2,1,0:T(8,128)(2,1)S(1)} %pad_maximum_fusion.15), channel_id=1, source_target_pairs={{0,16},{4,20},{8,24},{12,28},{16,0},{20,4},{24,8},{28,12},{1,17},{... | collective-permute-start | bytes 884744 | tf_op jit(solution)/shard_map/ppermute | solution.py:51
  134.1 20.7 %collective-permute-start.22 = (bf16[192,2048]{1,0:T(8,128)(2,1)}, bf16[192,2048]{1,0:T(8,128)(2,1)S(1)}, u32[]{:S(2)}, u32[]{:S(2)}) collective-permute-start(bf16[192,2048]{1,0:T(8,128)(2,1)} %bitcast.207), channel_id=1, source_target_pairs={{0,8},{4,12},{8,0},{12,4},{16,24},{20,28},{24,16},{28,20},{1,9},{5... | collective-permute-start | bytes 2359304 | tf_op jit(solution)/shard_map/ppermute | solution.py:51
  134.8 20.7 %collective-permute-start.23 = (bf16[192,2048]{1,0:T(8,128)(2,1)}, bf16[192,2048]{1,0:T(8,128)(2,1)S(1)}, u32[]{:S(2)}, u32[]{:S(2)}) collective-permute-start(bf16[192,2048]{1,0:T(8,128)(2,1)} %bitcast.208), channel_id=1, source_target_pairs={{0,16},{4,20},{8,24},{12,28},{16,0},{20,4},{24,8},{28,12},{1,17},{... | collective-permute-start | bytes 2359304 | tf_op jit(solution)/shard_map/ppermute | solution.py:51
  135.3 56.5 %collective-permute-start.34 = (bf16[384,2048]{1,0:T(8,128)(2,1)}, bf16[384,2048]{1,0:T(8,128)(2,1)}, u32[]{:S(2)}, u32[]{:S(2)}) collective-permute-start(bf16[384,2048]{1,0:T(8,128)(2,1)} %copy-done.33), channel_id=1, source_target_pairs={{0,1},{1,0},{2,3},{3,2},{4,5},{5,4},{6,7},{7,6},{8,9},{9,8},{10,11... | collective-permute-start | bytes 4718600 | tf_op jit(solution)/shard_map/ppermute | solution.py:51
  163.4 24.6 %collective-permute-start.29 = (bf16[192,2048]{1,0:T(8,128)(2,1)S(1)}, bf16[192,2048]{1,0:T(8,128)(2,1)}, u32[]{:S(2)}, u32[]{:S(2)}) collective-permute-start(bf16[192,2048]{1,0:T(8,128)(2,1)S(1)} %pad_maximum_fusion.6), channel_id=1, source_target_pairs={{0,16},{4,20},{8,24},{12,28},{16,0},{20,4},{24,8},{28,12},{1,17},{... | collective-permute-start | bytes 2359304 | tf_op jit(solution)/shard_map/ppermute | solution.py:51
  164.2 23.8 %collective-permute-start.28 = (bf16[192,2048]{1,0:T(8,128)(2,1)S(1)}, bf16[192,2048]{1,0:T(8,128)(2,1)}, u32[]{:S(2)}, u32[]{:S(2)}) collective-permute-start(bf16[192,2048]{1,0:T(8,128)(2,1)S(1)} %pad_maximum_fusion.5), channel_id=1, source_target_pairs={{0,8},{4,12},{8,0},{12,4},{16,24},{20,28},{24,16},{28,20},{1,9},{5... | collective-permute-start | bytes 2359304 | tf_op jit(solution)/shard_map/ppermute | solution.py:51
  191.7 26.5 %collective-permute-start.36 = (bf16[384,2048]{1,0:T(8,128)(2,1)}, bf16[384,2048]{1,0:T(8,128)(2,1)}, u32[]{:S(2)}, u32[]{:S(2)}) collective-permute-start(bf16[384,2048]{1,0:T(8,128)(2,1)} %copy-done.33), channel_id=1, source_target_pairs={{0,4},{4,0},{8,12},{12,8},{16,20},{20,16},{24,28},{28,24},{1,5},{5... | collective-permute-start | bytes 4718600 | tf_op jit(solution)/shard_map/ppermute | solution.py:51
  191.7 26.5 %collective-permute-start.37 = (bf16[384,2048]{1,0:T(8,128)(2,1)}, bf16[384,2048]{1,0:T(8,128)(2,1)}, u32[]{:S(2)}, u32[]{:S(2)}) collective-permute-start(bf16[384,2048]{1,0:T(8,128)(2,1)} %collective-permute-done.34.refs_2_), channel_id=1, source_target_pairs={{0,4},{4,0},{8,12},{12,8},{16,20},{20,16},{24,28},{28,24},{1,5},{5... | collective-permute-start | bytes 4718600 | tf_op jit(solution)/shard_map/ppermute | solution.py:51
  192.9 19.7 %collective-permute-start.30 = (bf16[192,2048]{1,0:T(8,128)(2,1)}, bf16[192,2048]{1,0:T(8,128)(2,1)S(1)}, u32[]{:S(2)}, u32[]{:S(2)}) collective-permute-start(bf16[192,2048]{1,0:T(8,128)(2,1)} %get-tuple-element.163), channel_id=1, source_target_pairs={{0,8},{4,12},{8,0},{12,4},{16,24},{20,28},{24,16},{28,20},{1,9},{5... | collective-permute-start | bytes 2359304 | tf_op jit(solution)/shard_map/ppermute | solution.py:51
  195.0 23.2 %collective-permute-start.35 = (bf16[256,2048]{1,0:T(8,128)(2,1)}, bf16[256,2048]{1,0:T(8,128)(2,1)}, u32[]{:S(2)}, u32[]{:S(2)}) collective-permute-start(bf16[256,2048]{1,0:T(8,128)(2,1)} %get-tuple-element.166.refs_0_), channel_id=1, source_target_pairs={{0,4},{4,0},{8,12},{12,8},{16,20},{20,16},{24,28},{28,24},{1,5},{5... | collective-permute-start | bytes 3145736 | tf_op jit(solution)/shard_map/ppermute | solution.py:51
  288.1 89.6 %collective-permute-start.61 = (bf16[2,64,2048]{2,1,0:T(8,128)(2,1)}, bf16[2,64,2048]{2,1,0:T(8,128)(2,1)}, u32[]{:S(2)}, u32[]{:S(2)}) collective-permute-start(bf16[2,64,2048]{2,1,0:T(8,128)(2,1)} %pad_maximum_fusion.12), channel_id=1, source_target_pairs={{0,2},{1,3},{2,0},{3,1},{4,6},{5,7},{6,4},{7,5},{8,10},{9,11},{10,... | collective-permute-start | bytes 1572872 | tf_op jit(solution)/shard_map/ppermute | solution.py:51
  356.6 49.0 %collective-permute-start.54 = (bf16[192,2304]{1,0:T(8,128)(2,1)}, bf16[192,2304]{1,0:T(8,128)(2,1)}, u32[]{:S(2)}, u32[]{:S(2)}) collective-permute-start(bf16[192,2304]{1,0:T(8,128)(2,1)} %pad_maximum_fusion.3), channel_id=1, source_target_pairs={{0,8},{4,12},{8,0},{12,4},{16,24},{20,28},{24,16},{28,20},{1,9},{5... | collective-permute-start | bytes 2654216 | tf_op jit(solution)/shard_map/ppermute | solution.py:51
  360.0 45.5 %collective-permute-start.56 = (bf16[192,2304]{1,0:T(8,128)(2,1)}, bf16[192,2304]{1,0:T(8,128)(2,1)}, u32[]{:S(2)}, u32[]{:S(2)}) collective-permute-start(bf16[192,2304]{1,0:T(8,128)(2,1)} %pad_maximum_fusion.4), channel_id=1, source_target_pairs={{0,16},{4,20},{8,24},{12,28},{16,0},{20,4},{24,8},{28,12},{1,17},{... | collective-permute-start | bytes 2654216 | tf_op jit(solution)/shard_map/ppermute | solution.py:51
  416.0 23.5 %collective-permute-start.68 = (bf16[2,48,768]{2,1,0:T(8,128)(2,1)S(1)}, bf16[2,48,768]{2,1,0:T(8,128)(2,1)}, u32[]{:S(2)}, u32[]{:S(2)}) collective-permute-start(bf16[2,48,768]{2,1,0:T(8,128)(2,1)S(1)} %pad_maximum_fusion.22), channel_id=1, source_target_pairs={{0,2},{1,3},{2,0},{3,1},{4,6},{5,7},{6,4},{7,5},{8,10},{9,11},{10,... | collective-permute-start | bytes 442376 | tf_op jit(solution)/shard_map/ppermute | solution.py:51
  419.5 20.2 %collective-permute-start.65 = (bf16[2,48,1792]{2,1,0:T(8,128)(2,1)}, bf16[2,48,1792]{2,1,0:T(8,128)(2,1)S(1)}, u32[]{:S(2)}, u32[]{:S(2)}) collective-permute-start(bf16[2,48,1792]{2,1,0:T(8,128)(2,1)} %pad_maximum_fusion.14), channel_id=1, source_target_pairs={{0,2},{1,3},{2,0},{3,1},{4,6},{5,7},{6,4},{7,5},{8,10},{9,11},{10,... | collective-permute-start | bytes 1032200 | tf_op jit(solution)/shard_map/ppermute | solution.py:51
  (183 other events, 1850.7 us)

commit v12 on v11

--- a/solution.py
+++ b/solution.py
@@ -648,17 +648,11 @@
         return value.reshape(chips * block, value.shape[-1])
 
     def block_products(products, low, table):
-        parts = {}
-        for i in reversed(range(chips)):
-            at = slice(i * block, (i + 1) * block)
-            total = mm(low[at], table)
-            for value, weight, main in products:
-                total = total + main(value[at], weight)
-            parts[2 * i] = total.astype(BF16)
-            if i == chips - 1:
-                low = after(low, parts[2 * i])
-                products = [(after(v, parts[2 * i]), w, main) for v, w, main in products]
-        return parts
+        total = mm(low, table)
+        for value, weight, main in products:
+            total = total + main(value, weight)
+        total = total.astype(BF16)
+        return {2 * i: total[i * block : (i + 1) * block] for i in range(chips)}
 
     low_qkv = keep_own(mm_t(hidden_one, in_qkv))
     qkv_away = (
@@ -718,8 +712,7 @@
 
     act_late = after(act, grad_block)
     low_red = keep_own(mm_t(act_late, in_red))
-    down = (mm(act_late, w_down_chip) + mm(low_red, out_red)).astype(BF16)
-    down_parts = {2 * i: down[i * block : (i + 1) * block] for i in range(chips)}
+    down_parts = block_products([(act_late, w_down_chip, mm)], low_red, out_red)
     glow_att = keep_own(mm_t(grad_branch, out_att))
     grad_att = (mm_t(grad_branch, w_out_chip) + mm(glow_att, in_att)).astype(BF16)
     ga_own = by_chip(grad_att[:, :span])

time: 452 us -> 448 us (level)
  matrix products: 118 us -> 101 us
  waiting for transfers between devices: 110 us -> 118 us
  local copies, waits for them, and re-layouts: 52.4 us -> 60.1 us
    dot_general x26 -> x14, matrix products: 56.2 us -> 46.1 us  [mm(): lax.dot_general(a, b, (((1,), (0,)), ((), ())), preferred_element_type=F32)]
    ppermute x69, waiting for transfers between devices: 110 us -> 118 us  [swap(): return lax.ppermute(value, axis, [(i, i ^ mask) for i in range(size)])]
    dot_general x23 -> x14, matrix products: 53.9 us -> 49.7 us  [mm_t(): lax.dot_general(a, b, (((1,), (1,)), ((), ())), preferred_element_type=F32)]
    unnamed x295 -> x227, local copies, waits for them, and re-layouts: 26.2 us -> 26.8 us
  transfers between devices with their start and end apart: 69 -> 69, of which waited for: 25 -> 27; matrix products, arithmetic and copies ran while one was open for 34% -> 33% of each run, Pallas kernels for 10% -> 11%
where the time goes in v12:
time: 448 us; the launch traced here: 441 us
  waiting for transfers between devices  118 us (26%)
  matrix products  101 us (23%)
  Pallas kernels  64.8 us (14%)
  local copies, waits for them, and re-layouts  60.1 us (13%)
  starting transfers between devices  58.4 us (13%)
  other arithmetic  34.5 us (8%)
  between operations  5.15 us (1%)
    ppermute x69, waiting for transfers between devices, swap(): return lax.ppermute(value, axis, [(i, i ^ mask) for i in range(size)])  118 us
    ppermute x69, starting transfers between devices, swap(): return lax.ppermute(value, axis, [(i, i ^ mask) for i in range(size)])  58.4 us
    dot_general x14, matrix products, mm_t(): lax.dot_general(a, b, (((1,), (1,)), ((), ())), preferred_element_type=F32)  49.7 us
    dot_general x14, matrix products, mm(): lax.dot_general(a, b, (((1,), (0,)), ((), ())), preferred_element_type=F32)  46.1 us
    unnamed x227, local copies, waits for them, and re-layouts  26.8 us
    pallas_call x2, Pallas kernels, place_weights(): pl.pallas_call(functools.partial(place_kernel, count=count, width=width,...  14 us
    pallas_call x3, Pallas kernels, row_call(): pl.pallas_call(kernel, out_shape=[jax.ShapeDtypeStruct((rows, wide), d) f...  13.2 us
    pallas_call x1, Pallas kernels, attend_back(): pl.pallas_call(functools.partial(attend_back_kernel, heads=heads, factor=...  9.74 us
  transfers between devices with their start and end apart: 69, of which 27 were waited for; matrix products, arithmetic and copies ran while one was open for 33% of the time, Pallas kernels for 11%

profile of v12, /device:TPU:0, one launch (start us, length us, event | category | flops | bytes accessed | tf_op | source)
XLA Modules:
  0.0 441.1 jit_solution(8469398923412153602)
XLA Ops:
  21.6 5.8 %collective-permute-done.5 = bf16[128,1536]{1,0:T(8,128)(2,1)S(1)} collective-permute-done((bf16[128,1536]{1,0:T(8,128)(2,1)}, bf16[128,1536]{1,0:T(8,128)(2,1)S(1)}, u32[]{:S(2)}, u32[]{:S(2)}) %collective-permute-start.5) | collective-permute-done | bytes 393248 | tf_op jit(solution)/shard_map/ppermute | solution.py:51
  37.6 14.8 %collective-permute-done.3 = bf16[1,288,256]{2,1,0:T(8,128)(2,1)S(1)} collective-permute-done((bf16[1,288,256]{2,1,0:T(8,128)(2,1)}, bf16[1,288,256]{2,1,0:T(8,128)(2,1)S(1)}, u32[]{:S(2)}, u32[]{:S(2)}) %collective-permute-start.3) | collective-permute-done | bytes 147488 | tf_op jit(solution)/shard_map/ppermute | solution.py:51
  106.7 6.5 %place_weights.2 = (bf16[2048,768]{1,0:T(8,128)(2,1)}, bf16[2048,768]{1,0:T(8,128)(2,1)}) custom-call(s32[2]{0:T(128)} %pad_add_fusion.1.at_ref, bf16[256,1536]{1,0:T(8,128)(2,1)} %get-tuple-element.135.refs_0_, bf16[384,1536]{1,0:T(8,128)(2,1)} %constant_dynamic-update-slice_fusion.12.refs_1_, bf16[384,1536]{1,0:T(8,128)(2,1)} %collective-permute-done.14.refs_2_, ...), custom_call_target="tpu_custom_call" | custom-call | bytes 12582912 | tf_op jit(solution)/shard_map/place_weights/pallas_call | solution.py:208
  113.2 5.9 %add_convert_fusion.5 = bf16[768,768]{1,0:T(8,128)(2,1)} fusion(f32[768,768]{1,0:T(8,128)} %fusion.134, bf16[768,2048]{1,0:T(8,128)(2,1)S(1)} %constant_dynamic-update-slice_fusion, bf16[2048,768]{1,0:T(8,128)(2,1)} %get-tuple-element.143, f32[768]{0:T(1024)S(1)} %get-tuple-element.292), kind=kOutput, calls=%fused_computation.32 | convolution fusion | flops 2417688576 | bytes 9833472 | tf_op jit(solution)/shard_map/dot_general | solution.py:38
  127.2 7.2 %attend.1 = (bf16[4,3,64,256]{3,2,1,0:T(8,128)(2,1)}, bf16[4,3,64,256]{3,2,1,0:T(8,128)(2,1)}, f32[3,512,2]{2,1,0:T(8,128)}) custom-call(s32[512,1]{1,0:T(8,128)} %copy.49.pq, s32[1,512]{1,0:T(1,128)} %bitcast.221, s32[3,512,1]{2,1,0:T(8,128)} %copy.50.lq, s32[3,1,512]{2,1,0:T(1,128)} %broadcast_in_dim.87.lk, bf16[4,3,64,768]{3,2,1,0:T(8,128)(2,1)} %bitcast.203, ...), custom_call_target="tpu_custom_call" | custom-call | flops 805306368 | bytes 3145728 | tf_op jit(solution)/shard_map/attend/pallas_call | solution.py:430
  147.6 7.9 %collective-permute-done.22 = bf16[192,2048]{1,0:T(8,128)(2,1)S(1)} collective-permute-done((bf16[192,2048]{1,0:T(8,128)(2,1)S(1)}, bf16[192,2048]{1,0:T(8,128)(2,1)S(1)}, u32[]{:S(2)}, u32[]{:S(2)}) %collective-permute-start.22) | collective-permute-done | bytes 786464 | tf_op jit(solution)/shard_map/ppermute | solution.py:51
  157.7 6.3 %collective-permute-done.27 = bf16[96,2048]{1,0:T(8,128)(2,1)S(1)} collective-permute-done((bf16[96,2048]{1,0:T(8,128)(2,1)S(1)}, bf16[96,2048]{1,0:T(8,128)(2,1)S(1)}, u32[]{:S(2)}, u32[]{:S(2)}) %collective-permute-start.27) | collective-permute-done | bytes 393248 | tf_op jit(solution)/shard_map/ppermute | solution.py:51
  167.2 5.9 %collective-permute-done.24 = bf16[96,2048]{1,0:T(8,128)(2,1)S(1)} collective-permute-done((bf16[96,2048]{1,0:T(8,128)(2,1)S(1)}, bf16[96,2048]{1,0:T(8,128)(2,1)S(1)}, u32[]{:S(2)}, u32[]{:S(2)}) %collective-permute-start.24) | collective-permute-done | bytes 393248 | tf_op jit(solution)/shard_map/ppermute | solution.py:51
  176.6 10.7 %add_convert_fusion.3 = bf16[768,2048]{1,0:T(8,128)(2,1)} fusion(f32[768,2048]{1,0:T(8,128)S(1)} %fusion.74, bf16[768,2048]{1,0:T(8,128)(2,1)S(1)} %constant_dynamic-update-slice_fusion.15, bf16[2048,2048]{1,0:T(8,128)(2,1)} %copy-done.16), kind=kOutput, calls=%fused_computation.13 | convolution fusion | flops 6445596672 | bytes 20971520 | tf_op jit(solution)/shard_map/dot_general | solution.py:42
  198.4 16.4 %collective-permute-done.30 = bf16[192,2048]{1,0:T(8,128)(2,1)S(1)} collective-permute-done((bf16[192,2048]{1,0:T(8,128)(2,1)}, bf16[192,2048]{1,0:T(8,128)(2,1)S(1)}, u32[]{:S(2)}, u32[]{:S(2)}) %collective-permute-start.30) | collective-permute-done | bytes 786464 | tf_op jit(solution)/shard_map/ppermute | solution.py:51
  217.9 7.5 %place_weights.3 = bf16[2048,2048]{1,0:T(8,128)(2,1)} custom-call(s32[2]{0:T(128)} %pad_add_fusion.1.at_ref, bf16[256,2048]{1,0:T(8,128)(2,1)} %get-tuple-element.157.refs_0_, bf16[384,2048]{1,0:T(8,128)(2,1)} %constant_dynamic-update-slice_fusion.5.refs_1_, bf16[384,2048]{1,0:T(8,128)(2,1)} %collective-permute-done.34.refs_2_, ...), custom_call_target="tpu_custom_call" | custom-call | bytes 16777216 | tf_op jit(solution)/shard_map/place_weights/pallas_call | solution.py:208
  233.7 12.3 %multiply_convert_fusion = (bf16[768,2048]{1,0:T(8,128)(2,1)S(1)}, bf16[768,2048]{1,0:T(8,128)(2,1)}) fusion(bf16[768,2048]{1,0:T(8,128)(2,1)} %add_convert_fusion.3, f32[2048]{0:T(1024)S(1)} %maximum_convert_fusion, f32[768,2048]{1,0:T(8,128)S(1)} %fusion.73, bf16[768,2048]{1,0:T(8,128)(2,1)S(1)} %constant_dynamic-update-slice_fusion.20, ...), kind=kOutput, calls=%fused_computation.10 | convolution fusion | flops 6466043904 | bytes 27271168 | tf_op jit(solution)/shard_map/dot_general | solution.py:38
  250.2 6.7 %fusion.135 = f32[768,2048]{1,0:T(8,128)S(1)} fusion(bf16[768,2048]{1,0:T(8,128)(2,1)S(1)} %copy-done.14, bf16[2048,2048]{1,0:T(8,128)(2,1)S(1)} %bitcast.191), kind=kOutput, calls=%fused_computation.335 | convolution fusion | flops 6442450944 | bytes 17825792 | tf_op jit(solution)/shard_map/dot_general | solution.py:42
  263.9 5.9 %collective-permute-done.40 = bf16[96,2048]{1,0:T(8,128)(2,1)S(1)} collective-permute-done((bf16[96,2048]{1,0:T(8,128)(2,1)S(1)}, bf16[96,2048]{1,0:T(8,128)(2,1)S(1)}, u32[]{:S(2)}, u32[]{:S(2)}) %collective-permute-start.40) | collective-permute-done | bytes 393248 | tf_op jit(solution)/shard_map/ppermute | solution.py:51
  277.8 5.0 %collective-permute-done.60.refs_1_ = bf16[1,64,2048]{2,1,0:T(8,128)(2,1)} collective-permute-done((bf16[1,64,2048]{2,1,0:T(8,128)(2,1)}, bf16[1,64,2048]{2,1,0:T(8,128)(2,1)}, u32[]{:S(2)}, u32[]{:S(2)}) %collective-permute-start.60) | collective-permute-done | bytes 262176 | tf_op jit(solution)/shard_map/ppermute | solution.py:51
  290.3 5.0 %norm_back.2 = (f32[192,2048]{1,0:T(8,128)}, bf16[192,2048]{1,0:T(8,128)(2,1)}) custom-call(f32[192,2048]{1,0:T(8,128)} %get-tuple-element.153.values, f32[4,2048]{1,0:T(4,128)} %convert_element_type.279.vectors, bf16[192,2048]{1,0:T(8,128)(2,1)} %bitcast.192, bf16[192,2048]{1,0:T(8,128)(2,1)} %slice.452.refs_0_, ...), custom_call_target="tpu_custom_call" | custom-call | flops 7864320 | bytes 78643200 | tf_op jit(solution)/shard_map/norm_back/pallas_call | solution.py:335
  300.5 9.3 %fusion.138 = f32[768,2048]{1,0:T(8,128)S(1)} fusion(bf16[768,2048]{1,0:T(8,128)(2,1)S(1)} %copy-done.12, bf16[2048,2048]{1,0:T(8,128)(2,1)} %copy-done.16), kind=kOutput, calls=%fused_computation.338 | convolution fusion | flops 6442450944 | bytes 17825792 | tf_op jit(solution)/shard_map/dot_general | solution.py:38
  317.6 9.1 %collective-permute-done.45 = bf16[96,2048]{1,0:T(8,128)(2,1)S(1)} collective-permute-done((bf16[96,2048]{1,0:T(8,128)(2,1)S(1)}, bf16[96,2048]{1,0:T(8,128)(2,1)S(1)}, u32[]{:S(2)}, u32[]{:S(2)}) %collective-permute-start.45) | collective-permute-done | bytes 393248 | tf_op jit(solution)/shard_map/ppermute | solution.py:51
  339.4 9.7 %attend_back.1 = (bf16[4,3,64,768]{3,2,1,0:T(8,128)(2,1)}, bf16[4,3,64,768]{3,2,1,0:T(8,128)(2,1)}) custom-call(s32[512,1]{1,0:T(8,128)} %copy.49.pq, s32[1,512]{1,0:T(1,128)} %bitcast.222, s32[3,512,1]{2,1,0:T(8,128)} %copy.50.lq, s32[3,1,512]{2,1,0:T(1,128)} %broadcast_in_dim.87.lk, bf16[4,3,64,768]{3,2,1,0:T(8,128)(2,1)} %bitcast.204, ...), custom_call_target="tpu_custom_call" | custom-call | flops 2013265920 | bytes 5505024 | tf_op jit(solution)/shard_map/attend_back/pallas_call | solution.py:487
  349.2 7.6 %fusion.144 = f32[768,2048]{1,0:T(8,128)} fusion(bf16[768,768]{1,0:T(8,128)(2,1)} %bitcast.200, bf16[2048,768]{1,0:T(8,128)(2,1)} %get-tuple-element.138), kind=kOutput, calls=%fused_computation.344 | convolution fusion | flops 2415919104 | bytes 10616832 | tf_op jit(solution)/shard_map/dot_general | solution.py:42
  366.6 5.0 %add_convert_fusion = bf16[768,2048]{1,0:T(8,128)(2,1)S(1)} fusion(f32[768,2048]{1,0:T(8,128)S(1)} %fusion.29, f32[768,2048]{1,0:T(8,128)} %fusion.144, bf16[768,768]{1,0:T(8,128)(2,1)S(1)} %collective-permute-done.48, bf16[2048,768]{1,0:T(8,128)(2,1)S(1)} %copy-done.80), kind=kOutput, calls=%fused_computation.7 | convolution fusion | flops 2420637696 | bytes 20054016 | tf_op jit(solution)/shard_map/dot_general | solution.py:42
  380.8 12.4 %collective-permute-done.50 = bf16[96,2048]{1,0:T(8,128)(2,1)} collective-permute-done((bf16[96,2048]{1,0:T(8,128)(2,1)}, bf16[96,2048]{1,0:T(8,128)(2,1)}, u32[]{:S(2)}, u32[]{:S(2)}) %collective-permute-start.50) | collective-permute-done | bytes 393248 | tf_op jit(solution)/shard_map/ppermute | solution.py:51
  420.1 8.1 %collective-permute-done.57.refs_1_ = bf16[192,2048]{1,0:T(8,128)(2,1)S(1)} collective-permute-done((bf16[192,2048]{1,0:T(8,128)(2,1)}, bf16[192,2048]{1,0:T(8,128)(2,1)S(1)}, u32[]{:S(2)}, u32[]{:S(2)}) %collective-permute-start.57) | collective-permute-done | bytes 786464 | tf_op jit(solution)/shard_map/ppermute | solution.py:51
  429.1 4.5 %norm_back.3 = bf16[192,2048]{1,0:T(8,128)(2,1)} custom-call(bf16[192,2048]{1,0:T(8,128)(2,1)} %bitcast.186, f32[4,2048]{1,0:T(4,128)} %convert_element_type.279.vectors, f32[192,2048]{1,0:T(8,128)} %get-tuple-element.192.base, bf16[192,2048]{1,0:T(8,128)(2,1)} %fusion.118, bf16[192,2048]{1,0:T(8,128)(2,1)} %copy-done.31, ...), custom_call_target="tpu_custom_call" | custom-call | flops 7864320 | bytes 78643200 | tf_op jit(solution)/shard_map/norm_back/pallas_call | solution.py:335
  (523 shorter events, 240.3 us)
Async XLA Ops:
  0.7 30.5 %collective-permute-start.1 = (bf16[1024,2048]{1,0:T(8,128)(2,1)}, bf16[1024,2048]{1,0:T(8,128)(2,1)}, u32[]{:S(2)}, u32[]{:S(2)}) collective-permute-start(bf16[1024,2048]{1,0:T(8,128)(2,1)} %param.47), channel_id=1, source_target_pairs={{0,4},{4,0},{8,12},{12,8},{16,20},{20,16},{24,28},{28,24},{1,5},{5... | collective-permute-start | bytes 12582920 | tf_op jit(solution)/shard_map/ppermute | solution.py:51
  1.2 30.0 %collective-permute-start = (bf16[256,2048]{1,0:T(8,128)(2,1)}, bf16[256,2048]{1,0:T(8,128)(2,1)S(1)}, u32[]{:S(2)}, u32[]{:S(2)}) collective-permute-start(bf16[256,2048]{1,0:T(8,128)(2,1)} %param.41), channel_id=1, source_target_pairs={{0,4},{4,0},{8,12},{12,8},{16,20},{20,16},{24,28},{28,24},{1,5},{5... | collective-permute-start | bytes 3145736 | tf_op jit(solution)/shard_map/ppermute | solution.py:51
  18.8 36.1 %collective-permute-start.7 = (bf16[128,2048]{1,0:T(8,128)(2,1)}, bf16[128,2048]{1,0:T(8,128)(2,1)}, u32[]{:S(2)}, u32[]{:S(2)}) collective-permute-start(bf16[128,2048]{1,0:T(8,128)(2,1)} %get-tuple-element.122), channel_id=1, source_target_pairs={{0,8},{4,12},{8,0},{12,4},{16,24},{20,28},{24,16},{28,20},{1,9},{5... | collective-permute-start | bytes 1572872 | tf_op jit(solution)/shard_map/ppermute | solution.py:51
  27.4 27.5 %collective-permute-start.8 = (bf16[128,2048]{1,0:T(8,128)(2,1)}, bf16[128,2048]{1,0:T(8,128)(2,1)S(1)}, u32[]{:S(2)}, u32[]{:S(2)}) collective-permute-start(bf16[128,2048]{1,0:T(8,128)(2,1)} %get-tuple-element.123), channel_id=1, source_target_pairs={{0,16},{4,20},{8,24},{12,28},{16,0},{20,4},{24,8},{28,12},{1,17},{... | collective-permute-start | bytes 1572872 | tf_op jit(solution)/shard_map/ppermute | solution.py:51
  30.4 24.5 %collective-permute-start.9 = (bf16[128,2048]{1,0:T(8,128)(2,1)}, bf16[128,2048]{1,0:T(8,128)(2,1)S(1)}, u32[]{:S(2)}, u32[]{:S(2)}) collective-permute-start(bf16[128,2048]{1,0:T(8,128)(2,1)} %get-tuple-element.124), channel_id=1, source_target_pairs={{0,24},{4,28},{8,16},{12,20},{16,8},{20,12},{24,0},{28,4},{1,25},{... | collective-permute-start | bytes 1572872 | tf_op jit(solution)/shard_map/ppermute | solution.py:51
  34.7 21.8 %collective-permute-start.2 = (bf16[48,3072]{1,0:T(8,128)(2,1)}, bf16[48,3072]{1,0:T(8,128)(2,1)S(1)}, u32[]{:S(2)}, u32[]{:S(2)}) collective-permute-start(bf16[48,3072]{1,0:T(8,128)(2,1)} %get-tuple-element.140), channel_id=1, source_target_pairs={{0,4},{4,0},{8,12},{12,8},{16,20},{20,16},{24,28},{28,24},{1,5},{5... | collective-permute-start | bytes 884744 | tf_op jit(solution)/shard_map/ppermute | solution.py:51
  52.3 37.8 %collective-permute-start.14 = (bf16[384,1536]{1,0:T(8,128)(2,1)}, bf16[384,1536]{1,0:T(8,128)(2,1)}, u32[]{:S(2)}, u32[]{:S(2)}) collective-permute-start(bf16[384,1536]{1,0:T(8,128)(2,1)} %constant_dynamic-update-slice_fusion.12.refs_1_), channel_id=1, source_target_pairs={{0,1},{1,0},{2,3},{3,2},{4,5},{5,4},{6,7},{7,6},{8,9},{9,8},{10,11... | collective-permute-start | bytes 3538952 | tf_op jit(solution)/shard_map/ppermute | solution.py:51
  57.8 26.4 %collective-permute-start.10 = (bf16[192,2048]{1,0:T(8,128)(2,1)}, bf16[192,2048]{1,0:T(8,128)(2,1)}, u32[]{:S(2)}, u32[]{:S(2)}) collective-permute-start(bf16[192,2048]{1,0:T(8,128)(2,1)} %fusion.15), channel_id=1, source_target_pairs={{0,8},{4,12},{8,0},{12,4},{16,24},{20,28},{24,16},{28,20},{1,9},{5... | collective-permute-start | bytes 2359304 | tf_op jit(solution)/shard_map/ppermute | solution.py:51
  59.4 28.4 %collective-permute-start.11 = (bf16[192,2048]{1,0:T(8,128)(2,1)}, bf16[192,2048]{1,0:T(8,128)(2,1)}, u32[]{:S(2)}, u32[]{:S(2)}) collective-permute-start(bf16[192,2048]{1,0:T(8,128)(2,1)} %fusion.15), channel_id=1, source_target_pairs={{0,16},{4,20},{8,24},{12,28},{16,0},{20,4},{24,8},{28,12},{1,17},{... | collective-permute-start | bytes 2359304 | tf_op jit(solution)/shard_map/ppermute | solution.py:51
  135.7 20.5 %collective-permute-start.23 = (bf16[192,2048]{1,0:T(8,128)(2,1)S(1)}, bf16[192,2048]{1,0:T(8,128)(2,1)S(1)}, u32[]{:S(2)}, u32[]{:S(2)}) collective-permute-start(bf16[192,2048]{1,0:T(8,128)(2,1)S(1)} %bitcast.194), channel_id=1, source_target_pairs={{0,16},{4,20},{8,24},{12,28},{16,0},{20,4},{24,8},{28,12},{1,17},{... | collective-permute-start | bytes 2359304 | tf_op jit(solution)/shard_map/ppermute | solution.py:51
  142.1 21.9 %collective-permute-start.27 = (bf16[96,2048]{1,0:T(8,128)(2,1)S(1)}, bf16[96,2048]{1,0:T(8,128)(2,1)S(1)}, u32[]{:S(2)}, u32[]{:S(2)}) collective-permute-start(bf16[96,2048]{1,0:T(8,128)(2,1)S(1)} %get-tuple-element.231), channel_id=1, source_target_pairs={{0,8},{4,12},{8,0},{12,4},{16,24},{20,28},{24,16},{28,20},{1,9},{5... | collective-permute-start | bytes 1179656 | tf_op jit(solution)/shard_map/ppermute | solution.py:51
  143.4 21.2 %collective-permute-start.26 = (bf16[96,2048]{1,0:T(8,128)(2,1)S(1)}, bf16[96,2048]{1,0:T(8,128)(2,1)S(1)}, u32[]{:S(2)}, u32[]{:S(2)}) collective-permute-start(bf16[96,2048]{1,0:T(8,128)(2,1)S(1)} %get-tuple-element.233), channel_id=1, source_target_pairs={{0,16},{4,20},{8,24},{12,28},{16,0},{20,4},{24,8},{28,12},{1,17},{... | collective-permute-start | bytes 1179656 | tf_op jit(solution)/shard_map/ppermute | solution.py:51
  146.2 47.6 %collective-permute-start.34 = (bf16[384,2048]{1,0:T(8,128)(2,1)}, bf16[384,2048]{1,0:T(8,128)(2,1)}, u32[]{:S(2)}, u32[]{:S(2)}) collective-permute-start(bf16[384,2048]{1,0:T(8,128)(2,1)} %constant_dynamic-update-slice_fusion.5.refs_1_), channel_id=1, source_target_pairs={{0,1},{1,0},{2,3},{3,2},{4,5},{5,4},{6,7},{7,6},{8,9},{9,8},{10,11... | collective-permute-start | bytes 4718600 | tf_op jit(solution)/shard_map/ppermute | solution.py:51
  164.9 23.4 %collective-permute-start.28 = (bf16[192,2048]{1,0:T(8,128)(2,1)S(1)}, bf16[192,2048]{1,0:T(8,128)(2,1)S(1)}, u32[]{:S(2)}, u32[]{:S(2)}) collective-permute-start(bf16[192,2048]{1,0:T(8,128)(2,1)S(1)} %pad_maximum_fusion.5), channel_id=1, source_target_pairs={{0,8},{4,12},{8,0},{12,4},{16,24},{20,28},{24,16},{28,20},{1,9},{5... | collective-permute-start | bytes 2359304 | tf_op jit(solution)/shard_map/ppermute | solution.py:51
  166.5 22.1 %collective-permute-start.29 = (bf16[192,2048]{1,0:T(8,128)(2,1)S(1)}, bf16[192,2048]{1,0:T(8,128)(2,1)S(1)}, u32[]{:S(2)}, u32[]{:S(2)}) collective-permute-start(bf16[192,2048]{1,0:T(8,128)(2,1)S(1)} %pad_maximum_fusion.6), channel_id=1, source_target_pairs={{0,16},{4,20},{8,24},{12,28},{16,0},{20,4},{24,8},{28,12},{1,17},{... | collective-permute-start | bytes 2359304 | tf_op jit(solution)/shard_map/ppermute | solution.py:51
  193.9 24.0 %collective-permute-start.36 = (bf16[384,2048]{1,0:T(8,128)(2,1)}, bf16[384,2048]{1,0:T(8,128)(2,1)}, u32[]{:S(2)}, u32[]{:S(2)}) collective-permute-start(bf16[384,2048]{1,0:T(8,128)(2,1)} %constant_dynamic-update-slice_fusion.5.refs_1_), channel_id=1, source_target_pairs={{0,4},{4,0},{8,12},{12,8},{16,20},{20,16},{24,28},{28,24},{1,5},{5... | collective-permute-start | bytes 4718600 | tf_op jit(solution)/shard_map/ppermute | solution.py:51
  193.9 24.0 %collective-permute-start.37 = (bf16[384,2048]{1,0:T(8,128)(2,1)}, bf16[384,2048]{1,0:T(8,128)(2,1)}, u32[]{:S(2)}, u32[]{:S(2)}) collective-permute-start(bf16[384,2048]{1,0:T(8,128)(2,1)} %collective-permute-done.34.refs_2_), channel_id=1, source_target_pairs={{0,4},{4,0},{8,12},{12,8},{16,20},{20,16},{24,28},{28,24},{1,5},{5... | collective-permute-start | bytes 4718600 | tf_op jit(solution)/shard_map/ppermute | solution.py:51
  196.6 21.3 %collective-permute-start.35 = (bf16[256,2048]{1,0:T(8,128)(2,1)}, bf16[256,2048]{1,0:T(8,128)(2,1)}, u32[]{:S(2)}, u32[]{:S(2)}) collective-permute-start(bf16[256,2048]{1,0:T(8,128)(2,1)} %get-tuple-element.157.refs_0_), channel_id=1, source_target_pairs={{0,4},{4,0},{8,12},{12,8},{16,20},{20,16},{24,28},{28,24},{1,5},{5... | collective-permute-start | bytes 3145736 | tf_op jit(solution)/shard_map/ppermute | solution.py:51
  284.6 95.3 %collective-permute-start.61 = (bf16[2,64,2048]{2,1,0:T(8,128)(2,1)}, bf16[2,64,2048]{2,1,0:T(8,128)(2,1)}, u32[]{:S(2)}, u32[]{:S(2)}) collective-permute-start(bf16[2,64,2048]{2,1,0:T(8,128)(2,1)} %pad_maximum_fusion.12), channel_id=1, source_target_pairs={{0,2},{1,3},{2,0},{3,1},{4,6},{5,7},{6,4},{7,5},{8,10},{9,11},{10,... | collective-permute-start | bytes 1572872 | tf_op jit(solution)/shard_map/ppermute | solution.py:51
  334.6 22.3 %collective-permute-start.55 = (bf16[96,2304]{1,0:T(8,128)(2,1)}, bf16[96,2304]{1,0:T(8,128)(2,1)}, u32[]{:S(2)}, u32[]{:S(2)}) collective-permute-start(bf16[96,2304]{1,0:T(8,128)(2,1)} %get-tuple-element.245), channel_id=1, source_target_pairs={{0,8},{4,12},{8,0},{12,4},{16,24},{20,28},{24,16},{28,20},{1,9},{5... | collective-permute-start | bytes 1327112 | tf_op jit(solution)/shard_map/ppermute | solution.py:51
  337.4 23.1 %collective-permute-start.53 = (bf16[96,2304]{1,0:T(8,128)(2,1)}, bf16[96,2304]{1,0:T(8,128)(2,1)}, u32[]{:S(2)}, u32[]{:S(2)}) collective-permute-start(bf16[96,2304]{1,0:T(8,128)(2,1)} %get-tuple-element.244), channel_id=1, source_target_pairs={{0,16},{4,20},{8,24},{12,28},{16,0},{20,4},{24,8},{28,12},{1,17},{... | collective-permute-start | bytes 1327112 | tf_op jit(solution)/shard_map/ppermute | solution.py:51
  359.1 42.5 %collective-permute-start.56 = (bf16[192,2304]{1,0:T(8,128)(2,1)}, bf16[192,2304]{1,0:T(8,128)(2,1)}, u32[]{:S(2)}, u32[]{:S(2)}) collective-permute-start(bf16[192,2304]{1,0:T(8,128)(2,1)} %pad_maximum_fusion.3), channel_id=1, source_target_pairs={{0,16},{4,20},{8,24},{12,28},{16,0},{20,4},{24,8},{28,12},{1,17},{... | collective-permute-start | bytes 2654216 | tf_op jit(solution)/shard_map/ppermute | solution.py:51
  362.7 38.9 %collective-permute-start.54 = (bf16[192,2304]{1,0:T(8,128)(2,1)}, bf16[192,2304]{1,0:T(8,128)(2,1)}, u32[]{:S(2)}, u32[]{:S(2)}) collective-permute-start(bf16[192,2304]{1,0:T(8,128)(2,1)} %pad_maximum_fusion.2), channel_id=1, source_target_pairs={{0,8},{4,12},{8,0},{12,4},{16,24},{20,28},{24,16},{28,20},{1,9},{5... | collective-permute-start | bytes 2654216 | tf_op jit(solution)/shard_map/ppermute | solution.py:51
  412.7 23.3 %collective-permute-start.68 = (bf16[2,48,768]{2,1,0:T(8,128)(2,1)}, bf16[2,48,768]{2,1,0:T(8,128)(2,1)}, u32[]{:S(2)}, u32[]{:S(2)}) collective-permute-start(bf16[2,48,768]{2,1,0:T(8,128)(2,1)} %pad_maximum_fusion.25), channel_id=1, source_target_pairs={{0,2},{1,3},{2,0},{3,1},{4,6},{5,7},{6,4},{7,5},{8,10},{9,11},{10,... | collective-permute-start | bytes 442376 | tf_op jit(solution)/shard_map/ppermute | solution.py:51
  (146 other events, 1858.8 us)
